TPU v7x, 32 devices: a whole 2x2x4 slice. The times are simulated.
32 devices in a mesh: blk: 4 (over z), shard: 4 (over x, core), head: 2 (over y).
Axes of the slice: x: 2, y: 2, z: 4, core: 2. Of those that a mesh axis runs over, the one named last changes fastest.
Arguments:
- inputs: float32 [2048, 768], P(('blk', 'shard')), may hold values from -6 to 6
- cotangent: float32 [2048, 768], P(('blk', 'shard')), may hold values from -6 to 6
- weights: float32 [768, 6528], P(('blk', 'shard'), 'head'), may hold values from -80 to 80
- gains: float32 [2, 768], P(None, ('blk', 'shard')), may hold values from 0.25 to 1.75
- weight_moment: float32 [768, 6528], P(('blk', 'shard'), 'head'), may hold values from -4 to 4
- weight_second: float32 [768, 6528], P(('blk', 'shard'), 'head'), may hold values from 0.5 to 5
- gain_moment: float32 [2, 768], P(None, ('blk', 'shard')), may hold values from -4 to 4
- gain_second: float32 [2, 768], P(None, ('blk', 'shard')), may hold values from 512 to 20480
Outputs:
- outputs: float32 [2048, 768], P(('blk', 'shard'))
- input_grad: float32 [2048, 768], P(('blk', 'shard'))
- weight_grad: float32 [768, 6528], P(('blk', 'shard'), 'head')
- gain_grad: float32 [2, 768], P(None, ('blk', 'shard'))
- new_weights: float32 [768, 6528], P(('blk', 'shard'), 'head')
- new_weight_moment: float32 [768, 6528], P(('blk', 'shard'), 'head')
- new_weight_second: float32 [768, 6528], P(('blk', 'shard'), 'head')
- new_gains: float32 [2, 768], P(None, ('blk', 'shard'))
- new_gain_moment: float32 [2, 768], P(None, ('blk', 'shard'))
- new_gain_second: float32 [2, 768], P(None, ('blk', 'shard'))
All inputs are finite; a program needn't handle non-finite values.
Results may differ from a plain program's by a relative error of at most 0.025.
The roundings to bfloat16 on the way count: a program that leaves them out, or rounds other values in their place, can miss the bound.
Values may be sent and summed in bfloat16 or wider, within the bound.
No kernel may reach another device: no remote copies, remote signals or barrier semaphores. Data moves between devices by JAX's collectives and lax.ppermute only.
A program may use at most 192 MiB of HBM per device.

v0:
```python
from functools import partial
import math

import jax
import jax.numpy as jnp
from jax import lax
from jax.experimental import pallas as pl
from jax.experimental.pallas import tpu as pltpu
from jax.sharding import PartitionSpec as P


HEADS = 12
HEAD_DIM = 64
FF = 1152
STEP = 3

NORM_EPS = 1e-05
THETA = 160000.0
BETA_ONE = 0.9
BETA_TWO = 0.98
LEARN_RATE = 0.2
ADAM_EPS = 1e-06
DECAY = 0.01
NEG_LARGE = -1e30
SCALE = 1.0 / math.sqrt(HEAD_DIM)
TOKENS_AX = ("blk", "shard")
F32 = jnp.float32
BF16 = jnp.bfloat16
KEY_ROWS = 2048
SUB_ROWS = 512


VM = pl.BlockSpec(memory_space=pltpu.VMEM)
SM = pl.BlockSpec(memory_space=pltpu.SMEM)
ANY = pl.BlockSpec(memory_space=pl.ANY)


def sds(shape, dtype):
    return jax.ShapeDtypeStruct(shape, dtype)


def dot_nn(a, b):
    return lax.dot_general(a, b, (((1,), (0,)), ((), ())), preferred_element_type=F32)


def dot_nt(a, b):
    return lax.dot_general(a, b, (((1,), (1,)), ((), ())), preferred_element_type=F32)


def dot_tn(a, b):
    return lax.dot_general(a, b, (((0,), (0,)), ((), ())), preferred_element_type=F32)


def swap(x, axis, bits):
    size = lax.axis_size(axis)
    return lax.ppermute(x, axis, [(i, i ^ bits) for i in range(size)])


def staged():
    return lax.axis_size("blk") == 4 and lax.axis_size("shard") == 4


def chunk_order():
    return [z * 4 + x * 2 + c for c in range(2) for x in range(2) for z in range(4)]


def gather(x):
    if not staged():
        return [lax.all_gather(x, TOKENS_AX, axis=0, tiled=True)]
    got = {0: x}
    for z in range(1, 4):
        got[z * 4] = swap(x, "blk", z)
    for z in range(4):
        got[z * 4 + 2] = swap(got[z * 4], "shard", 2)
    for z in range(4):
        for h in (0, 2):
            got[z * 4 + h + 1] = swap(got[z * 4 + h], "shard", 1)
    return [got[j] for j in chunk_order()]


def add_kernel(*refs):
    keep, recv = refs[0], refs[1]
    for i, out in enumerate(refs[2:]):
        rows = out.shape[0]
        at = pl.ds(i * rows, rows)
        out[...] = (keep[at, :].astype(F32) + recv[at, :].astype(F32)).astype(BF16)


def scatter_sum(parts):
    if not staged():
        return [lax.psum_scatter(parts[0], TOKENS_AX, scatter_dimension=0, tiled=True)]
    keep, send = parts
    rows, cols = keep.shape[0] // 8, keep.shape[1]
    recv = swap(send, "shard", 1)
    s = pl.pallas_call(
        add_kernel,
        out_shape=[sds((rows, cols), BF16)] * 8,
        in_specs=[VM, VM],
        out_specs=[VM] * 8,
        name="pair_add",
    )(keep, recv)
    t = {}
    for z in (3, 2, 1, 0):
        got = swap(s[4 + z], "shard", 2)
        t[z] = (s[z].astype(F32) + got.astype(F32)).astype(BF16)
    return [t[0]] + [swap(t[z], "blk", z) for z in (3, 2, 1)]


def total(terms):
    out = terms[0].astype(F32)
    for term in terms[1:]:
        out = out + term.astype(F32)
    return out


def weight_copies(order_ref, chunks, dst, sems, cols=None):
    rows = chunks[0].shape[0]
    copies = []
    for i, chunk in enumerate(chunks):
        src = chunk if cols is None else chunk.at[:, pl.ds(cols[0], cols[1])]
        if len(chunks) == 1:
            at = pl.ds(0, rows)
        else:
            at = pl.ds(pl.multiple_of((order_ref[0] ^ chunk_order()[i]) * rows, 16), rows)
        copies.append(pltpu.make_async_copy(src, dst.at[at, :], sems.at[i]))
    for copy in copies:
        copy.start()
    return copies


def emit_blocks(order_ref, acc, outs):
    if len(outs) == 1:
        outs[0][...] = acc[...].astype(BF16)
        return
    rows = outs[0].shape[0] // 8
    for i, j in enumerate(chunk_order()):
        at = pl.ds(pl.multiple_of((order_ref[0] ^ j) * rows, 8), rows)
        outs[i // 8][pl.ds((i % 8) * rows, rows), :] = acc[at, :].astype(BF16)


def norm_parts(v):
    centre = v - jnp.mean(v, axis=-1, keepdims=True)
    inv = lax.rsqrt(jnp.mean(centre * centre, axis=-1, keepdims=True) + NORM_EPS)
    return centre * inv, inv


def norm_back(u, xhat, inv, g):
    s = u * g
    return inv * (
        s
        - jnp.mean(s, axis=-1, keepdims=True)
        - xhat * jnp.mean(s * xhat, axis=-1, keepdims=True)
    )


def low_half(shape):
    lane = lax.broadcasted_iota(jnp.int32, shape, 1)
    return (lane & (HEAD_DIM - 1)) < HEAD_DIM // 2


def turn(u):
    width = u.shape[1]
    half = HEAD_DIM // 2
    left = pltpu.roll(u, width - half, 1)
    right = pltpu.roll(u, half, 1)
    return left, right, low_half(u.shape)


def rope(u, cos, sin):
    left, right, low = turn(u)
    return u * cos + jnp.where(low, -left, right) * sin


def rope_back(w, cos, sin):
    left, right, low = turn(w * sin)
    return w * cos + jnp.where(low, left, -right)


def wide(table, width):
    return jnp.concatenate([table] * (width // table.shape[1]), axis=1)


def two_heads(pair):
    lane = lax.broadcasted_iota(jnp.int32, pair.shape, 1)
    zero = jnp.zeros_like(pair)
    first = lane < HEAD_DIM
    return jnp.concatenate(
        [jnp.where(first, pair, zero), jnp.where(first, zero, pair)], axis=0
    )


def join_heads(both):
    rows = both.shape[0] // 2
    lane = lax.broadcasted_iota(jnp.int32, (rows, both.shape[1]), 1)
    return jnp.where(lane < HEAD_DIM, both[:rows], both[rows:])


def as_row(col):
    return jnp.transpose(jnp.broadcast_to(col, (col.shape[0], 128)))[0:1, :]


def qkv_kernel(n, order_ref, x_ref, cos_ref, sin_ref, *rest):
    chunks = rest[:n]
    a_ref, q_ref, kv_ref, g_ref, w, sems = rest[n:]
    width = q_ref.shape[1]
    copies = weight_copies(order_ref, chunks, w, sems)
    xhat, _ = norm_parts(x_ref[...])
    for copy in copies:
        copy.wait()
    row = lax.broadcasted_iota(jnp.int32, (8, 128), 0)
    lane = lax.broadcasted_iota(jnp.int32, (8, 128), 1)
    pick = jnp.where(row == lane, 1.0, 0.0).astype(BF16)
    g = dot_nt(pick, w[:, 4 * width : 4 * width + 128])
    g_ref[...] = g
    a = (xhat * g[0:1, :]).astype(BF16)
    a_ref[...] = a
    cos = wide(cos_ref[...], width)
    sin = wide(sin_ref[...], width)
    q_ref[...] = rope(dot_nn(a, w[:, :width]), cos, sin).astype(BF16)
    kv_ref[:, :width] = rope(dot_nn(a, w[:, width : 2 * width]), cos, sin).astype(BF16)
    kv_ref[:, width:] = dot_nn(a, w[:, 2 * width : 3 * width]).astype(BF16)


def key_copies(chunks, dst, sems, block):
    if len(chunks) == 1:
        rows = dst.shape[0]
        at = pl.ds(pl.multiple_of(block * rows, rows), rows)
        copies = [pltpu.make_async_copy(chunks[0].at[at, :], dst, sems.at[0])]
    else:
        rows = chunks[0].shape[0]
        copies = [
            pltpu.make_async_copy(chunk, dst.at[pl.ds(i * rows, rows), :], sems.at[i])
            for i, chunk in enumerate(chunks)
        ]
    for copy in copies:
        copy.start()
    return copies


def each(count, body):
    if count == 1:
        body(0)
    else:
        lax.fori_loop(0, count, lambda i, c: (body(i), c)[1], 0)


def attend_kernel(n, nw, blocks, order_ref, q_ref, *rest):
    keys = rest[:n]
    wos = rest[n : n + nw]
    attn_ref, lse_ref, out_ref, kv, wo, m_s, l_s, acc_s, ksem, wsem = rest[n + nw :]
    width = q_ref.shape[1]
    pairs = width // 128
    wcopies = weight_copies(order_ref, wos, wo, wsem, (3 * width, width))
    m_s[...] = jnp.full(m_s.shape, NEG_LARGE, F32)
    l_s[...] = jnp.zeros(l_s.shape, F32)
    acc_s[...] = jnp.zeros(acc_s.shape, F32)

    def block_work(block):
        for copy in key_copies(keys, kv, ksem, block):
            copy.wait()
        for p in range(pairs):
            at = slice(p * 128, p * 128 + 128)
            qm = two_heads(q_ref[:, at]) * jnp.asarray(SCALE, BF16)
            s = dot_nt(qm, kv[:, at])
            m_old = m_s[p]
            m_new = jnp.maximum(m_old, jnp.max(s, axis=1, keepdims=True))
            factor = jnp.exp(m_old - m_new)
            e = jnp.exp(s - m_new)
            l_s[p] = l_s[p] * factor + jnp.sum(e, axis=1, keepdims=True)
            m_s[p] = m_new
            acc_s[p] = acc_s[p] * factor + dot_nn(
                e.astype(BF16), kv[:, width + p * 128 : width + p * 128 + 128]
            )

    each(blocks, block_work)
    for p in range(pairs):
        attn_ref[:, p * 128 : p * 128 + 128] = join_heads(acc_s[p] / l_s[p]).astype(BF16)
        lse_ref[p : p + 1, :] = as_row(m_s[p] + jnp.log(l_s[p]))
    for copy in wcopies:
        copy.wait()
    out_ref[...] = dot_nt(attn_ref[...], wo[...]).astype(BF16)


def gelu_parts(z):
    cdf = 0.5 * (1.0 + lax.erf(z * 0.7071067811865476))
    density = jnp.exp(-0.5 * z * z) * 0.3989422804014327
    return z * cdf, cdf + z * density


def ffn_kernel(nw, order_ref, x_ref, pa_ref, pb_ref, cot_ref, g_ref, *rest):
    ws = rest[:nw]
    hid_ref, out_ref, db_ref, b_ref, dz_ref, mixed_ref, w, wsem = rest[nw:]
    units = mixed_ref.shape[1]
    copies = weight_copies(order_ref, ws, w, wsem)
    hidden = x_ref[...] + (pa_ref[...].astype(F32) + pb_ref[...].astype(F32))
    hid_ref[...] = hidden
    xhat, _ = norm_parts(hidden)
    b = (xhat * g_ref[1:2, :]).astype(BF16)
    b_ref[...] = b
    cb = cot_ref[...].astype(BF16)
    for copy in copies:
        copy.wait()
    z = dot_nn(b, w[:, : 2 * units])
    gate = z[:, units:]
    act, slope = gelu_parts(z[:, :units])
    dmix = dot_nn(cb, w[:, 2 * units : 3 * units])
    dz = jnp.concatenate([dmix * gate * slope, dmix * act], axis=1).astype(BF16)
    dz_ref[...] = dz
    db_ref[...] = dot_nt(dz, w[:, : 2 * units]).astype(BF16)
    mixed = (act * gate).astype(BF16)
    mixed_ref[...] = mixed
    out_ref[...] = dot_nt(mixed, w[:, 2 * units : 3 * units]).astype(BF16)


def ffn_grad_kernel(no, order_ref, b_ref, dz_ref, cot_ref, mixed_ref, *rest):
    outs, acc = rest[:no], rest[no]
    two = dz_ref.shape[1]
    acc[:, :two] = dot_tn(b_ref[...], dz_ref[...])
    half = mixed_ref.shape[1]
    acc[:, two : two + half] = dot_tn(cot_ref[...].astype(BF16), mixed_ref[...])
    acc[:, two + half :] = jnp.zeros((acc.shape[0], acc.shape[1] - two - half), F32)
    emit_blocks(order_ref, acc, outs)


def attend_back_kernel(
    n, nw, no, blocks, order_ref, q_ref, attn_ref, lse_ref, hid_ref, cot_ref, g_ref,
    da_ref, db_ref, cos_ref, sin_ref, *rest
):
    keys = rest[:n]
    wos = rest[n : n + nw]
    outs = rest[n + nw : n + nw + no]
    dhid_ref, dqp_ref, kv, wo, dq_s, qm_s, dom_s, row_s, ksem, wsem = rest[n + nw + no :]
    width = q_ref.shape[1]
    pairs = width // 128
    wcopies = weight_copies(order_ref, wos, wo, wsem, (3 * width, width))
    first = key_copies(keys, kv, ksem, 0) if blocks == 1 else None
    xhat, inv = norm_parts(hid_ref[...])
    db = da_ref[...].astype(F32) + db_ref[...].astype(F32)
    dhid = cot_ref[...] + norm_back(db, xhat, inv, g_ref[1:2, :])
    dhid_ref[...] = dhid
    for copy in wcopies:
        copy.wait()
    dattn = dot_nn(dhid.astype(BF16), wo[...]).astype(BF16)
    for p in range(pairs):
        at = slice(p * 128, p * 128 + 128)
        qm_s[p] = two_heads(q_ref[:, at]) * jnp.asarray(SCALE, BF16)
        dom = two_heads(dattn[:, at])
        dom_s[p] = dom
        both = jnp.concatenate([attn_ref[:, at]] * 2, axis=0)
        dots = jnp.sum(dom.astype(F32) * both.astype(F32), axis=1, keepdims=True)
        row_s[p : p + 1, :] = as_row(dots)
    dq_s[...] = jnp.zeros(dq_s.shape, F32)
    halves = len(outs)
    block_rows = kv.shape[0]

    def block_work(block):
        for copy in first or key_copies(keys, kv, ksem, block):
            copy.wait()
        for half in range(halves):
            count = block_rows // halves // SUB_ROWS

            def sub_work(sub):
                src = pl.ds(
                    pl.multiple_of(half * (block_rows // halves) + sub * SUB_ROWS, SUB_ROWS),
                    SUB_ROWS,
                )
                dst = pl.ds(
                    pl.multiple_of(block * block_rows + sub * SUB_ROWS, SUB_ROWS), SUB_ROWS
                )
                for p in range(pairs):
                    at = slice(p * 128, p * 128 + 128)
                    vat = slice(width + p * 128, width + p * 128 + 128)
                    k = kv[src, at]
                    prob = jnp.exp(dot_nt(k, qm_s[p]) - lse_ref[p : p + 1, :])
                    dprob = dot_nt(kv[src, vat], dom_s[p])
                    ds = (prob * (dprob - row_s[p : p + 1, :])).astype(BF16)
                    outs[half][dst, at] = dot_nn(ds, qm_s[p]).astype(BF16)
                    outs[half][dst, vat] = dot_nn(prob.astype(BF16), dom_s[p]).astype(BF16)
                    dq_s[p] += dot_tn(ds, k)

            each(count, sub_work)

    each(blocks, block_work)
    dq = jnp.concatenate([join_heads(dq_s[p]) for p in range(pairs)], axis=1) * SCALE
    dqp_ref[...] = rope_back(
        dq, wide(cos_ref[...], width), wide(sin_ref[...], width)
    ).astype(BF16)


def qkv_grad_kernel(
    n, nt, no, order_ref, a_ref, dqp_ref, dhid_ref, attn_ref, cos_ref, sin_ref, *rest
):
    terms = rest[:nt]
    chunks = rest[nt : nt + n]
    outs = rest[nt + n : nt + n + no]
    da_ref, w, acc, sems = rest[nt + n + no :]
    width = dqp_ref.shape[1]
    copies = weight_copies(order_ref, chunks, w, sems)
    dkv = terms[0][...].astype(F32)
    for term in terms[1:]:
        dkv = dkv + term[...].astype(F32)
    dkp = rope_back(
        dkv[:, :width], wide(cos_ref[...], width), wide(sin_ref[...], width)
    ).astype(BF16)
    d = jnp.concatenate([dqp_ref[...], dkp, dkv[:, width:].astype(BF16)], axis=1)
    for copy in copies:
        copy.wait()
    da_ref[...] = dot_nt(d, w[:, : 3 * width]).astype(BF16)
    acc[:, : 3 * width] = dot_tn(a_ref[...], d)
    acc[:, 3 * width :] = dot_tn(dhid_ref[...].astype(BF16), attn_ref[...])
    emit_blocks(order_ref, acc, outs)


def call(kernel, out_shape, specs, scratch, args):
    return pl.pallas_call(
        kernel,
        out_shape=out_shape,
        in_specs=specs,
        out_specs=jax.tree.map(lambda _: VM, out_shape),
        scratch_shapes=scratch,
    )(*args)


def rotary_tables(positions):
    half = HEAD_DIM // 2
    inverse = jnp.exp(jnp.arange(half, dtype=F32) * (-2.0 * math.log(THETA) / HEAD_DIM))
    angles = positions.astype(F32)[:, None] * inverse[None, :]
    angles = jnp.concatenate([angles] * 4, axis=-1)
    return jnp.cos(angles), jnp.sin(angles)


def adam_update(tensor, gradient, moment, second):
    moment = BETA_ONE * moment + (1.0 - BETA_ONE) * gradient
    second = BETA_TWO * second + (1.0 - BETA_TWO) * gradient * gradient
    first_hat = moment / (1.0 - BETA_ONE**STEP)
    second_hat = second / (1.0 - BETA_TWO**STEP)
    tensor = tensor - LEARN_RATE * (first_hat / (jnp.sqrt(second_hat) + ADAM_EPS) + DECAY * tensor)
    return tensor, moment, second


def adam_kernel(nf, width, units, w_ref, m_ref, v_ref, *rest):
    firsts, lasts = rest[:nf], rest[nf : 2 * nf]
    g_ref, w_out, m_out, v_out, gain_ref = rest[2 * nf :]
    one = total([term[...] for term in firsts])
    two = total([term[...] for term in lasts])[:, : 3 * units]
    w = w_ref[...]
    wf = w.astype(BF16).astype(F32)
    cut = 4 * width
    sums = [
        jnp.sum(wf[:, : 3 * width] * one[:, : 3 * width], axis=1, keepdims=True),
        jnp.sum(wf[:, cut : cut + 2 * units] * two[:, : 2 * units], axis=1, keepdims=True),
    ]
    lane = lax.broadcasted_iota(jnp.int32, gain_ref.shape, 1)
    gain_ref[...] = jnp.where(lane == 0, sums[0], jnp.where(lane == 1, sums[1], 0.0))
    grad = jnp.concatenate([one, two], axis=1)
    g_ref[...] = grad
    w_out[...], m_out[...], v_out[...] = adam_update(w, grad, m_ref[...], v_ref[...])


def head_swap(x):
    if lax.axis_size("head") == 1:
        return jnp.zeros_like(x)
    return swap(x, "head", 1)


def layer(
    inputs, cotangent, weights, gains, weight_moment, weight_second, gain_moment, gain_second
):
    heads = lax.axis_size("head")
    width = HEADS // heads * HEAD_DIM
    units = FF // heads
    toks, d = inputs.shape
    rows = weights.shape[0]
    n = lax.axis_size(TOKENS_AX)
    seq = toks * n
    me = lax.axis_index(TOKENS_AX).astype(jnp.int32)
    order = me.reshape(1)
    pairs = width // 128

    wb = weights.astype(BF16)
    gb = gains.astype(BF16)
    wq_cols = 4 * width + 128
    rest_pad = -(3 * units) % 128
    rest_cols = 3 * units + rest_pad
    w_first = jnp.concatenate([wb[:, : 4 * width], jnp.pad(gb.T, ((0, 0), (0, 126)))], axis=1)
    w_rest = jnp.pad(wb[:, 4 * width :], ((0, 0), (0, rest_pad)))
    first_chunks = gather(w_first)
    cos, sin = rotary_tables(me * toks + jnp.arange(toks, dtype=jnp.int32))

    nw = len(first_chunks)
    wsem = pltpu.SemaphoreType.DMA((nw,))
    halves = 2 if staged() else 1

    a, q, kv, g = call(
        partial(qkv_kernel, nw),
        [sds((toks, d), BF16), sds((toks, width), BF16), sds((toks, 2 * width), BF16), sds((8, d), F32)],
        [SM, VM, VM, VM] + [ANY] * nw,
        [pltpu.VMEM((d, wq_cols), BF16), wsem],
        [order, inputs, cos, sin] + first_chunks,
    )
    keys = gather(kv)
    rest_chunks = gather(w_rest)
    nk = len(keys)
    block_rows = min(KEY_ROWS, seq)
    blocks = seq // block_rows
    ksem = pltpu.SemaphoreType.DMA((nk,))

    attn, lse, out_part = call(
        partial(attend_kernel, nk, nw, blocks),
        [sds((toks, width), BF16), sds((8, 2 * toks), F32), sds((toks, d), BF16)],
        [SM, VM] + [ANY] * (nk + nw),
        [
            pltpu.VMEM((block_rows, 2 * width), BF16),
            pltpu.VMEM((d, width), BF16),
            pltpu.VMEM((pairs, 2 * toks, 1), F32),
            pltpu.VMEM((pairs, 2 * toks, 1), F32),
            pltpu.VMEM((pairs, 2 * toks, 128), F32),
            ksem,
            wsem,
        ],
        [order, q] + keys + first_chunks,
    )
    out_other = head_swap(out_part)

    hidden, ffn_part, db_part, b, dz, mixed = call(
        partial(ffn_kernel, nw),
        [
            sds((toks, d), F32),
            sds((toks, d), BF16),
            sds((toks, d), BF16),
            sds((toks, d), BF16),
            sds((toks, 2 * units), BF16),
            sds((toks, units), BF16),
        ],
        [SM] + [VM] * 5 + [ANY] * nw,
        [pltpu.VMEM((d, rest_cols), BF16), wsem],
        [order, inputs, out_part, out_other, cotangent, g] + rest_chunks,
    )
    db_other = head_swap(db_part)
    ffn_other = head_swap(ffn_part)
    outputs = hidden + (ffn_part.astype(F32) + ffn_other.astype(F32))
    ffn_grads = call(
        partial(ffn_grad_kernel, halves),
        [sds((d // halves, rest_cols), BF16)] * halves,
        [SM] + [VM] * 4,
        [pltpu.VMEM((d, rest_cols), F32)],
        [order, b, dz, cotangent, mixed],
    )
    ffn_terms = scatter_sum(ffn_grads)

    back = call(
        partial(attend_back_kernel, nk, nw, halves, blocks),
        [sds((seq // halves, 2 * width), BF16)] * halves
        + [sds((toks, d), F32), sds((toks, width), BF16)],
        [SM] + [VM] * 10 + [ANY] * (nk + nw),
        [
            pltpu.VMEM((block_rows, 2 * width), BF16),
            pltpu.VMEM((d, width), BF16),
            pltpu.VMEM((pairs, 2 * toks, 128), F32),
            pltpu.VMEM((pairs, 2 * toks, 128), BF16),
            pltpu.VMEM((pairs, 2 * toks, 128), BF16),
            pltpu.VMEM((8, 2 * toks), F32),
            ksem,
            wsem,
        ],
        [order, q, attn, lse, hidden, cotangent, g, db_part, db_other, cos, sin] + keys + first_chunks,
    )
    dhid, dqp = back[halves:]
    kv_terms = scatter_sum(back[:halves])
    nt = len(kv_terms)
    grads = call(
        partial(qkv_grad_kernel, nw, nt, halves),
        [sds((d // halves, 4 * width), BF16)] * halves + [sds((toks, d), BF16)],
        [SM] + [VM] * 6 + [VM] * nt + [ANY] * nw,
        [pltpu.VMEM((d, wq_cols), BF16), pltpu.VMEM((d, 4 * width), F32), wsem],
        [order, a, dqp, dhid, attn, cos, sin] + kv_terms + first_chunks,
    )
    da_part = grads[halves]
    da_other = head_swap(da_part)
    da = da_part.astype(F32) + da_other.astype(F32)
    xhat, inv = norm_parts(inputs)
    input_grad = dhid + norm_back(da, xhat, inv, g[0:1, :])

    first_terms = scatter_sum(grads[:halves])
    full = weights.shape
    weight_grad, new_weights, new_weight_moment, new_weight_second, gain_part = call(
        partial(adam_kernel, nt, width, units),
        [sds(full, F32)] * 4 + [sds((rows, 128), F32)],
        [VM] * (3 + 2 * nt),
        [],
        [weights, weight_moment, weight_second] + first_terms + ffn_terms,
    )
    gain_part = gain_part[:, :2].T
    gain_grad = (gain_part + head_swap(gain_part)) / gb.astype(F32)
    new_gains, new_gain_moment, new_gain_second = adam_update(
        gains, gain_grad, gain_moment, gain_second
    )
    return (
        outputs,
        input_grad,
        weight_grad,
        gain_grad,
        new_weights,
        new_weight_moment,
        new_weight_second,
        new_gains,
        new_gain_moment,
        new_gain_second,
    )


def solution(mesh):
    rows = P(("blk", "shard"), None)
    cells = P(("blk", "shard"), "head")
    lanes = P(None, ("blk", "shard"))
    return jax.shard_map(
        layer,
        mesh=mesh,
        in_specs=(rows, rows, cells, lanes, cells, cells, lanes, lanes),
        out_specs=(rows, rows, cells, lanes, cells, cells, cells, lanes, lanes, lanes),
        check_vma=False,
    )
```

profile of v0, /device:TPU:0, one launch (start us, length us, event | category | flops | bytes accessed | tf_op | source)
XLA Modules:
  0.0 232.8 jit_solution(13194773753910150773)
XLA Ops:
  2.6 3.1 %collective-permute-start = (bf16[48,1664]{1,0:T(8,128)(2,1)S(1)}, bf16[48,1664]{1,0:T(8,128)(2,1)S(1)}, u32[]{:S(2)}, u32[]{:S(2)}) collective-permute-start(bf16[48,1664]{1,0:T(8,128)(2,1)S(1)} %fusion.2.rest_0_.rest_16_.rest_4_), channel_id=1, source_target_pairs={{0,8},{8,0},{16,24},{24,16},{1,9},{9,1},{17,25},{25,17},{2,10},{10... | collective-permute-start | bytes 479240 | tf_op jit(solution)/shard_map/ppermute | solution.py:56
  5.9 3.0 %collective-permute-start.1 = (bf16[48,1664]{1,0:T(8,128)(2,1)S(1)}, bf16[48,1664]{1,0:T(8,128)(2,1)S(1)}, u32[]{:S(2)}, u32[]{:S(2)}) collective-permute-start(bf16[48,1664]{1,0:T(8,128)(2,1)S(1)} %fusion.2.rest_0_.rest_16_.rest_4_), channel_id=1, source_target_pairs={{0,16},{8,24},{16,0},{24,8},{1,17},{9,25},{17,1},{25,9},{2,18},{10... | collective-permute-start | bytes 479240 | tf_op jit(solution)/shard_map/ppermute | solution.py:56
  10.2 1.5 collective-permute-start.3
  11.7 2.4 %collective-permute-done.rest_1_.rest_17_.rest_5_ = bf16[48,1664]{1,0:T(8,128)(2,1)S(1)} collective-permute-done((bf16[48,1664]{1,0:T(8,128)(2,1)S(1)}, bf16[48,1664]{1,0:T(8,128)(2,1)S(1)}, u32[]{:S(2)}, u32[]{:S(2)}) %collective-permute-start) | collective-permute-done | bytes 159776 | tf_op jit(solution)/shard_map/ppermute | solution.py:56
  14.1 3.3 %collective-permute-done.1.rest_2_.rest_18_.rest_6_ = bf16[48,1664]{1,0:T(8,128)(2,1)S(1)} collective-permute-done((bf16[48,1664]{1,0:T(8,128)(2,1)S(1)}, bf16[48,1664]{1,0:T(8,128)(2,1)S(1)}, u32[]{:S(2)}, u32[]{:S(2)}) %collective-permute-start.1) | collective-permute-done | bytes 159776 | tf_op jit(solution)/shard_map/ppermute | solution.py:56
  17.4 1.5 collective-permute-start.4
  18.9 3.8 %collective-permute-done.2.rest_3_.rest_19_.rest_7_ = bf16[48,1664]{1,0:T(8,128)(2,1)S(1)} collective-permute-done((bf16[48,1664]{1,0:T(8,128)(2,1)S(1)}, bf16[48,1664]{1,0:T(8,128)(2,1)S(1)}, u32[]{:S(2)}, u32[]{:S(2)}) %collective-permute-start.2) | collective-permute-done | bytes 159776 | tf_op jit(solution)/shard_map/ppermute | solution.py:56
  22.7 1.5 collective-permute-start.5
  25.3 4.0 %collective-permute-done.5.rest_6_.rest_22_.rest_10_ = bf16[48,1664]{1,0:T(8,128)(2,1)S(1)} collective-permute-done((bf16[48,1664]{1,0:T(8,128)(2,1)S(1)}, bf16[48,1664]{1,0:T(8,128)(2,1)S(1)}, u32[]{:S(2)}, u32[]{:S(2)}) %collective-permute-start.5) | collective-permute-done | bytes 159776 | tf_op jit(solution)/shard_map/ppermute | solution.py:56
  29.3 1.7 collective-permute-done.6.rest_7_.rest_23_.rest_11_
  31.7 2.4 %collective-permute-start.32 = (bf16[48,1792]{1,0:T(8,128)(2,1)S(1)}, bf16[48,1792]{1,0:T(8,128)(2,1)S(1)}, u32[]{:S(2)}, u32[]{:S(2)}) collective-permute-start(bf16[48,1792]{1,0:T(8,128)(2,1)S(1)} %pad.9.rest_0_), channel_id=1, source_target_pairs={{0,16},{8,24},{16,0},{24,8},{1,17},{9,25},{17,1},{25,9},{2,18},{10... | collective-permute-start | bytes 516104 | tf_op jit(solution)/shard_map/ppermute | solution.py:56
  34.1 2.0 collective-permute-start.33
  36.1 1.5 collective-permute-start.34
  39.5 4.3 %shard_map.159 = (bf16[128,768]{1,0:T(8,128)(2,1)}, bf16[128,384]{1,0:T(8,128)(2,1)}, bf16[128,768]{1,0:T(8,128)(2,1)}, f32[8,768]{1,0:T(8,128)}) custom-call(s32[1]{0:T(128)} %bitcast.order_ref, f32[128,768]{1,0:T(8,128)} %x_ref.3, f32[128,128]{1,0:T(8,128)} %get-tuple-element.140.cos_ref, f32[128,128]{1,0:T(8,128)} %get-tuple-element.139.sin_ref, ...), custom_call_target="tpu_custom_call" | custom-call | tf_op jit(solution)/shard_map/pallas_call | solution.py:415
  43.8 3.5 %collective-permute-done.32.rest_2_ = bf16[48,1792]{1,0:T(8,128)(2,1)S(1)} collective-permute-done((bf16[48,1792]{1,0:T(8,128)(2,1)S(1)}, bf16[48,1792]{1,0:T(8,128)(2,1)S(1)}, u32[]{:S(2)}, u32[]{:S(2)}) %collective-permute-start.32) | collective-permute-done | bytes 172064 | tf_op jit(solution)/shard_map/ppermute | solution.py:56
  47.3 5.3 %collective-permute-start.16 = (bf16[128,768]{1,0:T(8,128)(2,1)}, bf16[128,768]{1,0:T(8,128)(2,1)S(1)}, u32[]{:S(2)}, u32[]{:S(2)}) collective-permute-start(bf16[128,768]{1,0:T(8,128)(2,1)} %get-tuple-element.62.rest_0_), channel_id=1, source_target_pairs={{0,16},{8,24},{16,0},{24,8},{1,17},{9,25},{17,1},{25,9},{2,18},{10... | collective-permute-start | bytes 589832 | tf_op jit(solution)/shard_map/ppermute | solution.py:56
  53.3 1.5 collective-permute-start.18
  55.5 11.2 %collective-permute-done.16.rest_2_ = bf16[128,768]{1,0:T(8,128)(2,1)S(1)} collective-permute-done((bf16[128,768]{1,0:T(8,128)(2,1)}, bf16[128,768]{1,0:T(8,128)(2,1)S(1)}, u32[]{:S(2)}, u32[]{:S(2)}) %collective-permute-start.16) | collective-permute-done | bytes 196640 | tf_op jit(solution)/shard_map/ppermute | solution.py:56
  69.3 5.1 %collective-permute-done.20.rest_6_ = bf16[128,768]{1,0:T(8,128)(2,1)S(1)} collective-permute-done((bf16[128,768]{1,0:T(8,128)(2,1)S(1)}, bf16[128,768]{1,0:T(8,128)(2,1)S(1)}, u32[]{:S(2)}, u32[]{:S(2)}) %collective-permute-start.20) | collective-permute-done | bytes 196640 | tf_op jit(solution)/shard_map/ppermute | solution.py:56
  74.4 2.2 collective-permute-done.21.rest_7_
  77.3 1.5 collective-permute-start.36
  80.5 7.5 %shard_map.160 = (bf16[128,384]{1,0:T(8,128)(2,1)}, f32[8,256]{1,0:T(8,128)}, bf16[128,768]{1,0:T(8,128)(2,1)}) custom-call(s32[1]{0:T(128)} %bitcast.order_ref, bf16[128,384]{1,0:T(8,128)(2,1)} %get-tuple-element.61.q_ref, bf16[128,768]{1,0:T(8,128)(2,1)} %get-tuple-element.62.rest_0_, bf16[128,768]{1,0:T(8,128)(2,1)} %copy-done.21, ...), custom_call_target="tpu_custom_call" | custom-call | tf_op jit(solution)/shard_map/pallas_call | solution.py:415
  88.1 1.6 collective-permute-start.30
  92.1 3.2 %collective-permute-done.30.pb_ref = bf16[128,768]{1,0:T(8,128)(2,1)S(1)} collective-permute-done((bf16[128,768]{1,0:T(8,128)(2,1)}, bf16[128,768]{1,0:T(8,128)(2,1)S(1)}, u32[]{:S(2)}, u32[]{:S(2)}) %collective-permute-start.30) | collective-permute-done | bytes 196640 | tf_op jit(solution)/shard_map/ppermute | solution.py:56
  95.9 5.4 %shard_map.161 = (f32[128,768]{1,0:T(8,128)}, bf16[128,768]{1,0:T(8,128)(2,1)}, bf16[128,768]{1,0:T(8,128)(2,1)}, bf16[128,768]{1,0:T(8,128)(2,1)}, bf16[128,1152]{1,0:T(8,128)(2,1)}, /*index=5*/bf16[128,576]{1,0:T(8,128)(2,1)}) custom-call(s32[1]{0:T(128)} %bitcast.order_ref, f32[128,768]{1,0:T(8,128)} %x_ref.3, bf16[128,768]{1,0:T(8,128)(2,1)} %get-tuple-element.63.pa_ref, ...), custom_call_target="tpu_custom_call" | custom-call | tf_op jit(solution)/shard_map/pallas_call | solution.py:415
  101.3 1.6 collective-permute-start.47
  102.9 3.9 %shard_map.164 = (bf16[384,1792]{1,0:T(8,128)(2,1)}, bf16[384,1792]{1,0:T(8,128)(2,1)}) custom-call(s32[1]{0:T(128)} %bitcast.order_ref, bf16[128,768]{1,0:T(8,128)(2,1)} %get-tuple-element.94.b_ref, bf16[128,1152]{1,0:T(8,128)(2,1)} %get-tuple-element.95.dz_ref, f32[128,768]{1,0:T(8,128)} %cot_ref.5, bf16[128,576]{1,0:T(8,128)(2,1)} %get-tuple-element.96.mixed_ref), custom_call_target="tpu_custom_call" | custom-call | tf_op jit(solution)/shard_map/pallas_call | solution.py:415
  108.3 10.8 %shard_map.162 = (bf16[1024,768]{1,0:T(8,128)(2,1)}, bf16[1024,768]{1,0:T(8,128)(2,1)}, f32[128,768]{1,0:T(8,128)}, bf16[128,384]{1,0:T(8,128)(2,1)}) custom-call(s32[1]{0:T(128)} %bitcast.order_ref, bf16[128,384]{1,0:T(8,128)(2,1)} %get-tuple-element.61.q_ref, bf16[128,384]{1,0:T(8,128)(2,1)} %get-tuple-element.67.attn_ref, ...), custom_call_target="tpu_custom_call" | custom-call | tf_op jit(solution)/shard_map/pallas_call | solution.py:415
  119.6 1.6 collective-permute-start.46
  124.2 3.0 %pair_add.5 = (bf16[48,1792]{1,0:T(8,128)(2,1)}, bf16[48,1792]{1,0:T(8,128)(2,1)}, bf16[48,1792]{1,0:T(8,128)(2,1)}, bf16[48,1792]{1,0:T(8,128)(2,1)}, bf16[48,1...) custom-call(bf16[384,1792]{1,0:T(8,128)(2,1)} %get-tuple-element.97.refs_0_, ...), custom_call_target="tpu_custom_call" | custom-call | tf_op jit(solution)/shard_map/pair_add/pallas_call | solution.py:95
  132.7 3.1 %pair_add.3 = (bf16[128,768]{1,0:T(8,128)(2,1)}, bf16[128,768]{1,0:T(8,128)(2,1)}, bf16[128,768]{1,0:T(8,128)(2,1)}, bf16[128,768]{1,0:T(8,128)(2,1)}, bf16[128,...) custom-call(bf16[1024,768]{1,0:T(8,128)(2,1)} %get-tuple-element.73.refs_0_, ...), custom_call_target="tpu_custom_call" | custom-call | tf_op jit(solution)/shard_map/pair_add/pallas_call | solution.py:95
  136.4 1.5 collective-permute-start.52
  138.5 7.7 %collective-permute-done.54 = bf16[128,768]{1,0:T(8,128)(2,1)S(1)} collective-permute-done((bf16[128,768]{1,0:T(8,128)(2,1)}, bf16[128,768]{1,0:T(8,128)(2,1)S(1)}, u32[]{:S(2)}, u32[]{:S(2)}) %collective-permute-start.54) | collective-permute-done | bytes 196640 | tf_op jit(solution)/shard_map/ppermute | solution.py:56
  148.7 1.8 collective-permute-done.52
  152.0 2.7 %collective-permute-done.50 = bf16[128,768]{1,0:T(8,128)(2,1)S(1)} collective-permute-done((bf16[128,768]{1,0:T(8,128)(2,1)}, bf16[128,768]{1,0:T(8,128)(2,1)S(1)}, u32[]{:S(2)}, u32[]{:S(2)}) %collective-permute-start.50) | collective-permute-done | bytes 196640 | tf_op jit(solution)/shard_map/ppermute | solution.py:56
  154.7 3.4 %collective-permute-done.49 = bf16[128,768]{1,0:T(8,128)(2,1)S(1)} collective-permute-done((bf16[128,768]{1,0:T(8,128)(2,1)}, bf16[128,768]{1,0:T(8,128)(2,1)S(1)}, u32[]{:S(2)}, u32[]{:S(2)}) %collective-permute-start.49) | collective-permute-done | bytes 196640 | tf_op jit(solution)/shard_map/ppermute | solution.py:56
  158.9 1.5 collective-permute-start.66
  160.4 9.2 %collective-permute-done.53.rest_2_ = bf16[128,768]{1,0:T(8,128)(2,1)S(1)} collective-permute-done((bf16[128,768]{1,0:T(8,128)(2,1)S(1)}, bf16[128,768]{1,0:T(8,128)(2,1)S(1)}, u32[]{:S(2)}, u32[]{:S(2)}) %collective-permute-start.53) | collective-permute-done | bytes 196640 | tf_op jit(solution)/shard_map/ppermute | solution.py:56
  170.4 6.4 %shard_map.163 = (bf16[384,1536]{1,0:T(8,128)(2,1)}, bf16[384,1536]{1,0:T(8,128)(2,1)}, bf16[128,768]{1,0:T(8,128)(2,1)}) custom-call(s32[1]{0:T(128)} %bitcast.order_ref, bf16[128,768]{1,0:T(8,128)(2,1)} %get-tuple-element.71.a_ref, bf16[128,384]{1,0:T(8,128)(2,1)} %get-tuple-element.72.dqp_ref, f32[128,768]{1,0:T(8,128)} %get-tuple-element.70.dhid_ref, ...), custom_call_target="tpu_custom_call" | custom-call | tf_op jit(solution)/shard_map/pallas_call | solution.py:415
  176.9 3.5 %collective-permute-start.70 = (bf16[48,1792]{1,0:T(8,128)(2,1)S(1)}, bf16[48,1792]{1,0:T(8,128)(2,1)S(1)}, u32[]{:S(2)}, u32[]{:S(2)}) collective-permute-start(bf16[48,1792]{1,0:T(8,128)(2,1)S(1)} %add_convert_fusion.5), channel_id=1, source_target_pairs={{0,16},{8,24},{16,0},{24,8},{1,17},{9,25},{17,1},{25,9},{2,18},{10... | collective-permute-start | bytes 516104 | tf_op jit(solution)/shard_map/ppermute | solution.py:56
  180.5 3.4 %collective-permute-start.68 = (bf16[48,1792]{1,0:T(8,128)(2,1)S(1)}, bf16[48,1792]{1,0:T(8,128)(2,1)S(1)}, u32[]{:S(2)}, u32[]{:S(2)}) collective-permute-start(bf16[48,1792]{1,0:T(8,128)(2,1)S(1)} %add_convert_fusion.6), channel_id=1, source_target_pairs={{0,24},{8,16},{16,8},{24,0},{1,25},{9,17},{17,9},{25,1},{2,26},{10... | collective-permute-start | bytes 516104 | tf_op jit(solution)/shard_map/ppermute | solution.py:56
  185.1 5.7 %collective-permute-done.56 = bf16[128,768]{1,0:T(8,128)(2,1)S(1)} collective-permute-done((bf16[128,768]{1,0:T(8,128)(2,1)}, bf16[128,768]{1,0:T(8,128)(2,1)S(1)}, u32[]{:S(2)}, u32[]{:S(2)}) %collective-permute-start.56) | collective-permute-done | bytes 196640 | tf_op jit(solution)/shard_map/ppermute | solution.py:56
  192.1 2.7 %pair_add.4 = (bf16[48,1536]{1,0:T(8,128)(2,1)}, bf16[48,1536]{1,0:T(8,128)(2,1)}, bf16[48,1536]{1,0:T(8,128)(2,1)}, bf16[48,1536]{1,0:T(8,128)(2,1)}, bf16[48,1...) custom-call(bf16[384,1536]{1,0:T(8,128)(2,1)} %get-tuple-element.84.refs_0_, ...), custom_call_target="tpu_custom_call" | custom-call | tf_op jit(solution)/shard_map/pair_add/pallas_call | solution.py:95
  196.8 4.9 %collective-permute-done.63 = bf16[48,1536]{1,0:T(8,128)(2,1)S(1)} collective-permute-done((bf16[48,1536]{1,0:T(8,128)(2,1)}, bf16[48,1536]{1,0:T(8,128)(2,1)S(1)}, u32[]{:S(2)}, u32[]{:S(2)}) %collective-permute-start.63) | collective-permute-done | bytes 147488 | tf_op jit(solution)/shard_map/ppermute | solution.py:56
  210.2 2.9 %collective-permute-start.60 = (bf16[48,1536]{1,0:T(8,128)(2,1)S(1)}, bf16[48,1536]{1,0:T(8,128)(2,1)S(1)}, u32[]{:S(2)}, u32[]{:S(2)}) collective-permute-start(bf16[48,1536]{1,0:T(8,128)(2,1)S(1)} %add_convert_fusion.10), channel_id=1, source_target_pairs={{0,24},{8,16},{16,8},{24,0},{1,25},{9,17},{17,9},{25,1},{2,26},{10... | collective-permute-start | bytes 442376 | tf_op jit(solution)/shard_map/ppermute | solution.py:56
  213.8 6.1 %collective-permute-done.62.rest_2_ = bf16[48,1536]{1,0:T(8,128)(2,1)S(1)} collective-permute-done((bf16[48,1536]{1,0:T(8,128)(2,1)S(1)}, bf16[48,1536]{1,0:T(8,128)(2,1)S(1)}, u32[]{:S(2)}, u32[]{:S(2)}) %collective-permute-start.62) | collective-permute-done | bytes 147488 | tf_op jit(solution)/shard_map/ppermute | solution.py:56
  221.2 4.1 %shard_map.165 = (f32[48,3264]{1,0:T(8,128)}, f32[48,3264]{1,0:T(8,128)}, f32[48,3264]{1,0:T(8,128)}, f32[48,3264]{1,0:T(8,128)}, f32[48,128]{1,0:T(8,128)}) custom-call(f32[48,3264]{1,0:T(8,128)} %w_ref.1, f32[48,3264]{1,0:T(8,128)} %m_ref.1, f32[48,3264]{1,0:T(8,128)} %v_ref.1, bf16[48,1536]{1,0:T(8,128)(2,1)} %add_convert_fusion.11.rest_0_, ...), custom_call_target="tpu_custom_call" | custom-call | tf_op jit(solution)/shard_map/pallas_call | solution.py:415
  227.5 2.4 %collective-permute-done.73 = f32[2,48]{0,1:T(8,128)S(1)} collective-permute-done((f32[2,48]{0,1:T(8,128)S(1)}, f32[2,48]{0,1:T(8,128)S(1)}, u32[]{:S(2)}, u32[]{:S(2)}) %collective-permute-start.73) | collective-permute-done | bytes 416 | tf_op jit(solution)/shard_map/ppermute | solution.py:56
  (304 shorter events, 53.6 us)
Async XLA Ops:
  2.6 11.5 %collective-permute-start = (bf16[48,1664]{1,0:T(8,128)(2,1)S(1)}, bf16[48,1664]{1,0:T(8,128)(2,1)S(1)}, u32[]{:S(2)}, u32[]{:S(2)}) collective-permute-start(bf16[48,1664]{1,0:T(8,128)(2,1)S(1)} %fusion.2.rest_0_.rest_16_.rest_4_), channel_id=1, source_target_pairs={{0,8},{8,0},{16,24},{24,16},{1,9},{9,1},{17,25},{25,17},{2,10},{10... | collective-permute-start | bytes 479240 | tf_op jit(solution)/shard_map/ppermute | solution.py:56
  5.8 18.9 %collective-permute-start.31 = (bf16[48,1792]{1,0:T(8,128)(2,1)S(1)}, bf16[48,1792]{1,0:T(8,128)(2,1)S(1)}, u32[]{:S(2)}, u32[]{:S(2)}) collective-permute-start(bf16[48,1792]{1,0:T(8,128)(2,1)S(1)} %pad.9.rest_0_), channel_id=1, source_target_pairs={{0,8},{8,0},{16,24},{24,16},{1,9},{9,1},{17,25},{25,17},{2,10},{10... | collective-permute-start | bytes 516104 | tf_op jit(solution)/shard_map/ppermute | solution.py:56
  5.9 11.5 %collective-permute-start.1 = (bf16[48,1664]{1,0:T(8,128)(2,1)S(1)}, bf16[48,1664]{1,0:T(8,128)(2,1)S(1)}, u32[]{:S(2)}, u32[]{:S(2)}) collective-permute-start(bf16[48,1664]{1,0:T(8,128)(2,1)S(1)} %fusion.2.rest_0_.rest_16_.rest_4_), channel_id=1, source_target_pairs={{0,16},{8,24},{16,0},{24,8},{1,17},{9,25},{17,1},{25,9},{2,18},{10... | collective-permute-start | bytes 479240 | tf_op jit(solution)/shard_map/ppermute | solution.py:56
  8.9 13.8 %collective-permute-start.2 = (bf16[48,1664]{1,0:T(8,128)(2,1)S(1)}, bf16[48,1664]{1,0:T(8,128)(2,1)S(1)}, u32[]{:S(2)}, u32[]{:S(2)}) collective-permute-start(bf16[48,1664]{1,0:T(8,128)(2,1)S(1)} %fusion.2.rest_0_.rest_16_.rest_4_), channel_id=1, source_target_pairs={{0,24},{8,16},{16,8},{24,0},{1,25},{9,17},{17,9},{25,1},{2,26},{10... | collective-permute-start | bytes 479240 | tf_op jit(solution)/shard_map/ppermute | solution.py:56
  10.2 13.9 %collective-permute-start.3 = (bf16[48,1664]{1,0:T(8,128)(2,1)S(1)}, bf16[48,1664]{1,0:T(8,128)(2,1)S(1)}, u32[]{:S(2)}, u32[]{:S(2)}) collective-permute-start(bf16[48,1664]{1,0:T(8,128)(2,1)S(1)} %fusion.2.rest_0_.rest_16_.rest_4_), channel_id=1, source_target_pairs={{0,4},{2,6},{4,0},{6,2},{1,5},{3,7},{5,1},{7,3},{8,12},{10,14},{12... | collective-permute-start | bytes 479240 | tf_op jit(solution)/shard_map/ppermute | solution.py:56
  14.1 10.6 %collective-permute-start.7 = (bf16[48,1664]{1,0:T(8,128)(2,1)S(1)}, bf16[48,1664]{1,0:T(8,128)(2,1)S(1)}, u32[]{:S(2)}, u32[]{:S(2)}) collective-permute-start(bf16[48,1664]{1,0:T(8,128)(2,1)S(1)} %fusion.2.rest_0_.rest_16_.rest_4_), channel_id=1, source_target_pairs={{0,2},{2,0},{4,6},{6,4},{1,3},{3,1},{5,7},{7,5},{8,10},{10,8},{12,... | collective-permute-start | bytes 479240 | tf_op jit(solution)/shard_map/ppermute | solution.py:56
  17.4 7.8 %collective-permute-start.4 = (bf16[48,1664]{1,0:T(8,128)(2,1)S(1)}, bf16[48,1664]{1,0:T(8,128)(2,1)S(1)}, u32[]{:S(2)}, u32[]{:S(2)}) collective-permute-start(bf16[48,1664]{1,0:T(8,128)(2,1)S(1)} %collective-permute-done.rest_1_.rest_17_.rest_5_), channel_id=1, source_target_pairs={{0,4},{2,6},{4,0},{6,2},{1,5},{3,7},{5,1},{7,3},{8,12},{10,14},{12... | collective-permute-start | bytes 479240 | tf_op jit(solution)/shard_map/ppermute | solution.py:56
  31.7 15.6 %collective-permute-start.32 = (bf16[48,1792]{1,0:T(8,128)(2,1)S(1)}, bf16[48,1792]{1,0:T(8,128)(2,1)S(1)}, u32[]{:S(2)}, u32[]{:S(2)}) collective-permute-start(bf16[48,1792]{1,0:T(8,128)(2,1)S(1)} %pad.9.rest_0_), channel_id=1, source_target_pairs={{0,16},{8,24},{16,0},{24,8},{1,17},{9,25},{17,1},{25,9},{2,18},{10... | collective-permute-start | bytes 516104 | tf_op jit(solution)/shard_map/ppermute | solution.py:56
  34.1 13.2 %collective-permute-start.33 = (bf16[48,1792]{1,0:T(8,128)(2,1)S(1)}, bf16[48,1792]{1,0:T(8,128)(2,1)S(1)}, u32[]{:S(2)}, u32[]{:S(2)}) collective-permute-start(bf16[48,1792]{1,0:T(8,128)(2,1)S(1)} %pad.9.rest_0_), channel_id=1, source_target_pairs={{0,24},{8,16},{16,8},{24,0},{1,25},{9,17},{17,9},{25,1},{2,26},{10... | collective-permute-start | bytes 516104 | tf_op jit(solution)/shard_map/ppermute | solution.py:56
  36.1 16.4 %collective-permute-start.34 = (bf16[48,1792]{1,0:T(8,128)(2,1)S(1)}, bf16[48,1792]{1,0:T(8,128)(2,1)S(1)}, u32[]{:S(2)}, u32[]{:S(2)}) collective-permute-start(bf16[48,1792]{1,0:T(8,128)(2,1)S(1)} %pad.9.rest_0_), channel_id=1, source_target_pairs={{0,4},{2,6},{4,0},{6,2},{1,5},{3,7},{5,1},{7,3},{8,12},{10,14},{12... | collective-permute-start | bytes 516104 | tf_op jit(solution)/shard_map/ppermute | solution.py:56
  37.6 15.7 %collective-permute-start.38 = (bf16[48,1792]{1,0:T(8,128)(2,1)S(1)}, bf16[48,1792]{1,0:T(8,128)(2,1)}, u32[]{:S(2)}, u32[]{:S(2)}) collective-permute-start(bf16[48,1792]{1,0:T(8,128)(2,1)S(1)} %pad.9.rest_0_), channel_id=1, source_target_pairs={{0,2},{2,0},{4,6},{6,4},{1,3},{3,1},{5,7},{7,5},{8,10},{10,8},{12,... | collective-permute-start | bytes 516104 | tf_op jit(solution)/shard_map/ppermute | solution.py:56
  37.7 17.2 %collective-permute-start.35 = (bf16[48,1792]{1,0:T(8,128)(2,1)S(1)}, bf16[48,1792]{1,0:T(8,128)(2,1)}, u32[]{:S(2)}, u32[]{:S(2)}) collective-permute-start(bf16[48,1792]{1,0:T(8,128)(2,1)S(1)} %collective-permute-done.31.rest_1_), channel_id=1, source_target_pairs={{0,4},{2,6},{4,0},{6,2},{1,5},{3,7},{5,1},{7,3},{8,12},{10,14},{12... | collective-permute-start | bytes 516104 | tf_op jit(solution)/shard_map/ppermute | solution.py:56
  47.3 19.3 %collective-permute-start.16 = (bf16[128,768]{1,0:T(8,128)(2,1)}, bf16[128,768]{1,0:T(8,128)(2,1)S(1)}, u32[]{:S(2)}, u32[]{:S(2)}) collective-permute-start(bf16[128,768]{1,0:T(8,128)(2,1)} %get-tuple-element.62.rest_0_), channel_id=1, source_target_pairs={{0,16},{8,24},{16,0},{24,8},{1,17},{9,25},{17,1},{25,9},{2,18},{10... | collective-permute-start | bytes 589832 | tf_op jit(solution)/shard_map/ppermute | solution.py:56
  52.6 15.6 %collective-permute-start.17 = (bf16[128,768]{1,0:T(8,128)(2,1)}, bf16[128,768]{1,0:T(8,128)(2,1)S(1)}, u32[]{:S(2)}, u32[]{:S(2)}) collective-permute-start(bf16[128,768]{1,0:T(8,128)(2,1)} %get-tuple-element.62.rest_0_), channel_id=1, source_target_pairs={{0,24},{8,16},{16,8},{24,0},{1,25},{9,17},{17,9},{25,1},{2,26},{10... | collective-permute-start | bytes 589832 | tf_op jit(solution)/shard_map/ppermute | solution.py:56
  53.3 15.3 %collective-permute-start.18 = (bf16[128,768]{1,0:T(8,128)(2,1)}, bf16[128,768]{1,0:T(8,128)(2,1)S(1)}, u32[]{:S(2)}, u32[]{:S(2)}) collective-permute-start(bf16[128,768]{1,0:T(8,128)(2,1)} %get-tuple-element.62.rest_0_), channel_id=1, source_target_pairs={{0,4},{2,6},{4,0},{6,2},{1,5},{3,7},{5,1},{7,3},{8,12},{10,14},{12... | collective-permute-start | bytes 589832 | tf_op jit(solution)/shard_map/ppermute | solution.py:56
  54.8 13.8 %collective-permute-start.22 = (bf16[128,768]{1,0:T(8,128)(2,1)}, bf16[128,768]{1,0:T(8,128)(2,1)S(1)}, u32[]{:S(2)}, u32[]{:S(2)}) collective-permute-start(bf16[128,768]{1,0:T(8,128)(2,1)} %get-tuple-element.62.rest_0_), channel_id=1, source_target_pairs={{0,2},{2,0},{4,6},{6,4},{1,3},{3,1},{5,7},{7,5},{8,10},{10,8},{12,... | collective-permute-start | bytes 589832 | tf_op jit(solution)/shard_map/ppermute | solution.py:56
  54.9 14.3 %collective-permute-start.19 = (bf16[128,768]{1,0:T(8,128)(2,1)S(1)}, bf16[128,768]{1,0:T(8,128)(2,1)S(1)}, u32[]{:S(2)}, u32[]{:S(2)}) collective-permute-start(bf16[128,768]{1,0:T(8,128)(2,1)S(1)} %collective-permute-done.15.rest_1_), channel_id=1, source_target_pairs={{0,4},{2,6},{4,0},{6,2},{1,5},{3,7},{5,1},{7,3},{8,12},{10,14},{12... | collective-permute-start | bytes 589832 | tf_op jit(solution)/shard_map/ppermute | solution.py:56
  66.6 7.8 %collective-permute-start.20 = (bf16[128,768]{1,0:T(8,128)(2,1)S(1)}, bf16[128,768]{1,0:T(8,128)(2,1)S(1)}, u32[]{:S(2)}, u32[]{:S(2)}) collective-permute-start(bf16[128,768]{1,0:T(8,128)(2,1)S(1)} %collective-permute-done.16.rest_2_), channel_id=1, source_target_pairs={{0,4},{2,6},{4,0},{6,2},{1,5},{3,7},{5,1},{7,3},{8,12},{10,14},{12... | collective-permute-start | bytes 589832 | tf_op jit(solution)/shard_map/ppermute | solution.py:56
  68.1 8.5 %collective-permute-start.21 = (bf16[128,768]{1,0:T(8,128)(2,1)S(1)}, bf16[128,768]{1,0:T(8,128)(2,1)S(1)}, u32[]{:S(2)}, u32[]{:S(2)}) collective-permute-start(bf16[128,768]{1,0:T(8,128)(2,1)S(1)} %collective-permute-done.17.rest_3_), channel_id=1, source_target_pairs={{0,4},{2,6},{4,0},{6,2},{1,5},{3,7},{5,1},{7,3},{8,12},{10,14},{12... | collective-permute-start | bytes 589832 | tf_op jit(solution)/shard_map/ppermute | solution.py:56
  68.7 8.0 %collective-permute-start.23 = (bf16[128,768]{1,0:T(8,128)(2,1)S(1)}, bf16[128,768]{1,0:T(8,128)(2,1)S(1)}, u32[]{:S(2)}, u32[]{:S(2)}) collective-permute-start(bf16[128,768]{1,0:T(8,128)(2,1)S(1)} %collective-permute-done.15.rest_1_), channel_id=1, source_target_pairs={{0,2},{2,0},{4,6},{6,4},{1,3},{3,1},{5,7},{7,5},{8,10},{10,8},{12,... | collective-permute-start | bytes 589832 | tf_op jit(solution)/shard_map/ppermute | solution.py:56
  68.7 8.5 %collective-permute-start.24 = (bf16[128,768]{1,0:T(8,128)(2,1)S(1)}, bf16[128,768]{1,0:T(8,128)(2,1)S(1)}, u32[]{:S(2)}, u32[]{:S(2)}) collective-permute-start(bf16[128,768]{1,0:T(8,128)(2,1)S(1)} %collective-permute-done.16.rest_2_), channel_id=1, source_target_pairs={{0,2},{2,0},{4,6},{6,4},{1,3},{3,1},{5,7},{7,5},{8,10},{10,8},{12,... | collective-permute-start | bytes 589832 | tf_op jit(solution)/shard_map/ppermute | solution.py:56
  69.2 8.1 %collective-permute-start.25 = (bf16[128,768]{1,0:T(8,128)(2,1)S(1)}, bf16[128,768]{1,0:T(8,128)(2,1)S(1)}, u32[]{:S(2)}, u32[]{:S(2)}) collective-permute-start(bf16[128,768]{1,0:T(8,128)(2,1)S(1)} %collective-permute-done.17.rest_3_), channel_id=1, source_target_pairs={{0,2},{2,0},{4,6},{6,4},{1,3},{3,1},{5,7},{7,5},{8,10},{10,8},{12,... | collective-permute-start | bytes 589832 | tf_op jit(solution)/shard_map/ppermute | solution.py:56
  77.3 10.8 %collective-permute-start.36 = (bf16[48,1792]{1,0:T(8,128)(2,1)S(1)}, bf16[48,1792]{1,0:T(8,128)(2,1)}, u32[]{:S(2)}, u32[]{:S(2)}) collective-permute-start(bf16[48,1792]{1,0:T(8,128)(2,1)S(1)} %collective-permute-done.32.rest_2_), channel_id=1, source_target_pairs={{0,4},{2,6},{4,0},{6,2},{1,5},{3,7},{5,1},{7,3},{8,12},{10,14},{12... | collective-permute-start | bytes 516104 | tf_op jit(solution)/shard_map/ppermute | solution.py:56
  78.8 10.9 %collective-permute-start.37 = (bf16[48,1792]{1,0:T(8,128)(2,1)}, bf16[48,1792]{1,0:T(8,128)(2,1)}, u32[]{:S(2)}, u32[]{:S(2)}) collective-permute-start(bf16[48,1792]{1,0:T(8,128)(2,1)} %copy-done.48), channel_id=1, source_target_pairs={{0,4},{2,6},{4,0},{6,2},{1,5},{3,7},{5,1},{7,3},{8,12},{10,14},{12... | collective-permute-start | bytes 516104 | tf_op jit(solution)/shard_map/ppermute | solution.py:56
  79.3 10.4 %collective-permute-start.39 = (bf16[48,1792]{1,0:T(8,128)(2,1)S(1)}, bf16[48,1792]{1,0:T(8,128)(2,1)}, u32[]{:S(2)}, u32[]{:S(2)}) collective-permute-start(bf16[48,1792]{1,0:T(8,128)(2,1)S(1)} %collective-permute-done.31.rest_1_), channel_id=1, source_target_pairs={{0,2},{2,0},{4,6},{6,4},{1,3},{3,1},{5,7},{7,5},{8,10},{10,8},{12,... | collective-permute-start | bytes 516104 | tf_op jit(solution)/shard_map/ppermute | solution.py:56
  79.4 10.8 %collective-permute-start.40 = (bf16[48,1792]{1,0:T(8,128)(2,1)S(1)}, bf16[48,1792]{1,0:T(8,128)(2,1)}, u32[]{:S(2)}, u32[]{:S(2)}) collective-permute-start(bf16[48,1792]{1,0:T(8,128)(2,1)S(1)} %collective-permute-done.32.rest_2_), channel_id=1, source_target_pairs={{0,2},{2,0},{4,6},{6,4},{1,3},{3,1},{5,7},{7,5},{8,10},{10,8},{12,... | collective-permute-start | bytes 516104 | tf_op jit(solution)/shard_map/ppermute | solution.py:56
  79.9 10.4 %collective-permute-start.41 = (bf16[48,1792]{1,0:T(8,128)(2,1)}, bf16[48,1792]{1,0:T(8,128)(2,1)}, u32[]{:S(2)}, u32[]{:S(2)}) collective-permute-start(bf16[48,1792]{1,0:T(8,128)(2,1)} %copy-done.48), channel_id=1, source_target_pairs={{0,2},{2,0},{4,6},{6,4},{1,3},{3,1},{5,7},{7,5},{8,10},{10,8},{12,... | collective-permute-start | bytes 516104 | tf_op jit(solution)/shard_map/ppermute | solution.py:56
  106.8 17.4 %collective-permute-start.65 = (bf16[384,1792]{1,0:T(8,128)(2,1)}, bf16[384,1792]{1,0:T(8,128)(2,1)}, u32[]{:S(2)}, u32[]{:S(2)}) collective-permute-start(bf16[384,1792]{1,0:T(8,128)(2,1)} %get-tuple-element.98), channel_id=1, source_target_pairs={{0,2},{2,0},{4,6},{6,4},{1,3},{3,1},{5,7},{7,5},{8,10},{10,8},{12,... | collective-permute-start | bytes 4128776 | tf_op jit(solution)/shard_map/ppermute | solution.py:56
  119.1 12.4 %collective-permute-start.48 = (bf16[1024,768]{1,0:T(8,128)(2,1)}, bf16[1024,768]{1,0:T(8,128)(2,1)S(1)}, u32[]{:S(2)}, u32[]{:S(2)}) collective-permute-start(bf16[1024,768]{1,0:T(8,128)(2,1)} %get-tuple-element.74), channel_id=1, source_target_pairs={{0,2},{2,0},{4,6},{6,4},{1,3},{3,1},{5,7},{7,5},{8,10},{10,8},{12,... | collective-permute-start | bytes 4718600 | tf_op jit(solution)/shard_map/ppermute | solution.py:56
  119.6 9.1 %collective-permute-start.46 = (bf16[128,768]{1,0:T(8,128)(2,1)S(1)}, bf16[128,768]{1,0:T(8,128)(2,1)S(1)}, u32[]{:S(2)}, u32[]{:S(2)}) collective-permute-start(bf16[128,768]{1,0:T(8,128)(2,1)S(1)} %copy-done.42), channel_id=1, source_target_pairs={{0,1},{1,0},{2,3},{3,2},{4,5},{5,4},{6,7},{7,6},{8,9},{9,8},{10,11... | collective-permute-start | bytes 589832 | tf_op jit(solution)/shard_map/ppermute | solution.py:56
  127.2 9.2 %collective-permute-start.71 = (bf16[48,1792]{1,0:T(8,128)(2,1)}, bf16[48,1792]{1,0:T(8,128)(2,1)S(1)}, u32[]{:S(2)}, u32[]{:S(2)}) collective-permute-start(bf16[48,1792]{1,0:T(8,128)(2,1)} %get-tuple-element.106), channel_id=1, source_target_pairs={{0,4},{2,6},{4,0},{6,2},{1,5},{3,7},{5,1},{7,3},{8,12},{10,14},{12... | collective-permute-start | bytes 516104 | tf_op jit(solution)/shard_map/ppermute | solution.py:56
  129.5 47.4 %collective-permute-start.69 = (bf16[48,1792]{1,0:T(8,128)(2,1)}, bf16[48,1792]{1,0:T(8,128)(2,1)S(1)}, u32[]{:S(2)}, u32[]{:S(2)}) collective-permute-start(bf16[48,1792]{1,0:T(8,128)(2,1)} %get-tuple-element.104), channel_id=1, source_target_pairs={{0,4},{2,6},{4,0},{6,2},{1,5},{3,7},{5,1},{7,3},{8,12},{10,14},{12... | collective-permute-start | bytes 516104 | tf_op jit(solution)/shard_map/ppermute | solution.py:56
  130.0 50.4 %collective-permute-start.67 = (bf16[48,1792]{1,0:T(8,128)(2,1)}, bf16[48,1792]{1,0:T(8,128)(2,1)S(1)}, u32[]{:S(2)}, u32[]{:S(2)}) collective-permute-start(bf16[48,1792]{1,0:T(8,128)(2,1)} %get-tuple-element.102), channel_id=1, source_target_pairs={{0,4},{2,6},{4,0},{6,2},{1,5},{3,7},{5,1},{7,3},{8,12},{10,14},{12... | collective-permute-start | bytes 516104 | tf_op jit(solution)/shard_map/ppermute | solution.py:56
  135.8 10.5 %collective-permute-start.54 = (bf16[128,768]{1,0:T(8,128)(2,1)}, bf16[128,768]{1,0:T(8,128)(2,1)S(1)}, u32[]{:S(2)}, u32[]{:S(2)}) collective-permute-start(bf16[128,768]{1,0:T(8,128)(2,1)} %get-tuple-element.82), channel_id=1, source_target_pairs={{0,4},{2,6},{4,0},{6,2},{1,5},{3,7},{5,1},{7,3},{8,12},{10,14},{12... | collective-permute-start | bytes 589832 | tf_op jit(solution)/shard_map/ppermute | solution.py:56
  136.4 14.0 %collective-permute-start.52 = (bf16[128,768]{1,0:T(8,128)(2,1)}, bf16[128,768]{1,0:T(8,128)(2,1)S(1)}, u32[]{:S(2)}, u32[]{:S(2)}) collective-permute-start(bf16[128,768]{1,0:T(8,128)(2,1)} %get-tuple-element.80), channel_id=1, source_target_pairs={{0,4},{2,6},{4,0},{6,2},{1,5},{3,7},{5,1},{7,3},{8,12},{10,14},{12... | collective-permute-start | bytes 589832 | tf_op jit(solution)/shard_map/ppermute | solution.py:56
  137.9 16.7 %collective-permute-start.50 = (bf16[128,768]{1,0:T(8,128)(2,1)}, bf16[128,768]{1,0:T(8,128)(2,1)S(1)}, u32[]{:S(2)}, u32[]{:S(2)}) collective-permute-start(bf16[128,768]{1,0:T(8,128)(2,1)} %get-tuple-element.78), channel_id=1, source_target_pairs={{0,4},{2,6},{4,0},{6,2},{1,5},{3,7},{5,1},{7,3},{8,12},{10,14},{12... | collective-permute-start | bytes 589832 | tf_op jit(solution)/shard_map/ppermute | solution.py:56
  146.2 11.9 %collective-permute-start.49 = (bf16[128,768]{1,0:T(8,128)(2,1)}, bf16[128,768]{1,0:T(8,128)(2,1)S(1)}, u32[]{:S(2)}, u32[]{:S(2)}) collective-permute-start(bf16[128,768]{1,0:T(8,128)(2,1)} %get-tuple-element.76), channel_id=1, source_target_pairs={{0,4},{2,6},{4,0},{6,2},{1,5},{3,7},{5,1},{7,3},{8,12},{10,14},{12... | collective-permute-start | bytes 589832 | tf_op jit(solution)/shard_map/ppermute | solution.py:56
  150.4 8.5 %collective-permute-start.55 = (bf16[128,768]{1,0:T(8,128)(2,1)S(1)}, bf16[128,768]{1,0:T(8,128)(2,1)S(1)}, u32[]{:S(2)}, u32[]{:S(2)}) collective-permute-start(bf16[128,768]{1,0:T(8,128)(2,1)S(1)} %add_convert_fusion), channel_id=1, source_target_pairs={{0,8},{8,0},{16,24},{24,16},{1,9},{9,1},{17,25},{25,17},{2,10},{10... | collective-permute-start | bytes 589832 | tf_op jit(solution)/shard_map/ppermute | solution.py:56
  154.6 15.0 %collective-permute-start.53 = (bf16[128,768]{1,0:T(8,128)(2,1)S(1)}, bf16[128,768]{1,0:T(8,128)(2,1)S(1)}, u32[]{:S(2)}, u32[]{:S(2)}) collective-permute-start(bf16[128,768]{1,0:T(8,128)(2,1)S(1)} %add_convert_fusion.1), channel_id=1, source_target_pairs={{0,16},{8,24},{16,0},{24,8},{1,17},{9,25},{17,1},{25,9},{2,18},{10... | collective-permute-start | bytes 589832 | tf_op jit(solution)/shard_map/ppermute | solution.py:56
  158.1 11.5 %collective-permute-start.51 = (bf16[128,768]{1,0:T(8,128)(2,1)S(1)}, bf16[128,768]{1,0:T(8,128)(2,1)S(1)}, u32[]{:S(2)}, u32[]{:S(2)}) collective-permute-start(bf16[128,768]{1,0:T(8,128)(2,1)S(1)} %add_convert_fusion.2), channel_id=1, source_target_pairs={{0,24},{8,16},{16,8},{24,0},{1,25},{9,17},{17,9},{25,1},{2,26},{10... | collective-permute-start | bytes 589832 | tf_op jit(solution)/shard_map/ppermute | solution.py:56
  158.9 25.0 %collective-permute-start.66 = (bf16[48,1792]{1,0:T(8,128)(2,1)}, bf16[48,1792]{1,0:T(8,128)(2,1)S(1)}, u32[]{:S(2)}, u32[]{:S(2)}) collective-permute-start(bf16[48,1792]{1,0:T(8,128)(2,1)} %get-tuple-element.100), channel_id=1, source_target_pairs={{0,4},{2,6},{4,0},{6,2},{1,5},{3,7},{5,1},{7,3},{8,12},{10,14},{12... | collective-permute-start | bytes 516104 | tf_op jit(solution)/shard_map/ppermute | solution.py:56
  169.6 39.0 %collective-permute-start.72 = (bf16[48,1792]{1,0:T(8,128)(2,1)S(1)}, bf16[48,1792]{1,0:T(8,128)(2,1)S(1)}, u32[]{:S(2)}, u32[]{:S(2)}) collective-permute-start(bf16[48,1792]{1,0:T(8,128)(2,1)S(1)} %add_convert_fusion.4), channel_id=1, source_target_pairs={{0,8},{8,0},{16,24},{24,16},{1,9},{9,1},{17,25},{25,17},{2,10},{10... | collective-permute-start | bytes 516104 | tf_op jit(solution)/shard_map/ppermute | solution.py:56
  176.8 14.3 %collective-permute-start.57 = (bf16[384,1536]{1,0:T(8,128)(2,1)}, bf16[384,1536]{1,0:T(8,128)(2,1)S(1)}, u32[]{:S(2)}, u32[]{:S(2)}) collective-permute-start(bf16[384,1536]{1,0:T(8,128)(2,1)} %get-tuple-element.85), channel_id=1, source_target_pairs={{0,2},{2,0},{4,6},{6,4},{1,3},{3,1},{5,7},{7,5},{8,10},{10,8},{12,... | collective-permute-start | bytes 3538952 | tf_op jit(solution)/shard_map/ppermute | solution.py:56
  176.9 36.9 %collective-permute-start.70 = (bf16[48,1792]{1,0:T(8,128)(2,1)S(1)}, bf16[48,1792]{1,0:T(8,128)(2,1)S(1)}, u32[]{:S(2)}, u32[]{:S(2)}) collective-permute-start(bf16[48,1792]{1,0:T(8,128)(2,1)S(1)} %add_convert_fusion.5), channel_id=1, source_target_pairs={{0,16},{8,24},{16,0},{24,8},{1,17},{9,25},{17,1},{25,9},{2,18},{10... | collective-permute-start | bytes 516104 | tf_op jit(solution)/shard_map/ppermute | solution.py:56
  180.5 33.4 %collective-permute-start.68 = (bf16[48,1792]{1,0:T(8,128)(2,1)S(1)}, bf16[48,1792]{1,0:T(8,128)(2,1)S(1)}, u32[]{:S(2)}, u32[]{:S(2)}) collective-permute-start(bf16[48,1792]{1,0:T(8,128)(2,1)S(1)} %add_convert_fusion.6), channel_id=1, source_target_pairs={{0,24},{8,16},{16,8},{24,0},{1,25},{9,17},{17,9},{25,1},{2,26},{10... | collective-permute-start | bytes 516104 | tf_op jit(solution)/shard_map/ppermute | solution.py:56
  196.2 8.6 %collective-permute-start.61 = (bf16[48,1536]{1,0:T(8,128)(2,1)}, bf16[48,1536]{1,0:T(8,128)(2,1)S(1)}, u32[]{:S(2)}, u32[]{:S(2)}) collective-permute-start(bf16[48,1536]{1,0:T(8,128)(2,1)} %get-tuple-element.91), channel_id=1, source_target_pairs={{0,4},{2,6},{4,0},{6,2},{1,5},{3,7},{5,1},{7,3},{8,12},{10,14},{12... | collective-permute-start | bytes 442376 | tf_op jit(solution)/shard_map/ppermute | solution.py:56
  208.7 11.2 %collective-permute-start.62 = (bf16[48,1536]{1,0:T(8,128)(2,1)S(1)}, bf16[48,1536]{1,0:T(8,128)(2,1)S(1)}, u32[]{:S(2)}, u32[]{:S(2)}) collective-permute-start(bf16[48,1536]{1,0:T(8,128)(2,1)S(1)} %add_convert_fusion.9), channel_id=1, source_target_pairs={{0,16},{8,24},{16,0},{24,8},{1,17},{9,25},{17,1},{25,9},{2,18},{10... | collective-permute-start | bytes 442376 | tf_op jit(solution)/shard_map/ppermute | solution.py:56
  210.2 9.7 %collective-permute-start.60 = (bf16[48,1536]{1,0:T(8,128)(2,1)S(1)}, bf16[48,1536]{1,0:T(8,128)(2,1)S(1)}, u32[]{:S(2)}, u32[]{:S(2)}) collective-permute-start(bf16[48,1536]{1,0:T(8,128)(2,1)S(1)} %add_convert_fusion.10), channel_id=1, source_target_pairs={{0,24},{8,16},{16,8},{24,0},{1,25},{9,17},{17,9},{25,1},{2,26},{10... | collective-permute-start | bytes 442376 | tf_op jit(solution)/shard_map/ppermute | solution.py:56
  (98 other events, 944.4 us)
where the time goes:
time: 234 us; the launch traced here: 233 us
  waiting for transfers between devices  88 us (38%)
  starting transfers between devices  67 us (29%)
  Pallas kernels  51.1 us (22%)
  local copies, waits for them, and re-layouts  12.9 us (6%)
  other arithmetic  12.3 us (5%)
    ppermute x74, waiting for transfers between devices, swap(): return lax.ppermute(x, axis, [(i, i ^ bits) for i in range(size)])  88 us
    ppermute x74, starting transfers between devices, swap(): return lax.ppermute(x, axis, [(i, i ^ bits) for i in range(size)])  67 us
    pallas_call x7, Pallas kernels, call(): pl.pallas_call(kernel, out_shape=out_shape, in_specs=specs, out_specs=jax...  42.3 us
    unnamed x149, local copies, waits for them, and re-layouts  8.85 us
    pallas_call x3, Pallas kernels, scatter_sum(): pl.pallas_call(add_kernel, out_shape=[sds((rows, cols), BF16)] * 8, in_sp...  8.78 us
    convert_element_type x12, other arithmetic, scatter_sum(): t[z] = (s[z].astype(F32) + got.astype(F32)).astype(BF16)  7.1 us
  transfers between devices with their start and end apart: 74, of which 27 were waited for; matrix products, arithmetic and copies ran while one was open for 6% of the time, Pallas kernels for 18%

commit v1 on v0

--- a/solution.py
+++ b/solution.py
@@ -68,8 +68,9 @@
     if not staged():
         return [lax.all_gather(x, TOKENS_AX, axis=0, tiled=True)]
     got = {0: x}
-    for z in range(1, 4):
-        got[z * 4] = swap(x, "blk", z)
+    got[8] = swap(x, "blk", 2)
+    got[4] = swap(x, "blk", 1)
+    got[12] = swap(got[8], "blk", 1)
     for z in range(4):
         got[z * 4 + 2] = swap(got[z * 4], "shard", 2)
     for z in range(4):
@@ -99,11 +100,15 @@
         out_specs=[VM] * 8,
         name="pair_add",
     )(keep, recv)
-    t = {}
-    for z in (3, 2, 1, 0):
-        got = swap(s[4 + z], "shard", 2)
-        t[z] = (s[z].astype(F32) + got.astype(F32)).astype(BF16)
-    return [t[0]] + [swap(t[z], "blk", z) for z in (3, 2, 1)]
+    got = {z: swap(s[4 + z], "shard", 2) for z in (3, 2, 1, 0)}
+
+    def block(z, *more):
+        return total([s[z], got[z], *more]).astype(BF16)
+
+    far = swap(block(3), "blk", 1)
+    two = swap(block(2, far), "blk", 2)
+    one = swap(block(1), "blk", 1)
+    return [s[0], got[0], one, two]
 
 
 def total(terms):
@@ -438,13 +443,12 @@
     return tensor, moment, second
 
 
-def adam_kernel(nf, width, units, w_ref, m_ref, v_ref, *rest):
+def gsum_kernel(nf, width, units, w_ref, *rest):
     firsts, lasts = rest[:nf], rest[nf : 2 * nf]
-    g_ref, w_out, m_out, v_out, gain_ref = rest[2 * nf :]
+    g_ref, gain_ref = rest[2 * nf :]
     one = total([term[...] for term in firsts])
     two = total([term[...] for term in lasts])[:, : 3 * units]
-    w = w_ref[...]
-    wf = w.astype(BF16).astype(F32)
+    wf = w_ref[...].astype(BF16).astype(F32)
     cut = 4 * width
     sums = [
         jnp.sum(wf[:, : 3 * width] * one[:, : 3 * width], axis=1, keepdims=True),
@@ -452,9 +456,14 @@
     ]
     lane = lax.broadcasted_iota(jnp.int32, gain_ref.shape, 1)
     gain_ref[...] = jnp.where(lane == 0, sums[0], jnp.where(lane == 1, sums[1], 0.0))
-    grad = jnp.concatenate([one, two], axis=1)
-    g_ref[...] = grad
-    w_out[...], m_out[...], v_out[...] = adam_update(w, grad, m_ref[...], v_ref[...])
+    g_ref[:, :cut] = one
+    g_ref[:, cut:] = two
+
+
+def adam_kernel(w_ref, g_ref, m_ref, v_ref, w_out, m_out, v_out):
+    w_out[...], m_out[...], v_out[...] = adam_update(
+        w_ref[...], g_ref[...], m_ref[...], v_ref[...]
+    )
 
 
 def head_swap(x):
@@ -583,15 +592,25 @@
 
     first_terms = scatter_sum(grads[:halves])
     full = weights.shape
-    weight_grad, new_weights, new_weight_moment, new_weight_second, gain_part = call(
-        partial(adam_kernel, nt, width, units),
-        [sds(full, F32)] * 4 + [sds((rows, 128), F32)],
-        [VM] * (3 + 2 * nt),
+    weight_grad, gain_part = call(
+        partial(gsum_kernel, nt, width, units),
+        [sds(full, F32), sds((rows, 128), F32)],
+        [VM] * (1 + 2 * nt),
         [],
-        [weights, weight_moment, weight_second] + first_terms + ffn_terms,
+        [weights] + first_terms + ffn_terms,
     )
     gain_part = gain_part[:, :2].T
     gain_grad = (gain_part + head_swap(gain_part)) / gb.astype(F32)
+    step_rows = 8 if rows % 8 == 0 else rows
+    cells = pl.BlockSpec((step_rows, full[1]), lambda i: (i, 0))
+    new_weights, new_weight_moment, new_weight_second = pl.pallas_call(
+        adam_kernel,
+        grid=(rows // step_rows,),
+        out_shape=[sds(full, F32)] * 3,
+        in_specs=[cells] * 4,
+        out_specs=[cells] * 3,
+        name="adam",
+    )(weights, weight_grad, weight_moment, weight_second)
     new_gains, new_gain_moment, new_gain_second = adam_update(
         gains, gain_grad, gain_moment, gain_second
     )

time: 234 us -> 225 us (0.962)
  waiting for transfers between devices: 88 us -> 81 us
  Pallas kernels: 51.1 us -> 54.4 us
  starting transfers between devices: 67 us -> 63.8 us
  other arithmetic: 12.3 us -> 9.21 us
    ppermute x74, waiting for transfers between devices: 88 us -> 81 us  [swap(): return lax.ppermute(x, axis, [(i, i ^ bits) for i in range(size)])]
    pallas_call x0 -> x1, Pallas kernels: none -> 5.08 us  [layer(): pl.pallas_call(adam_kernel, grid=(rows // step_rows,), out_shape=[sds(ful...]
    convert_element_type x12 -> x9, other arithmetic: 7.1 us -> 2.28 us  [block(): return total([s[z], got[z], *more]).astype(BF16)]
    ppermute x74, starting transfers between devices: 67 us -> 63.8 us  [swap(): return lax.ppermute(x, axis, [(i, i ^ bits) for i in range(size)])]
    unnamed x149 -> x157, local copies, waits for them, and re-layouts: 8.85 us -> 9.99 us
  transfers between devices with their start and end apart: 74 -> 74, of which waited for: 27 -> 29; matrix products, arithmetic and copies ran while one was open for 6% -> 5% of each run, Pallas kernels for 18% -> 16%
where the time goes in v1:
time: 225 us
  waiting for transfers between devices  81 us (36%)
  starting transfers between devices  63.8 us (28%)
  Pallas kernels  54.4 us (24%)
  local copies, waits for them, and re-layouts  14.6 us (6%)
  other arithmetic  9.21 us (4%)
    ppermute x74, waiting for transfers between devices, swap(): return lax.ppermute(x, axis, [(i, i ^ bits) for i in range(size)])  81 us
    ppermute x74, starting transfers between devices, swap(): return lax.ppermute(x, axis, [(i, i ^ bits) for i in range(size)])  63.8 us
    pallas_call x7, Pallas kernels, call(): pl.pallas_call(kernel, out_shape=out_shape, in_specs=specs, out_specs=jax...  40.7 us
    unnamed x157, local copies, waits for them, and re-layouts  9.99 us
    pallas_call x3, Pallas kernels, scatter_sum(): pl.pallas_call(add_kernel, out_shape=[sds((rows, cols), BF16)] * 8, in_sp...  8.7 us
    pallas_call x1, Pallas kernels, layer(): pl.pallas_call(adam_kernel, grid=(rows // step_rows,), out_shape=[sds(ful...  5.08 us
  transfers between devices with their start and end apart: 74, of which 29 were waited for; matrix products, arithmetic and copies ran while one was open for 5% of the time, Pallas kernels for 16%

profile of v1, /device:TPU:0, one launch (start us, length us, event | category | flops | bytes accessed | tf_op | source)
XLA Modules:
  0.0 224.6 jit_solution(17223806427559127614)
XLA Ops:
  2.6 4.1 %collective-permute-start.1 = (bf16[48,1664]{1,0:T(8,128)(2,1)S(1)}, bf16[48,1664]{1,0:T(8,128)(2,1)S(1)}, u32[]{:S(2)}, u32[]{:S(2)}) collective-permute-start(bf16[48,1664]{1,0:T(8,128)(2,1)S(1)} %fusion.2.rest_0_.rest_16_.rest_4_), channel_id=1, source_target_pairs={{0,16},{8,24},{16,0},{24,8},{1,17},{9,25},{17,1},{25,9},{2,18},{10... | collective-permute-start | bytes 479240 | tf_op jit(solution)/shard_map/ppermute | solution.py:56
  6.7 1.6 collective-permute-start
  9.8 4.6 %collective-permute-done.1.rest_2_.rest_18_.rest_6_ = bf16[48,1664]{1,0:T(8,128)(2,1)S(1)} collective-permute-done((bf16[48,1664]{1,0:T(8,128)(2,1)S(1)}, bf16[48,1664]{1,0:T(8,128)(2,1)S(1)}, u32[]{:S(2)}, u32[]{:S(2)}) %collective-permute-start.1) | collective-permute-done | bytes 159776 | tf_op jit(solution)/shard_map/ppermute | solution.py:56
  15.0 1.5 collective-permute-start.5
  17.3 2.4 %collective-permute-done.2.rest_3_.rest_19_.rest_7_ = bf16[48,1664]{1,0:T(8,128)(2,1)S(1)} collective-permute-done((bf16[48,1664]{1,0:T(8,128)(2,1)S(1)}, bf16[48,1664]{1,0:T(8,128)(2,1)S(1)}, u32[]{:S(2)}, u32[]{:S(2)}) %collective-permute-start.2) | collective-permute-done | bytes 159776 | tf_op jit(solution)/shard_map/ppermute | solution.py:56
  19.7 2.2 collective-permute-done.5.rest_6_.rest_22_.rest_10_
  21.9 1.6 collective-permute-start.6
  23.6 1.8 collective-permute-done.4.rest_5_.rest_21_.rest_9_
  25.3 3.4 %collective-permute-start.32 = (bf16[48,1792]{1,0:T(8,128)(2,1)S(1)}, bf16[48,1792]{1,0:T(8,128)(2,1)S(1)}, u32[]{:S(2)}, u32[]{:S(2)}) collective-permute-start(bf16[48,1792]{1,0:T(8,128)(2,1)S(1)} %pad.9.rest_0_), channel_id=1, source_target_pairs={{0,16},{8,24},{16,0},{24,8},{1,17},{9,25},{17,1},{25,9},{2,18},{10... | collective-permute-start | bytes 516104 | tf_op jit(solution)/shard_map/ppermute | solution.py:56
  31.7 4.3 %shard_map.159 = (bf16[128,768]{1,0:T(8,128)(2,1)}, bf16[128,384]{1,0:T(8,128)(2,1)}, bf16[128,768]{1,0:T(8,128)(2,1)}, f32[8,768]{1,0:T(8,128)}) custom-call(s32[1]{0:T(128)} %bitcast.order_ref, f32[128,768]{1,0:T(8,128)} %x_ref.3, f32[128,128]{1,0:T(8,128)} %get-tuple-element.140.cos_ref, f32[128,128]{1,0:T(8,128)} %get-tuple-element.139.sin_ref, ...), custom_call_target="tpu_custom_call" | custom-call | tf_op jit(solution)/shard_map/pallas_call | solution.py:420
  36.0 1.6 collective-permute-start.16
  37.5 1.5 collective-permute-start.34
  39.0 1.8 collective-permute-start.33
  41.1 2.7 %collective-permute-done.34.rest_4_ = bf16[48,1792]{1,0:T(8,128)(2,1)} collective-permute-done((bf16[48,1792]{1,0:T(8,128)(2,1)S(1)}, bf16[48,1792]{1,0:T(8,128)(2,1)}, u32[]{:S(2)}, u32[]{:S(2)}) %collective-permute-start.34) | collective-permute-done | bytes 172064 | tf_op jit(solution)/shard_map/ppermute | solution.py:56
  45.4 3.0 %collective-permute-done.16.rest_2_ = bf16[128,768]{1,0:T(8,128)(2,1)S(1)} collective-permute-done((bf16[128,768]{1,0:T(8,128)(2,1)}, bf16[128,768]{1,0:T(8,128)(2,1)S(1)}, u32[]{:S(2)}, u32[]{:S(2)}) %collective-permute-start.16) | collective-permute-done | bytes 196640 | tf_op jit(solution)/shard_map/ppermute | solution.py:56
  50.0 3.5 %collective-permute-done.15.rest_1_ = bf16[128,768]{1,0:T(8,128)(2,1)S(1)} collective-permute-done((bf16[128,768]{1,0:T(8,128)(2,1)}, bf16[128,768]{1,0:T(8,128)(2,1)S(1)}, u32[]{:S(2)}, u32[]{:S(2)}) %collective-permute-start.15) | collective-permute-done | bytes 196640 | tf_op jit(solution)/shard_map/ppermute | solution.py:56
  57.8 3.5 %collective-permute-done.19.rest_5_ = bf16[128,768]{1,0:T(8,128)(2,1)S(1)} collective-permute-done((bf16[128,768]{1,0:T(8,128)(2,1)S(1)}, bf16[128,768]{1,0:T(8,128)(2,1)S(1)}, u32[]{:S(2)}, u32[]{:S(2)}) %collective-permute-start.19) | collective-permute-done | bytes 196640 | tf_op jit(solution)/shard_map/ppermute | solution.py:56
  61.3 4.2 %collective-permute-done.20.rest_6_ = bf16[128,768]{1,0:T(8,128)(2,1)S(1)} collective-permute-done((bf16[128,768]{1,0:T(8,128)(2,1)S(1)}, bf16[128,768]{1,0:T(8,128)(2,1)S(1)}, u32[]{:S(2)}, u32[]{:S(2)}) %collective-permute-start.20) | collective-permute-done | bytes 196640 | tf_op jit(solution)/shard_map/ppermute | solution.py:56
  66.1 1.7 collective-permute-done.21.rest_7_
  70.7 7.6 %shard_map.160 = (bf16[128,384]{1,0:T(8,128)(2,1)}, f32[8,256]{1,0:T(8,128)}, bf16[128,768]{1,0:T(8,128)(2,1)}) custom-call(s32[1]{0:T(128)} %bitcast.order_ref, bf16[128,384]{1,0:T(8,128)(2,1)} %get-tuple-element.61.q_ref, bf16[128,768]{1,0:T(8,128)(2,1)} %get-tuple-element.62.rest_0_, bf16[128,768]{1,0:T(8,128)(2,1)} %copy-done.23, ...), custom_call_target="tpu_custom_call" | custom-call | tf_op jit(solution)/shard_map/pallas_call | solution.py:420
  78.4 1.6 collective-permute-start.30
  82.3 3.2 %collective-permute-done.30.pb_ref = bf16[128,768]{1,0:T(8,128)(2,1)S(1)} collective-permute-done((bf16[128,768]{1,0:T(8,128)(2,1)}, bf16[128,768]{1,0:T(8,128)(2,1)S(1)}, u32[]{:S(2)}, u32[]{:S(2)}) %collective-permute-start.30) | collective-permute-done | bytes 196640 | tf_op jit(solution)/shard_map/ppermute | solution.py:56
  86.2 5.4 %shard_map.161 = (f32[128,768]{1,0:T(8,128)}, bf16[128,768]{1,0:T(8,128)(2,1)}, bf16[128,768]{1,0:T(8,128)(2,1)}, bf16[128,768]{1,0:T(8,128)(2,1)}, bf16[128,1152]{1,0:T(8,128)(2,1)}, /*index=5*/bf16[128,576]{1,0:T(8,128)(2,1)}) custom-call(s32[1]{0:T(128)} %bitcast.order_ref, f32[128,768]{1,0:T(8,128)} %x_ref.3, bf16[128,768]{1,0:T(8,128)(2,1)} %get-tuple-element.63.pa_ref, ...), custom_call_target="tpu_custom_call" | custom-call | tf_op jit(solution)/shard_map/pallas_call | solution.py:420
  91.6 1.6 collective-permute-start.47
  93.2 4.7 %collective-permute-done.47.db_ref = bf16[128,768]{1,0:T(8,128)(2,1)S(1)} collective-permute-done((bf16[128,768]{1,0:T(8,128)(2,1)}, bf16[128,768]{1,0:T(8,128)(2,1)S(1)}, u32[]{:S(2)}, u32[]{:S(2)}) %collective-permute-start.47) | collective-permute-done | bytes 196640 | tf_op jit(solution)/shard_map/ppermute | solution.py:56
  98.5 10.7 %shard_map.162 = (bf16[1024,768]{1,0:T(8,128)(2,1)}, bf16[1024,768]{1,0:T(8,128)(2,1)}, f32[128,768]{1,0:T(8,128)}, bf16[128,384]{1,0:T(8,128)(2,1)}) custom-call(s32[1]{0:T(128)} %bitcast.order_ref, bf16[128,384]{1,0:T(8,128)(2,1)} %get-tuple-element.61.q_ref, bf16[128,384]{1,0:T(8,128)(2,1)} %get-tuple-element.67.attn_ref, ...), custom_call_target="tpu_custom_call" | custom-call | tf_op jit(solution)/shard_map/pallas_call | solution.py:420
  109.3 3.8 %shard_map.164 = (bf16[384,1792]{1,0:T(8,128)(2,1)}, bf16[384,1792]{1,0:T(8,128)(2,1)}) custom-call(s32[1]{0:T(128)} %bitcast.order_ref, bf16[128,768]{1,0:T(8,128)(2,1)} %get-tuple-element.94.b_ref, bf16[128,1152]{1,0:T(8,128)(2,1)} %get-tuple-element.95.dz_ref, f32[128,768]{1,0:T(8,128)} %cot_ref.5, bf16[128,576]{1,0:T(8,128)(2,1)} %get-tuple-element.96.mixed_ref), custom_call_target="tpu_custom_call" | custom-call | tf_op jit(solution)/shard_map/pallas_call | solution.py:420
  115.6 3.1 %pair_add.3 = (bf16[128,768]{1,0:T(8,128)(2,1)}, bf16[128,768]{1,0:T(8,128)(2,1)}, bf16[128,768]{1,0:T(8,128)(2,1)}, bf16[128,768]{1,0:T(8,128)(2,1)}, bf16[128,...) custom-call(bf16[1024,768]{1,0:T(8,128)(2,1)} %get-tuple-element.73.refs_0_, ...), custom_call_target="tpu_custom_call" | custom-call | tf_op jit(solution)/shard_map/pair_add/pallas_call | solution.py:96
  125.0 1.6 collective-permute-start.46
  127.7 2.9 %pair_add.5 = (bf16[48,1792]{1,0:T(8,128)(2,1)}, bf16[48,1792]{1,0:T(8,128)(2,1)}, bf16[48,1792]{1,0:T(8,128)(2,1)}, bf16[48,1792]{1,0:T(8,128)(2,1)}, bf16[48,1...) custom-call(bf16[384,1792]{1,0:T(8,128)(2,1)} %get-tuple-element.97.refs_0_, ...), custom_call_target="tpu_custom_call" | custom-call | tf_op jit(solution)/shard_map/pair_add/pallas_call | solution.py:96
  134.8 11.8 %collective-permute-done.50 = bf16[128,768]{1,0:T(8,128)(2,1)S(1)} collective-permute-done((bf16[128,768]{1,0:T(8,128)(2,1)}, bf16[128,768]{1,0:T(8,128)(2,1)S(1)}, u32[]{:S(2)}, u32[]{:S(2)}) %collective-permute-start.50) | collective-permute-done | bytes 196640 | tf_op jit(solution)/shard_map/ppermute | solution.py:56
  148.7 5.1 %collective-permute-done.54 = bf16[128,768]{1,0:T(8,128)(2,1)S(1)} collective-permute-done((bf16[128,768]{1,0:T(8,128)(2,1)S(1)}, bf16[128,768]{1,0:T(8,128)(2,1)S(1)}, u32[]{:S(2)}, u32[]{:S(2)}) %collective-permute-start.54) | collective-permute-done | bytes 196640 | tf_op jit(solution)/shard_map/ppermute | solution.py:56
  153.9 3.0 %collective-permute-start.55 = (bf16[128,768]{1,0:T(8,128)(2,1)S(1)}, bf16[128,768]{1,0:T(8,128)(2,1)S(1)}, u32[]{:S(2)}, u32[]{:S(2)}) collective-permute-start(bf16[128,768]{1,0:T(8,128)(2,1)S(1)} %add_convert_fusion), channel_id=1, source_target_pairs={{0,16},{8,24},{16,0},{24,8},{1,17},{9,25},{17,1},{25,9},{2,18},{10... | collective-permute-start | bytes 589832 | tf_op jit(solution)/shard_map/ppermute | solution.py:56
  160.9 1.8 collective-permute-done.55.rest_3_
  163.4 6.4 %shard_map.163 = (bf16[384,1536]{1,0:T(8,128)(2,1)}, bf16[384,1536]{1,0:T(8,128)(2,1)}, bf16[128,768]{1,0:T(8,128)(2,1)}) custom-call(s32[1]{0:T(128)} %bitcast.order_ref, bf16[128,768]{1,0:T(8,128)(2,1)} %get-tuple-element.71.a_ref, bf16[128,384]{1,0:T(8,128)(2,1)} %get-tuple-element.72.dqp_ref, f32[128,768]{1,0:T(8,128)} %get-tuple-element.70.dhid_ref, ...), custom_call_target="tpu_custom_call" | custom-call | tf_op jit(solution)/shard_map/pallas_call | solution.py:420
  170.4 1.7 collective-permute-start.68
  172.7 4.6 %collective-permute-done.71 = bf16[48,1792]{1,0:T(8,128)(2,1)S(1)} collective-permute-done((bf16[48,1792]{1,0:T(8,128)(2,1)S(1)}, bf16[48,1792]{1,0:T(8,128)(2,1)S(1)}, u32[]{:S(2)}, u32[]{:S(2)}) %collective-permute-start.71) | collective-permute-done | bytes 172064 | tf_op jit(solution)/shard_map/ppermute | solution.py:56
  177.3 1.8 collective-permute-start.72
  180.2 2.7 %pair_add.4 = (bf16[48,1536]{1,0:T(8,128)(2,1)}, bf16[48,1536]{1,0:T(8,128)(2,1)}, bf16[48,1536]{1,0:T(8,128)(2,1)}, bf16[48,1536]{1,0:T(8,128)(2,1)}, bf16[48,1...) custom-call(bf16[384,1536]{1,0:T(8,128)(2,1)} %get-tuple-element.84.refs_0_, ...), custom_call_target="tpu_custom_call" | custom-call | tf_op jit(solution)/shard_map/pair_add/pallas_call | solution.py:96
  185.2 4.6 %collective-permute-done.62 = bf16[48,1536]{1,0:T(8,128)(2,1)S(1)} collective-permute-done((bf16[48,1536]{1,0:T(8,128)(2,1)}, bf16[48,1536]{1,0:T(8,128)(2,1)S(1)}, u32[]{:S(2)}, u32[]{:S(2)}) %collective-permute-start.62) | collective-permute-done | bytes 147488 | tf_op jit(solution)/shard_map/ppermute | solution.py:56
  191.9 3.3 %collective-permute-done.59 = bf16[48,1536]{1,0:T(8,128)(2,1)S(1)} collective-permute-done((bf16[48,1536]{1,0:T(8,128)(2,1)}, bf16[48,1536]{1,0:T(8,128)(2,1)S(1)}, u32[]{:S(2)}, u32[]{:S(2)}) %collective-permute-start.59) | collective-permute-done | bytes 147488 | tf_op jit(solution)/shard_map/ppermute | solution.py:56
  195.2 2.0 collective-permute-start.63
  199.4 2.1 collective-permute-done.63
  201.4 2.5 %collective-permute-start.60 = (bf16[48,1536]{1,0:T(8,128)(2,1)S(1)}, bf16[48,1536]{1,0:T(8,128)(2,1)S(1)}, u32[]{:S(2)}, u32[]{:S(2)}) collective-permute-start(bf16[48,1536]{1,0:T(8,128)(2,1)S(1)} %add_convert_fusion.8), channel_id=1, source_target_pairs={{0,8},{8,0},{16,24},{24,16},{1,9},{9,1},{17,25},{25,17},{2,10},{10... | collective-permute-start | bytes 442376 | tf_op jit(solution)/shard_map/ppermute | solution.py:56
  205.2 1.8 collective-permute-done.60.rest_2_
  207.0 4.1 %collective-permute-done.64.rest_3_ = bf16[48,1536]{1,0:T(8,128)(2,1)S(1)} collective-permute-done((bf16[48,1536]{1,0:T(8,128)(2,1)S(1)}, bf16[48,1536]{1,0:T(8,128)(2,1)S(1)}, u32[]{:S(2)}, u32[]{:S(2)}) %collective-permute-start.64) | collective-permute-done | bytes 147488 | tf_op jit(solution)/shard_map/ppermute | solution.py:56
  211.8 2.6 %shard_map.165 = (f32[48,3264]{1,0:T(8,128)}, f32[48,128]{1,0:T(8,128)}) custom-call(f32[48,3264]{1,0:T(8,128)} %w_ref.3, bf16[48,1536]{1,0:T(8,128)(2,1)} %get-tuple-element.86.rest_0_, bf16[48,1536]{1,0:T(8,128)(2,1)} %copy-done.61, bf16[48,1536]{1,0:T(8,128)(2,1)} %copy-done.62, bf16[48,1536]{1,0:T(8,128)(2,1)} %copy-done.63, ...), custom_call_target="tpu_custom_call" | custom-call | tf_op jit(solution)/shard_map/pallas_call | solution.py:420
  216.6 5.1 %adam.1 = (f32[48,3264]{1,0:T(8,128)}, f32[48,3264]{1,0:T(8,128)}, f32[48,3264]{1,0:T(8,128)}) custom-call(f32[48,3264]{1,0:T(8,128)} %w_ref.3, f32[48,3264]{1,0:T(8,128)} %get-tuple-element.124.g_ref, f32[48,3264]{1,0:T(8,128)} %m_ref.1, f32[48,3264]{1,0:T(8,128)} %v_ref.1), custom_call_target="tpu_custom_call" | custom-call | tf_op jit(solution)/shard_map/adam/pallas_call | solution.py:606
  (310 shorter events, 59.2 us)
Async XLA Ops:
  2.6 11.8 %collective-permute-start.1 = (bf16[48,1664]{1,0:T(8,128)(2,1)S(1)}, bf16[48,1664]{1,0:T(8,128)(2,1)S(1)}, u32[]{:S(2)}, u32[]{:S(2)}) collective-permute-start(bf16[48,1664]{1,0:T(8,128)(2,1)S(1)} %fusion.2.rest_0_.rest_16_.rest_4_), channel_id=1, source_target_pairs={{0,16},{8,24},{16,0},{24,8},{1,17},{9,25},{17,1},{25,9},{2,18},{10... | collective-permute-start | bytes 479240 | tf_op jit(solution)/shard_map/ppermute | solution.py:56
  6.7 9.8 %collective-permute-start = (bf16[48,1664]{1,0:T(8,128)(2,1)S(1)}, bf16[48,1664]{1,0:T(8,128)(2,1)S(1)}, u32[]{:S(2)}, u32[]{:S(2)}) collective-permute-start(bf16[48,1664]{1,0:T(8,128)(2,1)S(1)} %fusion.2.rest_0_.rest_16_.rest_4_), channel_id=1, source_target_pairs={{0,8},{8,0},{16,24},{24,16},{1,9},{9,1},{17,25},{25,17},{2,10},{10... | collective-permute-start | bytes 479240 | tf_op jit(solution)/shard_map/ppermute | solution.py:56
  8.3 8.2 %collective-permute-start.3 = (bf16[48,1664]{1,0:T(8,128)(2,1)S(1)}, bf16[48,1664]{1,0:T(8,128)(2,1)S(1)}, u32[]{:S(2)}, u32[]{:S(2)}) collective-permute-start(bf16[48,1664]{1,0:T(8,128)(2,1)S(1)} %fusion.2.rest_0_.rest_16_.rest_4_), channel_id=1, source_target_pairs={{0,4},{2,6},{4,0},{6,2},{1,5},{3,7},{5,1},{7,3},{8,12},{10,14},{12... | collective-permute-start | bytes 479240 | tf_op jit(solution)/shard_map/ppermute | solution.py:56
  9.8 7.3 %collective-permute-start.7 = (bf16[48,1664]{1,0:T(8,128)(2,1)S(1)}, bf16[48,1664]{1,0:T(8,128)(2,1)S(1)}, u32[]{:S(2)}, u32[]{:S(2)}) collective-permute-start(bf16[48,1664]{1,0:T(8,128)(2,1)S(1)} %fusion.2.rest_0_.rest_16_.rest_4_), channel_id=1, source_target_pairs={{0,2},{2,0},{4,6},{6,4},{1,3},{3,1},{5,7},{7,5},{8,10},{10,8},{12,... | collective-permute-start | bytes 479240 | tf_op jit(solution)/shard_map/ppermute | solution.py:56
  16.5 12.2 %collective-permute-start.9 = (bf16[48,1664]{1,0:T(8,128)(2,1)S(1)}, bf16[48,1664]{1,0:T(8,128)(2,1)S(1)}, u32[]{:S(2)}, u32[]{:S(2)}) collective-permute-start(bf16[48,1664]{1,0:T(8,128)(2,1)S(1)} %collective-permute-done.1.rest_2_.rest_18_.rest_6_), channel_id=1, source_target_pairs={{0,2},{2,0},{4,6},{6,4},{1,3},{3,1},{5,7},{7,5},{8,10},{10,8},{12,... | collective-permute-start | bytes 479240 | tf_op jit(solution)/shard_map/ppermute | solution.py:56
  16.5 8.8 %collective-permute-start.4 = (bf16[48,1664]{1,0:T(8,128)(2,1)S(1)}, bf16[48,1664]{1,0:T(8,128)(2,1)S(1)}, u32[]{:S(2)}, u32[]{:S(2)}) collective-permute-start(bf16[48,1664]{1,0:T(8,128)(2,1)S(1)} %collective-permute-done.rest_1_.rest_17_.rest_5_), channel_id=1, source_target_pairs={{0,4},{2,6},{4,0},{6,2},{1,5},{3,7},{5,1},{7,3},{8,12},{10,14},{12... | collective-permute-start | bytes 479240 | tf_op jit(solution)/shard_map/ppermute | solution.py:56
  17.1 11.6 %collective-permute-start.8 = (bf16[48,1664]{1,0:T(8,128)(2,1)S(1)}, bf16[48,1664]{1,0:T(8,128)(2,1)S(1)}, u32[]{:S(2)}, u32[]{:S(2)}) collective-permute-start(bf16[48,1664]{1,0:T(8,128)(2,1)S(1)} %collective-permute-done.rest_1_.rest_17_.rest_5_), channel_id=1, source_target_pairs={{0,2},{2,0},{4,6},{6,4},{1,3},{3,1},{5,7},{7,5},{8,10},{10,8},{12,... | collective-permute-start | bytes 479240 | tf_op jit(solution)/shard_map/ppermute | solution.py:56
  19.7 9.6 %collective-permute-start.11 = (bf16[48,1664]{1,0:T(8,128)(2,1)S(1)}, bf16[48,1664]{1,0:T(8,128)(2,1)S(1)}, u32[]{:S(2)}, u32[]{:S(2)}) collective-permute-start(bf16[48,1664]{1,0:T(8,128)(2,1)S(1)} %collective-permute-done.3.rest_4_.rest_20_.rest_8_), channel_id=1, source_target_pairs={{0,2},{2,0},{4,6},{6,4},{1,3},{3,1},{5,7},{7,5},{8,10},{10,8},{12,... | collective-permute-start | bytes 479240 | tf_op jit(solution)/shard_map/ppermute | solution.py:56
  21.9 7.4 %collective-permute-start.6 = (bf16[48,1664]{1,0:T(8,128)(2,1)S(1)}, bf16[48,1664]{1,0:T(8,128)(2,1)S(1)}, u32[]{:S(2)}, u32[]{:S(2)}) collective-permute-start(bf16[48,1664]{1,0:T(8,128)(2,1)S(1)} %collective-permute-done.2.rest_3_.rest_19_.rest_7_), channel_id=1, source_target_pairs={{0,4},{2,6},{4,0},{6,2},{1,5},{3,7},{5,1},{7,3},{8,12},{10,14},{12... | collective-permute-start | bytes 479240 | tf_op jit(solution)/shard_map/ppermute | solution.py:56
  25.3 13.7 %collective-permute-start.32 = (bf16[48,1792]{1,0:T(8,128)(2,1)S(1)}, bf16[48,1792]{1,0:T(8,128)(2,1)S(1)}, u32[]{:S(2)}, u32[]{:S(2)}) collective-permute-start(bf16[48,1792]{1,0:T(8,128)(2,1)S(1)} %pad.9.rest_0_), channel_id=1, source_target_pairs={{0,16},{8,24},{16,0},{24,8},{1,17},{9,25},{17,1},{25,9},{2,18},{10... | collective-permute-start | bytes 516104 | tf_op jit(solution)/shard_map/ppermute | solution.py:56
  30.8 10.0 %collective-permute-start.31 = (bf16[48,1792]{1,0:T(8,128)(2,1)S(1)}, bf16[48,1792]{1,0:T(8,128)(2,1)S(1)}, u32[]{:S(2)}, u32[]{:S(2)}) collective-permute-start(bf16[48,1792]{1,0:T(8,128)(2,1)S(1)} %pad.9.rest_0_), channel_id=1, source_target_pairs={{0,8},{8,0},{16,24},{24,16},{1,9},{9,1},{17,25},{25,17},{2,10},{10... | collective-permute-start | bytes 516104 | tf_op jit(solution)/shard_map/ppermute | solution.py:56
  36.0 12.4 %collective-permute-start.16 = (bf16[128,768]{1,0:T(8,128)(2,1)}, bf16[128,768]{1,0:T(8,128)(2,1)S(1)}, u32[]{:S(2)}, u32[]{:S(2)}) collective-permute-start(bf16[128,768]{1,0:T(8,128)(2,1)} %get-tuple-element.62.rest_0_), channel_id=1, source_target_pairs={{0,16},{8,24},{16,0},{24,8},{1,17},{9,25},{17,1},{25,9},{2,18},{10... | collective-permute-start | bytes 589832 | tf_op jit(solution)/shard_map/ppermute | solution.py:56
  39.0 10.4 %collective-permute-start.33 = (bf16[48,1792]{1,0:T(8,128)(2,1)S(1)}, bf16[48,1792]{1,0:T(8,128)(2,1)}, u32[]{:S(2)}, u32[]{:S(2)}) collective-permute-start(bf16[48,1792]{1,0:T(8,128)(2,1)S(1)} %collective-permute-done.32.rest_2_), channel_id=1, source_target_pairs={{0,8},{8,0},{16,24},{24,16},{1,9},{9,1},{17,25},{25,17},{2,10},{10... | collective-permute-start | bytes 516104 | tf_op jit(solution)/shard_map/ppermute | solution.py:56
  40.9 12.7 %collective-permute-start.15 = (bf16[128,768]{1,0:T(8,128)(2,1)}, bf16[128,768]{1,0:T(8,128)(2,1)S(1)}, u32[]{:S(2)}, u32[]{:S(2)}) collective-permute-start(bf16[128,768]{1,0:T(8,128)(2,1)} %get-tuple-element.62.rest_0_), channel_id=1, source_target_pairs={{0,8},{8,0},{16,24},{24,16},{1,9},{9,1},{17,25},{25,17},{2,10},{10... | collective-permute-start | bytes 589832 | tf_op jit(solution)/shard_map/ppermute | solution.py:56
  43.9 11.9 %collective-permute-start.18 = (bf16[128,768]{1,0:T(8,128)(2,1)}, bf16[128,768]{1,0:T(8,128)(2,1)S(1)}, u32[]{:S(2)}, u32[]{:S(2)}) collective-permute-start(bf16[128,768]{1,0:T(8,128)(2,1)} %get-tuple-element.62.rest_0_), channel_id=1, source_target_pairs={{0,4},{2,6},{4,0},{6,2},{1,5},{3,7},{5,1},{7,3},{8,12},{10,14},{12... | collective-permute-start | bytes 589832 | tf_op jit(solution)/shard_map/ppermute | solution.py:56
  45.4 10.4 %collective-permute-start.22 = (bf16[128,768]{1,0:T(8,128)(2,1)}, bf16[128,768]{1,0:T(8,128)(2,1)S(1)}, u32[]{:S(2)}, u32[]{:S(2)}) collective-permute-start(bf16[128,768]{1,0:T(8,128)(2,1)} %get-tuple-element.62.rest_0_), channel_id=1, source_target_pairs={{0,2},{2,0},{4,6},{6,4},{1,3},{3,1},{5,7},{7,5},{8,10},{10,8},{12,... | collective-permute-start | bytes 589832 | tf_op jit(solution)/shard_map/ppermute | solution.py:56
  48.4 8.9 %collective-permute-start.17 = (bf16[128,768]{1,0:T(8,128)(2,1)S(1)}, bf16[128,768]{1,0:T(8,128)(2,1)S(1)}, u32[]{:S(2)}, u32[]{:S(2)}) collective-permute-start(bf16[128,768]{1,0:T(8,128)(2,1)S(1)} %collective-permute-done.16.rest_2_), channel_id=1, source_target_pairs={{0,8},{8,0},{16,24},{24,16},{1,9},{9,1},{17,25},{25,17},{2,10},{10... | collective-permute-start | bytes 589832 | tf_op jit(solution)/shard_map/ppermute | solution.py:56
  53.5 7.8 %collective-permute-start.19 = (bf16[128,768]{1,0:T(8,128)(2,1)S(1)}, bf16[128,768]{1,0:T(8,128)(2,1)S(1)}, u32[]{:S(2)}, u32[]{:S(2)}) collective-permute-start(bf16[128,768]{1,0:T(8,128)(2,1)S(1)} %collective-permute-done.15.rest_1_), channel_id=1, source_target_pairs={{0,4},{2,6},{4,0},{6,2},{1,5},{3,7},{5,1},{7,3},{8,12},{10,14},{12... | collective-permute-start | bytes 589832 | tf_op jit(solution)/shard_map/ppermute | solution.py:56
  54.9 10.6 %collective-permute-start.20 = (bf16[128,768]{1,0:T(8,128)(2,1)S(1)}, bf16[128,768]{1,0:T(8,128)(2,1)S(1)}, u32[]{:S(2)}, u32[]{:S(2)}) collective-permute-start(bf16[128,768]{1,0:T(8,128)(2,1)S(1)} %collective-permute-done.16.rest_2_), channel_id=1, source_target_pairs={{0,4},{2,6},{4,0},{6,2},{1,5},{3,7},{5,1},{7,3},{8,12},{10,14},{12... | collective-permute-start | bytes 589832 | tf_op jit(solution)/shard_map/ppermute | solution.py:56
  55.8 9.7 %collective-permute-start.23 = (bf16[128,768]{1,0:T(8,128)(2,1)S(1)}, bf16[128,768]{1,0:T(8,128)(2,1)S(1)}, u32[]{:S(2)}, u32[]{:S(2)}) collective-permute-start(bf16[128,768]{1,0:T(8,128)(2,1)S(1)} %collective-permute-done.15.rest_1_), channel_id=1, source_target_pairs={{0,2},{2,0},{4,6},{6,4},{1,3},{3,1},{5,7},{7,5},{8,10},{10,8},{12,... | collective-permute-start | bytes 589832 | tf_op jit(solution)/shard_map/ppermute | solution.py:56
  55.8 10.2 %collective-permute-start.24 = (bf16[128,768]{1,0:T(8,128)(2,1)S(1)}, bf16[128,768]{1,0:T(8,128)(2,1)S(1)}, u32[]{:S(2)}, u32[]{:S(2)}) collective-permute-start(bf16[128,768]{1,0:T(8,128)(2,1)S(1)} %collective-permute-done.16.rest_2_), channel_id=1, source_target_pairs={{0,2},{2,0},{4,6},{6,4},{1,3},{3,1},{5,7},{7,5},{8,10},{10,8},{12,... | collective-permute-start | bytes 589832 | tf_op jit(solution)/shard_map/ppermute | solution.py:56
  57.2 10.6 %collective-permute-start.21 = (bf16[128,768]{1,0:T(8,128)(2,1)S(1)}, bf16[128,768]{1,0:T(8,128)(2,1)S(1)}, u32[]{:S(2)}, u32[]{:S(2)}) collective-permute-start(bf16[128,768]{1,0:T(8,128)(2,1)S(1)} %collective-permute-done.17.rest_3_), channel_id=1, source_target_pairs={{0,4},{2,6},{4,0},{6,2},{1,5},{3,7},{5,1},{7,3},{8,12},{10,14},{12... | collective-permute-start | bytes 589832 | tf_op jit(solution)/shard_map/ppermute | solution.py:56
  67.8 10.5 %collective-permute-start.35 = (bf16[48,1792]{1,0:T(8,128)(2,1)S(1)}, bf16[48,1792]{1,0:T(8,128)(2,1)}, u32[]{:S(2)}, u32[]{:S(2)}) collective-permute-start(bf16[48,1792]{1,0:T(8,128)(2,1)S(1)} %collective-permute-done.31.rest_1_), channel_id=1, source_target_pairs={{0,4},{2,6},{4,0},{6,2},{1,5},{3,7},{5,1},{7,3},{8,12},{10,14},{12... | collective-permute-start | bytes 516104 | tf_op jit(solution)/shard_map/ppermute | solution.py:56
  68.5 11.5 %collective-permute-start.40 = (bf16[48,1792]{1,0:T(8,128)(2,1)S(1)}, bf16[48,1792]{1,0:T(8,128)(2,1)}, u32[]{:S(2)}, u32[]{:S(2)}) collective-permute-start(bf16[48,1792]{1,0:T(8,128)(2,1)S(1)} %collective-permute-done.32.rest_2_), channel_id=1, source_target_pairs={{0,2},{2,0},{4,6},{6,4},{1,3},{3,1},{5,7},{7,5},{8,10},{10,8},{12,... | collective-permute-start | bytes 516104 | tf_op jit(solution)/shard_map/ppermute | solution.py:56
  68.6 11.3 %collective-permute-start.39 = (bf16[48,1792]{1,0:T(8,128)(2,1)S(1)}, bf16[48,1792]{1,0:T(8,128)(2,1)}, u32[]{:S(2)}, u32[]{:S(2)}) collective-permute-start(bf16[48,1792]{1,0:T(8,128)(2,1)S(1)} %collective-permute-done.31.rest_1_), channel_id=1, source_target_pairs={{0,2},{2,0},{4,6},{6,4},{1,3},{3,1},{5,7},{7,5},{8,10},{10,8},{12,... | collective-permute-start | bytes 516104 | tf_op jit(solution)/shard_map/ppermute | solution.py:56
  69.0 11.5 %collective-permute-start.42 = (bf16[48,1792]{1,0:T(8,128)(2,1)}, bf16[48,1792]{1,0:T(8,128)(2,1)}, u32[]{:S(2)}, u32[]{:S(2)}) collective-permute-start(bf16[48,1792]{1,0:T(8,128)(2,1)} %collective-permute-done.34.rest_4_), channel_id=1, source_target_pairs={{0,2},{2,0},{4,6},{6,4},{1,3},{3,1},{5,7},{7,5},{8,10},{10,8},{12,... | collective-permute-start | bytes 516104 | tf_op jit(solution)/shard_map/ppermute | solution.py:56
  69.3 11.3 %collective-permute-start.37 = (bf16[48,1792]{1,0:T(8,128)(2,1)}, bf16[48,1792]{1,0:T(8,128)(2,1)}, u32[]{:S(2)}, u32[]{:S(2)}) collective-permute-start(bf16[48,1792]{1,0:T(8,128)(2,1)} %collective-permute-done.33.rest_3_), channel_id=1, source_target_pairs={{0,4},{2,6},{4,0},{6,2},{1,5},{3,7},{5,1},{7,3},{8,12},{10,14},{12... | collective-permute-start | bytes 516104 | tf_op jit(solution)/shard_map/ppermute | solution.py:56
  78.4 7.1 %collective-permute-start.30 = (bf16[128,768]{1,0:T(8,128)(2,1)}, bf16[128,768]{1,0:T(8,128)(2,1)S(1)}, u32[]{:S(2)}, u32[]{:S(2)}) collective-permute-start(bf16[128,768]{1,0:T(8,128)(2,1)} %get-tuple-element.63.pa_ref), channel_id=1, source_target_pairs={{0,1},{1,0},{2,3},{3,2},{4,5},{5,4},{6,7},{7,6},{8,9},{9,8},{10,11... | collective-permute-start | bytes 589832 | tf_op jit(solution)/shard_map/ppermute | solution.py:56
  113.1 13.5 %collective-permute-start.65 = (bf16[384,1792]{1,0:T(8,128)(2,1)}, bf16[384,1792]{1,0:T(8,128)(2,1)S(1)}, u32[]{:S(2)}, u32[]{:S(2)}) collective-permute-start(bf16[384,1792]{1,0:T(8,128)(2,1)} %get-tuple-element.98), channel_id=1, source_target_pairs={{0,2},{2,0},{4,6},{6,4},{1,3},{3,1},{5,7},{7,5},{8,10},{10,8},{12,... | collective-permute-start | bytes 4128776 | tf_op jit(solution)/shard_map/ppermute | solution.py:56
  118.7 15.1 %collective-permute-start.53 = (bf16[128,768]{1,0:T(8,128)(2,1)}, bf16[128,768]{1,0:T(8,128)(2,1)S(1)}, u32[]{:S(2)}, u32[]{:S(2)}) collective-permute-start(bf16[128,768]{1,0:T(8,128)(2,1)} %get-tuple-element.82), channel_id=1, source_target_pairs={{0,4},{2,6},{4,0},{6,2},{1,5},{3,7},{5,1},{7,3},{8,12},{10,14},{12... | collective-permute-start | bytes 589832 | tf_op jit(solution)/shard_map/ppermute | solution.py:56
  125.0 31.9 %collective-permute-start.46 = (bf16[128,768]{1,0:T(8,128)(2,1)S(1)}, bf16[128,768]{1,0:T(8,128)(2,1)S(1)}, u32[]{:S(2)}, u32[]{:S(2)}) collective-permute-start(bf16[128,768]{1,0:T(8,128)(2,1)S(1)} %copy-done.43), channel_id=1, source_target_pairs={{0,1},{1,0},{2,3},{3,2},{4,5},{5,4},{6,7},{7,6},{8,9},{9,8},{10,11... | collective-permute-start | bytes 589832 | tf_op jit(solution)/shard_map/ppermute | solution.py:56
  130.7 39.2 %collective-permute-start.70 = (bf16[48,1792]{1,0:T(8,128)(2,1)}, bf16[48,1792]{1,0:T(8,128)(2,1)S(1)}, u32[]{:S(2)}, u32[]{:S(2)}) collective-permute-start(bf16[48,1792]{1,0:T(8,128)(2,1)} %get-tuple-element.106), channel_id=1, source_target_pairs={{0,4},{2,6},{4,0},{6,2},{1,5},{3,7},{5,1},{7,3},{8,12},{10,14},{12... | collective-permute-start | bytes 516104 | tf_op jit(solution)/shard_map/ppermute | solution.py:56
  131.8 16.1 %collective-permute-start.52 = (bf16[128,768]{1,0:T(8,128)(2,1)}, bf16[128,768]{1,0:T(8,128)(2,1)S(1)}, u32[]{:S(2)}, u32[]{:S(2)}) collective-permute-start(bf16[128,768]{1,0:T(8,128)(2,1)} %get-tuple-element.80), channel_id=1, source_target_pairs={{0,4},{2,6},{4,0},{6,2},{1,5},{3,7},{5,1},{7,3},{8,12},{10,14},{12... | collective-permute-start | bytes 589832 | tf_op jit(solution)/shard_map/ppermute | solution.py:56
  132.7 13.9 %collective-permute-start.50 = (bf16[128,768]{1,0:T(8,128)(2,1)}, bf16[128,768]{1,0:T(8,128)(2,1)S(1)}, u32[]{:S(2)}, u32[]{:S(2)}) collective-permute-start(bf16[128,768]{1,0:T(8,128)(2,1)} %get-tuple-element.78), channel_id=1, source_target_pairs={{0,4},{2,6},{4,0},{6,2},{1,5},{3,7},{5,1},{7,3},{8,12},{10,14},{12... | collective-permute-start | bytes 589832 | tf_op jit(solution)/shard_map/ppermute | solution.py:56
  133.8 25.1 %collective-permute-start.49 = (bf16[128,768]{1,0:T(8,128)(2,1)}, bf16[128,768]{1,0:T(8,128)(2,1)S(1)}, u32[]{:S(2)}, u32[]{:S(2)}) collective-permute-start(bf16[128,768]{1,0:T(8,128)(2,1)} %get-tuple-element.76), channel_id=1, source_target_pairs={{0,4},{2,6},{4,0},{6,2},{1,5},{3,7},{5,1},{7,3},{8,12},{10,14},{12... | collective-permute-start | bytes 589832 | tf_op jit(solution)/shard_map/ppermute | solution.py:56
  146.5 7.3 %collective-permute-start.54 = (bf16[128,768]{1,0:T(8,128)(2,1)S(1)}, bf16[128,768]{1,0:T(8,128)(2,1)S(1)}, u32[]{:S(2)}, u32[]{:S(2)}) collective-permute-start(bf16[128,768]{1,0:T(8,128)(2,1)S(1)} %add_convert_fusion.1), channel_id=1, source_target_pairs={{0,8},{8,0},{16,24},{24,16},{1,9},{9,1},{17,25},{25,17},{2,10},{10... | collective-permute-start | bytes 589832 | tf_op jit(solution)/shard_map/ppermute | solution.py:56
  147.9 11.9 %collective-permute-start.51 = (bf16[128,768]{1,0:T(8,128)(2,1)S(1)}, bf16[128,768]{1,0:T(8,128)(2,1)S(1)}, u32[]{:S(2)}, u32[]{:S(2)}) collective-permute-start(bf16[128,768]{1,0:T(8,128)(2,1)S(1)} %add_convert_fusion.2), channel_id=1, source_target_pairs={{0,8},{8,0},{16,24},{24,16},{1,9},{9,1},{17,25},{25,17},{2,10},{10... | collective-permute-start | bytes 589832 | tf_op jit(solution)/shard_map/ppermute | solution.py:56
  153.9 8.8 %collective-permute-start.55 = (bf16[128,768]{1,0:T(8,128)(2,1)S(1)}, bf16[128,768]{1,0:T(8,128)(2,1)S(1)}, u32[]{:S(2)}, u32[]{:S(2)}) collective-permute-start(bf16[128,768]{1,0:T(8,128)(2,1)S(1)} %add_convert_fusion), channel_id=1, source_target_pairs={{0,16},{8,24},{16,0},{24,8},{1,17},{9,25},{17,1},{25,9},{2,18},{10... | collective-permute-start | bytes 589832 | tf_op jit(solution)/shard_map/ppermute | solution.py:56
  157.8 14.4 %collective-permute-start.69 = (bf16[48,1792]{1,0:T(8,128)(2,1)S(1)}, bf16[48,1792]{1,0:T(8,128)(2,1)S(1)}, u32[]{:S(2)}, u32[]{:S(2)}) collective-permute-start(bf16[48,1792]{1,0:T(8,128)(2,1)S(1)} %copy-done.74), channel_id=1, source_target_pairs={{0,4},{2,6},{4,0},{6,2},{1,5},{3,7},{5,1},{7,3},{8,12},{10,14},{12... | collective-permute-start | bytes 516104 | tf_op jit(solution)/shard_map/ppermute | solution.py:56
  158.9 11.5 %collective-permute-start.67 = (bf16[48,1792]{1,0:T(8,128)(2,1)}, bf16[48,1792]{1,0:T(8,128)(2,1)S(1)}, u32[]{:S(2)}, u32[]{:S(2)}) collective-permute-start(bf16[48,1792]{1,0:T(8,128)(2,1)} %get-tuple-element.102), channel_id=1, source_target_pairs={{0,4},{2,6},{4,0},{6,2},{1,5},{3,7},{5,1},{7,3},{8,12},{10,14},{12... | collective-permute-start | bytes 516104 | tf_op jit(solution)/shard_map/ppermute | solution.py:56
  159.8 44.2 %collective-permute-start.66 = (bf16[48,1792]{1,0:T(8,128)(2,1)}, bf16[48,1792]{1,0:T(8,128)(2,1)S(1)}, u32[]{:S(2)}, u32[]{:S(2)}) collective-permute-start(bf16[48,1792]{1,0:T(8,128)(2,1)} %get-tuple-element.100), channel_id=1, source_target_pairs={{0,4},{2,6},{4,0},{6,2},{1,5},{3,7},{5,1},{7,3},{8,12},{10,14},{12... | collective-permute-start | bytes 516104 | tf_op jit(solution)/shard_map/ppermute | solution.py:56
  169.8 9.4 %collective-permute-start.57 = (bf16[384,1536]{1,0:T(8,128)(2,1)}, bf16[384,1536]{1,0:T(8,128)(2,1)S(1)}, u32[]{:S(2)}, u32[]{:S(2)}) collective-permute-start(bf16[384,1536]{1,0:T(8,128)(2,1)} %get-tuple-element.85), channel_id=1, source_target_pairs={{0,2},{2,0},{4,6},{6,4},{1,3},{3,1},{5,7},{7,5},{8,10},{10,8},{12,... | collective-permute-start | bytes 3538952 | tf_op jit(solution)/shard_map/ppermute | solution.py:56
  169.9 7.3 %collective-permute-start.71 = (bf16[48,1792]{1,0:T(8,128)(2,1)S(1)}, bf16[48,1792]{1,0:T(8,128)(2,1)S(1)}, u32[]{:S(2)}, u32[]{:S(2)}) collective-permute-start(bf16[48,1792]{1,0:T(8,128)(2,1)S(1)} %add_convert_fusion.4), channel_id=1, source_target_pairs={{0,8},{8,0},{16,24},{24,16},{1,9},{9,1},{17,25},{25,17},{2,10},{10... | collective-permute-start | bytes 516104 | tf_op jit(solution)/shard_map/ppermute | solution.py:56
  170.4 34.8 %collective-permute-start.68 = (bf16[48,1792]{1,0:T(8,128)(2,1)S(1)}, bf16[48,1792]{1,0:T(8,128)(2,1)S(1)}, u32[]{:S(2)}, u32[]{:S(2)}) collective-permute-start(bf16[48,1792]{1,0:T(8,128)(2,1)S(1)} %add_convert_fusion.5), channel_id=1, source_target_pairs={{0,8},{8,0},{16,24},{24,16},{1,9},{9,1},{17,25},{25,17},{2,10},{10... | collective-permute-start | bytes 516104 | tf_op jit(solution)/shard_map/ppermute | solution.py:56
  172.2 11.9 %collective-permute-start.56 = (bf16[128,768]{1,0:T(8,128)(2,1)}, bf16[128,768]{1,0:T(8,128)(2,1)S(1)}, u32[]{:S(2)}, u32[]{:S(2)}) collective-permute-start(bf16[128,768]{1,0:T(8,128)(2,1)} %get-tuple-element.83), channel_id=1, source_target_pairs={{0,1},{1,0},{2,3},{3,2},{4,5},{5,4},{6,7},{7,6},{8,9},{9,8},{10,11... | collective-permute-start | bytes 589832 | tf_op jit(solution)/shard_map/ppermute | solution.py:56
  177.3 27.9 %collective-permute-start.72 = (bf16[48,1792]{1,0:T(8,128)(2,1)S(1)}, bf16[48,1792]{1,0:T(8,128)(2,1)S(1)}, u32[]{:S(2)}, u32[]{:S(2)}) collective-permute-start(bf16[48,1792]{1,0:T(8,128)(2,1)S(1)} %add_convert_fusion.3), channel_id=1, source_target_pairs={{0,16},{8,24},{16,0},{24,8},{1,17},{9,25},{17,1},{25,9},{2,18},{10... | collective-permute-start | bytes 516104 | tf_op jit(solution)/shard_map/ppermute | solution.py:56
  184.2 13.9 %collective-permute-start.61 = (bf16[48,1536]{1,0:T(8,128)(2,1)}, bf16[48,1536]{1,0:T(8,128)(2,1)S(1)}, u32[]{:S(2)}, u32[]{:S(2)}) collective-permute-start(bf16[48,1536]{1,0:T(8,128)(2,1)} %get-tuple-element.91), channel_id=1, source_target_pairs={{0,4},{2,6},{4,0},{6,2},{1,5},{3,7},{5,1},{7,3},{8,12},{10,14},{12... | collective-permute-start | bytes 442376 | tf_op jit(solution)/shard_map/ppermute | solution.py:56
  204.0 7.1 %collective-permute-start.64 = (bf16[48,1536]{1,0:T(8,128)(2,1)S(1)}, bf16[48,1536]{1,0:T(8,128)(2,1)S(1)}, u32[]{:S(2)}, u32[]{:S(2)}) collective-permute-start(bf16[48,1536]{1,0:T(8,128)(2,1)S(1)} %add_convert_fusion.6), channel_id=1, source_target_pairs={{0,16},{8,24},{16,0},{24,8},{1,17},{9,25},{17,1},{25,9},{2,18},{10... | collective-permute-start | bytes 442376 | tf_op jit(solution)/shard_map/ppermute | solution.py:56
  (102 other events, 852.7 us)

commit v2 on v1

--- a/solution.py
+++ b/solution.py
@@ -454,8 +454,9 @@
         jnp.sum(wf[:, : 3 * width] * one[:, : 3 * width], axis=1, keepdims=True),
         jnp.sum(wf[:, cut : cut + 2 * units] * two[:, : 2 * units], axis=1, keepdims=True),
     ]
-    lane = lax.broadcasted_iota(jnp.int32, gain_ref.shape, 1)
-    gain_ref[...] = jnp.where(lane == 0, sums[0], jnp.where(lane == 1, sums[1], 0.0))
+    lane = lax.broadcasted_iota(jnp.int32, (wf.shape[0], 128), 1)
+    cols = jnp.where(lane == 0, sums[0], jnp.where(lane == 1, sums[1], 0.0))
+    gain_ref[...] = jnp.transpose(cols)[:2, :]
     g_ref[:, :cut] = one
     g_ref[:, cut:] = two
 
@@ -464,6 +465,19 @@
     w_out[...], m_out[...], v_out[...] = adam_update(
         w_ref[...], g_ref[...], m_ref[...], v_ref[...]
     )
+
+
+def gadam_kernel(a_ref, b_ref, w_ref, m_ref, v_ref, g_out, w_out, m_out, v_out):
+    w = w_ref[...]
+    grad = (a_ref[...] + b_ref[...]) / w.astype(BF16).astype(F32)
+    g_out[...] = grad
+    w_out[...], m_out[...], v_out[...] = adam_update(w, grad, m_ref[...], v_ref[...])
+
+
+def lnback_kernel(x_ref, da_ref, db_ref, dhid_ref, g_ref, out_ref):
+    xhat, inv = norm_parts(x_ref[...])
+    da = da_ref[...].astype(F32) + db_ref[...].astype(F32)
+    out_ref[...] = dhid_ref[...] + norm_back(da, xhat, inv, g_ref[0:1, :])
 
 
 def head_swap(x):
@@ -586,22 +600,21 @@
     )
     da_part = grads[halves]
     da_other = head_swap(da_part)
-    da = da_part.astype(F32) + da_other.astype(F32)
-    xhat, inv = norm_parts(inputs)
-    input_grad = dhid + norm_back(da, xhat, inv, g[0:1, :])
+    (input_grad,) = call(
+        lnback_kernel, [sds((toks, d), F32)], [VM] * 5, [], [inputs, da_part, da_other, dhid, g]
+    )
 
     first_terms = scatter_sum(grads[:halves])
     full = weights.shape
     weight_grad, gain_part = call(
         partial(gsum_kernel, nt, width, units),
-        [sds(full, F32), sds((rows, 128), F32)],
+        [sds(full, F32), sds(gains.shape, F32)],
         [VM] * (1 + 2 * nt),
         [],
         [weights] + first_terms + ffn_terms,
     )
-    gain_part = gain_part[:, :2].T
-    gain_grad = (gain_part + head_swap(gain_part)) / gb.astype(F32)
-    step_rows = 8 if rows % 8 == 0 else rows
+    gain_other = head_swap(gain_part)
+    step_rows = rows // 2 if rows % 16 == 0 else rows
     cells = pl.BlockSpec((step_rows, full[1]), lambda i: (i, 0))
     new_weights, new_weight_moment, new_weight_second = pl.pallas_call(
         adam_kernel,
@@ -611,8 +624,12 @@
         out_specs=[cells] * 3,
         name="adam",
     )(weights, weight_grad, weight_moment, weight_second)
-    new_gains, new_gain_moment, new_gain_second = adam_update(
-        gains, gain_grad, gain_moment, gain_second
+    gain_grad, new_gains, new_gain_moment, new_gain_second = call(
+        gadam_kernel,
+        [sds(gains.shape, F32)] * 4,
+        [VM] * 5,
+        [],
+        [gain_part, gain_other, gains, gain_moment, gain_second],
     )
     return (
         outputs,

time: 225 us -> 227 us (level)
  local copies, waits for them, and re-layouts: 14.6 us -> 7.07 us
  waiting for transfers between devices: 81 us -> 87.8 us
    ppermute x74, waiting for transfers between devices: 81 us -> 87.8 us  [swap(): return lax.ppermute(x, axis, [(i, i ^ bits) for i in range(size)])]
    convert_element_type x9, other arithmetic: 2.28 us -> 6.99 us  [block(): return total([s[z], got[z], *more]).astype(BF16)]
    pallas_call x7 -> x9, Pallas kernels: 40.7 us -> 44.4 us  [call(): pl.pallas_call(kernel, out_shape=out_shape, in_specs=specs, out_specs=jax...]
    unnamed x157 -> x120, local copies, waits for them, and re-layouts: 9.99 us -> 6.92 us
  transfers between devices with their start and end apart: 74 -> 74, of which waited for: 29 -> 30; matrix products, arithmetic and copies ran while one was open for 5% -> 4% of each run, Pallas kernels for 16% -> 17%
where the time goes in v2:
time: 227 us; the launch traced here: 226 us
  waiting for transfers between devices  87.8 us (39%)
  starting transfers between devices  63.2 us (28%)
  Pallas kernels  55.9 us (25%)
  other arithmetic  10.7 us (5%)
  local copies, waits for them, and re-layouts  7.07 us (3%)
    ppermute x74, waiting for transfers between devices, swap(): return lax.ppermute(x, axis, [(i, i ^ bits) for i in range(size)])  87.8 us
    ppermute x74, starting transfers between devices, swap(): return lax.ppermute(x, axis, [(i, i ^ bits) for i in range(size)])  63.2 us
    pallas_call x9, Pallas kernels, call(): pl.pallas_call(kernel, out_shape=out_shape, in_specs=specs, out_specs=jax...  44.4 us
    pallas_call x3, Pallas kernels, scatter_sum(): pl.pallas_call(add_kernel, out_shape=[sds((rows, cols), BF16)] * 8, in_sp...  8.63 us
    convert_element_type x9, other arithmetic, block(): return total([s[z], got[z], *more]).astype(BF16)  6.99 us
    unnamed x120, local copies, waits for them, and re-layouts  6.92 us
  transfers between devices with their start and end apart: 74, of which 30 were waited for; matrix products, arithmetic and copies ran while one was open for 4% of the time, Pallas kernels for 17%

profile of v2, /device:TPU:0, one launch (start us, length us, event | category | flops | bytes accessed | tf_op | source)
XLA Modules:
  0.0 226.2 jit_solution(6029557403491342888)
XLA Ops:
  2.6 4.1 %collective-permute-start.1 = (bf16[48,1664]{1,0:T(8,128)(2,1)S(1)}, bf16[48,1664]{1,0:T(8,128)(2,1)S(1)}, u32[]{:S(2)}, u32[]{:S(2)}) collective-permute-start(bf16[48,1664]{1,0:T(8,128)(2,1)S(1)} %fusion.1.rest_0_.rest_16_.rest_4_), channel_id=1, source_target_pairs={{0,16},{8,24},{16,0},{24,8},{1,17},{9,25},{17,1},{25,9},{2,18},{10... | collective-permute-start | bytes 479240 | tf_op jit(solution)/shard_map/ppermute | solution.py:56
  6.7 1.6 collective-permute-start
  9.8 4.6 %collective-permute-done.1.rest_2_.rest_18_.rest_6_ = bf16[48,1664]{1,0:T(8,128)(2,1)S(1)} collective-permute-done((bf16[48,1664]{1,0:T(8,128)(2,1)S(1)}, bf16[48,1664]{1,0:T(8,128)(2,1)S(1)}, u32[]{:S(2)}, u32[]{:S(2)}) %collective-permute-start.1) | collective-permute-done | bytes 159776 | tf_op jit(solution)/shard_map/ppermute | solution.py:56
  17.3 2.4 %collective-permute-done.2.rest_3_.rest_19_.rest_7_ = bf16[48,1664]{1,0:T(8,128)(2,1)S(1)} collective-permute-done((bf16[48,1664]{1,0:T(8,128)(2,1)S(1)}, bf16[48,1664]{1,0:T(8,128)(2,1)S(1)}, u32[]{:S(2)}, u32[]{:S(2)}) %collective-permute-start.2) | collective-permute-done | bytes 159776 | tf_op jit(solution)/shard_map/ppermute | solution.py:56
  19.7 2.2 collective-permute-done.5.rest_6_.rest_22_.rest_10_
  21.9 1.6 collective-permute-start.6
  23.6 1.8 collective-permute-done.4.rest_5_.rest_21_.rest_9_
  25.3 3.4 %collective-permute-start.32 = (bf16[48,1792]{1,0:T(8,128)(2,1)S(1)}, bf16[48,1792]{1,0:T(8,128)(2,1)S(1)}, u32[]{:S(2)}, u32[]{:S(2)}) collective-permute-start(bf16[48,1792]{1,0:T(8,128)(2,1)S(1)} %pad.9.rest_0_), channel_id=1, source_target_pairs={{0,16},{8,24},{16,0},{24,8},{1,17},{9,25},{17,1},{25,9},{2,18},{10... | collective-permute-start | bytes 516104 | tf_op jit(solution)/shard_map/ppermute | solution.py:56
  31.7 4.3 %shard_map.159 = (bf16[128,768]{1,0:T(8,128)(2,1)}, bf16[128,384]{1,0:T(8,128)(2,1)}, bf16[128,768]{1,0:T(8,128)(2,1)}, f32[8,768]{1,0:T(8,128)}) custom-call(s32[1]{0:T(128)} %bitcast.order_ref, f32[128,768]{1,0:T(8,128)} %x_ref.5, f32[128,128]{1,0:T(8,128)} %get-tuple-element.121.cos_ref, f32[128,128]{1,0:T(8,128)} %get-tuple-element.120.sin_ref, ...), custom_call_target="tpu_custom_call" | custom-call | tf_op jit(solution)/shard_map/pallas_call | solution.py:420
  39.2 1.8 collective-permute-start.33
  41.0 7.8 %collective-permute-done.31.rest_1_ = bf16[48,1792]{1,0:T(8,128)(2,1)S(1)} collective-permute-done((bf16[48,1792]{1,0:T(8,128)(2,1)S(1)}, bf16[48,1792]{1,0:T(8,128)(2,1)S(1)}, u32[]{:S(2)}, u32[]{:S(2)}) %collective-permute-start.31) | collective-permute-done | bytes 172064 | tf_op jit(solution)/shard_map/ppermute | solution.py:56
  50.6 1.7 collective-permute-start.17
  54.1 2.7 %collective-permute-done.15.rest_1_ = bf16[128,768]{1,0:T(8,128)(2,1)S(1)} collective-permute-done((bf16[128,768]{1,0:T(8,128)(2,1)}, bf16[128,768]{1,0:T(8,128)(2,1)S(1)}, u32[]{:S(2)}, u32[]{:S(2)}) %collective-permute-start.15) | collective-permute-done | bytes 196640 | tf_op jit(solution)/shard_map/ppermute | solution.py:56
  58.3 1.7 collective-permute-done.36.rest_6_
  62.5 2.1 collective-permute-done.19.rest_5_
  64.5 4.2 %collective-permute-done.20.rest_6_ = bf16[128,768]{1,0:T(8,128)(2,1)S(1)} collective-permute-done((bf16[128,768]{1,0:T(8,128)(2,1)S(1)}, bf16[128,768]{1,0:T(8,128)(2,1)S(1)}, u32[]{:S(2)}, u32[]{:S(2)}) %collective-permute-start.20) | collective-permute-done | bytes 196640 | tf_op jit(solution)/shard_map/ppermute | solution.py:56
  69.4 2.1 collective-permute-done.21.rest_7_
  74.4 7.6 %shard_map.160 = (bf16[128,384]{1,0:T(8,128)(2,1)}, f32[8,256]{1,0:T(8,128)}, bf16[128,768]{1,0:T(8,128)(2,1)}) custom-call(s32[1]{0:T(128)} %bitcast.order_ref, bf16[128,384]{1,0:T(8,128)(2,1)} %get-tuple-element.65.q_ref, bf16[128,768]{1,0:T(8,128)(2,1)} %get-tuple-element.66.rest_0_, bf16[128,768]{1,0:T(8,128)(2,1)} %copy-done.21, ...), custom_call_target="tpu_custom_call" | custom-call | tf_op jit(solution)/shard_map/pallas_call | solution.py:420
  82.0 1.6 collective-permute-start.30
  86.0 3.3 %collective-permute-done.30.pb_ref = bf16[128,768]{1,0:T(8,128)(2,1)S(1)} collective-permute-done((bf16[128,768]{1,0:T(8,128)(2,1)}, bf16[128,768]{1,0:T(8,128)(2,1)S(1)}, u32[]{:S(2)}, u32[]{:S(2)}) %collective-permute-start.30) | collective-permute-done | bytes 196640 | tf_op jit(solution)/shard_map/ppermute | solution.py:56
  90.0 5.4 %shard_map.161 = (f32[128,768]{1,0:T(8,128)}, bf16[128,768]{1,0:T(8,128)(2,1)}, bf16[128,768]{1,0:T(8,128)(2,1)}, bf16[128,768]{1,0:T(8,128)(2,1)}, bf16[128,1152]{1,0:T(8,128)(2,1)}, /*index=5*/bf16[128,576]{1,0:T(8,128)(2,1)}) custom-call(s32[1]{0:T(128)} %bitcast.order_ref, f32[128,768]{1,0:T(8,128)} %x_ref.5, bf16[128,768]{1,0:T(8,128)(2,1)} %get-tuple-element.67.pa_ref, ...), custom_call_target="tpu_custom_call" | custom-call | tf_op jit(solution)/shard_map/pallas_call | solution.py:420
  95.4 1.6 collective-permute-start.47
  97.0 4.8 %collective-permute-done.47.db_ref = bf16[128,768]{1,0:T(8,128)(2,1)S(1)} collective-permute-done((bf16[128,768]{1,0:T(8,128)(2,1)}, bf16[128,768]{1,0:T(8,128)(2,1)S(1)}, u32[]{:S(2)}, u32[]{:S(2)}) %collective-permute-start.47) | collective-permute-done | bytes 196640 | tf_op jit(solution)/shard_map/ppermute | solution.py:56
  102.5 10.6 %shard_map.162 = (bf16[1024,768]{1,0:T(8,128)(2,1)}, bf16[1024,768]{1,0:T(8,128)(2,1)}, f32[128,768]{1,0:T(8,128)}, bf16[128,384]{1,0:T(8,128)(2,1)}) custom-call(s32[1]{0:T(128)} %bitcast.order_ref, bf16[128,384]{1,0:T(8,128)(2,1)} %get-tuple-element.65.q_ref, bf16[128,384]{1,0:T(8,128)(2,1)} %get-tuple-element.72.attn_ref, ...), custom_call_target="tpu_custom_call" | custom-call | tf_op jit(solution)/shard_map/pallas_call | solution.py:420
  113.2 3.8 %shard_map.165 = (bf16[384,1792]{1,0:T(8,128)(2,1)}, bf16[384,1792]{1,0:T(8,128)(2,1)}) custom-call(s32[1]{0:T(128)} %bitcast.order_ref, bf16[128,768]{1,0:T(8,128)(2,1)} %get-tuple-element.98.b_ref, bf16[128,1152]{1,0:T(8,128)(2,1)} %get-tuple-element.99.dz_ref, f32[128,768]{1,0:T(8,128)} %cot_ref.5, bf16[128,576]{1,0:T(8,128)(2,1)} %get-tuple-element.100.mixed_ref), custom_call_target="tpu_custom_call" | custom-call | tf_op jit(solution)/shard_map/pallas_call | solution.py:420
  118.7 3.1 %pair_add.3 = (bf16[128,768]{1,0:T(8,128)(2,1)}, bf16[128,768]{1,0:T(8,128)(2,1)}, bf16[128,768]{1,0:T(8,128)(2,1)}, bf16[128,768]{1,0:T(8,128)(2,1)}, bf16[128,...) custom-call(bf16[1024,768]{1,0:T(8,128)(2,1)} %get-tuple-element.77.refs_0_, ...), custom_call_target="tpu_custom_call" | custom-call | tf_op jit(solution)/shard_map/pair_add/pallas_call | solution.py:96
  125.8 3.9 %collective-permute-done.53 = bf16[128,768]{1,0:T(8,128)(2,1)S(1)} collective-permute-done((bf16[128,768]{1,0:T(8,128)(2,1)}, bf16[128,768]{1,0:T(8,128)(2,1)S(1)}, u32[]{:S(2)}, u32[]{:S(2)}) %collective-permute-start.53) | collective-permute-done | bytes 196640 | tf_op jit(solution)/shard_map/ppermute | solution.py:56
  130.7 1.7 collective-permute-start.54
  132.4 5.8 %collective-permute-done.50 = bf16[128,768]{1,0:T(8,128)(2,1)S(1)} collective-permute-done((bf16[128,768]{1,0:T(8,128)(2,1)}, bf16[128,768]{1,0:T(8,128)(2,1)S(1)}, u32[]{:S(2)}, u32[]{:S(2)}) %collective-permute-start.50) | collective-permute-done | bytes 196640 | tf_op jit(solution)/shard_map/ppermute | solution.py:56
  139.1 1.7 collective-permute-start.51
  141.9 3.7 %collective-permute-done.51.rest_2_ = bf16[128,768]{1,0:T(8,128)(2,1)S(1)} collective-permute-done((bf16[128,768]{1,0:T(8,128)(2,1)S(1)}, bf16[128,768]{1,0:T(8,128)(2,1)S(1)}, u32[]{:S(2)}, u32[]{:S(2)}) %collective-permute-start.51) | collective-permute-done | bytes 196640 | tf_op jit(solution)/shard_map/ppermute | solution.py:56
  145.6 6.1 %collective-permute-done.55.rest_3_ = bf16[128,768]{1,0:T(8,128)(2,1)S(1)} collective-permute-done((bf16[128,768]{1,0:T(8,128)(2,1)S(1)}, bf16[128,768]{1,0:T(8,128)(2,1)S(1)}, u32[]{:S(2)}, u32[]{:S(2)}) %collective-permute-start.55) | collective-permute-done | bytes 196640 | tf_op jit(solution)/shard_map/ppermute | solution.py:56
  152.3 6.4 %shard_map.163 = (bf16[384,1536]{1,0:T(8,128)(2,1)}, bf16[384,1536]{1,0:T(8,128)(2,1)}, bf16[128,768]{1,0:T(8,128)(2,1)}) custom-call(s32[1]{0:T(128)} %bitcast.order_ref, bf16[128,768]{1,0:T(8,128)(2,1)} %get-tuple-element.71.a_ref, bf16[128,384]{1,0:T(8,128)(2,1)} %get-tuple-element.75.dqp_ref, f32[128,768]{1,0:T(8,128)} %get-tuple-element.76.dhid_ref, ...), custom_call_target="tpu_custom_call" | custom-call | tf_op jit(solution)/shard_map/pallas_call | solution.py:420
  159.9 2.9 %pair_add.5 = (bf16[48,1792]{1,0:T(8,128)(2,1)}, bf16[48,1792]{1,0:T(8,128)(2,1)}, bf16[48,1792]{1,0:T(8,128)(2,1)}, bf16[48,1792]{1,0:T(8,128)(2,1)}, bf16[48,1...) custom-call(bf16[384,1792]{1,0:T(8,128)(2,1)} %get-tuple-element.101.refs_0_, ...), custom_call_target="tpu_custom_call" | custom-call | tf_op jit(solution)/shard_map/pair_add/pallas_call | solution.py:96
  163.9 1.5 collective-permute-start.46
  167.5 2.8 %collective-permute-done.70 = bf16[48,1792]{1,0:T(8,128)(2,1)S(1)} collective-permute-done((bf16[48,1792]{1,0:T(8,128)(2,1)}, bf16[48,1792]{1,0:T(8,128)(2,1)S(1)}, u32[]{:S(2)}, u32[]{:S(2)}) %collective-permute-start.70) | collective-permute-done | bytes 172064 | tf_op jit(solution)/shard_map/ppermute | solution.py:56
  172.3 5.3 %collective-permute-done.67 = bf16[48,1792]{1,0:T(8,128)(2,1)S(1)} collective-permute-done((bf16[48,1792]{1,0:T(8,128)(2,1)}, bf16[48,1792]{1,0:T(8,128)(2,1)S(1)}, u32[]{:S(2)}, u32[]{:S(2)}) %collective-permute-start.67) | collective-permute-done | bytes 172064 | tf_op jit(solution)/shard_map/ppermute | solution.py:56
  178.7 2.1 collective-permute-start.68
  180.8 2.7 %pair_add.4 = (bf16[48,1536]{1,0:T(8,128)(2,1)}, bf16[48,1536]{1,0:T(8,128)(2,1)}, bf16[48,1536]{1,0:T(8,128)(2,1)}, bf16[48,1536]{1,0:T(8,128)(2,1)}, bf16[48,1...) custom-call(bf16[384,1536]{1,0:T(8,128)(2,1)} %get-tuple-element.88.refs_0_, ...), custom_call_target="tpu_custom_call" | custom-call | tf_op jit(solution)/shard_map/pair_add/pallas_call | solution.py:96
  186.1 3.8 %collective-permute-done.62 = bf16[48,1536]{1,0:T(8,128)(2,1)S(1)} collective-permute-done((bf16[48,1536]{1,0:T(8,128)(2,1)}, bf16[48,1536]{1,0:T(8,128)(2,1)S(1)}, u32[]{:S(2)}, u32[]{:S(2)}) %collective-permute-start.62) | collective-permute-done | bytes 147488 | tf_op jit(solution)/shard_map/ppermute | solution.py:56
  192.0 3.3 %collective-permute-done.59 = bf16[48,1536]{1,0:T(8,128)(2,1)S(1)} collective-permute-done((bf16[48,1536]{1,0:T(8,128)(2,1)}, bf16[48,1536]{1,0:T(8,128)(2,1)S(1)}, u32[]{:S(2)}, u32[]{:S(2)}) %collective-permute-start.59) | collective-permute-done | bytes 147488 | tf_op jit(solution)/shard_map/ppermute | solution.py:56
  197.9 5.6 %collective-permute-done.63 = bf16[48,1536]{1,0:T(8,128)(2,1)S(1)} collective-permute-done((bf16[48,1536]{1,0:T(8,128)(2,1)S(1)}, bf16[48,1536]{1,0:T(8,128)(2,1)S(1)}, u32[]{:S(2)}, u32[]{:S(2)}) %collective-permute-start.63) | collective-permute-done | bytes 147488 | tf_op jit(solution)/shard_map/ppermute | solution.py:56
  205.1 3.6 %collective-permute-done.72.rest_7_ = bf16[48,1792]{1,0:T(8,128)(2,1)S(1)} collective-permute-done((bf16[48,1792]{1,0:T(8,128)(2,1)S(1)}, bf16[48,1792]{1,0:T(8,128)(2,1)S(1)}, u32[]{:S(2)}, u32[]{:S(2)}) %collective-permute-start.72) | collective-permute-done | bytes 172064 | tf_op jit(solution)/shard_map/ppermute | solution.py:56
  208.7 1.5 collective-permute-start.56
  213.4 2.7 %shard_map.166 = (f32[48,3264]{1,0:T(8,128)}, f32[2,48]{1,0:T(2,128)}) custom-call(f32[48,3264]{1,0:T(8,128)} %w_ref.5, bf16[48,1536]{1,0:T(8,128)(2,1)} %get-tuple-element.90.rest_0_, bf16[48,1536]{1,0:T(8,128)(2,1)} %copy-done.55, bf16[48,1536]{1,0:T(8,128)(2,1)} %copy-done.56, bf16[48,1536]{1,0:T(8,128)(2,1)} %copy-done.57, ...), custom_call_target="tpu_custom_call" | custom-call | tf_op jit(solution)/shard_map/pallas_call | solution.py:420
  216.1 1.5 collective-permute-start.73
  219.1 2.3 %shard_map.164 = f32[128,768]{1,0:T(8,128)} custom-call(f32[128,768]{1,0:T(8,128)} %x_ref.5, bf16[128,768]{1,0:T(8,128)(2,1)} %get-tuple-element.87.da_ref, bf16[128,768]{1,0:T(8,128)(2,1)} %copy-done.42, f32[128,768]{1,0:T(8,128)} %get-tuple-element.76.dhid_ref, f32[8,768]{1,0:T(8,128)} %get-tuple-element.68.g_ref), custom_call_target="tpu_custom_call" | custom-call | tf_op jit(solution)/shard_map/pallas_call | solution.py:420
  221.4 2.8 %adam.1 = (f32[48,3264]{1,0:T(8,128)}, f32[48,3264]{1,0:T(8,128)}, f32[48,3264]{1,0:T(8,128)}) custom-call(f32[48,3264]{1,0:T(8,128)} %w_ref.5, f32[48,3264]{1,0:T(8,128)} %get-tuple-element.57.g_ref, f32[48,3264]{1,0:T(8,128)} %m_ref.3, f32[48,3264]{1,0:T(8,128)} %v_ref.3), custom_call_target="tpu_custom_call" | custom-call | tf_op jit(solution)/shard_map/adam/pallas_call | solution.py:619
  (254 shorter events, 59.3 us)
Async XLA Ops:
  2.6 11.8 %collective-permute-start.1 = (bf16[48,1664]{1,0:T(8,128)(2,1)S(1)}, bf16[48,1664]{1,0:T(8,128)(2,1)S(1)}, u32[]{:S(2)}, u32[]{:S(2)}) collective-permute-start(bf16[48,1664]{1,0:T(8,128)(2,1)S(1)} %fusion.1.rest_0_.rest_16_.rest_4_), channel_id=1, source_target_pairs={{0,16},{8,24},{16,0},{24,8},{1,17},{9,25},{17,1},{25,9},{2,18},{10... | collective-permute-start | bytes 479240 | tf_op jit(solution)/shard_map/ppermute | solution.py:56
  6.7 9.8 %collective-permute-start = (bf16[48,1664]{1,0:T(8,128)(2,1)S(1)}, bf16[48,1664]{1,0:T(8,128)(2,1)S(1)}, u32[]{:S(2)}, u32[]{:S(2)}) collective-permute-start(bf16[48,1664]{1,0:T(8,128)(2,1)S(1)} %fusion.1.rest_0_.rest_16_.rest_4_), channel_id=1, source_target_pairs={{0,8},{8,0},{16,24},{24,16},{1,9},{9,1},{17,25},{25,17},{2,10},{10... | collective-permute-start | bytes 479240 | tf_op jit(solution)/shard_map/ppermute | solution.py:56
  8.3 8.2 %collective-permute-start.3 = (bf16[48,1664]{1,0:T(8,128)(2,1)S(1)}, bf16[48,1664]{1,0:T(8,128)(2,1)S(1)}, u32[]{:S(2)}, u32[]{:S(2)}) collective-permute-start(bf16[48,1664]{1,0:T(8,128)(2,1)S(1)} %fusion.1.rest_0_.rest_16_.rest_4_), channel_id=1, source_target_pairs={{0,4},{2,6},{4,0},{6,2},{1,5},{3,7},{5,1},{7,3},{8,12},{10,14},{12... | collective-permute-start | bytes 479240 | tf_op jit(solution)/shard_map/ppermute | solution.py:56
  16.5 12.2 %collective-permute-start.9 = (bf16[48,1664]{1,0:T(8,128)(2,1)S(1)}, bf16[48,1664]{1,0:T(8,128)(2,1)S(1)}, u32[]{:S(2)}, u32[]{:S(2)}) collective-permute-start(bf16[48,1664]{1,0:T(8,128)(2,1)S(1)} %collective-permute-done.1.rest_2_.rest_18_.rest_6_), channel_id=1, source_target_pairs={{0,2},{2,0},{4,6},{6,4},{1,3},{3,1},{5,7},{7,5},{8,10},{10,8},{12,... | collective-permute-start | bytes 479240 | tf_op jit(solution)/shard_map/ppermute | solution.py:56
  16.5 8.8 %collective-permute-start.4 = (bf16[48,1664]{1,0:T(8,128)(2,1)S(1)}, bf16[48,1664]{1,0:T(8,128)(2,1)S(1)}, u32[]{:S(2)}, u32[]{:S(2)}) collective-permute-start(bf16[48,1664]{1,0:T(8,128)(2,1)S(1)} %collective-permute-done.rest_1_.rest_17_.rest_5_), channel_id=1, source_target_pairs={{0,4},{2,6},{4,0},{6,2},{1,5},{3,7},{5,1},{7,3},{8,12},{10,14},{12... | collective-permute-start | bytes 479240 | tf_op jit(solution)/shard_map/ppermute | solution.py:56
  17.1 11.6 %collective-permute-start.8 = (bf16[48,1664]{1,0:T(8,128)(2,1)S(1)}, bf16[48,1664]{1,0:T(8,128)(2,1)S(1)}, u32[]{:S(2)}, u32[]{:S(2)}) collective-permute-start(bf16[48,1664]{1,0:T(8,128)(2,1)S(1)} %collective-permute-done.rest_1_.rest_17_.rest_5_), channel_id=1, source_target_pairs={{0,2},{2,0},{4,6},{6,4},{1,3},{3,1},{5,7},{7,5},{8,10},{10,8},{12,... | collective-permute-start | bytes 479240 | tf_op jit(solution)/shard_map/ppermute | solution.py:56
  19.7 9.6 %collective-permute-start.11 = (bf16[48,1664]{1,0:T(8,128)(2,1)S(1)}, bf16[48,1664]{1,0:T(8,128)(2,1)S(1)}, u32[]{:S(2)}, u32[]{:S(2)}) collective-permute-start(bf16[48,1664]{1,0:T(8,128)(2,1)S(1)} %collective-permute-done.3.rest_4_.rest_20_.rest_8_), channel_id=1, source_target_pairs={{0,2},{2,0},{4,6},{6,4},{1,3},{3,1},{5,7},{7,5},{8,10},{10,8},{12,... | collective-permute-start | bytes 479240 | tf_op jit(solution)/shard_map/ppermute | solution.py:56
  21.9 7.4 %collective-permute-start.6 = (bf16[48,1664]{1,0:T(8,128)(2,1)S(1)}, bf16[48,1664]{1,0:T(8,128)(2,1)S(1)}, u32[]{:S(2)}, u32[]{:S(2)}) collective-permute-start(bf16[48,1664]{1,0:T(8,128)(2,1)S(1)} %collective-permute-done.2.rest_3_.rest_19_.rest_7_), channel_id=1, source_target_pairs={{0,4},{2,6},{4,0},{6,2},{1,5},{3,7},{5,1},{7,3},{8,12},{10,14},{12... | collective-permute-start | bytes 479240 | tf_op jit(solution)/shard_map/ppermute | solution.py:56
  25.3 13.9 %collective-permute-start.32 = (bf16[48,1792]{1,0:T(8,128)(2,1)S(1)}, bf16[48,1792]{1,0:T(8,128)(2,1)S(1)}, u32[]{:S(2)}, u32[]{:S(2)}) collective-permute-start(bf16[48,1792]{1,0:T(8,128)(2,1)S(1)} %pad.9.rest_0_), channel_id=1, source_target_pairs={{0,16},{8,24},{16,0},{24,8},{1,17},{9,25},{17,1},{25,9},{2,18},{10... | collective-permute-start | bytes 516104 | tf_op jit(solution)/shard_map/ppermute | solution.py:56
  36.0 14.7 %collective-permute-start.16 = (bf16[128,768]{1,0:T(8,128)(2,1)}, bf16[128,768]{1,0:T(8,128)(2,1)S(1)}, u32[]{:S(2)}, u32[]{:S(2)}) collective-permute-start(bf16[128,768]{1,0:T(8,128)(2,1)} %get-tuple-element.66.rest_0_), channel_id=1, source_target_pairs={{0,16},{8,24},{16,0},{24,8},{1,17},{9,25},{17,1},{25,9},{2,18},{10... | collective-permute-start | bytes 589832 | tf_op jit(solution)/shard_map/ppermute | solution.py:56
  37.4 11.4 %collective-permute-start.31 = (bf16[48,1792]{1,0:T(8,128)(2,1)S(1)}, bf16[48,1792]{1,0:T(8,128)(2,1)S(1)}, u32[]{:S(2)}, u32[]{:S(2)}) collective-permute-start(bf16[48,1792]{1,0:T(8,128)(2,1)S(1)} %pad.9.rest_0_), channel_id=1, source_target_pairs={{0,8},{8,0},{16,24},{24,16},{1,9},{9,1},{17,25},{25,17},{2,10},{10... | collective-permute-start | bytes 516104 | tf_op jit(solution)/shard_map/ppermute | solution.py:56
  37.7 11.4 %collective-permute-start.34 = (bf16[48,1792]{1,0:T(8,128)(2,1)S(1)}, bf16[48,1792]{1,0:T(8,128)(2,1)}, u32[]{:S(2)}, u32[]{:S(2)}) collective-permute-start(bf16[48,1792]{1,0:T(8,128)(2,1)S(1)} %pad.9.rest_0_), channel_id=1, source_target_pairs={{0,4},{2,6},{4,0},{6,2},{1,5},{3,7},{5,1},{7,3},{8,12},{10,14},{12... | collective-permute-start | bytes 516104 | tf_op jit(solution)/shard_map/ppermute | solution.py:56
  39.2 11.4 %collective-permute-start.38 = (bf16[48,1792]{1,0:T(8,128)(2,1)S(1)}, bf16[48,1792]{1,0:T(8,128)(2,1)}, u32[]{:S(2)}, u32[]{:S(2)}) collective-permute-start(bf16[48,1792]{1,0:T(8,128)(2,1)S(1)} %pad.9.rest_0_), channel_id=1, source_target_pairs={{0,2},{2,0},{4,6},{6,4},{1,3},{3,1},{5,7},{7,5},{8,10},{10,8},{12,... | collective-permute-start | bytes 516104 | tf_op jit(solution)/shard_map/ppermute | solution.py:56
  39.2 13.4 %collective-permute-start.33 = (bf16[48,1792]{1,0:T(8,128)(2,1)S(1)}, bf16[48,1792]{1,0:T(8,128)(2,1)}, u32[]{:S(2)}, u32[]{:S(2)}) collective-permute-start(bf16[48,1792]{1,0:T(8,128)(2,1)S(1)} %collective-permute-done.32.rest_2_), channel_id=1, source_target_pairs={{0,8},{8,0},{16,24},{24,16},{1,9},{9,1},{17,25},{25,17},{2,10},{10... | collective-permute-start | bytes 516104 | tf_op jit(solution)/shard_map/ppermute | solution.py:56
  48.8 8.0 %collective-permute-start.15 = (bf16[128,768]{1,0:T(8,128)(2,1)}, bf16[128,768]{1,0:T(8,128)(2,1)S(1)}, u32[]{:S(2)}, u32[]{:S(2)}) collective-permute-start(bf16[128,768]{1,0:T(8,128)(2,1)} %get-tuple-element.66.rest_0_), channel_id=1, source_target_pairs={{0,8},{8,0},{16,24},{24,16},{1,9},{9,1},{17,25},{25,17},{2,10},{10... | collective-permute-start | bytes 589832 | tf_op jit(solution)/shard_map/ppermute | solution.py:56
  49.1 12.1 %collective-permute-start.18 = (bf16[128,768]{1,0:T(8,128)(2,1)}, bf16[128,768]{1,0:T(8,128)(2,1)S(1)}, u32[]{:S(2)}, u32[]{:S(2)}) collective-permute-start(bf16[128,768]{1,0:T(8,128)(2,1)} %get-tuple-element.66.rest_0_), channel_id=1, source_target_pairs={{0,4},{2,6},{4,0},{6,2},{1,5},{3,7},{5,1},{7,3},{8,12},{10,14},{12... | collective-permute-start | bytes 589832 | tf_op jit(solution)/shard_map/ppermute | solution.py:56
  50.6 10.6 %collective-permute-start.22 = (bf16[128,768]{1,0:T(8,128)(2,1)}, bf16[128,768]{1,0:T(8,128)(2,1)S(1)}, u32[]{:S(2)}, u32[]{:S(2)}) collective-permute-start(bf16[128,768]{1,0:T(8,128)(2,1)} %get-tuple-element.66.rest_0_), channel_id=1, source_target_pairs={{0,2},{2,0},{4,6},{6,4},{1,3},{3,1},{5,7},{7,5},{8,10},{10,8},{12,... | collective-permute-start | bytes 589832 | tf_op jit(solution)/shard_map/ppermute | solution.py:56
  50.6 11.1 %collective-permute-start.17 = (bf16[128,768]{1,0:T(8,128)(2,1)S(1)}, bf16[128,768]{1,0:T(8,128)(2,1)S(1)}, u32[]{:S(2)}, u32[]{:S(2)}) collective-permute-start(bf16[128,768]{1,0:T(8,128)(2,1)S(1)} %collective-permute-done.16.rest_2_), channel_id=1, source_target_pairs={{0,8},{8,0},{16,24},{24,16},{1,9},{9,1},{17,25},{25,17},{2,10},{10... | collective-permute-start | bytes 589832 | tf_op jit(solution)/shard_map/ppermute | solution.py:56
  56.8 7.8 %collective-permute-start.19 = (bf16[128,768]{1,0:T(8,128)(2,1)S(1)}, bf16[128,768]{1,0:T(8,128)(2,1)S(1)}, u32[]{:S(2)}, u32[]{:S(2)}) collective-permute-start(bf16[128,768]{1,0:T(8,128)(2,1)S(1)} %collective-permute-done.15.rest_1_), channel_id=1, source_target_pairs={{0,4},{2,6},{4,0},{6,2},{1,5},{3,7},{5,1},{7,3},{8,12},{10,14},{12... | collective-permute-start | bytes 589832 | tf_op jit(solution)/shard_map/ppermute | solution.py:56
  59.9 8.8 %collective-permute-start.20 = (bf16[128,768]{1,0:T(8,128)(2,1)S(1)}, bf16[128,768]{1,0:T(8,128)(2,1)S(1)}, u32[]{:S(2)}, u32[]{:S(2)}) collective-permute-start(bf16[128,768]{1,0:T(8,128)(2,1)S(1)} %collective-permute-done.16.rest_2_), channel_id=1, source_target_pairs={{0,4},{2,6},{4,0},{6,2},{1,5},{3,7},{5,1},{7,3},{8,12},{10,14},{12... | collective-permute-start | bytes 589832 | tf_op jit(solution)/shard_map/ppermute | solution.py:56
  61.3 7.5 %collective-permute-start.23 = (bf16[128,768]{1,0:T(8,128)(2,1)S(1)}, bf16[128,768]{1,0:T(8,128)(2,1)S(1)}, u32[]{:S(2)}, u32[]{:S(2)}) collective-permute-start(bf16[128,768]{1,0:T(8,128)(2,1)S(1)} %collective-permute-done.15.rest_1_), channel_id=1, source_target_pairs={{0,2},{2,0},{4,6},{6,4},{1,3},{3,1},{5,7},{7,5},{8,10},{10,8},{12,... | collective-permute-start | bytes 589832 | tf_op jit(solution)/shard_map/ppermute | solution.py:56
  61.3 8.0 %collective-permute-start.24 = (bf16[128,768]{1,0:T(8,128)(2,1)S(1)}, bf16[128,768]{1,0:T(8,128)(2,1)S(1)}, u32[]{:S(2)}, u32[]{:S(2)}) collective-permute-start(bf16[128,768]{1,0:T(8,128)(2,1)S(1)} %collective-permute-done.16.rest_2_), channel_id=1, source_target_pairs={{0,2},{2,0},{4,6},{6,4},{1,3},{3,1},{5,7},{7,5},{8,10},{10,8},{12,... | collective-permute-start | bytes 589832 | tf_op jit(solution)/shard_map/ppermute | solution.py:56
  61.8 9.7 %collective-permute-start.21 = (bf16[128,768]{1,0:T(8,128)(2,1)S(1)}, bf16[128,768]{1,0:T(8,128)(2,1)S(1)}, u32[]{:S(2)}, u32[]{:S(2)}) collective-permute-start(bf16[128,768]{1,0:T(8,128)(2,1)S(1)} %collective-permute-done.17.rest_3_), channel_id=1, source_target_pairs={{0,4},{2,6},{4,0},{6,2},{1,5},{3,7},{5,1},{7,3},{8,12},{10,14},{12... | collective-permute-start | bytes 589832 | tf_op jit(solution)/shard_map/ppermute | solution.py:56
  71.5 10.5 %collective-permute-start.35 = (bf16[48,1792]{1,0:T(8,128)(2,1)S(1)}, bf16[48,1792]{1,0:T(8,128)(2,1)}, u32[]{:S(2)}, u32[]{:S(2)}) collective-permute-start(bf16[48,1792]{1,0:T(8,128)(2,1)S(1)} %collective-permute-done.31.rest_1_), channel_id=1, source_target_pairs={{0,4},{2,6},{4,0},{6,2},{1,5},{3,7},{5,1},{7,3},{8,12},{10,14},{12... | collective-permute-start | bytes 516104 | tf_op jit(solution)/shard_map/ppermute | solution.py:56
  72.9 10.7 %collective-permute-start.40 = (bf16[48,1792]{1,0:T(8,128)(2,1)S(1)}, bf16[48,1792]{1,0:T(8,128)(2,1)}, u32[]{:S(2)}, u32[]{:S(2)}) collective-permute-start(bf16[48,1792]{1,0:T(8,128)(2,1)S(1)} %collective-permute-done.32.rest_2_), channel_id=1, source_target_pairs={{0,2},{2,0},{4,6},{6,4},{1,3},{3,1},{5,7},{7,5},{8,10},{10,8},{12,... | collective-permute-start | bytes 516104 | tf_op jit(solution)/shard_map/ppermute | solution.py:56
  73.1 10.5 %collective-permute-start.39 = (bf16[48,1792]{1,0:T(8,128)(2,1)S(1)}, bf16[48,1792]{1,0:T(8,128)(2,1)}, u32[]{:S(2)}, u32[]{:S(2)}) collective-permute-start(bf16[48,1792]{1,0:T(8,128)(2,1)S(1)} %collective-permute-done.31.rest_1_), channel_id=1, source_target_pairs={{0,2},{2,0},{4,6},{6,4},{1,3},{3,1},{5,7},{7,5},{8,10},{10,8},{12,... | collective-permute-start | bytes 516104 | tf_op jit(solution)/shard_map/ppermute | solution.py:56
  73.4 10.7 %collective-permute-start.42 = (bf16[48,1792]{1,0:T(8,128)(2,1)}, bf16[48,1792]{1,0:T(8,128)(2,1)}, u32[]{:S(2)}, u32[]{:S(2)}) collective-permute-start(bf16[48,1792]{1,0:T(8,128)(2,1)} %collective-permute-done.34.rest_4_), channel_id=1, source_target_pairs={{0,2},{2,0},{4,6},{6,4},{1,3},{3,1},{5,7},{7,5},{8,10},{10,8},{12,... | collective-permute-start | bytes 516104 | tf_op jit(solution)/shard_map/ppermute | solution.py:56
  73.6 10.6 %collective-permute-start.37 = (bf16[48,1792]{1,0:T(8,128)(2,1)}, bf16[48,1792]{1,0:T(8,128)(2,1)}, u32[]{:S(2)}, u32[]{:S(2)}) collective-permute-start(bf16[48,1792]{1,0:T(8,128)(2,1)} %collective-permute-done.33.rest_3_), channel_id=1, source_target_pairs={{0,4},{2,6},{4,0},{6,2},{1,5},{3,7},{5,1},{7,3},{8,12},{10,14},{12... | collective-permute-start | bytes 516104 | tf_op jit(solution)/shard_map/ppermute | solution.py:56
  117.0 41.8 %collective-permute-start.65 = (bf16[384,1792]{1,0:T(8,128)(2,1)}, bf16[384,1792]{1,0:T(8,128)(2,1)S(1)}, u32[]{:S(2)}, u32[]{:S(2)}) collective-permute-start(bf16[384,1792]{1,0:T(8,128)(2,1)} %get-tuple-element.102), channel_id=1, source_target_pairs={{0,2},{2,0},{4,6},{6,4},{1,3},{3,1},{5,7},{7,5},{8,10},{10,8},{12,... | collective-permute-start | bytes 4128776 | tf_op jit(solution)/shard_map/ppermute | solution.py:56
  121.7 8.0 %collective-permute-start.53 = (bf16[128,768]{1,0:T(8,128)(2,1)}, bf16[128,768]{1,0:T(8,128)(2,1)S(1)}, u32[]{:S(2)}, u32[]{:S(2)}) collective-permute-start(bf16[128,768]{1,0:T(8,128)(2,1)} %get-tuple-element.86), channel_id=1, source_target_pairs={{0,4},{2,6},{4,0},{6,2},{1,5},{3,7},{5,1},{7,3},{8,12},{10,14},{12... | collective-permute-start | bytes 589832 | tf_op jit(solution)/shard_map/ppermute | solution.py:56
  122.8 18.0 %collective-permute-start.52 = (bf16[128,768]{1,0:T(8,128)(2,1)}, bf16[128,768]{1,0:T(8,128)(2,1)S(1)}, u32[]{:S(2)}, u32[]{:S(2)}) collective-permute-start(bf16[128,768]{1,0:T(8,128)(2,1)} %get-tuple-element.84), channel_id=1, source_target_pairs={{0,4},{2,6},{4,0},{6,2},{1,5},{3,7},{5,1},{7,3},{8,12},{10,14},{12... | collective-permute-start | bytes 589832 | tf_op jit(solution)/shard_map/ppermute | solution.py:56
  123.7 14.4 %collective-permute-start.50 = (bf16[128,768]{1,0:T(8,128)(2,1)}, bf16[128,768]{1,0:T(8,128)(2,1)S(1)}, u32[]{:S(2)}, u32[]{:S(2)}) collective-permute-start(bf16[128,768]{1,0:T(8,128)(2,1)} %get-tuple-element.82), channel_id=1, source_target_pairs={{0,4},{2,6},{4,0},{6,2},{1,5},{3,7},{5,1},{7,3},{8,12},{10,14},{12... | collective-permute-start | bytes 589832 | tf_op jit(solution)/shard_map/ppermute | solution.py:56
  124.8 17.0 %collective-permute-start.49 = (bf16[128,768]{1,0:T(8,128)(2,1)}, bf16[128,768]{1,0:T(8,128)(2,1)S(1)}, u32[]{:S(2)}, u32[]{:S(2)}) collective-permute-start(bf16[128,768]{1,0:T(8,128)(2,1)} %get-tuple-element.80), channel_id=1, source_target_pairs={{0,4},{2,6},{4,0},{6,2},{1,5},{3,7},{5,1},{7,3},{8,12},{10,14},{12... | collective-permute-start | bytes 589832 | tf_op jit(solution)/shard_map/ppermute | solution.py:56
  130.7 10.1 %collective-permute-start.54 = (bf16[128,768]{1,0:T(8,128)(2,1)S(1)}, bf16[128,768]{1,0:T(8,128)(2,1)S(1)}, u32[]{:S(2)}, u32[]{:S(2)}) collective-permute-start(bf16[128,768]{1,0:T(8,128)(2,1)S(1)} %add_convert_fusion.1), channel_id=1, source_target_pairs={{0,8},{8,0},{16,24},{24,16},{1,9},{9,1},{17,25},{25,17},{2,10},{10... | collective-permute-start | bytes 589832 | tf_op jit(solution)/shard_map/ppermute | solution.py:56
  141.8 9.8 %collective-permute-start.55 = (bf16[128,768]{1,0:T(8,128)(2,1)S(1)}, bf16[128,768]{1,0:T(8,128)(2,1)S(1)}, u32[]{:S(2)}, u32[]{:S(2)}) collective-permute-start(bf16[128,768]{1,0:T(8,128)(2,1)S(1)} %add_convert_fusion), channel_id=1, source_target_pairs={{0,16},{8,24},{16,0},{24,8},{1,17},{9,25},{17,1},{25,9},{2,18},{10... | collective-permute-start | bytes 589832 | tf_op jit(solution)/shard_map/ppermute | solution.py:56
  158.7 19.9 %collective-permute-start.57 = (bf16[384,1536]{1,0:T(8,128)(2,1)}, bf16[384,1536]{1,0:T(8,128)(2,1)S(1)}, u32[]{:S(2)}, u32[]{:S(2)}) collective-permute-start(bf16[384,1536]{1,0:T(8,128)(2,1)} %get-tuple-element.89), channel_id=1, source_target_pairs={{0,2},{2,0},{4,6},{6,4},{1,3},{3,1},{5,7},{7,5},{8,10},{10,8},{12,... | collective-permute-start | bytes 3538952 | tf_op jit(solution)/shard_map/ppermute | solution.py:56
  162.8 7.5 %collective-permute-start.70 = (bf16[48,1792]{1,0:T(8,128)(2,1)}, bf16[48,1792]{1,0:T(8,128)(2,1)S(1)}, u32[]{:S(2)}, u32[]{:S(2)}) collective-permute-start(bf16[48,1792]{1,0:T(8,128)(2,1)} %get-tuple-element.110), channel_id=1, source_target_pairs={{0,4},{2,6},{4,0},{6,2},{1,5},{3,7},{5,1},{7,3},{8,12},{10,14},{12... | collective-permute-start | bytes 516104 | tf_op jit(solution)/shard_map/ppermute | solution.py:56
  163.9 53.7 %collective-permute-start.46 = (bf16[128,768]{1,0:T(8,128)(2,1)S(1)}, bf16[128,768]{1,0:T(8,128)(2,1)S(1)}, u32[]{:S(2)}, u32[]{:S(2)}) collective-permute-start(bf16[128,768]{1,0:T(8,128)(2,1)S(1)} %copy-done.40), channel_id=1, source_target_pairs={{0,1},{1,0},{2,3},{3,2},{4,5},{5,4},{6,7},{7,6},{8,9},{9,8},{10,11... | collective-permute-start | bytes 589832 | tf_op jit(solution)/shard_map/ppermute | solution.py:56
  165.4 18.0 %collective-permute-start.69 = (bf16[48,1792]{1,0:T(8,128)(2,1)}, bf16[48,1792]{1,0:T(8,128)(2,1)S(1)}, u32[]{:S(2)}, u32[]{:S(2)}) collective-permute-start(bf16[48,1792]{1,0:T(8,128)(2,1)} %get-tuple-element.108), channel_id=1, source_target_pairs={{0,4},{2,6},{4,0},{6,2},{1,5},{3,7},{5,1},{7,3},{8,12},{10,14},{12... | collective-permute-start | bytes 516104 | tf_op jit(solution)/shard_map/ppermute | solution.py:56
  166.3 11.3 %collective-permute-start.67 = (bf16[48,1792]{1,0:T(8,128)(2,1)}, bf16[48,1792]{1,0:T(8,128)(2,1)S(1)}, u32[]{:S(2)}, u32[]{:S(2)}) collective-permute-start(bf16[48,1792]{1,0:T(8,128)(2,1)} %get-tuple-element.106), channel_id=1, source_target_pairs={{0,4},{2,6},{4,0},{6,2},{1,5},{3,7},{5,1},{7,3},{8,12},{10,14},{12... | collective-permute-start | bytes 516104 | tf_op jit(solution)/shard_map/ppermute | solution.py:56
  170.3 34.6 %collective-permute-start.66 = (bf16[48,1792]{1,0:T(8,128)(2,1)}, bf16[48,1792]{1,0:T(8,128)(2,1)S(1)}, u32[]{:S(2)}, u32[]{:S(2)}) collective-permute-start(bf16[48,1792]{1,0:T(8,128)(2,1)} %get-tuple-element.104), channel_id=1, source_target_pairs={{0,4},{2,6},{4,0},{6,2},{1,5},{3,7},{5,1},{7,3},{8,12},{10,14},{12... | collective-permute-start | bytes 516104 | tf_op jit(solution)/shard_map/ppermute | solution.py:56
  178.7 26.4 %collective-permute-start.68 = (bf16[48,1792]{1,0:T(8,128)(2,1)S(1)}, bf16[48,1792]{1,0:T(8,128)(2,1)S(1)}, u32[]{:S(2)}, u32[]{:S(2)}) collective-permute-start(bf16[48,1792]{1,0:T(8,128)(2,1)S(1)} %add_convert_fusion.5), channel_id=1, source_target_pairs={{0,8},{8,0},{16,24},{24,16},{1,9},{9,1},{17,25},{25,17},{2,10},{10... | collective-permute-start | bytes 516104 | tf_op jit(solution)/shard_map/ppermute | solution.py:56
  185.0 12.8 %collective-permute-start.61 = (bf16[48,1536]{1,0:T(8,128)(2,1)}, bf16[48,1536]{1,0:T(8,128)(2,1)S(1)}, u32[]{:S(2)}, u32[]{:S(2)}) collective-permute-start(bf16[48,1536]{1,0:T(8,128)(2,1)} %get-tuple-element.95), channel_id=1, source_target_pairs={{0,4},{2,6},{4,0},{6,2},{1,5},{3,7},{5,1},{7,3},{8,12},{10,14},{12... | collective-permute-start | bytes 442376 | tf_op jit(solution)/shard_map/ppermute | solution.py:56
  195.3 8.2 %collective-permute-start.63 = (bf16[48,1536]{1,0:T(8,128)(2,1)S(1)}, bf16[48,1536]{1,0:T(8,128)(2,1)S(1)}, u32[]{:S(2)}, u32[]{:S(2)}) collective-permute-start(bf16[48,1536]{1,0:T(8,128)(2,1)S(1)} %add_convert_fusion.7), channel_id=1, source_target_pairs={{0,8},{8,0},{16,24},{24,16},{1,9},{9,1},{17,25},{25,17},{2,10},{10... | collective-permute-start | bytes 442376 | tf_op jit(solution)/shard_map/ppermute | solution.py:56
  197.8 10.9 %collective-permute-start.72 = (bf16[48,1792]{1,0:T(8,128)(2,1)S(1)}, bf16[48,1792]{1,0:T(8,128)(2,1)S(1)}, u32[]{:S(2)}, u32[]{:S(2)}) collective-permute-start(bf16[48,1792]{1,0:T(8,128)(2,1)S(1)} %add_convert_fusion.3), channel_id=1, source_target_pairs={{0,16},{8,24},{16,0},{24,8},{1,17},{9,25},{17,1},{25,9},{2,18},{10... | collective-permute-start | bytes 516104 | tf_op jit(solution)/shard_map/ppermute | solution.py:56
  205.0 7.7 %collective-permute-start.64 = (bf16[48,1536]{1,0:T(8,128)(2,1)S(1)}, bf16[48,1536]{1,0:T(8,128)(2,1)S(1)}, u32[]{:S(2)}, u32[]{:S(2)}) collective-permute-start(bf16[48,1536]{1,0:T(8,128)(2,1)S(1)} %add_convert_fusion.6), channel_id=1, source_target_pairs={{0,16},{8,24},{16,0},{24,8},{1,17},{9,25},{17,1},{25,9},{2,18},{10... | collective-permute-start | bytes 442376 | tf_op jit(solution)/shard_map/ppermute | solution.py:56
  208.7 9.7 %collective-permute-start.56 = (bf16[128,768]{1,0:T(8,128)(2,1)S(1)}, bf16[128,768]{1,0:T(8,128)(2,1)S(1)}, u32[]{:S(2)}, u32[]{:S(2)}) collective-permute-start(bf16[128,768]{1,0:T(8,128)(2,1)S(1)} %copy-done.41), channel_id=1, source_target_pairs={{0,1},{1,0},{2,3},{3,2},{4,5},{5,4},{6,7},{7,6},{8,9},{9,8},{10,11... | collective-permute-start | bytes 589832 | tf_op jit(solution)/shard_map/ppermute | solution.py:56
  216.1 8.2 %collective-permute-start.73 = (f32[2,48]{1,0:T(2,128)}, f32[2,48]{1,0:T(2,128)S(1)}, u32[]{:S(2)}, u32[]{:S(2)}) collective-permute-start(f32[2,48]{1,0:T(2,128)} %get-tuple-element.112.a_ref), channel_id=1, source_target_pairs={{0,1},{1,0},{2,3},{3,2},{4,5},{5,4},{6,7},{7,6},{8,9},{9,8},{10,11... | collective-permute-start | bytes 1160 | tf_op jit(solution)/shard_map/ppermute | solution.py:56
  (86 other events, 670.7 us)

commit v3 on v2

--- a/solution.py
+++ b/solution.py
@@ -87,19 +87,23 @@
         out[...] = (keep[at, :].astype(F32) + recv[at, :].astype(F32)).astype(BF16)
 
 
-def scatter_sum(parts):
-    if not staged():
-        return [lax.psum_scatter(parts[0], TOKENS_AX, scatter_dimension=0, tiled=True)]
-    keep, send = parts
+def pair_sum(keep, send):
     rows, cols = keep.shape[0] // 8, keep.shape[1]
     recv = swap(send, "shard", 1)
-    s = pl.pallas_call(
+    return pl.pallas_call(
         add_kernel,
         out_shape=[sds((rows, cols), BF16)] * 8,
         in_specs=[VM, VM],
         out_specs=[VM] * 8,
         name="pair_add",
     )(keep, recv)
+
+
+def native_sum(part):
+    return [lax.psum_scatter(part, TOKENS_AX, scatter_dimension=0, tiled=True)]
+
+
+def scatter_sum(s):
     got = {z: swap(s[4 + z], "shard", 2) for z in (3, 2, 1, 0)}
 
     def block(z, *more):
@@ -206,7 +210,7 @@
 
 def qkv_kernel(n, order_ref, x_ref, cos_ref, sin_ref, *rest):
     chunks = rest[:n]
-    a_ref, q_ref, kv_ref, g_ref, w, sems = rest[n:]
+    at_ref, q_ref, kv_ref, g_ref, w, sems = rest[n:]
     width = q_ref.shape[1]
     copies = weight_copies(order_ref, chunks, w, sems)
     xhat, _ = norm_parts(x_ref[...])
@@ -218,7 +222,7 @@
     g = dot_nt(pick, w[:, 4 * width : 4 * width + 128])
     g_ref[...] = g
     a = (xhat * g[0:1, :]).astype(BF16)
-    a_ref[...] = a
+    at_ref[...] = jnp.transpose(a)
     cos = wide(cos_ref[...], width)
     sin = wide(sin_ref[...], width)
     q_ref[...] = rope(dot_nn(a, w[:, :width]), cos, sin).astype(BF16)
@@ -327,14 +331,19 @@
     emit_blocks(order_ref, acc, outs)
 
 
-def attend_back_kernel(
-    n, nw, no, blocks, order_ref, q_ref, attn_ref, lse_ref, hid_ref, cot_ref, g_ref,
-    da_ref, db_ref, cos_ref, sin_ref, *rest
+def back_tile(k, v, qm, dom, lse_row, dot_row):
+    prob = jnp.exp(dot_nt(k, qm) - lse_row)
+    ds = (prob * (dot_nt(v, dom) - dot_row)).astype(BF16)
+    return dot_nn(ds, qm), dot_nn(prob.astype(BF16), dom), dot_tn(ds, k)
+
+
+def back_kernel(
+    n, nw, blocks, order_ref, q_ref, attn_ref, lse_ref, hid_ref, cot_ref, g_ref,
+    da_ref, db_ref, *rest
 ):
     keys = rest[:n]
     wos = rest[n : n + nw]
-    outs = rest[n + nw : n + nw + no]
-    dhid_ref, dqp_ref, kv, wo, dq_s, qm_s, dom_s, row_s, ksem, wsem = rest[n + nw + no :]
+    out_ref, dhid_ref, dq_ref, qm_ref, dom_ref, row_ref, kv, wo, ksem, wsem = rest[n + nw :]
     width = q_ref.shape[1]
     pairs = width // 128
     wcopies = weight_copies(order_ref, wos, wo, wsem, (3 * width, width))
@@ -348,72 +357,121 @@
     dattn = dot_nn(dhid.astype(BF16), wo[...]).astype(BF16)
     for p in range(pairs):
         at = slice(p * 128, p * 128 + 128)
-        qm_s[p] = two_heads(q_ref[:, at]) * jnp.asarray(SCALE, BF16)
+        qm_ref[p] = two_heads(q_ref[:, at]) * jnp.asarray(SCALE, BF16)
         dom = two_heads(dattn[:, at])
-        dom_s[p] = dom
+        dom_ref[p] = dom
         both = jnp.concatenate([attn_ref[:, at]] * 2, axis=0)
         dots = jnp.sum(dom.astype(F32) * both.astype(F32), axis=1, keepdims=True)
-        row_s[p : p + 1, :] = as_row(dots)
-    dq_s[...] = jnp.zeros(dq_s.shape, F32)
-    halves = len(outs)
+        row_ref[p : p + 1, :] = as_row(dots)
+    dq_ref[...] = jnp.zeros(dq_ref.shape, F32)
     block_rows = kv.shape[0]
 
     def block_work(block):
         for copy in first or key_copies(keys, kv, ksem, block):
             copy.wait()
-        for half in range(halves):
-            count = block_rows // halves // SUB_ROWS
-
-            def sub_work(sub):
-                src = pl.ds(
-                    pl.multiple_of(half * (block_rows // halves) + sub * SUB_ROWS, SUB_ROWS),
-                    SUB_ROWS,
+
+        def sub_work(sub):
+            src = pl.ds(pl.multiple_of(sub * SUB_ROWS, SUB_ROWS), SUB_ROWS)
+            dst = pl.ds(pl.multiple_of(block * block_rows + sub * SUB_ROWS, SUB_ROWS), SUB_ROWS)
+            for p in range(pairs):
+                at = slice(p * 128, p * 128 + 128)
+                vat = slice(width + p * 128, width + p * 128 + 128)
+                dk, dv, dq = back_tile(
+                    kv[src, at], kv[src, vat], qm_ref[p], dom_ref[p],
+                    lse_ref[p : p + 1, :], row_ref[p : p + 1, :],
                 )
-                dst = pl.ds(
-                    pl.multiple_of(block * block_rows + sub * SUB_ROWS, SUB_ROWS), SUB_ROWS
+                out_ref[dst, at] = dk.astype(BF16)
+                out_ref[dst, vat] = dv.astype(BF16)
+                dq_ref[p] += dq
+
+        each(block_rows // SUB_ROWS, sub_work)
+
+    each(blocks, block_work)
+
+
+def back_rest_kernel(n, lse_ref, dq_ref, qm_ref, dom_ref, row_ref, cos_ref, sin_ref, *rest):
+    if n:
+        keys, recv = rest[:n], rest[n]
+        sums = rest[n + 1 : 2 * n + 1]
+        dqp_ref, kv, ksem = rest[2 * n + 1 :]
+        copies = key_copies(keys, kv, ksem, 0)
+        each_rows = sums[0].shape[0]
+    else:
+        (dqp_ref,) = rest
+    width = dqp_ref.shape[1]
+    pairs = width // 128
+    dq = [dq_ref[p] for p in range(pairs)]
+    if n:
+        for copy in copies:
+            copy.wait()
+        per = SUB_ROWS // each_rows
+        for sub in range(kv.shape[0] // SUB_ROWS):
+            src = pl.ds(sub * SUB_ROWS, SUB_ROWS)
+            for p in range(pairs):
+                at = slice(p * 128, p * 128 + 128)
+                vat = slice(width + p * 128, width + p * 128 + 128)
+                dk, dv, more = back_tile(
+                    kv[src, at], kv[src, vat], qm_ref[p], dom_ref[p],
+                    lse_ref[p : p + 1, :], row_ref[p : p + 1, :],
                 )
-                for p in range(pairs):
-                    at = slice(p * 128, p * 128 + 128)
-                    vat = slice(width + p * 128, width + p * 128 + 128)
-                    k = kv[src, at]
-                    prob = jnp.exp(dot_nt(k, qm_s[p]) - lse_ref[p : p + 1, :])
-                    dprob = dot_nt(kv[src, vat], dom_s[p])
-                    ds = (prob * (dprob - row_s[p : p + 1, :])).astype(BF16)
-                    outs[half][dst, at] = dot_nn(ds, qm_s[p]).astype(BF16)
-                    outs[half][dst, vat] = dot_nn(prob.astype(BF16), dom_s[p]).astype(BF16)
-                    dq_s[p] += dot_tn(ds, k)
-
-            each(count, sub_work)
-
-    each(blocks, block_work)
-    dq = jnp.concatenate([join_heads(dq_s[p]) for p in range(pairs)], axis=1) * SCALE
+                dq[p] += more
+                dk = dk + recv[src, at].astype(F32)
+                dv = dv + recv[src, vat].astype(F32)
+                for i in range(per):
+                    part = slice(i * each_rows, (i + 1) * each_rows)
+                    sums[sub * per + i][:, at] = dk[part].astype(BF16)
+                    sums[sub * per + i][:, vat] = dv[part].astype(BF16)
+    dq = jnp.concatenate([join_heads(x) for x in dq], axis=1) * SCALE
     dqp_ref[...] = rope_back(
         dq, wide(cos_ref[...], width), wide(sin_ref[...], width)
     ).astype(BF16)
 
 
+def pick_rows(order_ref, ref, blocks, rows):
+    return jnp.concatenate(
+        [ref[pl.ds(pl.multiple_of((order_ref[0] ^ j) * rows, 16), rows), :] for j in blocks], axis=0
+    )
+
+
 def qkv_grad_kernel(
-    n, nt, no, order_ref, a_ref, dqp_ref, dhid_ref, attn_ref, cos_ref, sin_ref, *rest
+    n, nt, order_ref, at_ref, dqp_ref, dhid_ref, attn_ref, cos_ref, sin_ref, *rest
 ):
     terms = rest[:nt]
     chunks = rest[nt : nt + n]
-    outs = rest[nt + n : nt + n + no]
-    da_ref, w, acc, sems = rest[nt + n + no :]
+    out_ref, da_ref, d_ref, ht_ref, w, sems = rest[nt + n :]
     width = dqp_ref.shape[1]
-    copies = weight_copies(order_ref, chunks, w, sems)
-    dkv = terms[0][...].astype(F32)
-    for term in terms[1:]:
-        dkv = dkv + term[...].astype(F32)
+    copies = weight_copies(order_ref, chunks, w, sems, (0, 3 * width))
+    dkv = total([term[...] for term in terms])
     dkp = rope_back(
         dkv[:, :width], wide(cos_ref[...], width), wide(sin_ref[...], width)
     ).astype(BF16)
     d = jnp.concatenate([dqp_ref[...], dkp, dkv[:, width:].astype(BF16)], axis=1)
+    d_ref[...] = d
+    ht_ref[...] = jnp.transpose(dhid_ref[...].astype(BF16))
+    if n == 1:
+        a_t, h_t = at_ref[...], ht_ref[...]
+    else:
+        rows = at_ref.shape[0] // 16
+        a_t = pick_rows(order_ref, at_ref, chunk_order()[8:], rows)
+        h_t = pick_rows(order_ref, ht_ref, chunk_order()[8:], rows)
+    out_ref[:, : 3 * width] = dot_nn(a_t, d).astype(BF16)
+    out_ref[:, 3 * width :] = dot_nn(h_t, attn_ref[...]).astype(BF16)
     for copy in copies:
         copy.wait()
-    da_ref[...] = dot_nt(d, w[:, : 3 * width]).astype(BF16)
-    acc[:, : 3 * width] = dot_tn(a_ref[...], d)
-    acc[:, 3 * width :] = dot_tn(dhid_ref[...].astype(BF16), attn_ref[...])
-    emit_blocks(order_ref, acc, outs)
+    da_ref[...] = dot_nt(d, w[...]).astype(BF16)
+
+
+def qkv_grad_rest_kernel(order_ref, at_ref, ht_ref, d_ref, attn_ref, recv, *sums):
+    cut = d_ref.shape[1]
+    rows = at_ref.shape[0] // 16
+    a_t = pick_rows(order_ref, at_ref, chunk_order()[:8], rows)
+    h_t = pick_rows(order_ref, ht_ref, chunk_order()[:8], rows)
+    one = dot_nn(a_t, d_ref[...]) + recv[:, :cut].astype(F32)
+    two = dot_nn(h_t, attn_ref[...]) + recv[:, cut:].astype(F32)
+    for i, out in enumerate(sums):
+        part = slice(i * rows, (i + 1) * rows)
+        out[:, :cut] = one[part].astype(BF16)
+        out[:, cut:] = two[part].astype(BF16)
 
 
 def call(kernel, out_shape, specs, scratch, args):
@@ -514,9 +572,9 @@
     wsem = pltpu.SemaphoreType.DMA((nw,))
     halves = 2 if staged() else 1
 
-    a, q, kv, g = call(
+    a_t, q, kv, g = call(
         partial(qkv_kernel, nw),
-        [sds((toks, d), BF16), sds((toks, width), BF16), sds((toks, 2 * width), BF16), sds((8, d), F32)],
+        [sds((d, toks), BF16), sds((toks, width), BF16), sds((toks, 2 * width), BF16), sds((8, d), F32)],
         [SM, VM, VM, VM] + [ANY] * nw,
         [pltpu.VMEM((d, wq_cols), BF16), wsem],
         [order, inputs, cos, sin] + first_chunks,
@@ -569,42 +627,85 @@
         [pltpu.VMEM((d, rest_cols), F32)],
         [order, b, dz, cotangent, mixed],
     )
-    ffn_terms = scatter_sum(ffn_grads)
-
-    back = call(
-        partial(attend_back_kernel, nk, nw, halves, blocks),
-        [sds((seq // halves, 2 * width), BF16)] * halves
-        + [sds((toks, d), F32), sds((toks, width), BF16)],
-        [SM] + [VM] * 10 + [ANY] * (nk + nw),
+    if staged():
+        ffn_sums = pair_sum(*ffn_grads)
+    else:
+        ffn_terms = native_sum(*ffn_grads)
+
+    first_half = nk // 2 if staged() else 0
+    part_rows = block_rows // halves
+    part_sem = pltpu.SemaphoreType.DMA((nk - first_half,))
+    both = (pairs, 2 * toks, 128)
+    kv_part, dhid, dq, qm, dom, dots = call(
+        partial(back_kernel, nk - first_half, nw, blocks),
         [
-            pltpu.VMEM((block_rows, 2 * width), BF16),
+            sds((seq // halves, 2 * width), BF16),
+            sds((toks, d), F32),
+            sds(both, F32),
+            sds(both, BF16),
+            sds(both, BF16),
+            sds((8, 2 * toks), F32),
+        ],
+        [SM] + [VM] * 8 + [ANY] * (nk - first_half + nw),
+        [
+            pltpu.VMEM((part_rows, 2 * width), BF16),
             pltpu.VMEM((d, width), BF16),
-            pltpu.VMEM((pairs, 2 * toks, 128), F32),
-            pltpu.VMEM((pairs, 2 * toks, 128), BF16),
-            pltpu.VMEM((pairs, 2 * toks, 128), BF16),
-            pltpu.VMEM((8, 2 * toks), F32),
-            ksem,
+            part_sem,
             wsem,
         ],
-        [order, q, attn, lse, hidden, cotangent, g, db_part, db_other, cos, sin] + keys + first_chunks,
-    )
-    dhid, dqp = back[halves:]
-    kv_terms = scatter_sum(back[:halves])
+        [order, q, attn, lse, hidden, cotangent, g, db_part, db_other]
+        + keys[first_half:]
+        + first_chunks,
+    )
+    rest_args = [lse, dq, qm, dom, dots, cos, sin]
+    if staged():
+        *kv_sums, dqp = call(
+            partial(back_rest_kernel, first_half),
+            [sds((toks, 2 * width), BF16)] * first_half + [sds((toks, width), BF16)],
+            [VM] * 7 + [ANY] * first_half + [VM],
+            [pltpu.VMEM((part_rows, 2 * width), BF16), part_sem],
+            rest_args + keys[:first_half] + [swap(kv_part, "shard", 1)],
+        )
+        kv_terms = scatter_sum(kv_sums)
+        ffn_terms = scatter_sum(ffn_sums)
+    else:
+        (dqp,) = call(
+            partial(back_rest_kernel, 0), [sds((toks, width), BF16)], [VM] * 7, [], rest_args
+        )
+        kv_terms = native_sum(kv_part)
     nt = len(kv_terms)
-    grads = call(
-        partial(qkv_grad_kernel, nw, nt, halves),
-        [sds((d // halves, 4 * width), BF16)] * halves + [sds((toks, d), BF16)],
+    w_part, da_part, d_qkv, h_t = call(
+        partial(qkv_grad_kernel, nw, nt),
+        [
+            sds((d // halves, 4 * width), BF16),
+            sds((toks, d), BF16),
+            sds((toks, 3 * width), BF16),
+            sds((d, toks), BF16),
+        ],
         [SM] + [VM] * 6 + [VM] * nt + [ANY] * nw,
-        [pltpu.VMEM((d, wq_cols), BF16), pltpu.VMEM((d, 4 * width), F32), wsem],
-        [order, a, dqp, dhid, attn, cos, sin] + kv_terms + first_chunks,
-    )
-    da_part = grads[halves]
+        [pltpu.VMEM((d, 3 * width), BF16), wsem],
+        [order, a_t, dqp, dhid, attn, cos, sin] + kv_terms + first_chunks,
+    )
     da_other = head_swap(da_part)
     (input_grad,) = call(
-        lnback_kernel, [sds((toks, d), F32)], [VM] * 5, [], [inputs, da_part, da_other, dhid, g]
-    )
-
-    first_terms = scatter_sum(grads[:halves])
+        lnback_kernel,
+        [sds((toks, d), F32)],
+        [VM] * 5,
+        [],
+        [inputs, da_part, da_other, dhid, g],
+    )
+
+    if staged():
+        first_sums = call(
+            qkv_grad_rest_kernel,
+            [sds((rows, 4 * width), BF16)] * 8,
+            [SM] + [VM] * 5,
+            [],
+            [order, a_t, h_t, d_qkv, attn, swap(w_part, "shard", 1)],
+        )
+        first_terms = scatter_sum(first_sums)
+    else:
+        first_terms = native_sum(w_part)
     full = weights.shape
     weight_grad, gain_part = call(
         partial(gsum_kernel, nt, width, units),

time: 227 us -> 244 us (1.075)
  waiting for transfers between devices: 87.8 us -> 109 us
  starting transfers between devices: 63.2 us -> 58.1 us
    ppermute x74, waiting for transfers between devices: 87.8 us -> 109 us  [swap(): return lax.ppermute(x, axis, [(i, i ^ bits) for i in range(size)])]
    pallas_call x9 -> x11, Pallas kernels: 44.4 us -> 50.4 us  [call(): pl.pallas_call(kernel, out_shape=out_shape, in_specs=specs, out_specs=jax...]
    pallas_call x3 -> x1, Pallas kernels: 8.63 us -> 2.9 us  [pair_sum(): pl.pallas_call(add_kernel, out_shape=[sds((rows, cols), BF16)] * 8, in_sp...]
    ppermute x74, starting transfers between devices: 63.2 us -> 58.1 us  [swap(): return lax.ppermute(x, axis, [(i, i ^ bits) for i in range(size)])]
    unnamed x120 -> x122, local copies, waits for them, and re-layouts: 6.92 us -> 7.5 us
  transfers between devices with their start and end apart: 74 -> 74, of which waited for: 30 -> 32; matrix products, arithmetic and copies ran while one was open for 4% -> 4% of each run, Pallas kernels for 17% -> 17%
where the time goes in v3:
time: 244 us; the launch traced here: 243 us
  waiting for transfers between devices  109 us (45%)
  starting transfers between devices  58.1 us (24%)
  Pallas kernels  56.2 us (23%)
  other arithmetic  10.7 us (4%)
  local copies, waits for them, and re-layouts  7.65 us (3%)
    ppermute x74, waiting for transfers between devices, swap(): return lax.ppermute(x, axis, [(i, i ^ bits) for i in range(size)])  109 us
    ppermute x74, starting transfers between devices, swap(): return lax.ppermute(x, axis, [(i, i ^ bits) for i in range(size)])  58.1 us
    pallas_call x11, Pallas kernels, call(): pl.pallas_call(kernel, out_shape=out_shape, in_specs=specs, out_specs=jax...  50.4 us
    unnamed x122, local copies, waits for them, and re-layouts  7.5 us
    convert_element_type x9, other arithmetic, block(): return total([s[z], got[z], *more]).astype(BF16)  6.99 us
  transfers between devices with their start and end apart: 74, of which 32 were waited for; matrix products, arithmetic and copies ran while one was open for 4% of the time, Pallas kernels for 17%

profile of v3, /device:TPU:0, one launch (start us, length us, event | category | flops | bytes accessed | tf_op | source)
XLA Modules:
  0.0 243.1 jit_solution(16330769713442477718)
XLA Ops:
  2.6 3.0 %collective-permute-start.3 = (bf16[48,1664]{1,0:T(8,128)(2,1)S(1)}, bf16[48,1664]{1,0:T(8,128)(2,1)S(1)}, u32[]{:S(2)}, u32[]{:S(2)}) collective-permute-start(bf16[48,1664]{1,0:T(8,128)(2,1)S(1)} %fusion.1.rest_0_.rest_16_.rest_8_.rest_4_), channel_id=1, source_target_pairs={{0,4},{2,6},{4,0},{6,2},{1,5},{3,7},{5,1},{7,3},{8,12},{10,14},{12... | collective-permute-start | bytes 479240 | tf_op jit(solution)/shard_map/ppermute | solution.py:56
  5.6 2.6 %collective-permute-start.1 = (bf16[48,1664]{1,0:T(8,128)(2,1)S(1)}, bf16[48,1664]{1,0:T(8,128)(2,1)S(1)}, u32[]{:S(2)}, u32[]{:S(2)}) collective-permute-start(bf16[48,1664]{1,0:T(8,128)(2,1)S(1)} %fusion.1.rest_0_.rest_16_.rest_8_.rest_4_), channel_id=1, source_target_pairs={{0,16},{8,24},{16,0},{24,8},{1,17},{9,25},{17,1},{25,9},{2,18},{10... | collective-permute-start | bytes 479240 | tf_op jit(solution)/shard_map/ppermute | solution.py:56
  8.2 1.6 collective-permute-start
  10.0 5.6 %collective-permute-done.1.rest_2_.rest_18_.rest_10_.rest_6_ = bf16[48,1664]{1,0:T(8,128)(2,1)S(1)} collective-permute-done((bf16[48,1664]{1,0:T(8,128)(2,1)S(1)}, bf16[48,1664]{1,0:T(8,128)(2,1)S(1)}, u32[]{:S(2)}, u32[]{:S(2)}) %collective-permute-start.1) | collective-permute-done | bytes 159776 | tf_op jit(solution)/shard_map/ppermute | solution.py:56
  18.5 2.4 collective-permute-done.2.rest_3_.rest_19_.rest_11_.rest_7_
  21.5 1.6 collective-permute-start.34
  23.8 2.9 %collective-permute-done.4.rest_5_.rest_21_.rest_13_.rest_9_ = bf16[48,1664]{1,0:T(8,128)(2,1)S(1)} collective-permute-done((bf16[48,1664]{1,0:T(8,128)(2,1)S(1)}, bf16[48,1664]{1,0:T(8,128)(2,1)S(1)}, u32[]{:S(2)}, u32[]{:S(2)}) %collective-permute-start.4) | collective-permute-done | bytes 159776 | tf_op jit(solution)/shard_map/ppermute | solution.py:56
  26.7 3.4 %collective-permute-done.6.rest_7_.rest_23_.rest_15_.rest_11_ = bf16[48,1664]{1,0:T(8,128)(2,1)S(1)} collective-permute-done((bf16[48,1664]{1,0:T(8,128)(2,1)S(1)}, bf16[48,1664]{1,0:T(8,128)(2,1)S(1)}, u32[]{:S(2)}, u32[]{:S(2)}) %collective-permute-start.6) | collective-permute-done | bytes 159776 | tf_op jit(solution)/shard_map/ppermute | solution.py:56
  32.2 4.3 %shard_map.159 = (bf16[768,128]{1,0:T(8,128)(2,1)}, bf16[128,384]{1,0:T(8,128)(2,1)}, bf16[128,768]{1,0:T(8,128)(2,1)}, f32[8,768]{1,0:T(8,128)}) custom-call(s32[1]{0:T(128)} %bitcast.order_ref, f32[128,768]{1,0:T(8,128)} %x_ref.5, f32[128,128]{1,0:T(8,128)} %get-tuple-element.129.cos_ref, f32[128,128]{1,0:T(8,128)} %get-tuple-element.128.sin_ref, ...), custom_call_target="tpu_custom_call" | custom-call | tf_op jit(solution)/shard_map/pallas_call | solution.py:478
  36.5 3.5 %collective-permute-start.16 = (bf16[128,768]{1,0:T(8,128)(2,1)}, bf16[128,768]{1,0:T(8,128)(2,1)S(1)}, u32[]{:S(2)}, u32[]{:S(2)}) collective-permute-start(bf16[128,768]{1,0:T(8,128)(2,1)} %get-tuple-element.70.rest_0_), channel_id=1, source_target_pairs={{0,16},{8,24},{16,0},{24,8},{1,17},{9,25},{17,1},{25,9},{2,18},{10... | collective-permute-start | bytes 589832 | tf_op jit(solution)/shard_map/ppermute | solution.py:56
  41.9 15.4 %collective-permute-done.32.rest_2_ = bf16[48,1792]{1,0:T(8,128)(2,1)} collective-permute-done((bf16[48,1792]{1,0:T(8,128)(2,1)S(1)}, bf16[48,1792]{1,0:T(8,128)(2,1)}, u32[]{:S(2)}, u32[]{:S(2)}) %collective-permute-start.32) | collective-permute-done | bytes 172064 | tf_op jit(solution)/shard_map/ppermute | solution.py:56
  57.4 2.0 collective-permute-start.17
  60.0 12.8 %collective-permute-done.33.rest_3_ = bf16[48,1792]{1,0:T(8,128)(2,1)} collective-permute-done((bf16[48,1792]{1,0:T(8,128)(2,1)}, bf16[48,1792]{1,0:T(8,128)(2,1)}, u32[]{:S(2)}, u32[]{:S(2)}) %collective-permute-start.33) | collective-permute-done | bytes 172064 | tf_op jit(solution)/shard_map/ppermute | solution.py:56
  73.4 1.6 collective-permute-start.19
  75.6 5.1 %collective-permute-done.20.rest_6_ = bf16[128,768]{1,0:T(8,128)(2,1)S(1)} collective-permute-done((bf16[128,768]{1,0:T(8,128)(2,1)S(1)}, bf16[128,768]{1,0:T(8,128)(2,1)S(1)}, u32[]{:S(2)}, u32[]{:S(2)}) %collective-permute-start.20) | collective-permute-done | bytes 196640 | tf_op jit(solution)/shard_map/ppermute | solution.py:56
  81.2 3.7 %collective-permute-done.19.rest_5_ = bf16[128,768]{1,0:T(8,128)(2,1)S(1)} collective-permute-done((bf16[128,768]{1,0:T(8,128)(2,1)S(1)}, bf16[128,768]{1,0:T(8,128)(2,1)S(1)}, u32[]{:S(2)}, u32[]{:S(2)}) %collective-permute-start.19) | collective-permute-done | bytes 196640 | tf_op jit(solution)/shard_map/ppermute | solution.py:56
  84.9 2.9 %collective-permute-done.21.rest_7_ = bf16[128,768]{1,0:T(8,128)(2,1)S(1)} collective-permute-done((bf16[128,768]{1,0:T(8,128)(2,1)S(1)}, bf16[128,768]{1,0:T(8,128)(2,1)S(1)}, u32[]{:S(2)}, u32[]{:S(2)}) %collective-permute-start.21) | collective-permute-done | bytes 196640 | tf_op jit(solution)/shard_map/ppermute | solution.py:56
  88.8 1.6 collective-permute-start.35
  91.1 7.5 %shard_map.160 = (bf16[128,384]{1,0:T(8,128)(2,1)}, f32[8,256]{1,0:T(8,128)}, bf16[128,768]{1,0:T(8,128)(2,1)}) custom-call(s32[1]{0:T(128)} %bitcast.order_ref, bf16[128,384]{1,0:T(8,128)(2,1)} %get-tuple-element.69.q_ref, bf16[128,768]{1,0:T(8,128)(2,1)} %get-tuple-element.70.rest_0_, bf16[128,768]{1,0:T(8,128)(2,1)} %copy-done.22, ...), custom_call_target="tpu_custom_call" | custom-call | tf_op jit(solution)/shard_map/pallas_call | solution.py:478
  98.6 1.6 collective-permute-start.30
  100.9 1.5 collective-permute-done.37.rest_7_
  102.4 1.5 collective-permute-done.45.rest_15_
  104.0 1.9 collective-permute-done.30.pb_ref
  106.5 5.4 %shard_map.161 = (f32[128,768]{1,0:T(8,128)}, bf16[128,768]{1,0:T(8,128)(2,1)}, bf16[128,768]{1,0:T(8,128)(2,1)}, bf16[128,768]{1,0:T(8,128)(2,1)}, bf16[128,1152]{1,0:T(8,128)(2,1)}, /*index=5*/bf16[128,576]{1,0:T(8,128)(2,1)}) custom-call(s32[1]{0:T(128)} %bitcast.order_ref, f32[128,768]{1,0:T(8,128)} %x_ref.5, bf16[128,768]{1,0:T(8,128)(2,1)} %get-tuple-element.71.pa_ref, ...), custom_call_target="tpu_custom_call" | custom-call | tf_op jit(solution)/shard_map/pallas_call | solution.py:478
  112.0 1.6 collective-permute-start.47
  113.5 4.8 %collective-permute-done.47.db_ref = bf16[128,768]{1,0:T(8,128)(2,1)S(1)} collective-permute-done((bf16[128,768]{1,0:T(8,128)(2,1)}, bf16[128,768]{1,0:T(8,128)(2,1)S(1)}, u32[]{:S(2)}, u32[]{:S(2)}) %collective-permute-start.47) | collective-permute-done | bytes 196640 | tf_op jit(solution)/shard_map/ppermute | solution.py:56
  119.0 7.4 %shard_map.162 = (bf16[1024,768]{1,0:T(8,128)(2,1)}, f32[128,768]{1,0:T(8,128)}, f32[3,256,128]{2,1,0:T(8,128)}, bf16[3,256,128]{2,1,0:T(8,128)(2,1)}, bf16[3,256,128]{2,1,0:T(8,128)(2,1)}, /*index=5*/f32[8,256]{1,0:T(8,128)}) custom-call(s32[1]{0:T(128)} %bitcast.order_ref, bf16[128,384]{1,0:T(8,128)(2,1)} %get-tuple-element.69.q_ref, ...), custom_call_target="tpu_custom_call" | custom-call | tf_op jit(solution)/shard_map/pallas_call | solution.py:478
  126.5 3.8 %shard_map.167 = (bf16[384,1792]{1,0:T(8,128)(2,1)}, bf16[384,1792]{1,0:T(8,128)(2,1)}) custom-call(s32[1]{0:T(128)} %bitcast.order_ref, bf16[128,768]{1,0:T(8,128)(2,1)} %get-tuple-element.106.b_ref, bf16[128,1152]{1,0:T(8,128)(2,1)} %get-tuple-element.107.dz_ref, f32[128,768]{1,0:T(8,128)} %cot_ref.5, bf16[128,576]{1,0:T(8,128)(2,1)} %get-tuple-element.108.mixed_ref), custom_call_target="tpu_custom_call" | custom-call | tf_op jit(solution)/shard_map/pallas_call | solution.py:478
  132.0 7.4 %shard_map.163 = (bf16[128,768]{1,0:T(8,128)(2,1)}, bf16[128,768]{1,0:T(8,128)(2,1)}, bf16[128,768]{1,0:T(8,128)(2,1)}, bf16[128,768]{1,0:T(8,128)(2,1)}, bf16[1...) custom-call(f32[8,256]{1,0:T(8,128)} %get-tuple-element.76.lse_ref, ...), custom_call_target="tpu_custom_call" | custom-call | tf_op jit(solution)/shard_map/pallas_call | solution.py:478
  143.5 3.9 %collective-permute-done.53 = bf16[128,768]{1,0:T(8,128)(2,1)S(1)} collective-permute-done((bf16[128,768]{1,0:T(8,128)(2,1)}, bf16[128,768]{1,0:T(8,128)(2,1)S(1)}, u32[]{:S(2)}, u32[]{:S(2)}) %collective-permute-start.53) | collective-permute-done | bytes 196640 | tf_op jit(solution)/shard_map/ppermute | solution.py:56
  149.0 6.8 %collective-permute-done.50 = bf16[128,768]{1,0:T(8,128)(2,1)S(1)} collective-permute-done((bf16[128,768]{1,0:T(8,128)(2,1)}, bf16[128,768]{1,0:T(8,128)(2,1)S(1)}, u32[]{:S(2)}, u32[]{:S(2)}) %collective-permute-start.50) | collective-permute-done | bytes 196640 | tf_op jit(solution)/shard_map/ppermute | solution.py:56
  157.5 1.7 collective-permute-done.52
  162.6 8.7 %collective-permute-done.55.rest_3_ = bf16[128,768]{1,0:T(8,128)(2,1)S(1)} collective-permute-done((bf16[128,768]{1,0:T(8,128)(2,1)S(1)}, bf16[128,768]{1,0:T(8,128)(2,1)S(1)}, u32[]{:S(2)}, u32[]{:S(2)}) %collective-permute-start.55) | collective-permute-done | bytes 196640 | tf_op jit(solution)/shard_map/ppermute | solution.py:56
  171.9 5.2 %shard_map.164 = (bf16[384,1536]{1,0:T(8,128)(2,1)}, bf16[128,768]{1,0:T(8,128)(2,1)}, bf16[128,1152]{1,0:T(8,128)(2,1)}, bf16[768,128]{1,0:T(8,128)(2,1)}) custom-call(s32[1]{0:T(128)} %bitcast.order_ref, bf16[768,128]{1,0:T(8,128)(2,1)} %get-tuple-element.75.at_ref, bf16[128,384]{1,0:T(8,128)(2,1)} %get-tuple-element.84.dqp_ref, ...), custom_call_target="tpu_custom_call" | custom-call | tf_op jit(solution)/shard_map/pallas_call | solution.py:478
  178.4 2.9 %pair_add.1 = (bf16[48,1792]{1,0:T(8,128)(2,1)}, bf16[48,1792]{1,0:T(8,128)(2,1)}, bf16[48,1792]{1,0:T(8,128)(2,1)}, bf16[48,1792]{1,0:T(8,128)(2,1)}, bf16[48,1...) custom-call(bf16[384,1792]{1,0:T(8,128)(2,1)} %get-tuple-element.109.refs_0_, ...), custom_call_target="tpu_custom_call" | custom-call | tf_op jit(solution)/shard_map/pair_add/pallas_call | solution.py:93
  182.3 1.5 collective-permute-start.46
  185.8 2.9 %collective-permute-done.70 = bf16[48,1792]{1,0:T(8,128)(2,1)S(1)} collective-permute-done((bf16[48,1792]{1,0:T(8,128)(2,1)}, bf16[48,1792]{1,0:T(8,128)(2,1)S(1)}, u32[]{:S(2)}, u32[]{:S(2)}) %collective-permute-start.70) | collective-permute-done | bytes 172064 | tf_op jit(solution)/shard_map/ppermute | solution.py:56
  190.7 5.4 %collective-permute-done.67 = bf16[48,1792]{1,0:T(8,128)(2,1)S(1)} collective-permute-done((bf16[48,1792]{1,0:T(8,128)(2,1)}, bf16[48,1792]{1,0:T(8,128)(2,1)S(1)}, u32[]{:S(2)}, u32[]{:S(2)}) %collective-permute-start.67) | collective-permute-done | bytes 172064 | tf_op jit(solution)/shard_map/ppermute | solution.py:56
  197.1 2.1 collective-permute-start.68
  199.2 3.0 %shard_map.166 = (bf16[48,1536]{1,0:T(8,128)(2,1)}, bf16[48,1536]{1,0:T(8,128)(2,1)}, bf16[48,1536]{1,0:T(8,128)(2,1)}, bf16[48,1536]{1,0:T(8,128)(2,1)}, bf16[4...) custom-call(s32[1]{0:T(128)} %bitcast.order_ref, ...), custom_call_target="tpu_custom_call" | custom-call | tf_op jit(solution)/shard_map/pallas_call | solution.py:478
  204.5 4.3 %collective-permute-done.62 = bf16[48,1536]{1,0:T(8,128)(2,1)S(1)} collective-permute-done((bf16[48,1536]{1,0:T(8,128)(2,1)}, bf16[48,1536]{1,0:T(8,128)(2,1)S(1)}, u32[]{:S(2)}, u32[]{:S(2)}) %collective-permute-start.62) | collective-permute-done | bytes 147488 | tf_op jit(solution)/shard_map/ppermute | solution.py:56
  214.1 2.0 collective-permute-start.72
  216.2 4.5 %collective-permute-done.63 = bf16[48,1536]{1,0:T(8,128)(2,1)S(1)} collective-permute-done((bf16[48,1536]{1,0:T(8,128)(2,1)S(1)}, bf16[48,1536]{1,0:T(8,128)(2,1)S(1)}, u32[]{:S(2)}, u32[]{:S(2)}) %collective-permute-start.63) | collective-permute-done | bytes 147488 | tf_op jit(solution)/shard_map/ppermute | solution.py:56
  221.7 3.1 %collective-permute-start.64 = (bf16[48,1536]{1,0:T(8,128)(2,1)S(1)}, bf16[48,1536]{1,0:T(8,128)(2,1)S(1)}, u32[]{:S(2)}, u32[]{:S(2)}) collective-permute-start(bf16[48,1536]{1,0:T(8,128)(2,1)S(1)} %add_convert_fusion.6), channel_id=1, source_target_pairs={{0,16},{8,24},{16,0},{24,8},{1,17},{9,25},{17,1},{25,9},{2,18},{10... | collective-permute-start | bytes 442376 | tf_op jit(solution)/shard_map/ppermute | solution.py:56
  230.2 2.7 %shard_map.168 = (f32[48,3264]{1,0:T(8,128)}, f32[2,48]{1,0:T(2,128)}) custom-call(f32[48,3264]{1,0:T(8,128)} %w_ref.5, bf16[48,1536]{1,0:T(8,128)(2,1)} %get-tuple-element.98.rest_0_, bf16[48,1536]{1,0:T(8,128)(2,1)} %copy-done.56, bf16[48,1536]{1,0:T(8,128)(2,1)} %copy-done.57, bf16[48,1536]{1,0:T(8,128)(2,1)} %copy-done.58, ...), custom_call_target="tpu_custom_call" | custom-call | tf_op jit(solution)/shard_map/pallas_call | solution.py:478
  232.9 1.6 collective-permute-start.73
  236.0 2.3 shard_map.165
  238.3 2.8 %adam.1 = (f32[48,3264]{1,0:T(8,128)}, f32[48,3264]{1,0:T(8,128)}, f32[48,3264]{1,0:T(8,128)}) custom-call(f32[48,3264]{1,0:T(8,128)} %w_ref.5, f32[48,3264]{1,0:T(8,128)} %get-tuple-element.61.g_ref, f32[48,3264]{1,0:T(8,128)} %m_ref.3, f32[48,3264]{1,0:T(8,128)} %v_ref.3), custom_call_target="tpu_custom_call" | custom-call | tf_op jit(solution)/shard_map/adam/pallas_call | solution.py:720
  (256 shorter events, 53.6 us)
Async XLA Ops:
  5.6 10.0 %collective-permute-start.1 = (bf16[48,1664]{1,0:T(8,128)(2,1)S(1)}, bf16[48,1664]{1,0:T(8,128)(2,1)S(1)}, u32[]{:S(2)}, u32[]{:S(2)}) collective-permute-start(bf16[48,1664]{1,0:T(8,128)(2,1)S(1)} %fusion.1.rest_0_.rest_16_.rest_8_.rest_4_), channel_id=1, source_target_pairs={{0,16},{8,24},{16,0},{24,8},{1,17},{9,25},{17,1},{25,9},{2,18},{10... | collective-permute-start | bytes 479240 | tf_op jit(solution)/shard_map/ppermute | solution.py:56
  8.2 8.0 %collective-permute-start.7 = (bf16[48,1664]{1,0:T(8,128)(2,1)S(1)}, bf16[48,1664]{1,0:T(8,128)(2,1)S(1)}, u32[]{:S(2)}, u32[]{:S(2)}) collective-permute-start(bf16[48,1664]{1,0:T(8,128)(2,1)S(1)} %fusion.1.rest_0_.rest_16_.rest_8_.rest_4_), channel_id=1, source_target_pairs={{0,2},{2,0},{4,6},{6,4},{1,3},{3,1},{5,7},{7,5},{8,10},{10,8},{12,... | collective-permute-start | bytes 479240 | tf_op jit(solution)/shard_map/ppermute | solution.py:56
  8.2 8.8 %collective-permute-start = (bf16[48,1664]{1,0:T(8,128)(2,1)S(1)}, bf16[48,1664]{1,0:T(8,128)(2,1)S(1)}, u32[]{:S(2)}, u32[]{:S(2)}) collective-permute-start(bf16[48,1664]{1,0:T(8,128)(2,1)S(1)} %fusion.1.rest_0_.rest_16_.rest_8_.rest_4_), channel_id=1, source_target_pairs={{0,8},{8,0},{16,24},{24,16},{1,9},{9,1},{17,25},{25,17},{2,10},{10... | collective-permute-start | bytes 479240 | tf_op jit(solution)/shard_map/ppermute | solution.py:56
  17.1 9.6 %collective-permute-start.4 = (bf16[48,1664]{1,0:T(8,128)(2,1)S(1)}, bf16[48,1664]{1,0:T(8,128)(2,1)S(1)}, u32[]{:S(2)}, u32[]{:S(2)}) collective-permute-start(bf16[48,1664]{1,0:T(8,128)(2,1)S(1)} %collective-permute-done.rest_1_.rest_17_.rest_9_.rest_5_), channel_id=1, source_target_pairs={{0,4},{2,6},{4,0},{6,2},{1,5},{3,7},{5,1},{7,3},{8,12},{10,14},{12... | collective-permute-start | bytes 479240 | tf_op jit(solution)/shard_map/ppermute | solution.py:56
  20.9 9.2 %collective-permute-start.6 = (bf16[48,1664]{1,0:T(8,128)(2,1)S(1)}, bf16[48,1664]{1,0:T(8,128)(2,1)S(1)}, u32[]{:S(2)}, u32[]{:S(2)}) collective-permute-start(bf16[48,1664]{1,0:T(8,128)(2,1)S(1)} %collective-permute-done.2.rest_3_.rest_19_.rest_11_.rest_7_), channel_id=1, source_target_pairs={{0,4},{2,6},{4,0},{6,2},{1,5},{3,7},{5,1},{7,3},{8,12},{10,14},{12... | collective-permute-start | bytes 479240 | tf_op jit(solution)/shard_map/ppermute | solution.py:56
  21.5 19.5 %collective-permute-start.34 = (bf16[48,1792]{1,0:T(8,128)(2,1)S(1)}, bf16[48,1792]{1,0:T(8,128)(2,1)S(1)}, u32[]{:S(2)}, u32[]{:S(2)}) collective-permute-start(bf16[48,1792]{1,0:T(8,128)(2,1)S(1)} %pad.9.rest_0_), channel_id=1, source_target_pairs={{0,4},{2,6},{4,0},{6,2},{1,5},{3,7},{5,1},{7,3},{8,12},{10,14},{12... | collective-permute-start | bytes 516104 | tf_op jit(solution)/shard_map/ppermute | solution.py:56
  23.3 7.9 %collective-permute-start.10 = (bf16[48,1664]{1,0:T(8,128)(2,1)S(1)}, bf16[48,1664]{1,0:T(8,128)(2,1)S(1)}, u32[]{:S(2)}, u32[]{:S(2)}) collective-permute-start(bf16[48,1664]{1,0:T(8,128)(2,1)S(1)} %collective-permute-done.2.rest_3_.rest_19_.rest_11_.rest_7_), channel_id=1, source_target_pairs={{0,2},{2,0},{4,6},{6,4},{1,3},{3,1},{5,7},{7,5},{8,10},{10,8},{12,... | collective-permute-start | bytes 479240 | tf_op jit(solution)/shard_map/ppermute | solution.py:56
  23.3 7.9 %collective-permute-start.13 = (bf16[48,1664]{1,0:T(8,128)(2,1)S(1)}, bf16[48,1664]{1,0:T(8,128)(2,1)S(1)}, u32[]{:S(2)}, u32[]{:S(2)}) collective-permute-start(bf16[48,1664]{1,0:T(8,128)(2,1)S(1)} %collective-permute-done.5.rest_6_.rest_22_.rest_14_.rest_10_), channel_id=1, source_target_pairs={{0,2},{2,0},{4,6},{6,4},{1,3},{3,1},{5,7},{7,5},{8,10},{10,8},{12,... | collective-permute-start | bytes 479240 | tf_op jit(solution)/shard_map/ppermute | solution.py:56
  36.5 20.9 %collective-permute-start.16 = (bf16[128,768]{1,0:T(8,128)(2,1)}, bf16[128,768]{1,0:T(8,128)(2,1)S(1)}, u32[]{:S(2)}, u32[]{:S(2)}) collective-permute-start(bf16[128,768]{1,0:T(8,128)(2,1)} %get-tuple-element.70.rest_0_), channel_id=1, source_target_pairs={{0,16},{8,24},{16,0},{24,8},{1,17},{9,25},{17,1},{25,9},{2,18},{10... | collective-permute-start | bytes 589832 | tf_op jit(solution)/shard_map/ppermute | solution.py:56
  40.1 17.2 %collective-permute-start.32 = (bf16[48,1792]{1,0:T(8,128)(2,1)S(1)}, bf16[48,1792]{1,0:T(8,128)(2,1)}, u32[]{:S(2)}, u32[]{:S(2)}) collective-permute-start(bf16[48,1792]{1,0:T(8,128)(2,1)S(1)} %pad.9.rest_0_), channel_id=1, source_target_pairs={{0,16},{8,24},{16,0},{24,8},{1,17},{9,25},{17,1},{25,9},{2,18},{10... | collective-permute-start | bytes 516104 | tf_op jit(solution)/shard_map/ppermute | solution.py:56
  40.5 16.9 %collective-permute-start.31 = (bf16[48,1792]{1,0:T(8,128)(2,1)S(1)}, bf16[48,1792]{1,0:T(8,128)(2,1)}, u32[]{:S(2)}, u32[]{:S(2)}) collective-permute-start(bf16[48,1792]{1,0:T(8,128)(2,1)S(1)} %pad.9.rest_0_), channel_id=1, source_target_pairs={{0,8},{8,0},{16,24},{24,16},{1,9},{9,1},{17,25},{25,17},{2,10},{10... | collective-permute-start | bytes 516104 | tf_op jit(solution)/shard_map/ppermute | solution.py:56
  41.0 18.4 %collective-permute-start.42 = (bf16[48,1792]{1,0:T(8,128)(2,1)S(1)}, bf16[48,1792]{1,0:T(8,128)(2,1)S(1)}, u32[]{:S(2)}, u32[]{:S(2)}) collective-permute-start(bf16[48,1792]{1,0:T(8,128)(2,1)S(1)} %collective-permute-done.34.rest_4_), channel_id=1, source_target_pairs={{0,2},{2,0},{4,6},{6,4},{1,3},{3,1},{5,7},{7,5},{8,10},{10,8},{12,... | collective-permute-start | bytes 516104 | tf_op jit(solution)/shard_map/ppermute | solution.py:56
  41.4 18.1 %collective-permute-start.18 = (bf16[128,768]{1,0:T(8,128)(2,1)}, bf16[128,768]{1,0:T(8,128)(2,1)S(1)}, u32[]{:S(2)}, u32[]{:S(2)}) collective-permute-start(bf16[128,768]{1,0:T(8,128)(2,1)} %get-tuple-element.70.rest_0_), channel_id=1, source_target_pairs={{0,4},{2,6},{4,0},{6,2},{1,5},{3,7},{5,1},{7,3},{8,12},{10,14},{12... | collective-permute-start | bytes 589832 | tf_op jit(solution)/shard_map/ppermute | solution.py:56
  57.3 16.1 %collective-permute-start.22 = (bf16[128,768]{1,0:T(8,128)(2,1)}, bf16[128,768]{1,0:T(8,128)(2,1)S(1)}, u32[]{:S(2)}, u32[]{:S(2)}) collective-permute-start(bf16[128,768]{1,0:T(8,128)(2,1)} %get-tuple-element.70.rest_0_), channel_id=1, source_target_pairs={{0,2},{2,0},{4,6},{6,4},{1,3},{3,1},{5,7},{7,5},{8,10},{10,8},{12,... | collective-permute-start | bytes 589832 | tf_op jit(solution)/shard_map/ppermute | solution.py:56
  57.4 16.1 %collective-permute-start.15 = (bf16[128,768]{1,0:T(8,128)(2,1)}, bf16[128,768]{1,0:T(8,128)(2,1)S(1)}, u32[]{:S(2)}, u32[]{:S(2)}) collective-permute-start(bf16[128,768]{1,0:T(8,128)(2,1)} %get-tuple-element.70.rest_0_), channel_id=1, source_target_pairs={{0,8},{8,0},{16,24},{24,16},{1,9},{9,1},{17,25},{25,17},{2,10},{10... | collective-permute-start | bytes 589832 | tf_op jit(solution)/shard_map/ppermute | solution.py:56
  57.4 17.6 %collective-permute-start.17 = (bf16[128,768]{1,0:T(8,128)(2,1)S(1)}, bf16[128,768]{1,0:T(8,128)(2,1)S(1)}, u32[]{:S(2)}, u32[]{:S(2)}) collective-permute-start(bf16[128,768]{1,0:T(8,128)(2,1)S(1)} %collective-permute-done.16.rest_2_), channel_id=1, source_target_pairs={{0,8},{8,0},{16,24},{24,16},{1,9},{9,1},{17,25},{25,17},{2,10},{10... | collective-permute-start | bytes 589832 | tf_op jit(solution)/shard_map/ppermute | solution.py:56
  59.4 13.5 %collective-permute-start.33 = (bf16[48,1792]{1,0:T(8,128)(2,1)}, bf16[48,1792]{1,0:T(8,128)(2,1)}, u32[]{:S(2)}, u32[]{:S(2)}) collective-permute-start(bf16[48,1792]{1,0:T(8,128)(2,1)} %collective-permute-done.32.rest_2_), channel_id=1, source_target_pairs={{0,8},{8,0},{16,24},{24,16},{1,9},{9,1},{17,25},{25,17},{2,10},{10... | collective-permute-start | bytes 516104 | tf_op jit(solution)/shard_map/ppermute | solution.py:56
  59.5 16.1 %collective-permute-start.26 = (bf16[128,768]{1,0:T(8,128)(2,1)S(1)}, bf16[128,768]{1,0:T(8,128)(2,1)S(1)}, u32[]{:S(2)}, u32[]{:S(2)}) collective-permute-start(bf16[128,768]{1,0:T(8,128)(2,1)S(1)} %collective-permute-done.18.rest_4_), channel_id=1, source_target_pairs={{0,2},{2,0},{4,6},{6,4},{1,3},{3,1},{5,7},{7,5},{8,10},{10,8},{12,... | collective-permute-start | bytes 589832 | tf_op jit(solution)/shard_map/ppermute | solution.py:56
  72.9 7.8 %collective-permute-start.20 = (bf16[128,768]{1,0:T(8,128)(2,1)S(1)}, bf16[128,768]{1,0:T(8,128)(2,1)S(1)}, u32[]{:S(2)}, u32[]{:S(2)}) collective-permute-start(bf16[128,768]{1,0:T(8,128)(2,1)S(1)} %collective-permute-done.16.rest_2_), channel_id=1, source_target_pairs={{0,4},{2,6},{4,0},{6,2},{1,5},{3,7},{5,1},{7,3},{8,12},{10,14},{12... | collective-permute-start | bytes 589832 | tf_op jit(solution)/shard_map/ppermute | solution.py:56
  73.4 11.4 %collective-permute-start.19 = (bf16[128,768]{1,0:T(8,128)(2,1)S(1)}, bf16[128,768]{1,0:T(8,128)(2,1)S(1)}, u32[]{:S(2)}, u32[]{:S(2)}) collective-permute-start(bf16[128,768]{1,0:T(8,128)(2,1)S(1)} %collective-permute-done.15.rest_1_), channel_id=1, source_target_pairs={{0,4},{2,6},{4,0},{6,2},{1,5},{3,7},{5,1},{7,3},{8,12},{10,14},{12... | collective-permute-start | bytes 589832 | tf_op jit(solution)/shard_map/ppermute | solution.py:56
  75.0 12.8 %collective-permute-start.21 = (bf16[128,768]{1,0:T(8,128)(2,1)S(1)}, bf16[128,768]{1,0:T(8,128)(2,1)S(1)}, u32[]{:S(2)}, u32[]{:S(2)}) collective-permute-start(bf16[128,768]{1,0:T(8,128)(2,1)S(1)} %collective-permute-done.17.rest_3_), channel_id=1, source_target_pairs={{0,4},{2,6},{4,0},{6,2},{1,5},{3,7},{5,1},{7,3},{8,12},{10,14},{12... | collective-permute-start | bytes 589832 | tf_op jit(solution)/shard_map/ppermute | solution.py:56
  75.5 12.2 %collective-permute-start.23 = (bf16[128,768]{1,0:T(8,128)(2,1)S(1)}, bf16[128,768]{1,0:T(8,128)(2,1)S(1)}, u32[]{:S(2)}, u32[]{:S(2)}) collective-permute-start(bf16[128,768]{1,0:T(8,128)(2,1)S(1)} %collective-permute-done.15.rest_1_), channel_id=1, source_target_pairs={{0,2},{2,0},{4,6},{6,4},{1,3},{3,1},{5,7},{7,5},{8,10},{10,8},{12,... | collective-permute-start | bytes 589832 | tf_op jit(solution)/shard_map/ppermute | solution.py:56
  80.7 7.6 %collective-permute-start.28 = (bf16[128,768]{1,0:T(8,128)(2,1)S(1)}, bf16[128,768]{1,0:T(8,128)(2,1)S(1)}, u32[]{:S(2)}, u32[]{:S(2)}) collective-permute-start(bf16[128,768]{1,0:T(8,128)(2,1)S(1)} %collective-permute-done.20.rest_6_), channel_id=1, source_target_pairs={{0,2},{2,0},{4,6},{6,4},{1,3},{3,1},{5,7},{7,5},{8,10},{10,8},{12,... | collective-permute-start | bytes 589832 | tf_op jit(solution)/shard_map/ppermute | solution.py:56
  80.7 8.1 %collective-permute-start.25 = (bf16[128,768]{1,0:T(8,128)(2,1)S(1)}, bf16[128,768]{1,0:T(8,128)(2,1)S(1)}, u32[]{:S(2)}, u32[]{:S(2)}) collective-permute-start(bf16[128,768]{1,0:T(8,128)(2,1)S(1)} %collective-permute-done.17.rest_3_), channel_id=1, source_target_pairs={{0,2},{2,0},{4,6},{6,4},{1,3},{3,1},{5,7},{7,5},{8,10},{10,8},{12,... | collective-permute-start | bytes 589832 | tf_op jit(solution)/shard_map/ppermute | solution.py:56
  87.8 10.8 %collective-permute-start.40 = (bf16[48,1792]{1,0:T(8,128)(2,1)}, bf16[48,1792]{1,0:T(8,128)(2,1)}, u32[]{:S(2)}, u32[]{:S(2)}) collective-permute-start(bf16[48,1792]{1,0:T(8,128)(2,1)} %collective-permute-done.32.rest_2_), channel_id=1, source_target_pairs={{0,2},{2,0},{4,6},{6,4},{1,3},{3,1},{5,7},{7,5},{8,10},{10,8},{12,... | collective-permute-start | bytes 516104 | tf_op jit(solution)/shard_map/ppermute | solution.py:56
  88.3 12.0 %collective-permute-start.36 = (bf16[48,1792]{1,0:T(8,128)(2,1)}, bf16[48,1792]{1,0:T(8,128)(2,1)}, u32[]{:S(2)}, u32[]{:S(2)}) collective-permute-start(bf16[48,1792]{1,0:T(8,128)(2,1)} %collective-permute-done.32.rest_2_), channel_id=1, source_target_pairs={{0,4},{2,6},{4,0},{6,2},{1,5},{3,7},{5,1},{7,3},{8,12},{10,14},{12... | collective-permute-start | bytes 516104 | tf_op jit(solution)/shard_map/ppermute | solution.py:56
  88.7 11.5 %collective-permute-start.39 = (bf16[48,1792]{1,0:T(8,128)(2,1)}, bf16[48,1792]{1,0:T(8,128)(2,1)}, u32[]{:S(2)}, u32[]{:S(2)}) collective-permute-start(bf16[48,1792]{1,0:T(8,128)(2,1)} %collective-permute-done.31.rest_1_), channel_id=1, source_target_pairs={{0,2},{2,0},{4,6},{6,4},{1,3},{3,1},{5,7},{7,5},{8,10},{10,8},{12,... | collective-permute-start | bytes 516104 | tf_op jit(solution)/shard_map/ppermute | solution.py:56
  88.8 12.0 %collective-permute-start.35 = (bf16[48,1792]{1,0:T(8,128)(2,1)}, bf16[48,1792]{1,0:T(8,128)(2,1)}, u32[]{:S(2)}, u32[]{:S(2)}) collective-permute-start(bf16[48,1792]{1,0:T(8,128)(2,1)} %collective-permute-done.31.rest_1_), channel_id=1, source_target_pairs={{0,4},{2,6},{4,0},{6,2},{1,5},{3,7},{5,1},{7,3},{8,12},{10,14},{12... | collective-permute-start | bytes 516104 | tf_op jit(solution)/shard_map/ppermute | solution.py:56
  90.4 11.9 %collective-permute-start.37 = (bf16[48,1792]{1,0:T(8,128)(2,1)}, bf16[48,1792]{1,0:T(8,128)(2,1)}, u32[]{:S(2)}, u32[]{:S(2)}) collective-permute-start(bf16[48,1792]{1,0:T(8,128)(2,1)} %collective-permute-done.33.rest_3_), channel_id=1, source_target_pairs={{0,4},{2,6},{4,0},{6,2},{1,5},{3,7},{5,1},{7,3},{8,12},{10,14},{12... | collective-permute-start | bytes 516104 | tf_op jit(solution)/shard_map/ppermute | solution.py:56
  130.3 46.9 %collective-permute-start.65 = (bf16[384,1792]{1,0:T(8,128)(2,1)}, bf16[384,1792]{1,0:T(8,128)(2,1)S(1)}, u32[]{:S(2)}, u32[]{:S(2)}) collective-permute-start(bf16[384,1792]{1,0:T(8,128)(2,1)} %get-tuple-element.110), channel_id=1, source_target_pairs={{0,2},{2,0},{4,6},{6,4},{1,3},{3,1},{5,7},{7,5},{8,10},{10,8},{12,... | collective-permute-start | bytes 4128776 | tf_op jit(solution)/shard_map/ppermute | solution.py:56
  139.4 8.1 %collective-permute-start.53 = (bf16[128,768]{1,0:T(8,128)(2,1)}, bf16[128,768]{1,0:T(8,128)(2,1)S(1)}, u32[]{:S(2)}, u32[]{:S(2)}) collective-permute-start(bf16[128,768]{1,0:T(8,128)(2,1)} %get-tuple-element.93), channel_id=1, source_target_pairs={{0,4},{2,6},{4,0},{6,2},{1,5},{3,7},{5,1},{7,3},{8,12},{10,14},{12... | collective-permute-start | bytes 589832 | tf_op jit(solution)/shard_map/ppermute | solution.py:56
  140.4 20.9 %collective-permute-start.49 = (bf16[128,768]{1,0:T(8,128)(2,1)}, bf16[128,768]{1,0:T(8,128)(2,1)S(1)}, u32[]{:S(2)}, u32[]{:S(2)}) collective-permute-start(bf16[128,768]{1,0:T(8,128)(2,1)} %get-tuple-element.87), channel_id=1, source_target_pairs={{0,4},{2,6},{4,0},{6,2},{1,5},{3,7},{5,1},{7,3},{8,12},{10,14},{12... | collective-permute-start | bytes 589832 | tf_op jit(solution)/shard_map/ppermute | solution.py:56
  141.5 14.4 %collective-permute-start.50 = (bf16[128,768]{1,0:T(8,128)(2,1)}, bf16[128,768]{1,0:T(8,128)(2,1)S(1)}, u32[]{:S(2)}, u32[]{:S(2)}) collective-permute-start(bf16[128,768]{1,0:T(8,128)(2,1)} %get-tuple-element.89), channel_id=1, source_target_pairs={{0,4},{2,6},{4,0},{6,2},{1,5},{3,7},{5,1},{7,3},{8,12},{10,14},{12... | collective-permute-start | bytes 589832 | tf_op jit(solution)/shard_map/ppermute | solution.py:56
  142.5 16.7 %collective-permute-start.52 = (bf16[128,768]{1,0:T(8,128)(2,1)}, bf16[128,768]{1,0:T(8,128)(2,1)S(1)}, u32[]{:S(2)}, u32[]{:S(2)}) collective-permute-start(bf16[128,768]{1,0:T(8,128)(2,1)} %get-tuple-element.91), channel_id=1, source_target_pairs={{0,4},{2,6},{4,0},{6,2},{1,5},{3,7},{5,1},{7,3},{8,12},{10,14},{12... | collective-permute-start | bytes 589832 | tf_op jit(solution)/shard_map/ppermute | solution.py:56
  148.4 10.7 %collective-permute-start.54 = (bf16[128,768]{1,0:T(8,128)(2,1)S(1)}, bf16[128,768]{1,0:T(8,128)(2,1)S(1)}, u32[]{:S(2)}, u32[]{:S(2)}) collective-permute-start(bf16[128,768]{1,0:T(8,128)(2,1)S(1)} %add_convert_fusion.1), channel_id=1, source_target_pairs={{0,8},{8,0},{16,24},{24,16},{1,9},{9,1},{17,25},{25,17},{2,10},{10... | collective-permute-start | bytes 589832 | tf_op jit(solution)/shard_map/ppermute | solution.py:56
  160.1 11.1 %collective-permute-start.55 = (bf16[128,768]{1,0:T(8,128)(2,1)S(1)}, bf16[128,768]{1,0:T(8,128)(2,1)S(1)}, u32[]{:S(2)}, u32[]{:S(2)}) collective-permute-start(bf16[128,768]{1,0:T(8,128)(2,1)S(1)} %add_convert_fusion), channel_id=1, source_target_pairs={{0,16},{8,24},{16,0},{24,8},{1,17},{9,25},{17,1},{25,9},{2,18},{10... | collective-permute-start | bytes 589832 | tf_op jit(solution)/shard_map/ppermute | solution.py:56
  177.2 19.9 %collective-permute-start.57 = (bf16[384,1536]{1,0:T(8,128)(2,1)}, bf16[384,1536]{1,0:T(8,128)(2,1)S(1)}, u32[]{:S(2)}, u32[]{:S(2)}) collective-permute-start(bf16[384,1536]{1,0:T(8,128)(2,1)} %get-tuple-element.97), channel_id=1, source_target_pairs={{0,2},{2,0},{4,6},{6,4},{1,3},{3,1},{5,7},{7,5},{8,10},{10,8},{12,... | collective-permute-start | bytes 3538952 | tf_op jit(solution)/shard_map/ppermute | solution.py:56
  182.3 52.2 %collective-permute-start.46 = (bf16[128,768]{1,0:T(8,128)(2,1)S(1)}, bf16[128,768]{1,0:T(8,128)(2,1)S(1)}, u32[]{:S(2)}, u32[]{:S(2)}) collective-permute-start(bf16[128,768]{1,0:T(8,128)(2,1)S(1)} %copy-done.41), channel_id=1, source_target_pairs={{0,1},{1,0},{2,3},{3,2},{4,5},{5,4},{6,7},{7,6},{8,9},{9,8},{10,11... | collective-permute-start | bytes 589832 | tf_op jit(solution)/shard_map/ppermute | solution.py:56
  183.8 37.8 %collective-permute-start.66 = (bf16[48,1792]{1,0:T(8,128)(2,1)}, bf16[48,1792]{1,0:T(8,128)(2,1)S(1)}, u32[]{:S(2)}, u32[]{:S(2)}) collective-permute-start(bf16[48,1792]{1,0:T(8,128)(2,1)} %get-tuple-element.112), channel_id=1, source_target_pairs={{0,4},{2,6},{4,0},{6,2},{1,5},{3,7},{5,1},{7,3},{8,12},{10,14},{12... | collective-permute-start | bytes 516104 | tf_op jit(solution)/shard_map/ppermute | solution.py:56
  184.8 11.3 %collective-permute-start.67 = (bf16[48,1792]{1,0:T(8,128)(2,1)}, bf16[48,1792]{1,0:T(8,128)(2,1)S(1)}, u32[]{:S(2)}, u32[]{:S(2)}) collective-permute-start(bf16[48,1792]{1,0:T(8,128)(2,1)} %get-tuple-element.114), channel_id=1, source_target_pairs={{0,4},{2,6},{4,0},{6,2},{1,5},{3,7},{5,1},{7,3},{8,12},{10,14},{12... | collective-permute-start | bytes 516104 | tf_op jit(solution)/shard_map/ppermute | solution.py:56
  188.7 13.5 %collective-permute-start.69 = (bf16[48,1792]{1,0:T(8,128)(2,1)}, bf16[48,1792]{1,0:T(8,128)(2,1)S(1)}, u32[]{:S(2)}, u32[]{:S(2)}) collective-permute-start(bf16[48,1792]{1,0:T(8,128)(2,1)} %get-tuple-element.116), channel_id=1, source_target_pairs={{0,4},{2,6},{4,0},{6,2},{1,5},{3,7},{5,1},{7,3},{8,12},{10,14},{12... | collective-permute-start | bytes 516104 | tf_op jit(solution)/shard_map/ppermute | solution.py:56
  197.1 24.6 %collective-permute-start.68 = (bf16[48,1792]{1,0:T(8,128)(2,1)S(1)}, bf16[48,1792]{1,0:T(8,128)(2,1)S(1)}, u32[]{:S(2)}, u32[]{:S(2)}) collective-permute-start(bf16[48,1792]{1,0:T(8,128)(2,1)S(1)} %add_convert_fusion.5), channel_id=1, source_target_pairs={{0,8},{8,0},{16,24},{24,16},{1,9},{9,1},{17,25},{25,17},{2,10},{10... | collective-permute-start | bytes 516104 | tf_op jit(solution)/shard_map/ppermute | solution.py:56
  203.4 8.2 %collective-permute-start.59 = (bf16[48,1536]{1,0:T(8,128)(2,1)}, bf16[48,1536]{1,0:T(8,128)(2,1)S(1)}, u32[]{:S(2)}, u32[]{:S(2)}) collective-permute-start(bf16[48,1536]{1,0:T(8,128)(2,1)} %get-tuple-element.101), channel_id=1, source_target_pairs={{0,4},{2,6},{4,0},{6,2},{1,5},{3,7},{5,1},{7,3},{8,12},{10,14},{12... | collective-permute-start | bytes 442376 | tf_op jit(solution)/shard_map/ppermute | solution.py:56
  211.6 9.0 %collective-permute-start.63 = (bf16[48,1536]{1,0:T(8,128)(2,1)S(1)}, bf16[48,1536]{1,0:T(8,128)(2,1)S(1)}, u32[]{:S(2)}, u32[]{:S(2)}) collective-permute-start(bf16[48,1536]{1,0:T(8,128)(2,1)S(1)} %add_convert_fusion.7), channel_id=1, source_target_pairs={{0,8},{8,0},{16,24},{24,16},{1,9},{9,1},{17,25},{25,17},{2,10},{10... | collective-permute-start | bytes 442376 | tf_op jit(solution)/shard_map/ppermute | solution.py:56
  214.1 11.4 %collective-permute-start.72 = (bf16[48,1792]{1,0:T(8,128)(2,1)S(1)}, bf16[48,1792]{1,0:T(8,128)(2,1)S(1)}, u32[]{:S(2)}, u32[]{:S(2)}) collective-permute-start(bf16[48,1792]{1,0:T(8,128)(2,1)S(1)} %add_convert_fusion.3), channel_id=1, source_target_pairs={{0,16},{8,24},{16,0},{24,8},{1,17},{9,25},{17,1},{25,9},{2,18},{10... | collective-permute-start | bytes 516104 | tf_op jit(solution)/shard_map/ppermute | solution.py:56
  221.7 7.8 %collective-permute-start.64 = (bf16[48,1536]{1,0:T(8,128)(2,1)S(1)}, bf16[48,1536]{1,0:T(8,128)(2,1)S(1)}, u32[]{:S(2)}, u32[]{:S(2)}) collective-permute-start(bf16[48,1536]{1,0:T(8,128)(2,1)S(1)} %add_convert_fusion.6), channel_id=1, source_target_pairs={{0,16},{8,24},{16,0},{24,8},{1,17},{9,25},{17,1},{25,9},{2,18},{10... | collective-permute-start | bytes 442376 | tf_op jit(solution)/shard_map/ppermute | solution.py:56
  225.5 9.8 %collective-permute-start.56 = (bf16[128,768]{1,0:T(8,128)(2,1)S(1)}, bf16[128,768]{1,0:T(8,128)(2,1)S(1)}, u32[]{:S(2)}, u32[]{:S(2)}) collective-permute-start(bf16[128,768]{1,0:T(8,128)(2,1)S(1)} %copy-done.42), channel_id=1, source_target_pairs={{0,1},{1,0},{2,3},{3,2},{4,5},{5,4},{6,7},{7,6},{8,9},{9,8},{10,11... | collective-permute-start | bytes 589832 | tf_op jit(solution)/shard_map/ppermute | solution.py:56
  232.9 8.3 %collective-permute-start.73 = (f32[2,48]{1,0:T(2,128)}, f32[2,48]{1,0:T(2,128)S(1)}, u32[]{:S(2)}, u32[]{:S(2)}) collective-permute-start(f32[2,48]{1,0:T(2,128)} %get-tuple-element.120.a_ref), channel_id=1, source_target_pairs={{0,1},{1,0},{2,3},{3,2},{4,5},{5,4},{6,7},{7,6},{8,9},{9,8},{10,11... | collective-permute-start | bytes 1160 | tf_op jit(solution)/shard_map/ppermute | solution.py:56
  (87 other events, 829.8 us)

commit v4 on v2

--- a/solution.py
+++ b/solution.py
@@ -87,28 +87,50 @@
         out[...] = (keep[at, :].astype(F32) + recv[at, :].astype(F32)).astype(BF16)
 
 
-def scatter_sum(parts):
-    if not staged():
-        return [lax.psum_scatter(parts[0], TOKENS_AX, scatter_dimension=0, tiled=True)]
-    keep, send = parts
-    rows, cols = keep.shape[0] // 8, keep.shape[1]
-    recv = swap(send, "shard", 1)
+def block_kernel(*refs):
+    refs[-1][...] = total([ref[...] for ref in refs[:-1]]).astype(BF16)
+
+
+def native_sum(part):
+    return [lax.psum_scatter(part, TOKENS_AX, scatter_dimension=0, tiled=True)]
+
+
+def pair_swap(groups):
+    return [swap(groups[2 + x], "shard", 1) for x in (1, 0)][::-1]
+
+
+def scatter_sum(groups, recv):
+    keep = groups[0]
+    rows, cols = keep.shape[0] // 4, keep.shape[1]
     s = pl.pallas_call(
         add_kernel,
-        out_shape=[sds((rows, cols), BF16)] * 8,
+        out_shape=[sds((rows, cols), BF16)] * 4,
         in_specs=[VM, VM],
-        out_specs=[VM] * 8,
+        out_specs=[VM] * 4,
         name="pair_add",
-    )(keep, recv)
-    got = {z: swap(s[4 + z], "shard", 2) for z in (3, 2, 1, 0)}
+    )(groups[1], recv[1])
+    got = {z: swap(s[z], "shard", 2) for z in (3, 2, 1, 0)}
 
     def block(z, *more):
-        return total([s[z], got[z], *more]).astype(BF16)
+        head = pl.BlockSpec((rows, cols), lambda i: (z, 0))
+        return call(
+            block_kernel,
+            [sds((rows, cols), BF16)],
+            [head, head] + [VM] * (1 + len(more)),
+            [],
+            [keep, recv[0], got[z], *more],
+        )[0]
 
     far = swap(block(3), "blk", 1)
     two = swap(block(2, far), "blk", 2)
     one = swap(block(1), "blk", 1)
-    return [s[0], got[0], one, two]
+    return [keep, recv[0], got[0], one, two]
+
+
+def term_specs(terms):
+    shape = terms[-1].shape
+    head = pl.BlockSpec(shape, lambda i: (0, 0))
+    return [VM if term.shape == shape else head for term in terms]
 
 
 def total(terms):
@@ -137,10 +159,10 @@
     if len(outs) == 1:
         outs[0][...] = acc[...].astype(BF16)
         return
-    rows = outs[0].shape[0] // 8
+    rows = outs[0].shape[0] // 4
     for i, j in enumerate(chunk_order()):
         at = pl.ds(pl.multiple_of((order_ref[0] ^ j) * rows, 8), rows)
-        outs[i // 8][pl.ds((i % 8) * rows, rows), :] = acc[at, :].astype(BF16)
+        outs[i // 4][pl.ds((i % 4) * rows, rows), :] = acc[at, :].astype(BF16)
 
 
 def norm_parts(v):
@@ -206,7 +228,7 @@
 
 def qkv_kernel(n, order_ref, x_ref, cos_ref, sin_ref, *rest):
     chunks = rest[:n]
-    a_ref, q_ref, kv_ref, g_ref, w, sems = rest[n:]
+    at_ref, q_ref, kv_ref, g_ref, w, sems = rest[n:]
     width = q_ref.shape[1]
     copies = weight_copies(order_ref, chunks, w, sems)
     xhat, _ = norm_parts(x_ref[...])
@@ -218,7 +240,7 @@
     g = dot_nt(pick, w[:, 4 * width : 4 * width + 128])
     g_ref[...] = g
     a = (xhat * g[0:1, :]).astype(BF16)
-    a_ref[...] = a
+    at_ref[...] = jnp.transpose(a)
     cos = wide(cos_ref[...], width)
     sin = wide(sin_ref[...], width)
     q_ref[...] = rope(dot_nn(a, w[:, :width]), cos, sin).astype(BF16)
@@ -327,7 +349,13 @@
     emit_blocks(order_ref, acc, outs)
 
 
-def attend_back_kernel(
+def back_tile(k, v, qm, dom, lse_row, dot_row):
+    prob = jnp.exp(dot_nt(k, qm) - lse_row)
+    ds = (prob * (dot_nt(v, dom) - dot_row)).astype(BF16)
+    return dot_nn(ds, qm), dot_nn(prob.astype(BF16), dom), dot_tn(ds, k)
+
+
+def back_kernel(
     n, nw, no, blocks, order_ref, q_ref, attn_ref, lse_ref, hid_ref, cot_ref, g_ref,
     da_ref, db_ref, cos_ref, sin_ref, *rest
 ):
@@ -355,35 +383,32 @@
         dots = jnp.sum(dom.astype(F32) * both.astype(F32), axis=1, keepdims=True)
         row_s[p : p + 1, :] = as_row(dots)
     dq_s[...] = jnp.zeros(dq_s.shape, F32)
-    halves = len(outs)
     block_rows = kv.shape[0]
 
     def block_work(block):
         for copy in first or key_copies(keys, kv, ksem, block):
             copy.wait()
-        for half in range(halves):
-            count = block_rows // halves // SUB_ROWS
+        for group, out_ref in enumerate(outs):
+            size = block_rows // no
 
             def sub_work(sub):
-                src = pl.ds(
-                    pl.multiple_of(half * (block_rows // halves) + sub * SUB_ROWS, SUB_ROWS),
-                    SUB_ROWS,
-                )
+                start = group * size + sub * SUB_ROWS
+                src = pl.ds(pl.multiple_of(start, SUB_ROWS), SUB_ROWS)
                 dst = pl.ds(
                     pl.multiple_of(block * block_rows + sub * SUB_ROWS, SUB_ROWS), SUB_ROWS
                 )
                 for p in range(pairs):
                     at = slice(p * 128, p * 128 + 128)
                     vat = slice(width + p * 128, width + p * 128 + 128)
-                    k = kv[src, at]
-                    prob = jnp.exp(dot_nt(k, qm_s[p]) - lse_ref[p : p + 1, :])
-                    dprob = dot_nt(kv[src, vat], dom_s[p])
-                    ds = (prob * (dprob - row_s[p : p + 1, :])).astype(BF16)
-                    outs[half][dst, at] = dot_nn(ds, qm_s[p]).astype(BF16)
-                    outs[half][dst, vat] = dot_nn(prob.astype(BF16), dom_s[p]).astype(BF16)
-                    dq_s[p] += dot_tn(ds, k)
-
-            each(count, sub_work)
+                    dk, dv, dq = back_tile(
+                        kv[src, at], kv[src, vat], qm_s[p], dom_s[p],
+                        lse_ref[p : p + 1, :], row_s[p : p + 1, :],
+                    )
+                    out_ref[dst, at] = dk.astype(BF16)
+                    out_ref[dst, vat] = dv.astype(BF16)
+                    dq_s[p] += dq
+
+            each(size // SUB_ROWS, sub_work)
 
     each(blocks, block_work)
     dq = jnp.concatenate([join_heads(dq_s[p]) for p in range(pairs)], axis=1) * SCALE
@@ -392,28 +417,42 @@
     ).astype(BF16)
 
 
+def pick_rows(order_ref, ref, blocks, rows):
+    return jnp.concatenate(
+        [ref[pl.ds(pl.multiple_of((order_ref[0] ^ j) * rows, 16), rows), :] for j in blocks], axis=0
+    )
+
+
 def qkv_grad_kernel(
-    n, nt, no, order_ref, a_ref, dqp_ref, dhid_ref, attn_ref, cos_ref, sin_ref, *rest
+    n, nt, no, order_ref, at_ref, dqp_ref, dhid_ref, attn_ref, cos_ref, sin_ref, *rest
 ):
     terms = rest[:nt]
     chunks = rest[nt : nt + n]
     outs = rest[nt + n : nt + n + no]
-    da_ref, w, acc, sems = rest[nt + n + no :]
+    da_ref, w, ht, sems = rest[nt + n + no :]
     width = dqp_ref.shape[1]
-    copies = weight_copies(order_ref, chunks, w, sems)
-    dkv = terms[0][...].astype(F32)
-    for term in terms[1:]:
-        dkv = dkv + term[...].astype(F32)
+    copies = weight_copies(order_ref, chunks, w, sems, (0, 3 * width))
+    dkv = total([term[...] for term in terms])
     dkp = rope_back(
         dkv[:, :width], wide(cos_ref[...], width), wide(sin_ref[...], width)
     ).astype(BF16)
     d = jnp.concatenate([dqp_ref[...], dkp, dkv[:, width:].astype(BF16)], axis=1)
+    ht[...] = jnp.transpose(dhid_ref[...].astype(BF16))
+    if no == 1:
+        a_t, h_t = at_ref[...], ht[...]
+    else:
+        rows = at_ref.shape[0] // 16
+        a_t = pick_rows(order_ref, at_ref, chunk_order(), rows)
+        h_t = pick_rows(order_ref, ht, chunk_order(), rows)
+    one = dot_nn(a_t, d).astype(BF16)
+    two = dot_nn(h_t, attn_ref[...]).astype(BF16)
+    size = one.shape[0] // no
+    for i, out in enumerate(outs):
+        out[:, : 3 * width] = one[i * size : (i + 1) * size]
+        out[:, 3 * width :] = two[i * size : (i + 1) * size]
     for copy in copies:
         copy.wait()
-    da_ref[...] = dot_nt(d, w[:, : 3 * width]).astype(BF16)
-    acc[:, : 3 * width] = dot_tn(a_ref[...], d)
-    acc[:, 3 * width :] = dot_tn(dhid_ref[...].astype(BF16), attn_ref[...])
-    emit_blocks(order_ref, acc, outs)
+    da_ref[...] = dot_nt(d, w[...]).astype(BF16)
 
 
 def call(kernel, out_shape, specs, scratch, args):
@@ -423,6 +462,7 @@
         in_specs=specs,
         out_specs=jax.tree.map(lambda _: VM, out_shape),
         scratch_shapes=scratch,
+        grid=(1,) if any(spec.block_shape for spec in specs) else (),
     )(*args)
 
 
@@ -474,10 +514,13 @@
     w_out[...], m_out[...], v_out[...] = adam_update(w, grad, m_ref[...], v_ref[...])
 
 
-def lnback_kernel(x_ref, da_ref, db_ref, dhid_ref, g_ref, out_ref):
+def lnback_kernel(
+    x_ref, da_ref, db_ref, dhid_ref, g_ref, hid_ref, fa_ref, fb_ref, grad_ref, out_ref
+):
     xhat, inv = norm_parts(x_ref[...])
     da = da_ref[...].astype(F32) + db_ref[...].astype(F32)
-    out_ref[...] = dhid_ref[...] + norm_back(da, xhat, inv, g_ref[0:1, :])
+    grad_ref[...] = dhid_ref[...] + norm_back(da, xhat, inv, g_ref[0:1, :])
+    out_ref[...] = hid_ref[...] + (fa_ref[...].astype(F32) + fb_ref[...].astype(F32))
 
 
 def head_swap(x):
@@ -512,11 +555,11 @@
 
     nw = len(first_chunks)
     wsem = pltpu.SemaphoreType.DMA((nw,))
-    halves = 2 if staged() else 1
-
-    a, q, kv, g = call(
+    parts = 4 if staged() else 1
+
+    a_t, q, kv, g = call(
         partial(qkv_kernel, nw),
-        [sds((toks, d), BF16), sds((toks, width), BF16), sds((toks, 2 * width), BF16), sds((8, d), F32)],
+        [sds((d, toks), BF16), sds((toks, width), BF16), sds((toks, 2 * width), BF16), sds((8, d), F32)],
         [SM, VM, VM, VM] + [ANY] * nw,
         [pltpu.VMEM((d, wq_cols), BF16), wsem],
         [order, inputs, cos, sin] + first_chunks,
@@ -561,55 +604,68 @@
     )
     db_other = head_swap(db_part)
     ffn_other = head_swap(ffn_part)
-    outputs = hidden + (ffn_part.astype(F32) + ffn_other.astype(F32))
     ffn_grads = call(
-        partial(ffn_grad_kernel, halves),
-        [sds((d // halves, rest_cols), BF16)] * halves,
+        partial(ffn_grad_kernel, parts),
+        [sds((d // parts, rest_cols), BF16)] * parts,
         [SM] + [VM] * 4,
         [pltpu.VMEM((d, rest_cols), F32)],
         [order, b, dz, cotangent, mixed],
     )
-    ffn_terms = scatter_sum(ffn_grads)
-
-    back = call(
-        partial(attend_back_kernel, nk, nw, halves, blocks),
-        [sds((seq // halves, 2 * width), BF16)] * halves
+    if staged():
+        ffn_recv = pair_swap(ffn_grads)
+    else:
+        ffn_terms = native_sum(*ffn_grads)
+
+    both = (pairs, 2 * toks, 128)
+    *kv_groups, dhid, dqp = call(
+        partial(back_kernel, nk, nw, parts, blocks),
+        [sds((seq // parts, 2 * width), BF16)] * parts
         + [sds((toks, d), F32), sds((toks, width), BF16)],
         [SM] + [VM] * 10 + [ANY] * (nk + nw),
         [
             pltpu.VMEM((block_rows, 2 * width), BF16),
             pltpu.VMEM((d, width), BF16),
-            pltpu.VMEM((pairs, 2 * toks, 128), F32),
-            pltpu.VMEM((pairs, 2 * toks, 128), BF16),
-            pltpu.VMEM((pairs, 2 * toks, 128), BF16),
+            pltpu.VMEM(both, F32),
+            pltpu.VMEM(both, BF16),
+            pltpu.VMEM(both, BF16),
             pltpu.VMEM((8, 2 * toks), F32),
             ksem,
             wsem,
         ],
-        [order, q, attn, lse, hidden, cotangent, g, db_part, db_other, cos, sin] + keys + first_chunks,
-    )
-    dhid, dqp = back[halves:]
-    kv_terms = scatter_sum(back[:halves])
+        [order, q, attn, lse, hidden, cotangent, g, db_part, db_other, cos, sin]
+        + keys
+        + first_chunks,
+    )
+    if staged():
+        kv_terms = scatter_sum(kv_groups, pair_swap(kv_groups))
+        ffn_terms = scatter_sum(ffn_grads, ffn_recv)
+    else:
+        kv_terms = native_sum(*kv_groups)
     nt = len(kv_terms)
-    grads = call(
-        partial(qkv_grad_kernel, nw, nt, halves),
-        [sds((d // halves, 4 * width), BF16)] * halves + [sds((toks, d), BF16)],
-        [SM] + [VM] * 6 + [VM] * nt + [ANY] * nw,
-        [pltpu.VMEM((d, wq_cols), BF16), pltpu.VMEM((d, 4 * width), F32), wsem],
-        [order, a, dqp, dhid, attn, cos, sin] + kv_terms + first_chunks,
-    )
-    da_part = grads[halves]
+    *w_groups, da_part = call(
+        partial(qkv_grad_kernel, nw, nt, parts),
+        [sds((d // parts, 4 * width), BF16)] * parts + [sds((toks, d), BF16)],
+        [SM] + [VM] * 6 + term_specs(kv_terms) + [ANY] * nw,
+        [pltpu.VMEM((d, 3 * width), BF16), pltpu.VMEM((d, toks), BF16), wsem],
+        [order, a_t, dqp, dhid, attn, cos, sin] + kv_terms + first_chunks,
+    )
     da_other = head_swap(da_part)
-    (input_grad,) = call(
-        lnback_kernel, [sds((toks, d), F32)], [VM] * 5, [], [inputs, da_part, da_other, dhid, g]
-    )
-
-    first_terms = scatter_sum(grads[:halves])
+    input_grad, outputs = call(
+        lnback_kernel,
+        [sds((toks, d), F32)] * 2,
+        [VM] * 8,
+        [],
+        [inputs, da_part, da_other, dhid, g, hidden, ffn_part, ffn_other],
+    )
+    if staged():
+        first_terms = scatter_sum(w_groups, pair_swap(w_groups))
+    else:
+        first_terms = native_sum(*w_groups)
     full = weights.shape
     weight_grad, gain_part = call(
         partial(gsum_kernel, nt, width, units),
         [sds(full, F32), sds(gains.shape, F32)],
-        [VM] * (1 + 2 * nt),
+        [VM] + term_specs(first_terms) + term_specs(ffn_terms),
         [],
         [weights] + first_terms + ffn_terms,
     )

time: 227 us -> 242 us (1.066)
  Pallas kernels: 55.9 us -> 69.2 us
  waiting for transfers between devices: 87.8 us -> 96.8 us
  other arithmetic: 10.7 us -> 2.92 us
  local copies, waits for them, and re-layouts: 7.07 us -> 12.9 us
  starting transfers between devices: 63.2 us -> 57.8 us
    pallas_call x9 -> x18, Pallas kernels: 44.4 us -> 59.7 us  [call(): pl.pallas_call(kernel, out_shape=out_shape, in_specs=specs, out_specs=jax...]
    ppermute x74 -> x77, waiting for transfers between devices: 87.8 us -> 96.8 us  [swap(): return lax.ppermute(x, axis, [(i, i ^ bits) for i in range(size)])]
    convert_element_type x9 -> x0, other arithmetic: 6.99 us -> none  [block(): return total([s[z], got[z], *more]).astype(BF16)]
    unnamed x120 -> x160, local copies, waits for them, and re-layouts: 6.92 us -> 12.8 us
    ppermute x74 -> x77, starting transfers between devices: 63.2 us -> 57.8 us  [swap(): return lax.ppermute(x, axis, [(i, i ^ bits) for i in range(size)])]
  transfers between devices with their start and end apart: 74 -> 77, of which waited for: 30 -> 25; matrix products, arithmetic and copies ran while one was open for 4% -> 0% of each run, Pallas kernels for 17% -> 22%
where the time goes in v4:
time: 242 us; the launch traced here: 241 us
  waiting for transfers between devices  96.8 us (40%)
  Pallas kernels  69.2 us (29%)
  starting transfers between devices  57.8 us (24%)
  local copies, waits for them, and re-layouts  12.9 us (5%)
  other arithmetic  2.92 us (1%)
    ppermute x77, waiting for transfers between devices, swap(): return lax.ppermute(x, axis, [(i, i ^ bits) for i in range(size)])  96.8 us
    pallas_call x18, Pallas kernels, call(): pl.pallas_call(kernel, out_shape=out_shape, in_specs=specs, out_specs=jax...  59.7 us
    ppermute x77, starting transfers between devices, swap(): return lax.ppermute(x, axis, [(i, i ^ bits) for i in range(size)])  57.8 us
    unnamed x160, local copies, waits for them, and re-layouts  12.8 us
    pallas_call x3, Pallas kernels, scatter_sum(): pl.pallas_call(add_kernel, out_shape=[sds((rows, cols), BF16)] * 4, in_sp...  6.59 us
  transfers between devices with their start and end apart: 77, of which 25 were waited for; matrix products, arithmetic and copies ran while one was open for 0% of the time, Pallas kernels for 22%

profile of v4, /device:TPU:0, one launch (start us, length us, event | category | flops | bytes accessed | tf_op | source)
XLA Modules:
  0.0 241.0 jit_solution(7974919433640803523)
XLA Ops:
  2.6 3.0 %collective-permute-start.3 = (bf16[48,1664]{1,0:T(8,128)(2,1)S(1)}, bf16[48,1664]{1,0:T(8,128)(2,1)S(1)}, u32[]{:S(2)}, u32[]{:S(2)}) collective-permute-start(bf16[48,1664]{1,0:T(8,128)(2,1)S(1)} %fusion.1.rest_0_.rest_16_.rest_5_), channel_id=1, source_target_pairs={{0,4},{2,6},{4,0},{6,2},{1,5},{3,7},{5,1},{7,3},{8,12},{10,14},{12... | collective-permute-start | bytes 479240 | tf_op jit(solution)/shard_map/ppermute | solution.py:56
  5.6 2.6 %collective-permute-start.1 = (bf16[48,1664]{1,0:T(8,128)(2,1)S(1)}, bf16[48,1664]{1,0:T(8,128)(2,1)S(1)}, u32[]{:S(2)}, u32[]{:S(2)}) collective-permute-start(bf16[48,1664]{1,0:T(8,128)(2,1)S(1)} %fusion.1.rest_0_.rest_16_.rest_5_), channel_id=1, source_target_pairs={{0,16},{8,24},{16,0},{24,8},{1,17},{9,25},{17,1},{25,9},{2,18},{10... | collective-permute-start | bytes 479240 | tf_op jit(solution)/shard_map/ppermute | solution.py:56
  10.0 5.6 %collective-permute-done.1.rest_2_.rest_18_.rest_7_ = bf16[48,1664]{1,0:T(8,128)(2,1)S(1)} collective-permute-done((bf16[48,1664]{1,0:T(8,128)(2,1)S(1)}, bf16[48,1664]{1,0:T(8,128)(2,1)S(1)}, u32[]{:S(2)}, u32[]{:S(2)}) %collective-permute-start.1) | collective-permute-done | bytes 159776 | tf_op jit(solution)/shard_map/ppermute | solution.py:56
  18.5 2.4 collective-permute-done.2.rest_3_.rest_19_.rest_8_
  21.5 1.6 collective-permute-start.34
  23.8 2.9 %collective-permute-done.4.rest_5_.rest_21_.rest_10_ = bf16[48,1664]{1,0:T(8,128)(2,1)S(1)} collective-permute-done((bf16[48,1664]{1,0:T(8,128)(2,1)S(1)}, bf16[48,1664]{1,0:T(8,128)(2,1)S(1)}, u32[]{:S(2)}, u32[]{:S(2)}) %collective-permute-start.4) | collective-permute-done | bytes 159776 | tf_op jit(solution)/shard_map/ppermute | solution.py:56
  26.7 3.4 %collective-permute-done.6.rest_7_.rest_23_.rest_12_ = bf16[48,1664]{1,0:T(8,128)(2,1)S(1)} collective-permute-done((bf16[48,1664]{1,0:T(8,128)(2,1)S(1)}, bf16[48,1664]{1,0:T(8,128)(2,1)S(1)}, u32[]{:S(2)}, u32[]{:S(2)}) %collective-permute-start.6) | collective-permute-done | bytes 159776 | tf_op jit(solution)/shard_map/ppermute | solution.py:56
  32.7 4.3 %shard_map.159 = (bf16[768,128]{1,0:T(8,128)(2,1)}, bf16[128,384]{1,0:T(8,128)(2,1)}, bf16[128,768]{1,0:T(8,128)(2,1)}, f32[8,768]{1,0:T(8,128)}) custom-call(s32[1]{0:T(128)} %bitcast.order_ref, f32[128,768]{1,0:T(8,128)} %x_ref.5, f32[128,128]{1,0:T(8,128)} %get-tuple-element.113.cos_ref, f32[128,128]{1,0:T(8,128)} %get-tuple-element.112.sin_ref, ...), custom_call_target="tpu_custom_call" | custom-call | tf_op jit(solution)/shard_map/pallas_call | solution.py:459
  37.0 3.5 %collective-permute-start.16 = (bf16[128,768]{1,0:T(8,128)(2,1)}, bf16[128,768]{1,0:T(8,128)(2,1)S(1)}, u32[]{:S(2)}, u32[]{:S(2)}) collective-permute-start(bf16[128,768]{1,0:T(8,128)(2,1)} %get-tuple-element.63.rest_0_), channel_id=1, source_target_pairs={{0,16},{8,24},{16,0},{24,8},{1,17},{9,25},{17,1},{25,9},{2,18},{10... | collective-permute-start | bytes 589832 | tf_op jit(solution)/shard_map/ppermute | solution.py:56
  41.9 15.4 %collective-permute-done.32.rest_2_ = bf16[48,1792]{1,0:T(8,128)(2,1)S(1)} collective-permute-done((bf16[48,1792]{1,0:T(8,128)(2,1)S(1)}, bf16[48,1792]{1,0:T(8,128)(2,1)S(1)}, u32[]{:S(2)}, u32[]{:S(2)}) %collective-permute-start.32) | collective-permute-done | bytes 172064 | tf_op jit(solution)/shard_map/ppermute | solution.py:56
  57.5 2.0 collective-permute-start.17
  60.1 12.8 %collective-permute-done.33.rest_3_ = bf16[48,1792]{1,0:T(8,128)(2,1)} collective-permute-done((bf16[48,1792]{1,0:T(8,128)(2,1)S(1)}, bf16[48,1792]{1,0:T(8,128)(2,1)}, u32[]{:S(2)}, u32[]{:S(2)}) %collective-permute-start.33) | collective-permute-done | bytes 172064 | tf_op jit(solution)/shard_map/ppermute | solution.py:56
  75.6 5.1 %collective-permute-done.20.rest_6_ = bf16[128,768]{1,0:T(8,128)(2,1)S(1)} collective-permute-done((bf16[128,768]{1,0:T(8,128)(2,1)S(1)}, bf16[128,768]{1,0:T(8,128)(2,1)S(1)}, u32[]{:S(2)}, u32[]{:S(2)}) %collective-permute-start.20) | collective-permute-done | bytes 196640 | tf_op jit(solution)/shard_map/ppermute | solution.py:56
  81.2 3.7 %collective-permute-done.19.rest_5_ = bf16[128,768]{1,0:T(8,128)(2,1)S(1)} collective-permute-done((bf16[128,768]{1,0:T(8,128)(2,1)S(1)}, bf16[128,768]{1,0:T(8,128)(2,1)S(1)}, u32[]{:S(2)}, u32[]{:S(2)}) %collective-permute-start.19) | collective-permute-done | bytes 196640 | tf_op jit(solution)/shard_map/ppermute | solution.py:56
  84.9 2.8 %collective-permute-done.21.rest_7_ = bf16[128,768]{1,0:T(8,128)(2,1)S(1)} collective-permute-done((bf16[128,768]{1,0:T(8,128)(2,1)S(1)}, bf16[128,768]{1,0:T(8,128)(2,1)S(1)}, u32[]{:S(2)}, u32[]{:S(2)}) %collective-permute-start.21) | collective-permute-done | bytes 196640 | tf_op jit(solution)/shard_map/ppermute | solution.py:56
  91.0 7.5 %shard_map.160 = (bf16[128,384]{1,0:T(8,128)(2,1)}, f32[8,256]{1,0:T(8,128)}, bf16[128,768]{1,0:T(8,128)(2,1)}) custom-call(s32[1]{0:T(128)} %bitcast.order_ref, bf16[128,384]{1,0:T(8,128)(2,1)} %get-tuple-element.62.q_ref, bf16[128,768]{1,0:T(8,128)(2,1)} %get-tuple-element.63.rest_0_, bf16[128,768]{1,0:T(8,128)(2,1)} %copy-done.22, ...), custom_call_target="tpu_custom_call" | custom-call | tf_op jit(solution)/shard_map/pallas_call | solution.py:459
  103.7 2.1 collective-permute-done.30.pb_ref
  106.5 5.4 %shard_map.161 = (f32[128,768]{1,0:T(8,128)}, bf16[128,768]{1,0:T(8,128)(2,1)}, bf16[128,768]{1,0:T(8,128)(2,1)}, bf16[128,768]{1,0:T(8,128)(2,1)}, bf16[128,1152]{1,0:T(8,128)(2,1)}, /*index=5*/bf16[128,576]{1,0:T(8,128)(2,1)}) custom-call(s32[1]{0:T(128)} %bitcast.order_ref, f32[128,768]{1,0:T(8,128)} %x_ref.5, bf16[128,768]{1,0:T(8,128)(2,1)} %get-tuple-element.66.pa_ref, ...), custom_call_target="tpu_custom_call" | custom-call | tf_op jit(solution)/shard_map/pallas_call | solution.py:459
  113.5 4.8 %collective-permute-done.46.db_ref = bf16[128,768]{1,0:T(8,128)(2,1)S(1)} collective-permute-done((bf16[128,768]{1,0:T(8,128)(2,1)}, bf16[128,768]{1,0:T(8,128)(2,1)S(1)}, u32[]{:S(2)}, u32[]{:S(2)}) %collective-permute-start.46) | collective-permute-done | bytes 196640 | tf_op jit(solution)/shard_map/ppermute | solution.py:56
  118.9 9.9 %shard_map.162 = (bf16[512,768]{1,0:T(8,128)(2,1)}, bf16[512,768]{1,0:T(8,128)(2,1)}, bf16[512,768]{1,0:T(8,128)(2,1)}, bf16[512,768]{1,0:T(8,128)(2,1)}, f32[128,768]{1,0:T(8,128)}, /*index=5*/bf16[128,384]{1,0:T(8,128)(2,1)}) custom-call(s32[1]{0:T(128)} %bitcast.order_ref, bf16[128,384]{1,0:T(8,128)(2,1)} %get-tuple-element.62.q_ref, ...), custom_call_target="tpu_custom_call" | custom-call | tf_op jit(solution)/shard_map/pallas_call | solution.py:459
  129.4 2.0 collective-permute-done.48.refs_1_
  132.3 2.3 pair_add.3
  137.6 5.0 %collective-permute-done.53.refs_2_ = bf16[128,768]{1,0:T(8,128)(2,1)S(1)} collective-permute-done((bf16[128,768]{1,0:T(8,128)(2,1)}, bf16[128,768]{1,0:T(8,128)(2,1)S(1)}, u32[]{:S(2)}, u32[]{:S(2)}) %collective-permute-start.53) | collective-permute-done | bytes 196640 | tf_op jit(solution)/shard_map/ppermute | solution.py:56
  143.2 1.9 shard_map.164
  145.7 3.7 %shard_map.171 = (bf16[192,1792]{1,0:T(8,128)(2,1)}, bf16[192,1792]{1,0:T(8,128)(2,1)}, bf16[192,1792]{1,0:T(8,128)(2,1)}, bf16[192,1792]{1,0:T(8,128)(2,1)}) custom-call(s32[1]{0:T(128)} %bitcast.order_ref, bf16[128,768]{1,0:T(8,128)(2,1)} %get-tuple-element.92.b_ref, bf16[128,1152]{1,0:T(8,128)(2,1)} %get-tuple-element.93.dz_ref, f32[128,768]{1,0:T(8,128)} %cot_ref.5, ...), custom_call_target="tpu_custom_call" | custom-call | tf_op jit(solution)/shard_map/pallas_call | solution.py:459
  151.1 1.9 shard_map.163
  155.8 2.0 shard_map.165
  160.2 9.6 %collective-permute-done.55.rest_4_ = bf16[128,768]{1,0:T(8,128)(2,1)S(1)} collective-permute-done((bf16[128,768]{1,0:T(8,128)(2,1)}, bf16[128,768]{1,0:T(8,128)(2,1)S(1)}, u32[]{:S(2)}, u32[]{:S(2)}) %collective-permute-start.55) | collective-permute-done | bytes 196640 | tf_op jit(solution)/shard_map/ppermute | solution.py:56
  170.5 5.4 %shard_map.166 = (bf16[192,1536]{1,0:T(8,128)(2,1)}, bf16[192,1536]{1,0:T(8,128)(2,1)}, bf16[192,1536]{1,0:T(8,128)(2,1)}, bf16[192,1536]{1,0:T(8,128)(2,1)}, bf16[128,768]{1,0:T(8,128)(2,1)}) custom-call(s32[1]{0:T(128)} %bitcast.order_ref, bf16[768,128]{1,0:T(8,128)(2,1)} %get-tuple-element.61.at_ref, bf16[128,384]{1,0:T(8,128)(2,1)} %get-tuple-element.70.dqp_ref, ...), custom_call_target="tpu_custom_call" | custom-call | tf_op jit(solution)/shard_map/pallas_call | solution.py:459
  177.3 2.2 pair_add.5
  182.6 4.4 %collective-permute-done.73.refs_2_ = bf16[48,1792]{1,0:T(8,128)(2,1)S(1)} collective-permute-done((bf16[48,1792]{1,0:T(8,128)(2,1)}, bf16[48,1792]{1,0:T(8,128)(2,1)S(1)}, u32[]{:S(2)}, u32[]{:S(2)}) %collective-permute-start.73) | collective-permute-done | bytes 172064 | tf_op jit(solution)/shard_map/ppermute | solution.py:56
  187.7 1.8 shard_map.173
  190.3 2.1 pair_add.4
  194.4 4.1 %collective-permute-done.64.refs_2_ = bf16[48,1536]{1,0:T(8,128)(2,1)S(1)} collective-permute-done((bf16[48,1536]{1,0:T(8,128)(2,1)}, bf16[48,1536]{1,0:T(8,128)(2,1)S(1)}, u32[]{:S(2)}, u32[]{:S(2)}) %collective-permute-start.64) | collective-permute-done | bytes 147488 | tf_op jit(solution)/shard_map/ppermute | solution.py:56
  199.6 1.8 shard_map.169
  201.4 2.1 collective-permute-start.65
  203.4 1.8 shard_map.172
  207.0 1.9 shard_map.174
  208.9 2.0 collective-permute-start.75
  210.9 1.6 collective-permute-start.57
  213.1 1.8 shard_map.168
  214.9 1.9 shard_map.170
  218.6 1.6 collective-permute-start.66
  220.3 1.7 collective-permute-done.60.rest_2_
  223.1 3.4 %collective-permute-done.66.rest_4_ = bf16[48,1536]{1,0:T(8,128)(2,1)S(1)} collective-permute-done((bf16[48,1536]{1,0:T(8,128)(2,1)}, bf16[48,1536]{1,0:T(8,128)(2,1)S(1)}, u32[]{:S(2)}, u32[]{:S(2)}) %collective-permute-start.66) | collective-permute-done | bytes 147488 | tf_op jit(solution)/shard_map/ppermute | solution.py:56
  227.2 2.8 %shard_map.175 = (f32[48,3264]{1,0:T(8,128)}, f32[2,48]{1,0:T(2,128)}) custom-call(f32[48,3264]{1,0:T(8,128)} %w_ref.5, bf16[192,1536]{1,0:T(8,128)(2,1)} %get-tuple-element.84.refs_0_.rest_0_, bf16[192,1536]{1,0:T(8,128)(2,1)} %copy-done.2, bf16[48,1536]{1,0:T(8,128)(2,1)} %copy-done.69, bf16[48,1536]{1,0:T(8,128)(2,1)} %copy-done.71, ...), custom_call_target="tpu_custom_call" | custom-call | tf_op jit(solution)/shard_map/pallas_call | solution.py:459
  233.5 2.7 %shard_map.167 = (f32[128,768]{1,0:T(8,128)}, f32[128,768]{1,0:T(8,128)}) custom-call(f32[128,768]{1,0:T(8,128)} %x_ref.5, bf16[128,768]{1,0:T(8,128)(2,1)} %get-tuple-element.80.da_ref, bf16[128,768]{1,0:T(8,128)(2,1)} %copy-done.47, f32[128,768]{1,0:T(8,128)} %get-tuple-element.71.dhid_ref, f32[8,768]{1,0:T(8,128)} %get-tuple-element.67.g_ref, ...), custom_call_target="tpu_custom_call" | custom-call | tf_op jit(solution)/shard_map/pallas_call | solution.py:459
  236.2 2.8 %adam.1 = (f32[48,3264]{1,0:T(8,128)}, f32[48,3264]{1,0:T(8,128)}, f32[48,3264]{1,0:T(8,128)}) custom-call(f32[48,3264]{1,0:T(8,128)} %w_ref.5, f32[48,3264]{1,0:T(8,128)} %get-tuple-element.53.g_ref, f32[48,3264]{1,0:T(8,128)} %m_ref.3, f32[48,3264]{1,0:T(8,128)} %v_ref.3), custom_call_target="tpu_custom_call" | custom-call | tf_op jit(solution)/shard_map/adam/pallas_call | solution.py:675
  (299 shorter events, 60.6 us)
Async XLA Ops:
  5.6 10.0 %collective-permute-start.1 = (bf16[48,1664]{1,0:T(8,128)(2,1)S(1)}, bf16[48,1664]{1,0:T(8,128)(2,1)S(1)}, u32[]{:S(2)}, u32[]{:S(2)}) collective-permute-start(bf16[48,1664]{1,0:T(8,128)(2,1)S(1)} %fusion.1.rest_0_.rest_16_.rest_5_), channel_id=1, source_target_pairs={{0,16},{8,24},{16,0},{24,8},{1,17},{9,25},{17,1},{25,9},{2,18},{10... | collective-permute-start | bytes 479240 | tf_op jit(solution)/shard_map/ppermute | solution.py:56
  8.2 8.8 %collective-permute-start = (bf16[48,1664]{1,0:T(8,128)(2,1)S(1)}, bf16[48,1664]{1,0:T(8,128)(2,1)S(1)}, u32[]{:S(2)}, u32[]{:S(2)}) collective-permute-start(bf16[48,1664]{1,0:T(8,128)(2,1)S(1)} %fusion.1.rest_0_.rest_16_.rest_5_), channel_id=1, source_target_pairs={{0,8},{8,0},{16,24},{24,16},{1,9},{9,1},{17,25},{25,17},{2,10},{10... | collective-permute-start | bytes 479240 | tf_op jit(solution)/shard_map/ppermute | solution.py:56
  17.1 9.6 %collective-permute-start.4 = (bf16[48,1664]{1,0:T(8,128)(2,1)S(1)}, bf16[48,1664]{1,0:T(8,128)(2,1)S(1)}, u32[]{:S(2)}, u32[]{:S(2)}) collective-permute-start(bf16[48,1664]{1,0:T(8,128)(2,1)S(1)} %collective-permute-done.rest_1_.rest_17_.rest_6_), channel_id=1, source_target_pairs={{0,4},{2,6},{4,0},{6,2},{1,5},{3,7},{5,1},{7,3},{8,12},{10,14},{12... | collective-permute-start | bytes 479240 | tf_op jit(solution)/shard_map/ppermute | solution.py:56
  20.9 9.2 %collective-permute-start.6 = (bf16[48,1664]{1,0:T(8,128)(2,1)S(1)}, bf16[48,1664]{1,0:T(8,128)(2,1)S(1)}, u32[]{:S(2)}, u32[]{:S(2)}) collective-permute-start(bf16[48,1664]{1,0:T(8,128)(2,1)S(1)} %collective-permute-done.2.rest_3_.rest_19_.rest_8_), channel_id=1, source_target_pairs={{0,4},{2,6},{4,0},{6,2},{1,5},{3,7},{5,1},{7,3},{8,12},{10,14},{12... | collective-permute-start | bytes 479240 | tf_op jit(solution)/shard_map/ppermute | solution.py:56
  21.5 19.8 %collective-permute-start.34 = (bf16[48,1792]{1,0:T(8,128)(2,1)S(1)}, bf16[48,1792]{1,0:T(8,128)(2,1)S(1)}, u32[]{:S(2)}, u32[]{:S(2)}) collective-permute-start(bf16[48,1792]{1,0:T(8,128)(2,1)S(1)} %pad.9.rest_0_), channel_id=1, source_target_pairs={{0,4},{2,6},{4,0},{6,2},{1,5},{3,7},{5,1},{7,3},{8,12},{10,14},{12... | collective-permute-start | bytes 516104 | tf_op jit(solution)/shard_map/ppermute | solution.py:56
  23.3 8.6 %collective-permute-start.10 = (bf16[48,1664]{1,0:T(8,128)(2,1)S(1)}, bf16[48,1664]{1,0:T(8,128)(2,1)S(1)}, u32[]{:S(2)}, u32[]{:S(2)}) collective-permute-start(bf16[48,1664]{1,0:T(8,128)(2,1)S(1)} %collective-permute-done.2.rest_3_.rest_19_.rest_8_), channel_id=1, source_target_pairs={{0,2},{2,0},{4,6},{6,4},{1,3},{3,1},{5,7},{7,5},{8,10},{10,8},{12,... | collective-permute-start | bytes 479240 | tf_op jit(solution)/shard_map/ppermute | solution.py:56
  31.3 10.1 %collective-permute-start.38 = (bf16[48,1792]{1,0:T(8,128)(2,1)S(1)}, bf16[48,1792]{1,0:T(8,128)(2,1)S(1)}, u32[]{:S(2)}, u32[]{:S(2)}) collective-permute-start(bf16[48,1792]{1,0:T(8,128)(2,1)S(1)} %pad.9.rest_0_), channel_id=1, source_target_pairs={{0,2},{2,0},{4,6},{6,4},{1,3},{3,1},{5,7},{7,5},{8,10},{10,8},{12,... | collective-permute-start | bytes 516104 | tf_op jit(solution)/shard_map/ppermute | solution.py:56
  37.0 20.5 %collective-permute-start.16 = (bf16[128,768]{1,0:T(8,128)(2,1)}, bf16[128,768]{1,0:T(8,128)(2,1)S(1)}, u32[]{:S(2)}, u32[]{:S(2)}) collective-permute-start(bf16[128,768]{1,0:T(8,128)(2,1)} %get-tuple-element.63.rest_0_), channel_id=1, source_target_pairs={{0,16},{8,24},{16,0},{24,8},{1,17},{9,25},{17,1},{25,9},{2,18},{10... | collective-permute-start | bytes 589832 | tf_op jit(solution)/shard_map/ppermute | solution.py:56
  40.5 16.9 %collective-permute-start.32 = (bf16[48,1792]{1,0:T(8,128)(2,1)S(1)}, bf16[48,1792]{1,0:T(8,128)(2,1)S(1)}, u32[]{:S(2)}, u32[]{:S(2)}) collective-permute-start(bf16[48,1792]{1,0:T(8,128)(2,1)S(1)} %pad.9.rest_0_), channel_id=1, source_target_pairs={{0,16},{8,24},{16,0},{24,8},{1,17},{9,25},{17,1},{25,9},{2,18},{10... | collective-permute-start | bytes 516104 | tf_op jit(solution)/shard_map/ppermute | solution.py:56
  40.5 16.8 %collective-permute-start.31 = (bf16[48,1792]{1,0:T(8,128)(2,1)S(1)}, bf16[48,1792]{1,0:T(8,128)(2,1)}, u32[]{:S(2)}, u32[]{:S(2)}) collective-permute-start(bf16[48,1792]{1,0:T(8,128)(2,1)S(1)} %pad.9.rest_0_), channel_id=1, source_target_pairs={{0,8},{8,0},{16,24},{24,16},{1,9},{9,1},{17,25},{25,17},{2,10},{10... | collective-permute-start | bytes 516104 | tf_op jit(solution)/shard_map/ppermute | solution.py:56
  41.4 18.1 %collective-permute-start.42 = (bf16[48,1792]{1,0:T(8,128)(2,1)S(1)}, bf16[48,1792]{1,0:T(8,128)(2,1)S(1)}, u32[]{:S(2)}, u32[]{:S(2)}) collective-permute-start(bf16[48,1792]{1,0:T(8,128)(2,1)S(1)} %collective-permute-done.34.rest_4_), channel_id=1, source_target_pairs={{0,2},{2,0},{4,6},{6,4},{1,3},{3,1},{5,7},{7,5},{8,10},{10,8},{12,... | collective-permute-start | bytes 516104 | tf_op jit(solution)/shard_map/ppermute | solution.py:56
  41.4 18.7 %collective-permute-start.18 = (bf16[128,768]{1,0:T(8,128)(2,1)}, bf16[128,768]{1,0:T(8,128)(2,1)S(1)}, u32[]{:S(2)}, u32[]{:S(2)}) collective-permute-start(bf16[128,768]{1,0:T(8,128)(2,1)} %get-tuple-element.63.rest_0_), channel_id=1, source_target_pairs={{0,4},{2,6},{4,0},{6,2},{1,5},{3,7},{5,1},{7,3},{8,12},{10,14},{12... | collective-permute-start | bytes 589832 | tf_op jit(solution)/shard_map/ppermute | solution.py:56
  57.4 16.1 %collective-permute-start.22 = (bf16[128,768]{1,0:T(8,128)(2,1)}, bf16[128,768]{1,0:T(8,128)(2,1)S(1)}, u32[]{:S(2)}, u32[]{:S(2)}) collective-permute-start(bf16[128,768]{1,0:T(8,128)(2,1)} %get-tuple-element.63.rest_0_), channel_id=1, source_target_pairs={{0,2},{2,0},{4,6},{6,4},{1,3},{3,1},{5,7},{7,5},{8,10},{10,8},{12,... | collective-permute-start | bytes 589832 | tf_op jit(solution)/shard_map/ppermute | solution.py:56
  57.4 16.1 %collective-permute-start.15 = (bf16[128,768]{1,0:T(8,128)(2,1)}, bf16[128,768]{1,0:T(8,128)(2,1)S(1)}, u32[]{:S(2)}, u32[]{:S(2)}) collective-permute-start(bf16[128,768]{1,0:T(8,128)(2,1)} %get-tuple-element.63.rest_0_), channel_id=1, source_target_pairs={{0,8},{8,0},{16,24},{24,16},{1,9},{9,1},{17,25},{25,17},{2,10},{10... | collective-permute-start | bytes 589832 | tf_op jit(solution)/shard_map/ppermute | solution.py:56
  57.5 17.6 %collective-permute-start.17 = (bf16[128,768]{1,0:T(8,128)(2,1)S(1)}, bf16[128,768]{1,0:T(8,128)(2,1)S(1)}, u32[]{:S(2)}, u32[]{:S(2)}) collective-permute-start(bf16[128,768]{1,0:T(8,128)(2,1)S(1)} %collective-permute-done.16.rest_2_), channel_id=1, source_target_pairs={{0,8},{8,0},{16,24},{24,16},{1,9},{9,1},{17,25},{25,17},{2,10},{10... | collective-permute-start | bytes 589832 | tf_op jit(solution)/shard_map/ppermute | solution.py:56
  59.5 13.4 %collective-permute-start.33 = (bf16[48,1792]{1,0:T(8,128)(2,1)S(1)}, bf16[48,1792]{1,0:T(8,128)(2,1)}, u32[]{:S(2)}, u32[]{:S(2)}) collective-permute-start(bf16[48,1792]{1,0:T(8,128)(2,1)S(1)} %collective-permute-done.32.rest_2_), channel_id=1, source_target_pairs={{0,8},{8,0},{16,24},{24,16},{1,9},{9,1},{17,25},{25,17},{2,10},{10... | collective-permute-start | bytes 516104 | tf_op jit(solution)/shard_map/ppermute | solution.py:56
  60.1 15.4 %collective-permute-start.26 = (bf16[128,768]{1,0:T(8,128)(2,1)S(1)}, bf16[128,768]{1,0:T(8,128)(2,1)S(1)}, u32[]{:S(2)}, u32[]{:S(2)}) collective-permute-start(bf16[128,768]{1,0:T(8,128)(2,1)S(1)} %collective-permute-done.18.rest_4_), channel_id=1, source_target_pairs={{0,2},{2,0},{4,6},{6,4},{1,3},{3,1},{5,7},{7,5},{8,10},{10,8},{12,... | collective-permute-start | bytes 589832 | tf_op jit(solution)/shard_map/ppermute | solution.py:56
  73.5 11.4 %collective-permute-start.19 = (bf16[128,768]{1,0:T(8,128)(2,1)S(1)}, bf16[128,768]{1,0:T(8,128)(2,1)S(1)}, u32[]{:S(2)}, u32[]{:S(2)}) collective-permute-start(bf16[128,768]{1,0:T(8,128)(2,1)S(1)} %collective-permute-done.15.rest_1_), channel_id=1, source_target_pairs={{0,4},{2,6},{4,0},{6,2},{1,5},{3,7},{5,1},{7,3},{8,12},{10,14},{12... | collective-permute-start | bytes 589832 | tf_op jit(solution)/shard_map/ppermute | solution.py:56
  75.0 12.7 %collective-permute-start.21 = (bf16[128,768]{1,0:T(8,128)(2,1)S(1)}, bf16[128,768]{1,0:T(8,128)(2,1)S(1)}, u32[]{:S(2)}, u32[]{:S(2)}) collective-permute-start(bf16[128,768]{1,0:T(8,128)(2,1)S(1)} %collective-permute-done.17.rest_3_), channel_id=1, source_target_pairs={{0,4},{2,6},{4,0},{6,2},{1,5},{3,7},{5,1},{7,3},{8,12},{10,14},{12... | collective-permute-start | bytes 589832 | tf_op jit(solution)/shard_map/ppermute | solution.py:56
  75.6 12.2 %collective-permute-start.23 = (bf16[128,768]{1,0:T(8,128)(2,1)S(1)}, bf16[128,768]{1,0:T(8,128)(2,1)S(1)}, u32[]{:S(2)}, u32[]{:S(2)}) collective-permute-start(bf16[128,768]{1,0:T(8,128)(2,1)S(1)} %collective-permute-done.15.rest_1_), channel_id=1, source_target_pairs={{0,2},{2,0},{4,6},{6,4},{1,3},{3,1},{5,7},{7,5},{8,10},{10,8},{12,... | collective-permute-start | bytes 589832 | tf_op jit(solution)/shard_map/ppermute | solution.py:56
  80.7 8.1 %collective-permute-start.25 = (bf16[128,768]{1,0:T(8,128)(2,1)S(1)}, bf16[128,768]{1,0:T(8,128)(2,1)S(1)}, u32[]{:S(2)}, u32[]{:S(2)}) collective-permute-start(bf16[128,768]{1,0:T(8,128)(2,1)S(1)} %collective-permute-done.17.rest_3_), channel_id=1, source_target_pairs={{0,2},{2,0},{4,6},{6,4},{1,3},{3,1},{5,7},{7,5},{8,10},{10,8},{12,... | collective-permute-start | bytes 589832 | tf_op jit(solution)/shard_map/ppermute | solution.py:56
  87.7 10.9 %collective-permute-start.40 = (bf16[48,1792]{1,0:T(8,128)(2,1)S(1)}, bf16[48,1792]{1,0:T(8,128)(2,1)}, u32[]{:S(2)}, u32[]{:S(2)}) collective-permute-start(bf16[48,1792]{1,0:T(8,128)(2,1)S(1)} %collective-permute-done.32.rest_2_), channel_id=1, source_target_pairs={{0,2},{2,0},{4,6},{6,4},{1,3},{3,1},{5,7},{7,5},{8,10},{10,8},{12,... | collective-permute-start | bytes 516104 | tf_op jit(solution)/shard_map/ppermute | solution.py:56
  88.2 12.0 %collective-permute-start.36 = (bf16[48,1792]{1,0:T(8,128)(2,1)S(1)}, bf16[48,1792]{1,0:T(8,128)(2,1)}, u32[]{:S(2)}, u32[]{:S(2)}) collective-permute-start(bf16[48,1792]{1,0:T(8,128)(2,1)S(1)} %collective-permute-done.32.rest_2_), channel_id=1, source_target_pairs={{0,4},{2,6},{4,0},{6,2},{1,5},{3,7},{5,1},{7,3},{8,12},{10,14},{12... | collective-permute-start | bytes 516104 | tf_op jit(solution)/shard_map/ppermute | solution.py:56
  88.8 11.5 %collective-permute-start.39 = (bf16[48,1792]{1,0:T(8,128)(2,1)}, bf16[48,1792]{1,0:T(8,128)(2,1)}, u32[]{:S(2)}, u32[]{:S(2)}) collective-permute-start(bf16[48,1792]{1,0:T(8,128)(2,1)} %collective-permute-done.31.rest_1_), channel_id=1, source_target_pairs={{0,2},{2,0},{4,6},{6,4},{1,3},{3,1},{5,7},{7,5},{8,10},{10,8},{12,... | collective-permute-start | bytes 516104 | tf_op jit(solution)/shard_map/ppermute | solution.py:56
  88.8 12.0 %collective-permute-start.35 = (bf16[48,1792]{1,0:T(8,128)(2,1)}, bf16[48,1792]{1,0:T(8,128)(2,1)}, u32[]{:S(2)}, u32[]{:S(2)}) collective-permute-start(bf16[48,1792]{1,0:T(8,128)(2,1)} %collective-permute-done.31.rest_1_), channel_id=1, source_target_pairs={{0,4},{2,6},{4,0},{6,2},{1,5},{3,7},{5,1},{7,3},{8,12},{10,14},{12... | collective-permute-start | bytes 516104 | tf_op jit(solution)/shard_map/ppermute | solution.py:56
  90.4 11.7 %collective-permute-start.37 = (bf16[48,1792]{1,0:T(8,128)(2,1)}, bf16[48,1792]{1,0:T(8,128)(2,1)}, u32[]{:S(2)}, u32[]{:S(2)}) collective-permute-start(bf16[48,1792]{1,0:T(8,128)(2,1)} %collective-permute-done.33.rest_3_), channel_id=1, source_target_pairs={{0,4},{2,6},{4,0},{6,2},{1,5},{3,7},{5,1},{7,3},{8,12},{10,14},{12... | collective-permute-start | bytes 516104 | tf_op jit(solution)/shard_map/ppermute | solution.py:56
  128.9 8.7 %collective-permute-start.47 = (bf16[512,768]{1,0:T(8,128)(2,1)}, bf16[512,768]{1,0:T(8,128)(2,1)S(1)}, u32[]{:S(2)}, u32[]{:S(2)}) collective-permute-start(bf16[512,768]{1,0:T(8,128)(2,1)} %get-tuple-element.73), channel_id=1, source_target_pairs={{0,2},{2,0},{4,6},{6,4},{1,3},{3,1},{5,7},{7,5},{8,10},{10,8},{12,... | collective-permute-start | bytes 2359304 | tf_op jit(solution)/shard_map/ppermute | solution.py:56
  135.6 14.9 %collective-permute-start.50 = (bf16[128,768]{1,0:T(8,128)(2,1)}, bf16[128,768]{1,0:T(8,128)(2,1)S(1)}, u32[]{:S(2)}, u32[]{:S(2)}) collective-permute-start(bf16[128,768]{1,0:T(8,128)(2,1)} %get-tuple-element.77), channel_id=1, source_target_pairs={{0,4},{2,6},{4,0},{6,2},{1,5},{3,7},{5,1},{7,3},{8,12},{10,14},{12... | collective-permute-start | bytes 589832 | tf_op jit(solution)/shard_map/ppermute | solution.py:56
  136.6 17.9 %collective-permute-start.52 = (bf16[128,768]{1,0:T(8,128)(2,1)}, bf16[128,768]{1,0:T(8,128)(2,1)S(1)}, u32[]{:S(2)}, u32[]{:S(2)}) collective-permute-start(bf16[128,768]{1,0:T(8,128)(2,1)} %get-tuple-element.78), channel_id=1, source_target_pairs={{0,4},{2,6},{4,0},{6,2},{1,5},{3,7},{5,1},{7,3},{8,12},{10,14},{12... | collective-permute-start | bytes 589832 | tf_op jit(solution)/shard_map/ppermute | solution.py:56
  145.1 9.4 %collective-permute-start.54 = (bf16[128,768]{1,0:T(8,128)(2,1)}, bf16[128,768]{1,0:T(8,128)(2,1)S(1)}, u32[]{:S(2)}, u32[]{:S(2)}) collective-permute-start(bf16[128,768]{1,0:T(8,128)(2,1)} %shard_map.164), channel_id=1, source_target_pairs={{0,8},{8,0},{16,24},{24,16},{1,9},{9,1},{17,25},{25,17},{2,10},{10... | collective-permute-start | bytes 589832 | tf_op jit(solution)/shard_map/ppermute | solution.py:56
  149.4 27.1 %collective-permute-start.68 = (bf16[192,1792]{1,0:T(8,128)(2,1)}, bf16[192,1792]{1,0:T(8,128)(2,1)S(1)}, u32[]{:S(2)}, u32[]{:S(2)}) collective-permute-start(bf16[192,1792]{1,0:T(8,128)(2,1)} %get-tuple-element.98), channel_id=1, source_target_pairs={{0,2},{2,0},{4,6},{6,4},{1,3},{3,1},{5,7},{7,5},{8,10},{10,8},{12,... | collective-permute-start | bytes 2064392 | tf_op jit(solution)/shard_map/ppermute | solution.py:56
  149.4 9.6 %collective-permute-start.49 = (bf16[128,768]{1,0:T(8,128)(2,1)S(1)}, bf16[128,768]{1,0:T(8,128)(2,1)S(1)}, u32[]{:S(2)}, u32[]{:S(2)}) collective-permute-start(bf16[128,768]{1,0:T(8,128)(2,1)S(1)} %copy-done.77), channel_id=1, source_target_pairs={{0,4},{2,6},{4,0},{6,2},{1,5},{3,7},{5,1},{7,3},{8,12},{10,14},{12... | collective-permute-start | bytes 589832 | tf_op jit(solution)/shard_map/ppermute | solution.py:56
  157.8 12.0 %collective-permute-start.55 = (bf16[128,768]{1,0:T(8,128)(2,1)}, bf16[128,768]{1,0:T(8,128)(2,1)S(1)}, u32[]{:S(2)}, u32[]{:S(2)}) collective-permute-start(bf16[128,768]{1,0:T(8,128)(2,1)} %shard_map.165), channel_id=1, source_target_pairs={{0,16},{8,24},{16,0},{24,8},{1,17},{9,25},{17,1},{25,9},{2,18},{10... | collective-permute-start | bytes 589832 | tf_op jit(solution)/shard_map/ppermute | solution.py:56
  159.0 22.6 %collective-permute-start.67 = (bf16[192,1792]{1,0:T(8,128)(2,1)S(1)}, bf16[192,1792]{1,0:T(8,128)(2,1)S(1)}, u32[]{:S(2)}, u32[]{:S(2)}) collective-permute-start(bf16[192,1792]{1,0:T(8,128)(2,1)S(1)} %copy-done.76), channel_id=1, source_target_pairs={{0,2},{2,0},{4,6},{6,4},{1,3},{3,1},{5,7},{7,5},{8,10},{10,8},{12,... | collective-permute-start | bytes 2064392 | tf_op jit(solution)/shard_map/ppermute | solution.py:56
  175.9 13.6 %collective-permute-start.59 = (bf16[192,1536]{1,0:T(8,128)(2,1)}, bf16[192,1536]{1,0:T(8,128)(2,1)S(1)}, u32[]{:S(2)}, u32[]{:S(2)}) collective-permute-start(bf16[192,1536]{1,0:T(8,128)(2,1)} %get-tuple-element.87), channel_id=1, source_target_pairs={{0,2},{2,0},{4,6},{6,4},{1,3},{3,1},{5,7},{7,5},{8,10},{10,8},{12,... | collective-permute-start | bytes 1769480 | tf_op jit(solution)/shard_map/ppermute | solution.py:56
  176.0 17.5 %collective-permute-start.58 = (bf16[192,1536]{1,0:T(8,128)(2,1)}, bf16[192,1536]{1,0:T(8,128)(2,1)S(1)}, u32[]{:S(2)}, u32[]{:S(2)}) collective-permute-start(bf16[192,1536]{1,0:T(8,128)(2,1)} %get-tuple-element.85), channel_id=1, source_target_pairs={{0,2},{2,0},{4,6},{6,4},{1,3},{3,1},{5,7},{7,5},{8,10},{10,8},{12,... | collective-permute-start | bytes 1769480 | tf_op jit(solution)/shard_map/ppermute | solution.py:56
  180.6 20.8 %collective-permute-start.70 = (bf16[48,1792]{1,0:T(8,128)(2,1)}, bf16[48,1792]{1,0:T(8,128)(2,1)S(1)}, u32[]{:S(2)}, u32[]{:S(2)}) collective-permute-start(bf16[48,1792]{1,0:T(8,128)(2,1)} %get-tuple-element.100), channel_id=1, source_target_pairs={{0,4},{2,6},{4,0},{6,2},{1,5},{3,7},{5,1},{7,3},{8,12},{10,14},{12... | collective-permute-start | bytes 516104 | tf_op jit(solution)/shard_map/ppermute | solution.py:56
  181.6 23.7 %collective-permute-start.72 = (bf16[48,1792]{1,0:T(8,128)(2,1)}, bf16[48,1792]{1,0:T(8,128)(2,1)S(1)}, u32[]{:S(2)}, u32[]{:S(2)}) collective-permute-start(bf16[48,1792]{1,0:T(8,128)(2,1)} %get-tuple-element.101), channel_id=1, source_target_pairs={{0,4},{2,6},{4,0},{6,2},{1,5},{3,7},{5,1},{7,3},{8,12},{10,14},{12... | collective-permute-start | bytes 516104 | tf_op jit(solution)/shard_map/ppermute | solution.py:56
  189.5 16.9 %collective-permute-start.74 = (bf16[48,1792]{1,0:T(8,128)(2,1)}, bf16[48,1792]{1,0:T(8,128)(2,1)S(1)}, u32[]{:S(2)}, u32[]{:S(2)}) collective-permute-start(bf16[48,1792]{1,0:T(8,128)(2,1)} %shard_map.173), channel_id=1, source_target_pairs={{0,8},{8,0},{16,24},{24,16},{1,9},{9,1},{17,25},{25,17},{2,10},{10... | collective-permute-start | bytes 516104 | tf_op jit(solution)/shard_map/ppermute | solution.py:56
  193.5 15.5 %collective-permute-start.61 = (bf16[48,1536]{1,0:T(8,128)(2,1)}, bf16[48,1536]{1,0:T(8,128)(2,1)S(1)}, u32[]{:S(2)}, u32[]{:S(2)}) collective-permute-start(bf16[48,1536]{1,0:T(8,128)(2,1)} %get-tuple-element.89), channel_id=1, source_target_pairs={{0,4},{2,6},{4,0},{6,2},{1,5},{3,7},{5,1},{7,3},{8,12},{10,14},{12... | collective-permute-start | bytes 442376 | tf_op jit(solution)/shard_map/ppermute | solution.py:56
  198.6 12.4 %collective-permute-start.63 = (bf16[48,1536]{1,0:T(8,128)(2,1)}, bf16[48,1536]{1,0:T(8,128)(2,1)S(1)}, u32[]{:S(2)}, u32[]{:S(2)}) collective-permute-start(bf16[48,1536]{1,0:T(8,128)(2,1)} %get-tuple-element.90), channel_id=1, source_target_pairs={{0,4},{2,6},{4,0},{6,2},{1,5},{3,7},{5,1},{7,3},{8,12},{10,14},{12... | collective-permute-start | bytes 442376 | tf_op jit(solution)/shard_map/ppermute | solution.py:56
  201.4 11.2 %collective-permute-start.65 = (bf16[48,1536]{1,0:T(8,128)(2,1)}, bf16[48,1536]{1,0:T(8,128)(2,1)S(1)}, u32[]{:S(2)}, u32[]{:S(2)}) collective-permute-start(bf16[48,1536]{1,0:T(8,128)(2,1)} %shard_map.169), channel_id=1, source_target_pairs={{0,8},{8,0},{16,24},{24,16},{1,9},{9,1},{17,25},{25,17},{2,10},{10... | collective-permute-start | bytes 442376 | tf_op jit(solution)/shard_map/ppermute | solution.py:56
  205.3 11.5 %collective-permute-start.69 = (bf16[48,1792]{1,0:T(8,128)(2,1)S(1)}, bf16[48,1792]{1,0:T(8,128)(2,1)S(1)}, u32[]{:S(2)}, u32[]{:S(2)}) collective-permute-start(bf16[48,1792]{1,0:T(8,128)(2,1)S(1)} %copy-done.78), channel_id=1, source_target_pairs={{0,4},{2,6},{4,0},{6,2},{1,5},{3,7},{5,1},{7,3},{8,12},{10,14},{12... | collective-permute-start | bytes 516104 | tf_op jit(solution)/shard_map/ppermute | solution.py:56
  206.4 11.6 %collective-permute-start.71 = (bf16[48,1792]{1,0:T(8,128)(2,1)}, bf16[48,1792]{1,0:T(8,128)(2,1)S(1)}, u32[]{:S(2)}, u32[]{:S(2)}) collective-permute-start(bf16[48,1792]{1,0:T(8,128)(2,1)} %shard_map.172), channel_id=1, source_target_pairs={{0,8},{8,0},{16,24},{24,16},{1,9},{9,1},{17,25},{25,17},{2,10},{10... | collective-permute-start | bytes 516104 | tf_op jit(solution)/shard_map/ppermute | solution.py:56
  208.9 9.7 %collective-permute-start.75 = (bf16[48,1792]{1,0:T(8,128)(2,1)}, bf16[48,1792]{1,0:T(8,128)(2,1)S(1)}, u32[]{:S(2)}, u32[]{:S(2)}) collective-permute-start(bf16[48,1792]{1,0:T(8,128)(2,1)} %shard_map.174), channel_id=1, source_target_pairs={{0,16},{8,24},{16,0},{24,8},{1,17},{9,25},{17,1},{25,9},{2,18},{10... | collective-permute-start | bytes 516104 | tf_op jit(solution)/shard_map/ppermute | solution.py:56
  210.9 21.2 %collective-permute-start.57 = (bf16[128,768]{1,0:T(8,128)(2,1)S(1)}, bf16[128,768]{1,0:T(8,128)(2,1)S(1)}, u32[]{:S(2)}, u32[]{:S(2)}) collective-permute-start(bf16[128,768]{1,0:T(8,128)(2,1)S(1)} %copy-done.44), channel_id=1, source_target_pairs={{0,1},{1,0},{2,3},{3,2},{4,5},{5,4},{6,7},{7,6},{8,9},{9,8},{10,11... | collective-permute-start | bytes 589832 | tf_op jit(solution)/shard_map/ppermute | solution.py:56
  212.5 19.6 %collective-permute-start.56 = (bf16[128,768]{1,0:T(8,128)(2,1)S(1)}, bf16[128,768]{1,0:T(8,128)(2,1)S(1)}, u32[]{:S(2)}, u32[]{:S(2)}) collective-permute-start(bf16[128,768]{1,0:T(8,128)(2,1)S(1)} %copy-done.45), channel_id=1, source_target_pairs={{0,1},{1,0},{2,3},{3,2},{4,5},{5,4},{6,7},{7,6},{8,9},{9,8},{10,11... | collective-permute-start | bytes 589832 | tf_op jit(solution)/shard_map/ppermute | solution.py:56
  230.6 8.4 %collective-permute-start.76 = (f32[2,48]{1,0:T(2,128)S(1)}, f32[2,48]{1,0:T(2,128)S(1)}, u32[]{:S(2)}, u32[]{:S(2)}) collective-permute-start(f32[2,48]{1,0:T(2,128)S(1)} %copy-done.74), channel_id=1, source_target_pairs={{0,1},{1,0},{2,3},{3,2},{4,5},{5,4},{6,7},{7,6},{8,9},{9,8},{10,11... | collective-permute-start | bytes 1160 | tf_op jit(solution)/shard_map/ppermute | solution.py:56
  (109 other events, 787.3 us)

commit v5 on v4

--- a/solution.py
+++ b/solution.py
@@ -79,16 +79,41 @@
     return [got[j] for j in chunk_order()]
 
 
-def add_kernel(*refs):
-    keep, recv = refs[0], refs[1]
-    for i, out in enumerate(refs[2:]):
-        rows = out.shape[0]
-        at = pl.ds(i * rows, rows)
-        out[...] = (keep[at, :].astype(F32) + recv[at, :].astype(F32)).astype(BF16)
-
-
-def block_kernel(*refs):
-    refs[-1][...] = total([ref[...] for ref in refs[:-1]]).astype(BF16)
+def add_kernel(keep, recv, *rest):
+    outs = rest[:4]
+    kept, got, done, sems = rest[4:]
+    rows = outs[0].shape[0]
+    at = [pl.ds(i * rows, rows) for i in range(4)]
+    loads = [
+        [
+            pltpu.make_async_copy(src.at[at[i], :], dst.at[at[i], :], sems.at[k, i])
+            for k, (src, dst) in enumerate(((keep, kept), (recv, got)))
+        ]
+        for i in range(4)
+    ]
+    stores = [pltpu.make_async_copy(done.at[at[i], :], outs[i], sems.at[2, i]) for i in range(4)]
+    for pair in loads:
+        for copy in pair:
+            copy.start()
+    for i in range(4):
+        for copy in loads[i]:
+            copy.wait()
+        done[at[i], :] = (kept[at[i], :].astype(F32) + got[at[i], :].astype(F32)).astype(BF16)
+        stores[i].start()
+    for copy in stores:
+        copy.wait()
+
+
+def pair_add(keep, recv):
+    rows, cols = keep.shape[0] // 4, keep.shape[1]
+    return pl.pallas_call(
+        add_kernel,
+        out_shape=[sds((rows, cols), BF16)] * 4,
+        in_specs=[ANY, ANY],
+        out_specs=[ANY] * 4,
+        scratch_shapes=[pltpu.VMEM(keep.shape, BF16)] * 3 + [pltpu.SemaphoreType.DMA((3, 4))],
+        name="pair_add",
+    )(keep, recv)
 
 
 def native_sum(part):
@@ -100,37 +125,17 @@
 
 
 def scatter_sum(groups, recv):
-    keep = groups[0]
-    rows, cols = keep.shape[0] // 4, keep.shape[1]
-    s = pl.pallas_call(
-        add_kernel,
-        out_shape=[sds((rows, cols), BF16)] * 4,
-        in_specs=[VM, VM],
-        out_specs=[VM] * 4,
-        name="pair_add",
-    )(groups[1], recv[1])
+    s = pair_add(groups[1], recv[1])
     got = {z: swap(s[z], "shard", 2) for z in (3, 2, 1, 0)}
+    keep = pair_add(groups[0], recv[0])
 
     def block(z, *more):
-        head = pl.BlockSpec((rows, cols), lambda i: (z, 0))
-        return call(
-            block_kernel,
-            [sds((rows, cols), BF16)],
-            [head, head] + [VM] * (1 + len(more)),
-            [],
-            [keep, recv[0], got[z], *more],
-        )[0]
+        return total([keep[z], got[z], *more]).astype(BF16)
 
     far = swap(block(3), "blk", 1)
     two = swap(block(2, far), "blk", 2)
     one = swap(block(1), "blk", 1)
-    return [keep, recv[0], got[0], one, two]
-
-
-def term_specs(terms):
-    shape = terms[-1].shape
-    head = pl.BlockSpec(shape, lambda i: (0, 0))
-    return [VM if term.shape == shape else head for term in terms]
+    return [keep[0], got[0], one, two]
 
 
 def total(terms):
@@ -462,7 +467,6 @@
         in_specs=specs,
         out_specs=jax.tree.map(lambda _: VM, out_shape),
         scratch_shapes=scratch,
-        grid=(1,) if any(spec.block_shape for spec in specs) else (),
     )(*args)
 
 
@@ -645,7 +649,7 @@
     *w_groups, da_part = call(
         partial(qkv_grad_kernel, nw, nt, parts),
         [sds((d // parts, 4 * width), BF16)] * parts + [sds((toks, d), BF16)],
-        [SM] + [VM] * 6 + term_specs(kv_terms) + [ANY] * nw,
+        [SM] + [VM] * 6 + [VM] * nt + [ANY] * nw,
         [pltpu.VMEM((d, 3 * width), BF16), pltpu.VMEM((d, toks), BF16), wsem],
         [order, a_t, dqp, dhid, attn, cos, sin] + kv_terms + first_chunks,
     )
@@ -665,7 +669,7 @@
     weight_grad, gain_part = call(
         partial(gsum_kernel, nt, width, units),
         [sds(full, F32), sds(gains.shape, F32)],
-        [VM] + term_specs(first_terms) + term_specs(ffn_terms),
+        [VM] * (1 + 2 * nt),
         [],
         [weights] + first_terms + ffn_terms,
     )

time: 242 us -> 226 us (0.934)
  Pallas kernels: 69.2 us -> 59.2 us
  waiting for transfers between devices: 96.8 us -> 91.2 us
    pallas_call x18 -> x9, Pallas kernels: 59.7 us -> 42.9 us  [call(): pl.pallas_call(kernel, out_shape=out_shape, in_specs=specs, out_specs=jax...]
    pallas_call x3 -> x6, Pallas kernels: 6.59 us -> 13.5 us  [pair_add(): pl.pallas_call(add_kernel, out_shape=[sds((rows, cols), BF16)] * 4, in_sp...]
    ppermute x77, waiting for transfers between devices: 96.8 us -> 91.2 us  [swap(): return lax.ppermute(x, axis, [(i, i ^ bits) for i in range(size)])]
    unnamed x160 -> x158, local copies, waits for them, and re-layouts: 12.8 us -> 10.7 us
  transfers between devices with their start and end apart: 77 -> 77, of which waited for: 25 -> 27; matrix products, arithmetic and copies ran while one was open for 0% -> 2% of each run, Pallas kernels for 22% -> 19%
where the time goes in v5:
time: 226 us
  waiting for transfers between devices  91.2 us (40%)
  Pallas kernels  59.2 us (26%)
  starting transfers between devices  57.6 us (25%)
  local copies, waits for them, and re-layouts  10.8 us (5%)
  other arithmetic  5.3 us (2%)
    ppermute x77, waiting for transfers between devices, swap(): return lax.ppermute(x, axis, [(i, i ^ bits) for i in range(size)])  91.2 us
    ppermute x77, starting transfers between devices, swap(): return lax.ppermute(x, axis, [(i, i ^ bits) for i in range(size)])  57.6 us
    pallas_call x9, Pallas kernels, call(): pl.pallas_call(kernel, out_shape=out_shape, in_specs=specs, out_specs=jax...  42.9 us
    pallas_call x6, Pallas kernels, pair_add(): pl.pallas_call(add_kernel, out_shape=[sds((rows, cols), BF16)] * 4, in_sp...  13.5 us
    unnamed x158, local copies, waits for them, and re-layouts  10.7 us
  transfers between devices with their start and end apart: 77, of which 27 were waited for; matrix products, arithmetic and copies ran while one was open for 2% of the time, Pallas kernels for 19%

profile of v5, /device:TPU:0, one launch (start us, length us, event | category | flops | bytes accessed | tf_op | source)
XLA Modules:
  0.0 225.6 jit_solution(9761620305604381314)
XLA Ops:
  2.6 3.0 %collective-permute-start.3 = (bf16[48,1664]{1,0:T(8,128)(2,1)S(1)}, bf16[48,1664]{1,0:T(8,128)(2,1)S(1)}, u32[]{:S(2)}, u32[]{:S(2)}) collective-permute-start(bf16[48,1664]{1,0:T(8,128)(2,1)S(1)} %fusion.1.rest_0_.rest_16_.rest_4_), channel_id=1, source_target_pairs={{0,4},{2,6},{4,0},{6,2},{1,5},{3,7},{5,1},{7,3},{8,12},{10,14},{12... | collective-permute-start | bytes 479240 | tf_op jit(solution)/shard_map/ppermute | solution.py:56
  5.6 2.6 %collective-permute-start.1 = (bf16[48,1664]{1,0:T(8,128)(2,1)S(1)}, bf16[48,1664]{1,0:T(8,128)(2,1)S(1)}, u32[]{:S(2)}, u32[]{:S(2)}) collective-permute-start(bf16[48,1664]{1,0:T(8,128)(2,1)S(1)} %fusion.1.rest_0_.rest_16_.rest_4_), channel_id=1, source_target_pairs={{0,16},{8,24},{16,0},{24,8},{1,17},{9,25},{17,1},{25,9},{2,18},{10... | collective-permute-start | bytes 479240 | tf_op jit(solution)/shard_map/ppermute | solution.py:56
  8.2 1.6 collective-permute-start
  10.0 5.6 %collective-permute-done.1.rest_2_.rest_18_.rest_6_ = bf16[48,1664]{1,0:T(8,128)(2,1)S(1)} collective-permute-done((bf16[48,1664]{1,0:T(8,128)(2,1)S(1)}, bf16[48,1664]{1,0:T(8,128)(2,1)S(1)}, u32[]{:S(2)}, u32[]{:S(2)}) %collective-permute-start.1) | collective-permute-done | bytes 159776 | tf_op jit(solution)/shard_map/ppermute | solution.py:56
  18.5 2.4 %collective-permute-done.2.rest_3_.rest_19_.rest_7_ = bf16[48,1664]{1,0:T(8,128)(2,1)S(1)} collective-permute-done((bf16[48,1664]{1,0:T(8,128)(2,1)S(1)}, bf16[48,1664]{1,0:T(8,128)(2,1)S(1)}, u32[]{:S(2)}, u32[]{:S(2)}) %collective-permute-start.2) | collective-permute-done | bytes 159776 | tf_op jit(solution)/shard_map/ppermute | solution.py:56
  21.5 1.6 collective-permute-start.34
  23.8 2.9 %collective-permute-done.4.rest_5_.rest_21_.rest_9_ = bf16[48,1664]{1,0:T(8,128)(2,1)S(1)} collective-permute-done((bf16[48,1664]{1,0:T(8,128)(2,1)S(1)}, bf16[48,1664]{1,0:T(8,128)(2,1)S(1)}, u32[]{:S(2)}, u32[]{:S(2)}) %collective-permute-start.4) | collective-permute-done | bytes 159776 | tf_op jit(solution)/shard_map/ppermute | solution.py:56
  26.7 3.4 %collective-permute-done.6.rest_7_.rest_23_.rest_11_ = bf16[48,1664]{1,0:T(8,128)(2,1)S(1)} collective-permute-done((bf16[48,1664]{1,0:T(8,128)(2,1)S(1)}, bf16[48,1664]{1,0:T(8,128)(2,1)S(1)}, u32[]{:S(2)}, u32[]{:S(2)}) %collective-permute-start.6) | collective-permute-done | bytes 159776 | tf_op jit(solution)/shard_map/ppermute | solution.py:56
  32.7 4.3 %shard_map.159 = (bf16[768,128]{1,0:T(8,128)(2,1)}, bf16[128,384]{1,0:T(8,128)(2,1)}, bf16[128,768]{1,0:T(8,128)(2,1)}, f32[8,768]{1,0:T(8,128)}) custom-call(s32[1]{0:T(128)} %bitcast.order_ref, f32[128,768]{1,0:T(8,128)} %x_ref.5, f32[128,128]{1,0:T(8,128)} %get-tuple-element.137.cos_ref, f32[128,128]{1,0:T(8,128)} %get-tuple-element.136.sin_ref, ...), custom_call_target="tpu_custom_call" | custom-call | tf_op jit(solution)/shard_map/pallas_call | solution.py:464
  37.0 3.5 %collective-permute-start.16 = (bf16[128,768]{1,0:T(8,128)(2,1)}, bf16[128,768]{1,0:T(8,128)(2,1)S(1)}, u32[]{:S(2)}, u32[]{:S(2)}) collective-permute-start(bf16[128,768]{1,0:T(8,128)(2,1)} %get-tuple-element.75.rest_0_), channel_id=1, source_target_pairs={{0,16},{8,24},{16,0},{24,8},{1,17},{9,25},{17,1},{25,9},{2,18},{10... | collective-permute-start | bytes 589832 | tf_op jit(solution)/shard_map/ppermute | solution.py:56
  42.0 15.5 %collective-permute-done.32.rest_2_ = bf16[48,1792]{1,0:T(8,128)(2,1)} collective-permute-done((bf16[48,1792]{1,0:T(8,128)(2,1)S(1)}, bf16[48,1792]{1,0:T(8,128)(2,1)}, u32[]{:S(2)}, u32[]{:S(2)}) %collective-permute-start.32) | collective-permute-done | bytes 172064 | tf_op jit(solution)/shard_map/ppermute | solution.py:56
  57.5 2.0 collective-permute-start.17
  60.2 12.7 %collective-permute-done.33.rest_3_ = bf16[48,1792]{1,0:T(8,128)(2,1)S(1)} collective-permute-done((bf16[48,1792]{1,0:T(8,128)(2,1)}, bf16[48,1792]{1,0:T(8,128)(2,1)S(1)}, u32[]{:S(2)}, u32[]{:S(2)}) %collective-permute-start.33) | collective-permute-done | bytes 172064 | tf_op jit(solution)/shard_map/ppermute | solution.py:56
  73.5 1.6 collective-permute-start.19
  75.6 5.1 %collective-permute-done.20.rest_6_ = bf16[128,768]{1,0:T(8,128)(2,1)S(1)} collective-permute-done((bf16[128,768]{1,0:T(8,128)(2,1)S(1)}, bf16[128,768]{1,0:T(8,128)(2,1)S(1)}, u32[]{:S(2)}, u32[]{:S(2)}) %collective-permute-start.20) | collective-permute-done | bytes 196640 | tf_op jit(solution)/shard_map/ppermute | solution.py:56
  81.2 3.7 %collective-permute-done.19.rest_5_ = bf16[128,768]{1,0:T(8,128)(2,1)S(1)} collective-permute-done((bf16[128,768]{1,0:T(8,128)(2,1)S(1)}, bf16[128,768]{1,0:T(8,128)(2,1)S(1)}, u32[]{:S(2)}, u32[]{:S(2)}) %collective-permute-start.19) | collective-permute-done | bytes 196640 | tf_op jit(solution)/shard_map/ppermute | solution.py:56
  84.9 2.9 %collective-permute-done.21.rest_7_ = bf16[128,768]{1,0:T(8,128)(2,1)S(1)} collective-permute-done((bf16[128,768]{1,0:T(8,128)(2,1)S(1)}, bf16[128,768]{1,0:T(8,128)(2,1)S(1)}, u32[]{:S(2)}, u32[]{:S(2)}) %collective-permute-start.21) | collective-permute-done | bytes 196640 | tf_op jit(solution)/shard_map/ppermute | solution.py:56
  88.8 1.6 collective-permute-start.35
  91.1 7.5 %shard_map.160 = (bf16[128,384]{1,0:T(8,128)(2,1)}, f32[8,256]{1,0:T(8,128)}, bf16[128,768]{1,0:T(8,128)(2,1)}) custom-call(s32[1]{0:T(128)} %bitcast.order_ref, bf16[128,384]{1,0:T(8,128)(2,1)} %get-tuple-element.74.q_ref, bf16[128,768]{1,0:T(8,128)(2,1)} %get-tuple-element.75.rest_0_, bf16[128,768]{1,0:T(8,128)(2,1)} %copy-done.19, ...), custom_call_target="tpu_custom_call" | custom-call | tf_op jit(solution)/shard_map/pallas_call | solution.py:464
  98.7 1.6 collective-permute-start.30
  104.0 1.9 collective-permute-done.30.pb_ref
  106.6 5.4 %shard_map.161 = (f32[128,768]{1,0:T(8,128)}, bf16[128,768]{1,0:T(8,128)(2,1)}, bf16[128,768]{1,0:T(8,128)(2,1)}, bf16[128,768]{1,0:T(8,128)(2,1)}, bf16[128,1152]{1,0:T(8,128)(2,1)}, /*index=5*/bf16[128,576]{1,0:T(8,128)(2,1)}) custom-call(s32[1]{0:T(128)} %bitcast.order_ref, f32[128,768]{1,0:T(8,128)} %x_ref.5, bf16[128,768]{1,0:T(8,128)(2,1)} %get-tuple-element.78.pa_ref, ...), custom_call_target="tpu_custom_call" | custom-call | tf_op jit(solution)/shard_map/pallas_call | solution.py:464
  111.9 1.6 collective-permute-start.46
  113.5 4.8 %collective-permute-done.46.db_ref = bf16[128,768]{1,0:T(8,128)(2,1)S(1)} collective-permute-done((bf16[128,768]{1,0:T(8,128)(2,1)}, bf16[128,768]{1,0:T(8,128)(2,1)S(1)}, u32[]{:S(2)}, u32[]{:S(2)}) %collective-permute-start.46) | collective-permute-done | bytes 196640 | tf_op jit(solution)/shard_map/ppermute | solution.py:56
  119.0 9.9 %shard_map.162 = (bf16[512,768]{1,0:T(8,128)(2,1)}, bf16[512,768]{1,0:T(8,128)(2,1)}, bf16[512,768]{1,0:T(8,128)(2,1)}, bf16[512,768]{1,0:T(8,128)(2,1)}, f32[128,768]{1,0:T(8,128)}, /*index=5*/bf16[128,384]{1,0:T(8,128)(2,1)}) custom-call(s32[1]{0:T(128)} %bitcast.order_ref, bf16[128,384]{1,0:T(8,128)(2,1)} %get-tuple-element.74.q_ref, ...), custom_call_target="tpu_custom_call" | custom-call | tf_op jit(solution)/shard_map/pallas_call | solution.py:464
  129.4 2.0 collective-permute-done.48.recv
  132.3 2.3 %pair_add.7 = (bf16[128,768]{1,0:T(8,128)(2,1)}, bf16[128,768]{1,0:T(8,128)(2,1)}, bf16[128,768]{1,0:T(8,128)(2,1)}, bf16[128,768]{1,0:T(8,128)(2,1)}) custom-call(bf16[512,768]{1,0:T(8,128)(2,1)} %get-tuple-element.87.keep, bf16[512,768]{1,0:T(8,128)(2,1)} %copy-done.32), custom_call_target="tpu_custom_call" | custom-call | tf_op jit(solution)/shard_map/pair_add/pallas_call | solution.py:109
  135.7 3.7 %shard_map.165 = (bf16[192,1792]{1,0:T(8,128)(2,1)}, bf16[192,1792]{1,0:T(8,128)(2,1)}, bf16[192,1792]{1,0:T(8,128)(2,1)}, bf16[192,1792]{1,0:T(8,128)(2,1)}) custom-call(s32[1]{0:T(128)} %bitcast.order_ref, bf16[128,768]{1,0:T(8,128)(2,1)} %get-tuple-element.112.b_ref, bf16[128,1152]{1,0:T(8,128)(2,1)} %get-tuple-element.113.dz_ref, f32[128,768]{1,0:T(8,128)} %cot_ref.5, ...), custom_call_target="tpu_custom_call" | custom-call | tf_op jit(solution)/shard_map/pallas_call | solution.py:464
  142.1 2.3 %pair_add.6 = (bf16[128,768]{1,0:T(8,128)(2,1)}, bf16[128,768]{1,0:T(8,128)(2,1)}, bf16[128,768]{1,0:T(8,128)(2,1)}, bf16[128,768]{1,0:T(8,128)(2,1)}) custom-call(bf16[512,768]{1,0:T(8,128)(2,1)} %get-tuple-element.84.keep, bf16[512,768]{1,0:T(8,128)(2,1)} %copy-done.31), custom_call_target="tpu_custom_call" | custom-call | tf_op jit(solution)/shard_map/pair_add/pallas_call | solution.py:109
  146.5 5.4 %collective-permute-done.50 = bf16[128,768]{1,0:T(8,128)(2,1)S(1)} collective-permute-done((bf16[128,768]{1,0:T(8,128)(2,1)S(1)}, bf16[128,768]{1,0:T(8,128)(2,1)S(1)}, u32[]{:S(2)}, u32[]{:S(2)}) %collective-permute-start.50) | collective-permute-done | bytes 196640 | tf_op jit(solution)/shard_map/ppermute | solution.py:56
  152.5 2.7 %collective-permute-done.52 = bf16[128,768]{1,0:T(8,128)(2,1)S(1)} collective-permute-done((bf16[128,768]{1,0:T(8,128)(2,1)S(1)}, bf16[128,768]{1,0:T(8,128)(2,1)S(1)}, u32[]{:S(2)}, u32[]{:S(2)}) %collective-permute-start.52) | collective-permute-done | bytes 196640 | tf_op jit(solution)/shard_map/ppermute | solution.py:56
  155.7 2.6 %collective-permute-done.54 = bf16[128,768]{1,0:T(8,128)(2,1)S(1)} collective-permute-done((bf16[128,768]{1,0:T(8,128)(2,1)S(1)}, bf16[128,768]{1,0:T(8,128)(2,1)S(1)}, u32[]{:S(2)}, u32[]{:S(2)}) %collective-permute-start.54) | collective-permute-done | bytes 196640 | tf_op jit(solution)/shard_map/ppermute | solution.py:56
  160.5 2.3 %pair_add.11 = (bf16[48,1792]{1,0:T(8,128)(2,1)}, bf16[48,1792]{1,0:T(8,128)(2,1)}, bf16[48,1792]{1,0:T(8,128)(2,1)}, bf16[48,1792]{1,0:T(8,128)(2,1)}) custom-call(bf16[192,1792]{1,0:T(8,128)(2,1)} %get-tuple-element.118.keep, bf16[192,1792]{1,0:T(8,128)(2,1)} %copy-done.35), custom_call_target="tpu_custom_call" | custom-call | tf_op jit(solution)/shard_map/pair_add/pallas_call | solution.py:109
  163.9 1.6 collective-permute-start.57
  165.5 2.2 pair_add.10
  170.6 5.4 %shard_map.163 = (bf16[192,1536]{1,0:T(8,128)(2,1)}, bf16[192,1536]{1,0:T(8,128)(2,1)}, bf16[192,1536]{1,0:T(8,128)(2,1)}, bf16[192,1536]{1,0:T(8,128)(2,1)}, bf16[128,768]{1,0:T(8,128)(2,1)}) custom-call(s32[1]{0:T(128)} %bitcast.order_ref, bf16[768,128]{1,0:T(8,128)(2,1)} %get-tuple-element.73.at_ref, bf16[128,384]{1,0:T(8,128)(2,1)} %get-tuple-element.82.dqp_ref, ...), custom_call_target="tpu_custom_call" | custom-call | tf_op jit(solution)/shard_map/pallas_call | solution.py:464
  179.8 2.2 pair_add.9
  186.0 2.2 pair_add.8
  188.1 1.8 collective-permute-done.64
  195.1 1.7 collective-permute-start.75
  196.8 4.3 %collective-permute-done.65 = bf16[48,1536]{1,0:T(8,128)(2,1)S(1)} collective-permute-done((bf16[48,1536]{1,0:T(8,128)(2,1)S(1)}, bf16[48,1536]{1,0:T(8,128)(2,1)S(1)}, u32[]{:S(2)}, u32[]{:S(2)}) %collective-permute-start.65) | collective-permute-done | bytes 147488 | tf_op jit(solution)/shard_map/ppermute | solution.py:56
  203.7 1.8 collective-permute-start.66
  205.4 2.1 collective-permute-done.60.rest_1_
  207.5 2.7 %collective-permute-done.62.rest_2_ = bf16[48,1536]{1,0:T(8,128)(2,1)S(1)} collective-permute-done((bf16[48,1536]{1,0:T(8,128)(2,1)S(1)}, bf16[48,1536]{1,0:T(8,128)(2,1)S(1)}, u32[]{:S(2)}, u32[]{:S(2)}) %collective-permute-start.62) | collective-permute-done | bytes 147488 | tf_op jit(solution)/shard_map/ppermute | solution.py:56
  212.0 2.7 %shard_map.166 = (f32[48,3264]{1,0:T(8,128)}, f32[2,48]{1,0:T(2,128)}) custom-call(f32[48,3264]{1,0:T(8,128)} %w_ref.5, bf16[48,1536]{1,0:T(8,128)(2,1)} %get-tuple-element.102.rest_0_, bf16[48,1536]{1,0:T(8,128)(2,1)} %copy-done.65, bf16[48,1536]{1,0:T(8,128)(2,1)} %copy-done.66, bf16[48,1536]{1,0:T(8,128)(2,1)} %copy-done.67, ...), custom_call_target="tpu_custom_call" | custom-call | tf_op jit(solution)/shard_map/pallas_call | solution.py:464
  215.3 1.5 collective-permute-start.76
  218.2 2.7 %shard_map.164 = (f32[128,768]{1,0:T(8,128)}, f32[128,768]{1,0:T(8,128)}) custom-call(f32[128,768]{1,0:T(8,128)} %x_ref.5, bf16[128,768]{1,0:T(8,128)(2,1)} %get-tuple-element.96.da_ref, bf16[128,768]{1,0:T(8,128)(2,1)} %copy-done.47, f32[128,768]{1,0:T(8,128)} %get-tuple-element.83.dhid_ref, f32[8,768]{1,0:T(8,128)} %get-tuple-element.79.g_ref, ...), custom_call_target="tpu_custom_call" | custom-call | tf_op jit(solution)/shard_map/pallas_call | solution.py:464
  220.9 2.8 %adam.1 = (f32[48,3264]{1,0:T(8,128)}, f32[48,3264]{1,0:T(8,128)}, f32[48,3264]{1,0:T(8,128)}) custom-call(f32[48,3264]{1,0:T(8,128)} %w_ref.5, f32[48,3264]{1,0:T(8,128)} %get-tuple-element.65.g_ref, f32[48,3264]{1,0:T(8,128)} %m_ref.3, f32[48,3264]{1,0:T(8,128)} %v_ref.3), custom_call_target="tpu_custom_call" | custom-call | tf_op jit(solution)/shard_map/adam/pallas_call | solution.py:679
  (300 shorter events, 54.5 us)
Async XLA Ops:
  5.6 10.0 %collective-permute-start.1 = (bf16[48,1664]{1,0:T(8,128)(2,1)S(1)}, bf16[48,1664]{1,0:T(8,128)(2,1)S(1)}, u32[]{:S(2)}, u32[]{:S(2)}) collective-permute-start(bf16[48,1664]{1,0:T(8,128)(2,1)S(1)} %fusion.1.rest_0_.rest_16_.rest_4_), channel_id=1, source_target_pairs={{0,16},{8,24},{16,0},{24,8},{1,17},{9,25},{17,1},{25,9},{2,18},{10... | collective-permute-start | bytes 479240 | tf_op jit(solution)/shard_map/ppermute | solution.py:56
  8.2 8.0 %collective-permute-start.7 = (bf16[48,1664]{1,0:T(8,128)(2,1)S(1)}, bf16[48,1664]{1,0:T(8,128)(2,1)S(1)}, u32[]{:S(2)}, u32[]{:S(2)}) collective-permute-start(bf16[48,1664]{1,0:T(8,128)(2,1)S(1)} %fusion.1.rest_0_.rest_16_.rest_4_), channel_id=1, source_target_pairs={{0,2},{2,0},{4,6},{6,4},{1,3},{3,1},{5,7},{7,5},{8,10},{10,8},{12,... | collective-permute-start | bytes 479240 | tf_op jit(solution)/shard_map/ppermute | solution.py:56
  8.2 8.8 %collective-permute-start = (bf16[48,1664]{1,0:T(8,128)(2,1)S(1)}, bf16[48,1664]{1,0:T(8,128)(2,1)S(1)}, u32[]{:S(2)}, u32[]{:S(2)}) collective-permute-start(bf16[48,1664]{1,0:T(8,128)(2,1)S(1)} %fusion.1.rest_0_.rest_16_.rest_4_), channel_id=1, source_target_pairs={{0,8},{8,0},{16,24},{24,16},{1,9},{9,1},{17,25},{25,17},{2,10},{10... | collective-permute-start | bytes 479240 | tf_op jit(solution)/shard_map/ppermute | solution.py:56
  17.1 9.6 %collective-permute-start.4 = (bf16[48,1664]{1,0:T(8,128)(2,1)S(1)}, bf16[48,1664]{1,0:T(8,128)(2,1)S(1)}, u32[]{:S(2)}, u32[]{:S(2)}) collective-permute-start(bf16[48,1664]{1,0:T(8,128)(2,1)S(1)} %collective-permute-done.rest_1_.rest_17_.rest_5_), channel_id=1, source_target_pairs={{0,4},{2,6},{4,0},{6,2},{1,5},{3,7},{5,1},{7,3},{8,12},{10,14},{12... | collective-permute-start | bytes 479240 | tf_op jit(solution)/shard_map/ppermute | solution.py:56
  20.9 9.2 %collective-permute-start.6 = (bf16[48,1664]{1,0:T(8,128)(2,1)S(1)}, bf16[48,1664]{1,0:T(8,128)(2,1)S(1)}, u32[]{:S(2)}, u32[]{:S(2)}) collective-permute-start(bf16[48,1664]{1,0:T(8,128)(2,1)S(1)} %collective-permute-done.2.rest_3_.rest_19_.rest_7_), channel_id=1, source_target_pairs={{0,4},{2,6},{4,0},{6,2},{1,5},{3,7},{5,1},{7,3},{8,12},{10,14},{12... | collective-permute-start | bytes 479240 | tf_op jit(solution)/shard_map/ppermute | solution.py:56
  21.5 19.9 %collective-permute-start.34 = (bf16[48,1792]{1,0:T(8,128)(2,1)S(1)}, bf16[48,1792]{1,0:T(8,128)(2,1)S(1)}, u32[]{:S(2)}, u32[]{:S(2)}) collective-permute-start(bf16[48,1792]{1,0:T(8,128)(2,1)S(1)} %pad.9.rest_0_), channel_id=1, source_target_pairs={{0,4},{2,6},{4,0},{6,2},{1,5},{3,7},{5,1},{7,3},{8,12},{10,14},{12... | collective-permute-start | bytes 516104 | tf_op jit(solution)/shard_map/ppermute | solution.py:56
  23.3 8.6 %collective-permute-start.10 = (bf16[48,1664]{1,0:T(8,128)(2,1)S(1)}, bf16[48,1664]{1,0:T(8,128)(2,1)S(1)}, u32[]{:S(2)}, u32[]{:S(2)}) collective-permute-start(bf16[48,1664]{1,0:T(8,128)(2,1)S(1)} %collective-permute-done.2.rest_3_.rest_19_.rest_7_), channel_id=1, source_target_pairs={{0,2},{2,0},{4,6},{6,4},{1,3},{3,1},{5,7},{7,5},{8,10},{10,8},{12,... | collective-permute-start | bytes 479240 | tf_op jit(solution)/shard_map/ppermute | solution.py:56
  23.3 8.0 %collective-permute-start.13 = (bf16[48,1664]{1,0:T(8,128)(2,1)S(1)}, bf16[48,1664]{1,0:T(8,128)(2,1)S(1)}, u32[]{:S(2)}, u32[]{:S(2)}) collective-permute-start(bf16[48,1664]{1,0:T(8,128)(2,1)S(1)} %collective-permute-done.5.rest_6_.rest_22_.rest_10_), channel_id=1, source_target_pairs={{0,2},{2,0},{4,6},{6,4},{1,3},{3,1},{5,7},{7,5},{8,10},{10,8},{12,... | collective-permute-start | bytes 479240 | tf_op jit(solution)/shard_map/ppermute | solution.py:56
  31.3 10.1 %collective-permute-start.38 = (bf16[48,1792]{1,0:T(8,128)(2,1)S(1)}, bf16[48,1792]{1,0:T(8,128)(2,1)S(1)}, u32[]{:S(2)}, u32[]{:S(2)}) collective-permute-start(bf16[48,1792]{1,0:T(8,128)(2,1)S(1)} %pad.9.rest_0_), channel_id=1, source_target_pairs={{0,2},{2,0},{4,6},{6,4},{1,3},{3,1},{5,7},{7,5},{8,10},{10,8},{12,... | collective-permute-start | bytes 516104 | tf_op jit(solution)/shard_map/ppermute | solution.py:56
  37.0 20.5 %collective-permute-start.16 = (bf16[128,768]{1,0:T(8,128)(2,1)}, bf16[128,768]{1,0:T(8,128)(2,1)S(1)}, u32[]{:S(2)}, u32[]{:S(2)}) collective-permute-start(bf16[128,768]{1,0:T(8,128)(2,1)} %get-tuple-element.75.rest_0_), channel_id=1, source_target_pairs={{0,16},{8,24},{16,0},{24,8},{1,17},{9,25},{17,1},{25,9},{2,18},{10... | collective-permute-start | bytes 589832 | tf_op jit(solution)/shard_map/ppermute | solution.py:56
  40.5 17.0 %collective-permute-start.32 = (bf16[48,1792]{1,0:T(8,128)(2,1)S(1)}, bf16[48,1792]{1,0:T(8,128)(2,1)}, u32[]{:S(2)}, u32[]{:S(2)}) collective-permute-start(bf16[48,1792]{1,0:T(8,128)(2,1)S(1)} %pad.9.rest_0_), channel_id=1, source_target_pairs={{0,16},{8,24},{16,0},{24,8},{1,17},{9,25},{17,1},{25,9},{2,18},{10... | collective-permute-start | bytes 516104 | tf_op jit(solution)/shard_map/ppermute | solution.py:56
  40.6 16.9 %collective-permute-start.31 = (bf16[48,1792]{1,0:T(8,128)(2,1)S(1)}, bf16[48,1792]{1,0:T(8,128)(2,1)}, u32[]{:S(2)}, u32[]{:S(2)}) collective-permute-start(bf16[48,1792]{1,0:T(8,128)(2,1)S(1)} %pad.9.rest_0_), channel_id=1, source_target_pairs={{0,8},{8,0},{16,24},{24,16},{1,9},{9,1},{17,25},{25,17},{2,10},{10... | collective-permute-start | bytes 516104 | tf_op jit(solution)/shard_map/ppermute | solution.py:56
  41.4 18.1 %collective-permute-start.42 = (bf16[48,1792]{1,0:T(8,128)(2,1)S(1)}, bf16[48,1792]{1,0:T(8,128)(2,1)S(1)}, u32[]{:S(2)}, u32[]{:S(2)}) collective-permute-start(bf16[48,1792]{1,0:T(8,128)(2,1)S(1)} %collective-permute-done.34.rest_4_), channel_id=1, source_target_pairs={{0,2},{2,0},{4,6},{6,4},{1,3},{3,1},{5,7},{7,5},{8,10},{10,8},{12,... | collective-permute-start | bytes 516104 | tf_op jit(solution)/shard_map/ppermute | solution.py:56
  41.4 18.8 %collective-permute-start.18 = (bf16[128,768]{1,0:T(8,128)(2,1)}, bf16[128,768]{1,0:T(8,128)(2,1)S(1)}, u32[]{:S(2)}, u32[]{:S(2)}) collective-permute-start(bf16[128,768]{1,0:T(8,128)(2,1)} %get-tuple-element.75.rest_0_), channel_id=1, source_target_pairs={{0,4},{2,6},{4,0},{6,2},{1,5},{3,7},{5,1},{7,3},{8,12},{10,14},{12... | collective-permute-start | bytes 589832 | tf_op jit(solution)/shard_map/ppermute | solution.py:56
  57.5 16.0 %collective-permute-start.22 = (bf16[128,768]{1,0:T(8,128)(2,1)}, bf16[128,768]{1,0:T(8,128)(2,1)S(1)}, u32[]{:S(2)}, u32[]{:S(2)}) collective-permute-start(bf16[128,768]{1,0:T(8,128)(2,1)} %get-tuple-element.75.rest_0_), channel_id=1, source_target_pairs={{0,2},{2,0},{4,6},{6,4},{1,3},{3,1},{5,7},{7,5},{8,10},{10,8},{12,... | collective-permute-start | bytes 589832 | tf_op jit(solution)/shard_map/ppermute | solution.py:56
  57.5 16.0 %collective-permute-start.15 = (bf16[128,768]{1,0:T(8,128)(2,1)}, bf16[128,768]{1,0:T(8,128)(2,1)S(1)}, u32[]{:S(2)}, u32[]{:S(2)}) collective-permute-start(bf16[128,768]{1,0:T(8,128)(2,1)} %get-tuple-element.75.rest_0_), channel_id=1, source_target_pairs={{0,8},{8,0},{16,24},{24,16},{1,9},{9,1},{17,25},{25,17},{2,10},{10... | collective-permute-start | bytes 589832 | tf_op jit(solution)/shard_map/ppermute | solution.py:56
  57.5 17.5 %collective-permute-start.17 = (bf16[128,768]{1,0:T(8,128)(2,1)S(1)}, bf16[128,768]{1,0:T(8,128)(2,1)S(1)}, u32[]{:S(2)}, u32[]{:S(2)}) collective-permute-start(bf16[128,768]{1,0:T(8,128)(2,1)S(1)} %collective-permute-done.16.rest_2_), channel_id=1, source_target_pairs={{0,8},{8,0},{16,24},{24,16},{1,9},{9,1},{17,25},{25,17},{2,10},{10... | collective-permute-start | bytes 589832 | tf_op jit(solution)/shard_map/ppermute | solution.py:56
  59.5 13.4 %collective-permute-start.33 = (bf16[48,1792]{1,0:T(8,128)(2,1)}, bf16[48,1792]{1,0:T(8,128)(2,1)S(1)}, u32[]{:S(2)}, u32[]{:S(2)}) collective-permute-start(bf16[48,1792]{1,0:T(8,128)(2,1)} %collective-permute-done.32.rest_2_), channel_id=1, source_target_pairs={{0,8},{8,0},{16,24},{24,16},{1,9},{9,1},{17,25},{25,17},{2,10},{10... | collective-permute-start | bytes 516104 | tf_op jit(solution)/shard_map/ppermute | solution.py:56
  60.2 15.4 %collective-permute-start.26 = (bf16[128,768]{1,0:T(8,128)(2,1)S(1)}, bf16[128,768]{1,0:T(8,128)(2,1)S(1)}, u32[]{:S(2)}, u32[]{:S(2)}) collective-permute-start(bf16[128,768]{1,0:T(8,128)(2,1)S(1)} %collective-permute-done.18.rest_4_), channel_id=1, source_target_pairs={{0,2},{2,0},{4,6},{6,4},{1,3},{3,1},{5,7},{7,5},{8,10},{10,8},{12,... | collective-permute-start | bytes 589832 | tf_op jit(solution)/shard_map/ppermute | solution.py:56
  73.5 11.4 %collective-permute-start.19 = (bf16[128,768]{1,0:T(8,128)(2,1)S(1)}, bf16[128,768]{1,0:T(8,128)(2,1)S(1)}, u32[]{:S(2)}, u32[]{:S(2)}) collective-permute-start(bf16[128,768]{1,0:T(8,128)(2,1)S(1)} %collective-permute-done.15.rest_1_), channel_id=1, source_target_pairs={{0,4},{2,6},{4,0},{6,2},{1,5},{3,7},{5,1},{7,3},{8,12},{10,14},{12... | collective-permute-start | bytes 589832 | tf_op jit(solution)/shard_map/ppermute | solution.py:56
  75.0 12.8 %collective-permute-start.21 = (bf16[128,768]{1,0:T(8,128)(2,1)S(1)}, bf16[128,768]{1,0:T(8,128)(2,1)S(1)}, u32[]{:S(2)}, u32[]{:S(2)}) collective-permute-start(bf16[128,768]{1,0:T(8,128)(2,1)S(1)} %collective-permute-done.17.rest_3_), channel_id=1, source_target_pairs={{0,4},{2,6},{4,0},{6,2},{1,5},{3,7},{5,1},{7,3},{8,12},{10,14},{12... | collective-permute-start | bytes 589832 | tf_op jit(solution)/shard_map/ppermute | solution.py:56
  75.6 12.2 %collective-permute-start.23 = (bf16[128,768]{1,0:T(8,128)(2,1)S(1)}, bf16[128,768]{1,0:T(8,128)(2,1)S(1)}, u32[]{:S(2)}, u32[]{:S(2)}) collective-permute-start(bf16[128,768]{1,0:T(8,128)(2,1)S(1)} %collective-permute-done.15.rest_1_), channel_id=1, source_target_pairs={{0,2},{2,0},{4,6},{6,4},{1,3},{3,1},{5,7},{7,5},{8,10},{10,8},{12,... | collective-permute-start | bytes 589832 | tf_op jit(solution)/shard_map/ppermute | solution.py:56
  80.7 8.1 %collective-permute-start.25 = (bf16[128,768]{1,0:T(8,128)(2,1)S(1)}, bf16[128,768]{1,0:T(8,128)(2,1)S(1)}, u32[]{:S(2)}, u32[]{:S(2)}) collective-permute-start(bf16[128,768]{1,0:T(8,128)(2,1)S(1)} %collective-permute-done.17.rest_3_), channel_id=1, source_target_pairs={{0,2},{2,0},{4,6},{6,4},{1,3},{3,1},{5,7},{7,5},{8,10},{10,8},{12,... | collective-permute-start | bytes 589832 | tf_op jit(solution)/shard_map/ppermute | solution.py:56
  87.8 10.9 %collective-permute-start.40 = (bf16[48,1792]{1,0:T(8,128)(2,1)}, bf16[48,1792]{1,0:T(8,128)(2,1)}, u32[]{:S(2)}, u32[]{:S(2)}) collective-permute-start(bf16[48,1792]{1,0:T(8,128)(2,1)} %collective-permute-done.32.rest_2_), channel_id=1, source_target_pairs={{0,2},{2,0},{4,6},{6,4},{1,3},{3,1},{5,7},{7,5},{8,10},{10,8},{12,... | collective-permute-start | bytes 516104 | tf_op jit(solution)/shard_map/ppermute | solution.py:56
  88.3 12.0 %collective-permute-start.36 = (bf16[48,1792]{1,0:T(8,128)(2,1)}, bf16[48,1792]{1,0:T(8,128)(2,1)}, u32[]{:S(2)}, u32[]{:S(2)}) collective-permute-start(bf16[48,1792]{1,0:T(8,128)(2,1)} %collective-permute-done.32.rest_2_), channel_id=1, source_target_pairs={{0,4},{2,6},{4,0},{6,2},{1,5},{3,7},{5,1},{7,3},{8,12},{10,14},{12... | collective-permute-start | bytes 516104 | tf_op jit(solution)/shard_map/ppermute | solution.py:56
  88.8 11.5 %collective-permute-start.39 = (bf16[48,1792]{1,0:T(8,128)(2,1)}, bf16[48,1792]{1,0:T(8,128)(2,1)}, u32[]{:S(2)}, u32[]{:S(2)}) collective-permute-start(bf16[48,1792]{1,0:T(8,128)(2,1)} %collective-permute-done.31.rest_1_), channel_id=1, source_target_pairs={{0,2},{2,0},{4,6},{6,4},{1,3},{3,1},{5,7},{7,5},{8,10},{10,8},{12,... | collective-permute-start | bytes 516104 | tf_op jit(solution)/shard_map/ppermute | solution.py:56
  88.8 12.0 %collective-permute-start.35 = (bf16[48,1792]{1,0:T(8,128)(2,1)}, bf16[48,1792]{1,0:T(8,128)(2,1)}, u32[]{:S(2)}, u32[]{:S(2)}) collective-permute-start(bf16[48,1792]{1,0:T(8,128)(2,1)} %collective-permute-done.31.rest_1_), channel_id=1, source_target_pairs={{0,4},{2,6},{4,0},{6,2},{1,5},{3,7},{5,1},{7,3},{8,12},{10,14},{12... | collective-permute-start | bytes 516104 | tf_op jit(solution)/shard_map/ppermute | solution.py:56
  90.4 11.9 %collective-permute-start.37 = (bf16[48,1792]{1,0:T(8,128)(2,1)S(1)}, bf16[48,1792]{1,0:T(8,128)(2,1)}, u32[]{:S(2)}, u32[]{:S(2)}) collective-permute-start(bf16[48,1792]{1,0:T(8,128)(2,1)S(1)} %collective-permute-done.33.rest_3_), channel_id=1, source_target_pairs={{0,4},{2,6},{4,0},{6,2},{1,5},{3,7},{5,1},{7,3},{8,12},{10,14},{12... | collective-permute-start | bytes 516104 | tf_op jit(solution)/shard_map/ppermute | solution.py:56
  128.9 12.1 %collective-permute-start.47 = (bf16[512,768]{1,0:T(8,128)(2,1)}, bf16[512,768]{1,0:T(8,128)(2,1)S(1)}, u32[]{:S(2)}, u32[]{:S(2)}) collective-permute-start(bf16[512,768]{1,0:T(8,128)(2,1)} %get-tuple-element.85), channel_id=1, source_target_pairs={{0,2},{2,0},{4,6},{6,4},{1,3},{3,1},{5,7},{7,5},{8,10},{10,8},{12,... | collective-permute-start | bytes 2359304 | tf_op jit(solution)/shard_map/ppermute | solution.py:56
  134.6 9.8 %collective-permute-start.53 = (bf16[128,768]{1,0:T(8,128)(2,1)}, bf16[128,768]{1,0:T(8,128)(2,1)S(1)}, u32[]{:S(2)}, u32[]{:S(2)}) collective-permute-start(bf16[128,768]{1,0:T(8,128)(2,1)} %get-tuple-element.95), channel_id=1, source_target_pairs={{0,4},{2,6},{4,0},{6,2},{1,5},{3,7},{5,1},{7,3},{8,12},{10,14},{12... | collective-permute-start | bytes 589832 | tf_op jit(solution)/shard_map/ppermute | solution.py:56
  139.5 24.4 %collective-permute-start.67 = (bf16[192,1792]{1,0:T(8,128)(2,1)}, bf16[192,1792]{1,0:T(8,128)(2,1)S(1)}, u32[]{:S(2)}, u32[]{:S(2)}) collective-permute-start(bf16[192,1792]{1,0:T(8,128)(2,1)} %get-tuple-element.116), channel_id=1, source_target_pairs={{0,2},{2,0},{4,6},{6,4},{1,3},{3,1},{5,7},{7,5},{8,10},{10,8},{12,... | collective-permute-start | bytes 2064392 | tf_op jit(solution)/shard_map/ppermute | solution.py:56
  139.5 20.2 %collective-permute-start.68 = (bf16[192,1792]{1,0:T(8,128)(2,1)}, bf16[192,1792]{1,0:T(8,128)(2,1)S(1)}, u32[]{:S(2)}, u32[]{:S(2)}) collective-permute-start(bf16[192,1792]{1,0:T(8,128)(2,1)} %get-tuple-element.119), channel_id=1, source_target_pairs={{0,2},{2,0},{4,6},{6,4},{1,3},{3,1},{5,7},{7,5},{8,10},{10,8},{12,... | collective-permute-start | bytes 2064392 | tf_op jit(solution)/shard_map/ppermute | solution.py:56
  140.0 27.7 %collective-permute-start.49 = (bf16[128,768]{1,0:T(8,128)(2,1)S(1)}, bf16[128,768]{1,0:T(8,128)(2,1)S(1)}, u32[]{:S(2)}, u32[]{:S(2)}) collective-permute-start(bf16[128,768]{1,0:T(8,128)(2,1)S(1)} %copy-done.70), channel_id=1, source_target_pairs={{0,4},{2,6},{4,0},{6,2},{1,5},{3,7},{5,1},{7,3},{8,12},{10,14},{12... | collective-permute-start | bytes 589832 | tf_op jit(solution)/shard_map/ppermute | solution.py:56
  141.0 11.0 %collective-permute-start.50 = (bf16[128,768]{1,0:T(8,128)(2,1)S(1)}, bf16[128,768]{1,0:T(8,128)(2,1)S(1)}, u32[]{:S(2)}, u32[]{:S(2)}) collective-permute-start(bf16[128,768]{1,0:T(8,128)(2,1)S(1)} %copy-done.72), channel_id=1, source_target_pairs={{0,4},{2,6},{4,0},{6,2},{1,5},{3,7},{5,1},{7,3},{8,12},{10,14},{12... | collective-permute-start | bytes 589832 | tf_op jit(solution)/shard_map/ppermute | solution.py:56
  144.4 10.8 %collective-permute-start.52 = (bf16[128,768]{1,0:T(8,128)(2,1)S(1)}, bf16[128,768]{1,0:T(8,128)(2,1)S(1)}, u32[]{:S(2)}, u32[]{:S(2)}) collective-permute-start(bf16[128,768]{1,0:T(8,128)(2,1)S(1)} %copy-done.71), channel_id=1, source_target_pairs={{0,4},{2,6},{4,0},{6,2},{1,5},{3,7},{5,1},{7,3},{8,12},{10,14},{12... | collective-permute-start | bytes 589832 | tf_op jit(solution)/shard_map/ppermute | solution.py:56
  155.2 13.6 %collective-permute-start.51 = (bf16[128,768]{1,0:T(8,128)(2,1)S(1)}, bf16[128,768]{1,0:T(8,128)(2,1)S(1)}, u32[]{:S(2)}, u32[]{:S(2)}) collective-permute-start(bf16[128,768]{1,0:T(8,128)(2,1)S(1)} %add_convert_fusion.2), channel_id=1, source_target_pairs={{0,8},{8,0},{16,24},{24,16},{1,9},{9,1},{17,25},{25,17},{2,10},{10... | collective-permute-start | bytes 589832 | tf_op jit(solution)/shard_map/ppermute | solution.py:56
  158.4 11.5 %collective-permute-start.55 = (bf16[128,768]{1,0:T(8,128)(2,1)S(1)}, bf16[128,768]{1,0:T(8,128)(2,1)S(1)}, u32[]{:S(2)}, u32[]{:S(2)}) collective-permute-start(bf16[128,768]{1,0:T(8,128)(2,1)S(1)} %add_convert_fusion), channel_id=1, source_target_pairs={{0,16},{8,24},{16,0},{24,8},{1,17},{9,25},{17,1},{25,9},{2,18},{10... | collective-permute-start | bytes 589832 | tf_op jit(solution)/shard_map/ppermute | solution.py:56
  162.8 13.3 %collective-permute-start.73 = (bf16[48,1792]{1,0:T(8,128)(2,1)}, bf16[48,1792]{1,0:T(8,128)(2,1)S(1)}, u32[]{:S(2)}, u32[]{:S(2)}) collective-permute-start(bf16[48,1792]{1,0:T(8,128)(2,1)} %get-tuple-element.126), channel_id=1, source_target_pairs={{0,4},{2,6},{4,0},{6,2},{1,5},{3,7},{5,1},{7,3},{8,12},{10,14},{12... | collective-permute-start | bytes 516104 | tf_op jit(solution)/shard_map/ppermute | solution.py:56
  163.9 52.9 %collective-permute-start.57 = (bf16[128,768]{1,0:T(8,128)(2,1)S(1)}, bf16[128,768]{1,0:T(8,128)(2,1)S(1)}, u32[]{:S(2)}, u32[]{:S(2)}) collective-permute-start(bf16[128,768]{1,0:T(8,128)(2,1)S(1)} %copy-done.44), channel_id=1, source_target_pairs={{0,1},{1,0},{2,3},{3,2},{4,5},{5,4},{6,7},{7,6},{8,9},{9,8},{10,11... | collective-permute-start | bytes 589832 | tf_op jit(solution)/shard_map/ppermute | solution.py:56
  167.7 9.9 %collective-permute-start.70 = (bf16[48,1792]{1,0:T(8,128)(2,1)S(1)}, bf16[48,1792]{1,0:T(8,128)(2,1)S(1)}, u32[]{:S(2)}, u32[]{:S(2)}) collective-permute-start(bf16[48,1792]{1,0:T(8,128)(2,1)S(1)} %copy-done.75), channel_id=1, source_target_pairs={{0,4},{2,6},{4,0},{6,2},{1,5},{3,7},{5,1},{7,3},{8,12},{10,14},{12... | collective-permute-start | bytes 516104 | tf_op jit(solution)/shard_map/ppermute | solution.py:56
  168.8 13.2 %collective-permute-start.72 = (bf16[48,1792]{1,0:T(8,128)(2,1)S(1)}, bf16[48,1792]{1,0:T(8,128)(2,1)S(1)}, u32[]{:S(2)}, u32[]{:S(2)}) collective-permute-start(bf16[48,1792]{1,0:T(8,128)(2,1)S(1)} %copy-done.74), channel_id=1, source_target_pairs={{0,4},{2,6},{4,0},{6,2},{1,5},{3,7},{5,1},{7,3},{8,12},{10,14},{12... | collective-permute-start | bytes 516104 | tf_op jit(solution)/shard_map/ppermute | solution.py:56
  178.8 22.8 %collective-permute-start.69 = (bf16[48,1792]{1,0:T(8,128)(2,1)S(1)}, bf16[48,1792]{1,0:T(8,128)(2,1)S(1)}, u32[]{:S(2)}, u32[]{:S(2)}) collective-permute-start(bf16[48,1792]{1,0:T(8,128)(2,1)S(1)} %copy-done.73), channel_id=1, source_target_pairs={{0,4},{2,6},{4,0},{6,2},{1,5},{3,7},{5,1},{7,3},{8,12},{10,14},{12... | collective-permute-start | bytes 516104 | tf_op jit(solution)/shard_map/ppermute | solution.py:56
  182.0 21.5 %collective-permute-start.71 = (bf16[48,1792]{1,0:T(8,128)(2,1)S(1)}, bf16[48,1792]{1,0:T(8,128)(2,1)S(1)}, u32[]{:S(2)}, u32[]{:S(2)}) collective-permute-start(bf16[48,1792]{1,0:T(8,128)(2,1)S(1)} %add_convert_fusion.5), channel_id=1, source_target_pairs={{0,8},{8,0},{16,24},{24,16},{1,9},{9,1},{17,25},{25,17},{2,10},{10... | collective-permute-start | bytes 516104 | tf_op jit(solution)/shard_map/ppermute | solution.py:56
  184.9 8.2 %collective-permute-start.61 = (bf16[48,1536]{1,0:T(8,128)(2,1)S(1)}, bf16[48,1536]{1,0:T(8,128)(2,1)S(1)}, u32[]{:S(2)}, u32[]{:S(2)}) collective-permute-start(bf16[48,1536]{1,0:T(8,128)(2,1)S(1)} %copy-done.78), channel_id=1, source_target_pairs={{0,4},{2,6},{4,0},{6,2},{1,5},{3,7},{5,1},{7,3},{8,12},{10,14},{12... | collective-permute-start | bytes 442376 | tf_op jit(solution)/shard_map/ppermute | solution.py:56
  193.1 7.9 %collective-permute-start.65 = (bf16[48,1536]{1,0:T(8,128)(2,1)S(1)}, bf16[48,1536]{1,0:T(8,128)(2,1)S(1)}, u32[]{:S(2)}, u32[]{:S(2)}) collective-permute-start(bf16[48,1536]{1,0:T(8,128)(2,1)S(1)} %add_convert_fusion.7), channel_id=1, source_target_pairs={{0,8},{8,0},{16,24},{24,16},{1,9},{9,1},{17,25},{25,17},{2,10},{10... | collective-permute-start | bytes 442376 | tf_op jit(solution)/shard_map/ppermute | solution.py:56
  195.1 8.5 %collective-permute-start.75 = (bf16[48,1792]{1,0:T(8,128)(2,1)S(1)}, bf16[48,1792]{1,0:T(8,128)(2,1)S(1)}, u32[]{:S(2)}, u32[]{:S(2)}) collective-permute-start(bf16[48,1792]{1,0:T(8,128)(2,1)S(1)} %add_convert_fusion.3), channel_id=1, source_target_pairs={{0,16},{8,24},{16,0},{24,8},{1,17},{9,25},{17,1},{25,9},{2,18},{10... | collective-permute-start | bytes 516104 | tf_op jit(solution)/shard_map/ppermute | solution.py:56
  201.1 15.7 %collective-permute-start.56 = (bf16[128,768]{1,0:T(8,128)(2,1)S(1)}, bf16[128,768]{1,0:T(8,128)(2,1)S(1)}, u32[]{:S(2)}, u32[]{:S(2)}) collective-permute-start(bf16[128,768]{1,0:T(8,128)(2,1)S(1)} %copy-done.46), channel_id=1, source_target_pairs={{0,1},{1,0},{2,3},{3,2},{4,5},{5,4},{6,7},{7,6},{8,9},{9,8},{10,11... | collective-permute-start | bytes 589832 | tf_op jit(solution)/shard_map/ppermute | solution.py:56
  215.3 8.5 %collective-permute-start.76 = (f32[2,48]{1,0:T(2,128)S(1)}, f32[2,48]{1,0:T(2,128)S(1)}, u32[]{:S(2)}, u32[]{:S(2)}) collective-permute-start(f32[2,48]{1,0:T(2,128)S(1)} %copy-done.68), channel_id=1, source_target_pairs={{0,1},{1,0},{2,3},{3,2},{4,5},{5,4},{6,7},{7,6},{8,9},{9,8},{10,11... | collective-permute-start | bytes 1160 | tf_op jit(solution)/shard_map/ppermute | solution.py:56
  (108 other events, 749.8 us)

commit v6 on v5

--- a/solution.py
+++ b/solution.py
@@ -33,6 +33,7 @@
 VM = pl.BlockSpec(memory_space=pltpu.VMEM)
 SM = pl.BlockSpec(memory_space=pltpu.SMEM)
 ANY = pl.BlockSpec(memory_space=pl.ANY)
+HBM = pl.BlockSpec(memory_space=pltpu.HBM)
 
 
 def sds(shape, dtype):
@@ -109,8 +110,8 @@
     return pl.pallas_call(
         add_kernel,
         out_shape=[sds((rows, cols), BF16)] * 4,
-        in_specs=[ANY, ANY],
-        out_specs=[ANY] * 4,
+        in_specs=[HBM, HBM],
+        out_specs=[HBM] * 4,
         scratch_shapes=[pltpu.VMEM(keep.shape, BF16)] * 3 + [pltpu.SemaphoreType.DMA((3, 4))],
         name="pair_add",
     )(keep, recv)
@@ -160,14 +161,28 @@
     return copies
 
 
-def emit_blocks(order_ref, acc, outs):
-    if len(outs) == 1:
-        outs[0][...] = acc[...].astype(BF16)
+def group_copies(src, outs, sems, first_col):
+    rows, cols = src.shape[0] // len(outs), src.shape[1]
+    copies = [
+        pltpu.make_async_copy(
+            src.at[pl.ds(i * rows, rows), :], out.at[:, pl.ds(first_col, cols)], sems.at[i]
+        )
+        for i, out in enumerate(outs)
+    ]
+    for copy in copies:
+        copy.start()
+    for copy in copies:
+        copy.wait()
+
+
+def emit_blocks(order_ref, acc, dst, staged_rows):
+    if not staged_rows:
+        dst[...] = acc[...].astype(BF16)
         return
-    rows = outs[0].shape[0] // 4
+    rows = acc.shape[0] // 16
     for i, j in enumerate(chunk_order()):
         at = pl.ds(pl.multiple_of((order_ref[0] ^ j) * rows, 8), rows)
-        outs[i // 4][pl.ds((i % 4) * rows, rows), :] = acc[at, :].astype(BF16)
+        dst[pl.ds(i * rows, rows), :] = acc[at, :].astype(BF16)
 
 
 def norm_parts(v):
@@ -345,13 +360,26 @@
 
 
 def ffn_grad_kernel(no, order_ref, b_ref, dz_ref, cot_ref, mixed_ref, *rest):
-    outs, acc = rest[:no], rest[no]
+    outs = rest[:no]
+    acc, dst, sems = rest[no:]
     two = dz_ref.shape[1]
     acc[:, :two] = dot_tn(b_ref[...], dz_ref[...])
     half = mixed_ref.shape[1]
     acc[:, two : two + half] = dot_tn(cot_ref[...].astype(BF16), mixed_ref[...])
     acc[:, two + half :] = jnp.zeros((acc.shape[0], acc.shape[1] - two - half), F32)
-    emit_blocks(order_ref, acc, outs)
+    emit_blocks(order_ref, acc, dst, no > 1)
+    group_copies(dst, outs, sems, 0)
+
+
+def oq_grad_kernel(no, first_col, order_ref, at_ref, dqp_ref, dhid_ref, attn_ref, *rest):
+    outs = rest[no : 2 * no]
+    ht, dst, sems = rest[2 * no :]
+    width = dqp_ref.shape[1]
+    ht[...] = jnp.transpose(dhid_ref[...].astype(BF16))
+    a_t, h_t = rows_in_order(order_ref, at_ref, no), rows_in_order(order_ref, ht, no)
+    dst[:, :width] = dot_nn(a_t, dqp_ref[...]).astype(BF16)
+    dst[:, width:] = dot_nn(h_t, attn_ref[...]).astype(BF16)
+    group_copies(dst, outs, sems, first_col)
 
 
 def back_tile(k, v, qm, dom, lse_row, dot_row):
@@ -422,42 +450,39 @@
     ).astype(BF16)
 
 
-def pick_rows(order_ref, ref, blocks, rows):
+def rows_in_order(order_ref, ref, groups):
+    if groups == 1:
+        return ref[...]
+    rows = ref.shape[0] // 16
     return jnp.concatenate(
-        [ref[pl.ds(pl.multiple_of((order_ref[0] ^ j) * rows, 16), rows), :] for j in blocks], axis=0
-    )
-
-
-def qkv_grad_kernel(
-    n, nt, no, order_ref, at_ref, dqp_ref, dhid_ref, attn_ref, cos_ref, sin_ref, *rest
-):
+        [
+            ref[pl.ds(pl.multiple_of((order_ref[0] ^ j) * rows, 16), rows), :]
+            for j in chunk_order()
+        ],
+        axis=0,
+    )
+
+
+def qkv_grad_kernel(n, nt, no, order_ref, at_ref, dqp_ref, cos_ref, sin_ref, *rest):
     terms = rest[:nt]
     chunks = rest[nt : nt + n]
     outs = rest[nt + n : nt + n + no]
-    da_ref, w, ht, sems = rest[nt + n + no :]
+    da_ref, w, sems = rest[nt + n + no :]
     width = dqp_ref.shape[1]
     copies = weight_copies(order_ref, chunks, w, sems, (0, 3 * width))
     dkv = total([term[...] for term in terms])
     dkp = rope_back(
         dkv[:, :width], wide(cos_ref[...], width), wide(sin_ref[...], width)
     ).astype(BF16)
-    d = jnp.concatenate([dqp_ref[...], dkp, dkv[:, width:].astype(BF16)], axis=1)
-    ht[...] = jnp.transpose(dhid_ref[...].astype(BF16))
-    if no == 1:
-        a_t, h_t = at_ref[...], ht[...]
-    else:
-        rows = at_ref.shape[0] // 16
-        a_t = pick_rows(order_ref, at_ref, chunk_order(), rows)
-        h_t = pick_rows(order_ref, ht, chunk_order(), rows)
-    one = dot_nn(a_t, d).astype(BF16)
-    two = dot_nn(h_t, attn_ref[...]).astype(BF16)
-    size = one.shape[0] // no
+    d = jnp.concatenate([dkp, dkv[:, width:].astype(BF16)], axis=1)
+    both = dot_nn(rows_in_order(order_ref, at_ref, no), d).astype(BF16)
+    size = both.shape[0] // no
     for i, out in enumerate(outs):
-        out[:, : 3 * width] = one[i * size : (i + 1) * size]
-        out[:, 3 * width :] = two[i * size : (i + 1) * size]
+        out[...] = both[i * size : (i + 1) * size]
     for copy in copies:
         copy.wait()
-    da_ref[...] = dot_nt(d, w[...]).astype(BF16)
+    da = dot_nt(dqp_ref[...], w[:, :width]) + dot_nt(d, w[:, width:])
+    da_ref[...] = da.astype(BF16)
 
 
 def call(kernel, out_shape, specs, scratch, args):
@@ -490,8 +515,11 @@
 def gsum_kernel(nf, width, units, w_ref, *rest):
     firsts, lasts = rest[:nf], rest[nf : 2 * nf]
     g_ref, gain_ref = rest[2 * nf :]
-    one = total([term[...] for term in firsts])
-    two = total([term[...] for term in lasts])[:, : 3 * units]
+    kv = total([term[...] for term in firsts])
+    rest_sum = total([term[...] for term in lasts])
+    two = rest_sum[:, : 3 * units]
+    oq = rest_sum[:, rest_sum.shape[1] - 2 * width :]
+    one = jnp.concatenate([oq[:, :width], kv, oq[:, width:]], axis=1)
     wf = w_ref[...].astype(BF16).astype(F32)
     cut = 4 * width
     sums = [
@@ -608,17 +636,21 @@
     )
     db_other = head_swap(db_part)
     ffn_other = head_swap(ffn_part)
-    ffn_grads = call(
+    grad_cols = rest_cols + 2 * width
+    part_sem = pltpu.SemaphoreType.DMA((parts,))
+    group = [sds((d // parts, grad_cols), BF16)] * parts
+    rest_grads = pl.pallas_call(
         partial(ffn_grad_kernel, parts),
-        [sds((d // parts, rest_cols), BF16)] * parts,
-        [SM] + [VM] * 4,
-        [pltpu.VMEM((d, rest_cols), F32)],
-        [order, b, dz, cotangent, mixed],
-    )
-    if staged():
-        ffn_recv = pair_swap(ffn_grads)
-    else:
-        ffn_terms = native_sum(*ffn_grads)
+        out_shape=group,
+        in_specs=[SM] + [VM] * 4,
+        out_specs=[HBM] * parts,
+        scratch_shapes=[
+            pltpu.VMEM((d, rest_cols), F32),
+            pltpu.VMEM((d, rest_cols), BF16),
+            part_sem,
+        ],
+        name="ffngrad",
+    )(order, b, dz, cotangent, mixed)
 
     both = (pairs, 2 * toks, 128)
     *kv_groups, dhid, dqp = call(
@@ -640,18 +672,28 @@
         + keys
         + first_chunks,
     )
+    rest_grads = pl.pallas_call(
+        partial(oq_grad_kernel, parts, rest_cols),
+        out_shape=group,
+        in_specs=[SM] + [VM] * 4 + [HBM] * parts,
+        out_specs=[HBM] * parts,
+        scratch_shapes=[pltpu.VMEM((d, toks), BF16), pltpu.VMEM((d, 2 * width), BF16), part_sem],
+        input_output_aliases={5 + i: i for i in range(parts)},
+        name="oqgrad",
+    )(order, a_t, dqp, dhid, attn, *rest_grads)
     if staged():
         kv_terms = scatter_sum(kv_groups, pair_swap(kv_groups))
-        ffn_terms = scatter_sum(ffn_grads, ffn_recv)
+        rest_terms = scatter_sum(rest_grads, pair_swap(rest_grads))
     else:
         kv_terms = native_sum(*kv_groups)
+        rest_terms = native_sum(*rest_grads)
     nt = len(kv_terms)
     *w_groups, da_part = call(
         partial(qkv_grad_kernel, nw, nt, parts),
-        [sds((d // parts, 4 * width), BF16)] * parts + [sds((toks, d), BF16)],
-        [SM] + [VM] * 6 + [VM] * nt + [ANY] * nw,
-        [pltpu.VMEM((d, 3 * width), BF16), pltpu.VMEM((d, toks), BF16), wsem],
-        [order, a_t, dqp, dhid, attn, cos, sin] + kv_terms + first_chunks,
+        [sds((d // parts, 2 * width), BF16)] * parts + [sds((toks, d), BF16)],
+        [SM] + [VM] * 4 + [VM] * nt + [ANY] * nw,
+        [pltpu.VMEM((d, 3 * width), BF16), wsem],
+        [order, a_t, dqp, cos, sin] + kv_terms + first_chunks,
     )
     da_other = head_swap(da_part)
     input_grad, outputs = call(
@@ -671,7 +713,7 @@
         [sds(full, F32), sds(gains.shape, F32)],
         [VM] * (1 + 2 * nt),
         [],
-        [weights] + first_terms + ffn_terms,
+        [weights] + first_terms + rest_terms,
     )
     gain_other = head_swap(gain_part)
     step_rows = rows // 2 if rows % 16 == 0 else rows

time: 226 us -> 226 us (level)
  waiting for transfers between devices: 91.2 us -> 87.3 us
  Pallas kernels: 59.2 us -> 61.8 us
    pallas_call x0 -> x2, Pallas kernels: none -> 6.78 us  [the longest x1 4.01 us: layer(): pl.pallas_call(partial(ffn_grad_kernel, parts), out_shape=group, in_specs...]
    pallas_call x9 -> x8, Pallas kernels: 42.9 us -> 38.9 us  [call(): pl.pallas_call(kernel, out_shape=out_shape, in_specs=specs, out_specs=jax...]
    ppermute x77, waiting for transfers between devices: 91.2 us -> 87.3 us  [swap(): return lax.ppermute(x, axis, [(i, i ^ bits) for i in range(size)])]
    unnamed x158 -> x146, local copies, waits for them, and re-layouts: 10.7 us -> 9.89 us
  transfers between devices with their start and end apart: 77 -> 77, of which waited for: 27 -> 24; matrix products, arithmetic and copies ran while one was open for 2% -> 2% of each run, Pallas kernels for 19% -> 20%
where the time goes in v6:
time: 226 us; the launch traced here: 225 us
  waiting for transfers between devices  87.3 us (39%)
  Pallas kernels  61.8 us (27%)
  starting transfers between devices  57.2 us (25%)
  local copies, waits for them, and re-layouts  10 us (4%)
  other arithmetic  7.02 us (3%)
    ppermute x77, waiting for transfers between devices, swap(): return lax.ppermute(x, axis, [(i, i ^ bits) for i in range(size)])  87.3 us
    ppermute x77, starting transfers between devices, swap(): return lax.ppermute(x, axis, [(i, i ^ bits) for i in range(size)])  57.2 us
    pallas_call x8, Pallas kernels, call(): pl.pallas_call(kernel, out_shape=out_shape, in_specs=specs, out_specs=jax...  38.9 us
    pallas_call x6, Pallas kernels, pair_add(): pl.pallas_call(add_kernel, out_shape=[sds((rows, cols), BF16)] * 4, in_sp...  13.4 us
    unnamed x146, local copies, waits for them, and re-layouts  9.89 us
  transfers between devices with their start and end apart: 77, of which 24 were waited for; matrix products, arithmetic and copies ran while one was open for 2% of the time, Pallas kernels for 20%

profile of v6, /device:TPU:0, one launch (start us, length us, event | category | flops | bytes accessed | tf_op | source)
XLA Modules:
  0.0 225.0 jit_solution(8438613551602383437)
XLA Ops:
  2.6 3.0 %collective-permute-start.3 = (bf16[48,1664]{1,0:T(8,128)(2,1)S(1)}, bf16[48,1664]{1,0:T(8,128)(2,1)S(1)}, u32[]{:S(2)}, u32[]{:S(2)}) collective-permute-start(bf16[48,1664]{1,0:T(8,128)(2,1)S(1)} %fusion.1.rest_0_.rest_16_.rest_4_), channel_id=1, source_target_pairs={{0,4},{2,6},{4,0},{6,2},{1,5},{3,7},{5,1},{7,3},{8,12},{10,14},{12... | collective-permute-start | bytes 479240 | tf_op jit(solution)/shard_map/ppermute | solution.py:57
  5.6 2.6 %collective-permute-start.1 = (bf16[48,1664]{1,0:T(8,128)(2,1)S(1)}, bf16[48,1664]{1,0:T(8,128)(2,1)S(1)}, u32[]{:S(2)}, u32[]{:S(2)}) collective-permute-start(bf16[48,1664]{1,0:T(8,128)(2,1)S(1)} %fusion.1.rest_0_.rest_16_.rest_4_), channel_id=1, source_target_pairs={{0,16},{8,24},{16,0},{24,8},{1,17},{9,25},{17,1},{25,9},{2,18},{10... | collective-permute-start | bytes 479240 | tf_op jit(solution)/shard_map/ppermute | solution.py:57
  8.2 1.6 collective-permute-start
  10.0 5.6 %collective-permute-done.1.rest_2_.rest_18_.rest_6_ = bf16[48,1664]{1,0:T(8,128)(2,1)S(1)} collective-permute-done((bf16[48,1664]{1,0:T(8,128)(2,1)S(1)}, bf16[48,1664]{1,0:T(8,128)(2,1)S(1)}, u32[]{:S(2)}, u32[]{:S(2)}) %collective-permute-start.1) | collective-permute-done | bytes 159776 | tf_op jit(solution)/shard_map/ppermute | solution.py:57
  18.5 2.4 %collective-permute-done.2.rest_3_.rest_19_.rest_7_ = bf16[48,1664]{1,0:T(8,128)(2,1)S(1)} collective-permute-done((bf16[48,1664]{1,0:T(8,128)(2,1)S(1)}, bf16[48,1664]{1,0:T(8,128)(2,1)S(1)}, u32[]{:S(2)}, u32[]{:S(2)}) %collective-permute-start.2) | collective-permute-done | bytes 159776 | tf_op jit(solution)/shard_map/ppermute | solution.py:57
  21.5 1.6 collective-permute-start.34
  23.8 2.9 %collective-permute-done.4.rest_5_.rest_21_.rest_9_ = bf16[48,1664]{1,0:T(8,128)(2,1)S(1)} collective-permute-done((bf16[48,1664]{1,0:T(8,128)(2,1)S(1)}, bf16[48,1664]{1,0:T(8,128)(2,1)S(1)}, u32[]{:S(2)}, u32[]{:S(2)}) %collective-permute-start.4) | collective-permute-done | bytes 159776 | tf_op jit(solution)/shard_map/ppermute | solution.py:57
  26.7 3.4 %collective-permute-done.6.rest_7_.rest_23_.rest_11_ = bf16[48,1664]{1,0:T(8,128)(2,1)S(1)} collective-permute-done((bf16[48,1664]{1,0:T(8,128)(2,1)S(1)}, bf16[48,1664]{1,0:T(8,128)(2,1)S(1)}, u32[]{:S(2)}, u32[]{:S(2)}) %collective-permute-start.6) | collective-permute-done | bytes 159776 | tf_op jit(solution)/shard_map/ppermute | solution.py:57
  32.7 4.3 %shard_map.159 = (bf16[768,128]{1,0:T(8,128)(2,1)}, bf16[128,384]{1,0:T(8,128)(2,1)}, bf16[128,768]{1,0:T(8,128)(2,1)}, f32[8,768]{1,0:T(8,128)}) custom-call(s32[1]{0:T(128)} %bitcast.order_ref, f32[128,768]{1,0:T(8,128)} %x_ref.5, f32[128,128]{1,0:T(8,128)} %get-tuple-element.145.cos_ref, f32[128,128]{1,0:T(8,128)} %get-tuple-element.144.sin_ref, ...), custom_call_target="tpu_custom_call" | custom-call | tf_op jit(solution)/shard_map/pallas_call | solution.py:489
  36.9 3.5 %collective-permute-start.16 = (bf16[128,768]{1,0:T(8,128)(2,1)}, bf16[128,768]{1,0:T(8,128)(2,1)S(1)}, u32[]{:S(2)}, u32[]{:S(2)}) collective-permute-start(bf16[128,768]{1,0:T(8,128)(2,1)} %get-tuple-element.79.rest_0_), channel_id=1, source_target_pairs={{0,16},{8,24},{16,0},{24,8},{1,17},{9,25},{17,1},{25,9},{2,18},{10... | collective-permute-start | bytes 589832 | tf_op jit(solution)/shard_map/ppermute | solution.py:57
  41.9 15.5 %collective-permute-done.32.rest_2_ = bf16[48,1792]{1,0:T(8,128)(2,1)} collective-permute-done((bf16[48,1792]{1,0:T(8,128)(2,1)S(1)}, bf16[48,1792]{1,0:T(8,128)(2,1)}, u32[]{:S(2)}, u32[]{:S(2)}) %collective-permute-start.32) | collective-permute-done | bytes 172064 | tf_op jit(solution)/shard_map/ppermute | solution.py:57
  57.5 2.0 collective-permute-start.17
  60.2 12.7 %collective-permute-done.33.rest_3_ = bf16[48,1792]{1,0:T(8,128)(2,1)S(1)} collective-permute-done((bf16[48,1792]{1,0:T(8,128)(2,1)}, bf16[48,1792]{1,0:T(8,128)(2,1)S(1)}, u32[]{:S(2)}, u32[]{:S(2)}) %collective-permute-start.33) | collective-permute-done | bytes 172064 | tf_op jit(solution)/shard_map/ppermute | solution.py:57
  73.4 1.6 collective-permute-start.19
  75.5 5.1 %collective-permute-done.20.rest_6_ = bf16[128,768]{1,0:T(8,128)(2,1)S(1)} collective-permute-done((bf16[128,768]{1,0:T(8,128)(2,1)S(1)}, bf16[128,768]{1,0:T(8,128)(2,1)S(1)}, u32[]{:S(2)}, u32[]{:S(2)}) %collective-permute-start.20) | collective-permute-done | bytes 196640 | tf_op jit(solution)/shard_map/ppermute | solution.py:57
  81.2 3.7 %collective-permute-done.19.rest_5_ = bf16[128,768]{1,0:T(8,128)(2,1)S(1)} collective-permute-done((bf16[128,768]{1,0:T(8,128)(2,1)S(1)}, bf16[128,768]{1,0:T(8,128)(2,1)S(1)}, u32[]{:S(2)}, u32[]{:S(2)}) %collective-permute-start.19) | collective-permute-done | bytes 196640 | tf_op jit(solution)/shard_map/ppermute | solution.py:57
  84.9 2.9 %collective-permute-done.21.rest_7_ = bf16[128,768]{1,0:T(8,128)(2,1)S(1)} collective-permute-done((bf16[128,768]{1,0:T(8,128)(2,1)S(1)}, bf16[128,768]{1,0:T(8,128)(2,1)S(1)}, u32[]{:S(2)}, u32[]{:S(2)}) %collective-permute-start.21) | collective-permute-done | bytes 196640 | tf_op jit(solution)/shard_map/ppermute | solution.py:57
  88.8 1.6 collective-permute-start.35
  91.1 7.5 %shard_map.160 = (bf16[128,384]{1,0:T(8,128)(2,1)}, f32[8,256]{1,0:T(8,128)}, bf16[128,768]{1,0:T(8,128)(2,1)}) custom-call(s32[1]{0:T(128)} %bitcast.order_ref, bf16[128,384]{1,0:T(8,128)(2,1)} %get-tuple-element.78.q_ref, bf16[128,768]{1,0:T(8,128)(2,1)} %get-tuple-element.79.rest_0_, bf16[128,768]{1,0:T(8,128)(2,1)} %copy-done.21, ...), custom_call_target="tpu_custom_call" | custom-call | tf_op jit(solution)/shard_map/pallas_call | solution.py:489
  98.6 1.6 collective-permute-start.30
  102.4 1.5 collective-permute-done.45.rest_15_
  103.9 1.9 collective-permute-done.30.pb_ref
  106.6 5.4 %shard_map.161 = (f32[128,768]{1,0:T(8,128)}, bf16[128,768]{1,0:T(8,128)(2,1)}, bf16[128,768]{1,0:T(8,128)(2,1)}, bf16[128,768]{1,0:T(8,128)(2,1)}, bf16[128,1152]{1,0:T(8,128)(2,1)}, /*index=5*/bf16[128,576]{1,0:T(8,128)(2,1)}) custom-call(s32[1]{0:T(128)} %bitcast.order_ref, f32[128,768]{1,0:T(8,128)} %x_ref.5, bf16[128,768]{1,0:T(8,128)(2,1)} %get-tuple-element.82.pa_ref, ...), custom_call_target="tpu_custom_call" | custom-call | tf_op jit(solution)/shard_map/pallas_call | solution.py:489
  111.9 1.6 collective-permute-start.46
  113.5 4.8 %collective-permute-done.46.db_ref = bf16[128,768]{1,0:T(8,128)(2,1)S(1)} collective-permute-done((bf16[128,768]{1,0:T(8,128)(2,1)}, bf16[128,768]{1,0:T(8,128)(2,1)S(1)}, u32[]{:S(2)}, u32[]{:S(2)}) %collective-permute-start.46) | collective-permute-done | bytes 196640 | tf_op jit(solution)/shard_map/ppermute | solution.py:57
  119.0 9.8 %shard_map.162 = (bf16[512,768]{1,0:T(8,128)(2,1)}, bf16[512,768]{1,0:T(8,128)(2,1)}, bf16[512,768]{1,0:T(8,128)(2,1)}, bf16[512,768]{1,0:T(8,128)(2,1)}, f32[128,768]{1,0:T(8,128)}, /*index=5*/bf16[128,384]{1,0:T(8,128)(2,1)}) custom-call(s32[1]{0:T(128)} %bitcast.order_ref, bf16[128,384]{1,0:T(8,128)(2,1)} %get-tuple-element.78.q_ref, ...), custom_call_target="tpu_custom_call" | custom-call | tf_op jit(solution)/shard_map/pallas_call | solution.py:489
  129.4 4.0 %ffngrad.1 = (bf16[192,2560]{1,0:T(8,128)(2,1)}, bf16[192,2560]{1,0:T(8,128)(2,1)}, bf16[192,2560]{1,0:T(8,128)(2,1)}, bf16[192,2560]{1,0:T(8,128)(2,1)}) custom-call(s32[1]{0:T(128)} %bitcast.order_ref, bf16[128,768]{1,0:T(8,128)(2,1)} %get-tuple-element.116.b_ref, bf16[128,1152]{1,0:T(8,128)(2,1)} %get-tuple-element.117.dz_ref, f32[128,768]{1,0:T(8,128)} %cot_ref.5, ...), custom_call_target="tpu_custom_call" | custom-call | tf_op jit(solution)/shard_map/ffngrad/pallas_call | solution.py:642
  133.4 2.8 %oqgrad.1 = (bf16[192,2560]{1,0:T(8,128)(2,1)}, bf16[192,2560]{1,0:T(8,128)(2,1)}, bf16[192,2560]{1,0:T(8,128)(2,1)}, bf16[192,2560]{1,0:T(8,128)(2,1)}) custom-call(s32[1]{0:T(128)} %bitcast.order_ref, bf16[768,128]{1,0:T(8,128)(2,1)} %get-tuple-element.77.at_ref, ...), custom_call_target="tpu_custom_call", output_to_operand_aliasing={{0}: (5, {}), {1}: (6, {}), {2}: (7, {}), {3}: (8, {})} | custom-call | tf_op jit(solution)/shard_map/oqgrad/pallas_call | solution.py:675
  137.7 2.3 %pair_add.7 = (bf16[128,768]{1,0:T(8,128)(2,1)}, bf16[128,768]{1,0:T(8,128)(2,1)}, bf16[128,768]{1,0:T(8,128)(2,1)}, bf16[128,768]{1,0:T(8,128)(2,1)}) custom-call(bf16[512,768]{1,0:T(8,128)(2,1)} %get-tuple-element.90.keep, bf16[512,768]{1,0:T(8,128)(2,1)} %copy-done.34), custom_call_target="tpu_custom_call" | custom-call | tf_op jit(solution)/shard_map/pair_add/pallas_call | solution.py:110
  143.1 2.3 %pair_add.6 = (bf16[128,768]{1,0:T(8,128)(2,1)}, bf16[128,768]{1,0:T(8,128)(2,1)}, bf16[128,768]{1,0:T(8,128)(2,1)}, bf16[128,768]{1,0:T(8,128)(2,1)}) custom-call(bf16[512,768]{1,0:T(8,128)(2,1)} %get-tuple-element.87.keep, bf16[512,768]{1,0:T(8,128)(2,1)} %copy-done.33), custom_call_target="tpu_custom_call" | custom-call | tf_op jit(solution)/shard_map/pair_add/pallas_call | solution.py:110
  145.4 2.7 %collective-permute-done.53 = bf16[128,768]{1,0:T(8,128)(2,1)S(1)} collective-permute-done((bf16[128,768]{1,0:T(8,128)(2,1)}, bf16[128,768]{1,0:T(8,128)(2,1)S(1)}, u32[]{:S(2)}, u32[]{:S(2)}) %collective-permute-start.53) | collective-permute-done | bytes 196640 | tf_op jit(solution)/shard_map/ppermute | solution.py:57
  151.0 2.5 %pair_add.11 = (bf16[48,2560]{1,0:T(8,128)(2,1)}, bf16[48,2560]{1,0:T(8,128)(2,1)}, bf16[48,2560]{1,0:T(8,128)(2,1)}, bf16[48,2560]{1,0:T(8,128)(2,1)}) custom-call(bf16[192,2560]{1,0:T(8,128)(2,1)} %get-tuple-element.126.keep, bf16[192,2560]{1,0:T(8,128)(2,1)} %copy-done.17), custom_call_target="tpu_custom_call" | custom-call | tf_op jit(solution)/shard_map/pair_add/pallas_call | solution.py:110
  153.5 3.0 %collective-permute-done.50 = bf16[128,768]{1,0:T(8,128)(2,1)S(1)} collective-permute-done((bf16[128,768]{1,0:T(8,128)(2,1)}, bf16[128,768]{1,0:T(8,128)(2,1)S(1)}, u32[]{:S(2)}, u32[]{:S(2)}) %collective-permute-start.50) | collective-permute-done | bytes 196640 | tf_op jit(solution)/shard_map/ppermute | solution.py:57
  158.5 2.5 %pair_add.10 = (bf16[48,2560]{1,0:T(8,128)(2,1)}, bf16[48,2560]{1,0:T(8,128)(2,1)}, bf16[48,2560]{1,0:T(8,128)(2,1)}, bf16[48,2560]{1,0:T(8,128)(2,1)}) custom-call(bf16[192,2560]{1,0:T(8,128)(2,1)} %get-tuple-element.123.keep, bf16[192,2560]{1,0:T(8,128)(2,1)} %copy-done.16), custom_call_target="tpu_custom_call" | custom-call | tf_op jit(solution)/shard_map/pair_add/pallas_call | solution.py:110
  163.1 2.8 %collective-permute-done.73 = bf16[48,2560]{1,0:T(8,128)(2,1)S(1)} collective-permute-done((bf16[48,2560]{1,0:T(8,128)(2,1)}, bf16[48,2560]{1,0:T(8,128)(2,1)S(1)}, u32[]{:S(2)}, u32[]{:S(2)}) %collective-permute-start.73) | collective-permute-done | bytes 245792 | tf_op jit(solution)/shard_map/ppermute | solution.py:57
  170.6 5.6 %collective-permute-done.55.rest_3_ = bf16[128,768]{1,0:T(8,128)(2,1)S(1)} collective-permute-done((bf16[128,768]{1,0:T(8,128)(2,1)S(1)}, bf16[128,768]{1,0:T(8,128)(2,1)S(1)}, u32[]{:S(2)}, u32[]{:S(2)}) %collective-permute-start.55) | collective-permute-done | bytes 196640 | tf_op jit(solution)/shard_map/ppermute | solution.py:57
  176.9 5.2 %shard_map.163 = (bf16[192,768]{1,0:T(8,128)(2,1)}, bf16[192,768]{1,0:T(8,128)(2,1)}, bf16[192,768]{1,0:T(8,128)(2,1)}, bf16[192,768]{1,0:T(8,128)(2,1)}, bf16[128,768]{1,0:T(8,128)(2,1)}) custom-call(s32[1]{0:T(128)} %bitcast.order_ref, bf16[768,128]{1,0:T(8,128)(2,1)} %get-tuple-element.77.at_ref, bf16[128,384]{1,0:T(8,128)(2,1)} %get-tuple-element.86.dqp_ref, ...), custom_call_target="tpu_custom_call" | custom-call | tf_op jit(solution)/shard_map/pallas_call | solution.py:489
  182.3 1.6 collective-permute-done.59.recv
  184.6 1.9 pair_add.9
  189.9 1.9 pair_add.8
  193.9 1.7 collective-permute-start.65
  196.5 1.6 collective-permute-start.57
  198.1 4.5 %collective-permute-done.65 = bf16[48,768]{1,0:T(8,128)(2,1)S(1)} collective-permute-done((bf16[48,768]{1,0:T(8,128)(2,1)S(1)}, bf16[48,768]{1,0:T(8,128)(2,1)S(1)}, u32[]{:S(2)}, u32[]{:S(2)}) %collective-permute-start.65) | collective-permute-done | bytes 73760 | tf_op jit(solution)/shard_map/ppermute | solution.py:57
  202.5 2.0 collective-permute-start.56
  206.7 2.6 %collective-permute-start.66 = (bf16[48,768]{1,0:T(8,128)(2,1)S(1)}, bf16[48,768]{1,0:T(8,128)(2,1)S(1)}, u32[]{:S(2)}, u32[]{:S(2)}) collective-permute-start(bf16[48,768]{1,0:T(8,128)(2,1)S(1)} %add_convert_fusion.6), channel_id=1, source_target_pairs={{0,16},{8,24},{16,0},{24,8},{1,17},{9,25},{17,1},{25,9},{2,18},{10... | collective-permute-start | bytes 221192 | tf_op jit(solution)/shard_map/ppermute | solution.py:57
  212.7 2.7 %shard_map.165 = (f32[48,3264]{1,0:T(8,128)}, f32[2,48]{1,0:T(2,128)}) custom-call(f32[48,3264]{1,0:T(8,128)} %w_ref.5, bf16[48,768]{1,0:T(8,128)(2,1)} %get-tuple-element.106.rest_0_, bf16[48,768]{1,0:T(8,128)(2,1)} %copy-done.63, bf16[48,768]{1,0:T(8,128)(2,1)} %copy-done.64, bf16[48,768]{1,0:T(8,128)(2,1)} %copy-done.65, ...), custom_call_target="tpu_custom_call" | custom-call | tf_op jit(solution)/shard_map/pallas_call | solution.py:489
  217.5 2.7 %shard_map.164 = (f32[128,768]{1,0:T(8,128)}, f32[128,768]{1,0:T(8,128)}) custom-call(f32[128,768]{1,0:T(8,128)} %x_ref.5, bf16[128,768]{1,0:T(8,128)(2,1)} %get-tuple-element.99.da_ref, bf16[128,768]{1,0:T(8,128)(2,1)} %copy-done.53, f32[128,768]{1,0:T(8,128)} %get-tuple-element.100.dhid_ref, f32[8,768]{1,0:T(8,128)} %get-tuple-element.83.g_ref, ...), custom_call_target="tpu_custom_call" | custom-call | tf_op jit(solution)/shard_map/pallas_call | solution.py:489
  220.3 2.8 %adam.1 = (f32[48,3264]{1,0:T(8,128)}, f32[48,3264]{1,0:T(8,128)}, f32[48,3264]{1,0:T(8,128)}) custom-call(f32[48,3264]{1,0:T(8,128)} %w_ref.5, f32[48,3264]{1,0:T(8,128)} %get-tuple-element.69.g_ref, f32[48,3264]{1,0:T(8,128)} %m_ref.3, f32[48,3264]{1,0:T(8,128)} %v_ref.3), custom_call_target="tpu_custom_call" | custom-call | tf_op jit(solution)/shard_map/adam/pallas_call | solution.py:721
  (289 shorter events, 51.7 us)
Async XLA Ops:
  5.6 10.0 %collective-permute-start.1 = (bf16[48,1664]{1,0:T(8,128)(2,1)S(1)}, bf16[48,1664]{1,0:T(8,128)(2,1)S(1)}, u32[]{:S(2)}, u32[]{:S(2)}) collective-permute-start(bf16[48,1664]{1,0:T(8,128)(2,1)S(1)} %fusion.1.rest_0_.rest_16_.rest_4_), channel_id=1, source_target_pairs={{0,16},{8,24},{16,0},{24,8},{1,17},{9,25},{17,1},{25,9},{2,18},{10... | collective-permute-start | bytes 479240 | tf_op jit(solution)/shard_map/ppermute | solution.py:57
  8.2 8.0 %collective-permute-start.7 = (bf16[48,1664]{1,0:T(8,128)(2,1)S(1)}, bf16[48,1664]{1,0:T(8,128)(2,1)S(1)}, u32[]{:S(2)}, u32[]{:S(2)}) collective-permute-start(bf16[48,1664]{1,0:T(8,128)(2,1)S(1)} %fusion.1.rest_0_.rest_16_.rest_4_), channel_id=1, source_target_pairs={{0,2},{2,0},{4,6},{6,4},{1,3},{3,1},{5,7},{7,5},{8,10},{10,8},{12,... | collective-permute-start | bytes 479240 | tf_op jit(solution)/shard_map/ppermute | solution.py:57
  8.2 8.8 %collective-permute-start = (bf16[48,1664]{1,0:T(8,128)(2,1)S(1)}, bf16[48,1664]{1,0:T(8,128)(2,1)S(1)}, u32[]{:S(2)}, u32[]{:S(2)}) collective-permute-start(bf16[48,1664]{1,0:T(8,128)(2,1)S(1)} %fusion.1.rest_0_.rest_16_.rest_4_), channel_id=1, source_target_pairs={{0,8},{8,0},{16,24},{24,16},{1,9},{9,1},{17,25},{25,17},{2,10},{10... | collective-permute-start | bytes 479240 | tf_op jit(solution)/shard_map/ppermute | solution.py:57
  17.1 9.6 %collective-permute-start.4 = (bf16[48,1664]{1,0:T(8,128)(2,1)S(1)}, bf16[48,1664]{1,0:T(8,128)(2,1)S(1)}, u32[]{:S(2)}, u32[]{:S(2)}) collective-permute-start(bf16[48,1664]{1,0:T(8,128)(2,1)S(1)} %collective-permute-done.rest_1_.rest_17_.rest_5_), channel_id=1, source_target_pairs={{0,4},{2,6},{4,0},{6,2},{1,5},{3,7},{5,1},{7,3},{8,12},{10,14},{12... | collective-permute-start | bytes 479240 | tf_op jit(solution)/shard_map/ppermute | solution.py:57
  20.9 9.2 %collective-permute-start.6 = (bf16[48,1664]{1,0:T(8,128)(2,1)S(1)}, bf16[48,1664]{1,0:T(8,128)(2,1)S(1)}, u32[]{:S(2)}, u32[]{:S(2)}) collective-permute-start(bf16[48,1664]{1,0:T(8,128)(2,1)S(1)} %collective-permute-done.2.rest_3_.rest_19_.rest_7_), channel_id=1, source_target_pairs={{0,4},{2,6},{4,0},{6,2},{1,5},{3,7},{5,1},{7,3},{8,12},{10,14},{12... | collective-permute-start | bytes 479240 | tf_op jit(solution)/shard_map/ppermute | solution.py:57
  21.5 19.8 %collective-permute-start.34 = (bf16[48,1792]{1,0:T(8,128)(2,1)S(1)}, bf16[48,1792]{1,0:T(8,128)(2,1)S(1)}, u32[]{:S(2)}, u32[]{:S(2)}) collective-permute-start(bf16[48,1792]{1,0:T(8,128)(2,1)S(1)} %pad.9.rest_0_), channel_id=1, source_target_pairs={{0,4},{2,6},{4,0},{6,2},{1,5},{3,7},{5,1},{7,3},{8,12},{10,14},{12... | collective-permute-start | bytes 516104 | tf_op jit(solution)/shard_map/ppermute | solution.py:57
  23.3 8.6 %collective-permute-start.10 = (bf16[48,1664]{1,0:T(8,128)(2,1)S(1)}, bf16[48,1664]{1,0:T(8,128)(2,1)S(1)}, u32[]{:S(2)}, u32[]{:S(2)}) collective-permute-start(bf16[48,1664]{1,0:T(8,128)(2,1)S(1)} %collective-permute-done.2.rest_3_.rest_19_.rest_7_), channel_id=1, source_target_pairs={{0,2},{2,0},{4,6},{6,4},{1,3},{3,1},{5,7},{7,5},{8,10},{10,8},{12,... | collective-permute-start | bytes 479240 | tf_op jit(solution)/shard_map/ppermute | solution.py:57
  31.3 10.1 %collective-permute-start.38 = (bf16[48,1792]{1,0:T(8,128)(2,1)S(1)}, bf16[48,1792]{1,0:T(8,128)(2,1)S(1)}, u32[]{:S(2)}, u32[]{:S(2)}) collective-permute-start(bf16[48,1792]{1,0:T(8,128)(2,1)S(1)} %pad.9.rest_0_), channel_id=1, source_target_pairs={{0,2},{2,0},{4,6},{6,4},{1,3},{3,1},{5,7},{7,5},{8,10},{10,8},{12,... | collective-permute-start | bytes 516104 | tf_op jit(solution)/shard_map/ppermute | solution.py:57
  36.9 20.5 %collective-permute-start.16 = (bf16[128,768]{1,0:T(8,128)(2,1)}, bf16[128,768]{1,0:T(8,128)(2,1)S(1)}, u32[]{:S(2)}, u32[]{:S(2)}) collective-permute-start(bf16[128,768]{1,0:T(8,128)(2,1)} %get-tuple-element.79.rest_0_), channel_id=1, source_target_pairs={{0,16},{8,24},{16,0},{24,8},{1,17},{9,25},{17,1},{25,9},{2,18},{10... | collective-permute-start | bytes 589832 | tf_op jit(solution)/shard_map/ppermute | solution.py:57
  40.4 17.0 %collective-permute-start.32 = (bf16[48,1792]{1,0:T(8,128)(2,1)S(1)}, bf16[48,1792]{1,0:T(8,128)(2,1)}, u32[]{:S(2)}, u32[]{:S(2)}) collective-permute-start(bf16[48,1792]{1,0:T(8,128)(2,1)S(1)} %pad.9.rest_0_), channel_id=1, source_target_pairs={{0,16},{8,24},{16,0},{24,8},{1,17},{9,25},{17,1},{25,9},{2,18},{10... | collective-permute-start | bytes 516104 | tf_op jit(solution)/shard_map/ppermute | solution.py:57
  40.5 16.9 %collective-permute-start.31 = (bf16[48,1792]{1,0:T(8,128)(2,1)S(1)}, bf16[48,1792]{1,0:T(8,128)(2,1)}, u32[]{:S(2)}, u32[]{:S(2)}) collective-permute-start(bf16[48,1792]{1,0:T(8,128)(2,1)S(1)} %pad.9.rest_0_), channel_id=1, source_target_pairs={{0,8},{8,0},{16,24},{24,16},{1,9},{9,1},{17,25},{25,17},{2,10},{10... | collective-permute-start | bytes 516104 | tf_op jit(solution)/shard_map/ppermute | solution.py:57
  41.4 18.1 %collective-permute-start.42 = (bf16[48,1792]{1,0:T(8,128)(2,1)S(1)}, bf16[48,1792]{1,0:T(8,128)(2,1)S(1)}, u32[]{:S(2)}, u32[]{:S(2)}) collective-permute-start(bf16[48,1792]{1,0:T(8,128)(2,1)S(1)} %collective-permute-done.34.rest_4_), channel_id=1, source_target_pairs={{0,2},{2,0},{4,6},{6,4},{1,3},{3,1},{5,7},{7,5},{8,10},{10,8},{12,... | collective-permute-start | bytes 516104 | tf_op jit(solution)/shard_map/ppermute | solution.py:57
  41.4 18.8 %collective-permute-start.18 = (bf16[128,768]{1,0:T(8,128)(2,1)}, bf16[128,768]{1,0:T(8,128)(2,1)S(1)}, u32[]{:S(2)}, u32[]{:S(2)}) collective-permute-start(bf16[128,768]{1,0:T(8,128)(2,1)} %get-tuple-element.79.rest_0_), channel_id=1, source_target_pairs={{0,4},{2,6},{4,0},{6,2},{1,5},{3,7},{5,1},{7,3},{8,12},{10,14},{12... | collective-permute-start | bytes 589832 | tf_op jit(solution)/shard_map/ppermute | solution.py:57
  57.4 16.0 %collective-permute-start.22 = (bf16[128,768]{1,0:T(8,128)(2,1)}, bf16[128,768]{1,0:T(8,128)(2,1)S(1)}, u32[]{:S(2)}, u32[]{:S(2)}) collective-permute-start(bf16[128,768]{1,0:T(8,128)(2,1)} %get-tuple-element.79.rest_0_), channel_id=1, source_target_pairs={{0,2},{2,0},{4,6},{6,4},{1,3},{3,1},{5,7},{7,5},{8,10},{10,8},{12,... | collective-permute-start | bytes 589832 | tf_op jit(solution)/shard_map/ppermute | solution.py:57
  57.4 16.0 %collective-permute-start.15 = (bf16[128,768]{1,0:T(8,128)(2,1)}, bf16[128,768]{1,0:T(8,128)(2,1)S(1)}, u32[]{:S(2)}, u32[]{:S(2)}) collective-permute-start(bf16[128,768]{1,0:T(8,128)(2,1)} %get-tuple-element.79.rest_0_), channel_id=1, source_target_pairs={{0,8},{8,0},{16,24},{24,16},{1,9},{9,1},{17,25},{25,17},{2,10},{10... | collective-permute-start | bytes 589832 | tf_op jit(solution)/shard_map/ppermute | solution.py:57
  57.5 17.5 %collective-permute-start.17 = (bf16[128,768]{1,0:T(8,128)(2,1)S(1)}, bf16[128,768]{1,0:T(8,128)(2,1)S(1)}, u32[]{:S(2)}, u32[]{:S(2)}) collective-permute-start(bf16[128,768]{1,0:T(8,128)(2,1)S(1)} %collective-permute-done.16.rest_2_), channel_id=1, source_target_pairs={{0,8},{8,0},{16,24},{24,16},{1,9},{9,1},{17,25},{25,17},{2,10},{10... | collective-permute-start | bytes 589832 | tf_op jit(solution)/shard_map/ppermute | solution.py:57
  59.5 13.4 %collective-permute-start.33 = (bf16[48,1792]{1,0:T(8,128)(2,1)}, bf16[48,1792]{1,0:T(8,128)(2,1)S(1)}, u32[]{:S(2)}, u32[]{:S(2)}) collective-permute-start(bf16[48,1792]{1,0:T(8,128)(2,1)} %collective-permute-done.32.rest_2_), channel_id=1, source_target_pairs={{0,8},{8,0},{16,24},{24,16},{1,9},{9,1},{17,25},{25,17},{2,10},{10... | collective-permute-start | bytes 516104 | tf_op jit(solution)/shard_map/ppermute | solution.py:57
  60.2 15.4 %collective-permute-start.26 = (bf16[128,768]{1,0:T(8,128)(2,1)S(1)}, bf16[128,768]{1,0:T(8,128)(2,1)S(1)}, u32[]{:S(2)}, u32[]{:S(2)}) collective-permute-start(bf16[128,768]{1,0:T(8,128)(2,1)S(1)} %collective-permute-done.18.rest_4_), channel_id=1, source_target_pairs={{0,2},{2,0},{4,6},{6,4},{1,3},{3,1},{5,7},{7,5},{8,10},{10,8},{12,... | collective-permute-start | bytes 589832 | tf_op jit(solution)/shard_map/ppermute | solution.py:57
  73.4 11.4 %collective-permute-start.19 = (bf16[128,768]{1,0:T(8,128)(2,1)S(1)}, bf16[128,768]{1,0:T(8,128)(2,1)S(1)}, u32[]{:S(2)}, u32[]{:S(2)}) collective-permute-start(bf16[128,768]{1,0:T(8,128)(2,1)S(1)} %collective-permute-done.15.rest_1_), channel_id=1, source_target_pairs={{0,4},{2,6},{4,0},{6,2},{1,5},{3,7},{5,1},{7,3},{8,12},{10,14},{12... | collective-permute-start | bytes 589832 | tf_op jit(solution)/shard_map/ppermute | solution.py:57
  75.0 12.8 %collective-permute-start.21 = (bf16[128,768]{1,0:T(8,128)(2,1)S(1)}, bf16[128,768]{1,0:T(8,128)(2,1)S(1)}, u32[]{:S(2)}, u32[]{:S(2)}) collective-permute-start(bf16[128,768]{1,0:T(8,128)(2,1)S(1)} %collective-permute-done.17.rest_3_), channel_id=1, source_target_pairs={{0,4},{2,6},{4,0},{6,2},{1,5},{3,7},{5,1},{7,3},{8,12},{10,14},{12... | collective-permute-start | bytes 589832 | tf_op jit(solution)/shard_map/ppermute | solution.py:57
  75.5 12.2 %collective-permute-start.23 = (bf16[128,768]{1,0:T(8,128)(2,1)S(1)}, bf16[128,768]{1,0:T(8,128)(2,1)S(1)}, u32[]{:S(2)}, u32[]{:S(2)}) collective-permute-start(bf16[128,768]{1,0:T(8,128)(2,1)S(1)} %collective-permute-done.15.rest_1_), channel_id=1, source_target_pairs={{0,2},{2,0},{4,6},{6,4},{1,3},{3,1},{5,7},{7,5},{8,10},{10,8},{12,... | collective-permute-start | bytes 589832 | tf_op jit(solution)/shard_map/ppermute | solution.py:57
  80.7 8.1 %collective-permute-start.25 = (bf16[128,768]{1,0:T(8,128)(2,1)S(1)}, bf16[128,768]{1,0:T(8,128)(2,1)S(1)}, u32[]{:S(2)}, u32[]{:S(2)}) collective-permute-start(bf16[128,768]{1,0:T(8,128)(2,1)S(1)} %collective-permute-done.17.rest_3_), channel_id=1, source_target_pairs={{0,2},{2,0},{4,6},{6,4},{1,3},{3,1},{5,7},{7,5},{8,10},{10,8},{12,... | collective-permute-start | bytes 589832 | tf_op jit(solution)/shard_map/ppermute | solution.py:57
  87.8 10.9 %collective-permute-start.40 = (bf16[48,1792]{1,0:T(8,128)(2,1)}, bf16[48,1792]{1,0:T(8,128)(2,1)}, u32[]{:S(2)}, u32[]{:S(2)}) collective-permute-start(bf16[48,1792]{1,0:T(8,128)(2,1)} %collective-permute-done.32.rest_2_), channel_id=1, source_target_pairs={{0,2},{2,0},{4,6},{6,4},{1,3},{3,1},{5,7},{7,5},{8,10},{10,8},{12,... | collective-permute-start | bytes 516104 | tf_op jit(solution)/shard_map/ppermute | solution.py:57
  88.3 12.0 %collective-permute-start.36 = (bf16[48,1792]{1,0:T(8,128)(2,1)}, bf16[48,1792]{1,0:T(8,128)(2,1)}, u32[]{:S(2)}, u32[]{:S(2)}) collective-permute-start(bf16[48,1792]{1,0:T(8,128)(2,1)} %collective-permute-done.32.rest_2_), channel_id=1, source_target_pairs={{0,4},{2,6},{4,0},{6,2},{1,5},{3,7},{5,1},{7,3},{8,12},{10,14},{12... | collective-permute-start | bytes 516104 | tf_op jit(solution)/shard_map/ppermute | solution.py:57
  88.8 11.5 %collective-permute-start.39 = (bf16[48,1792]{1,0:T(8,128)(2,1)}, bf16[48,1792]{1,0:T(8,128)(2,1)}, u32[]{:S(2)}, u32[]{:S(2)}) collective-permute-start(bf16[48,1792]{1,0:T(8,128)(2,1)} %collective-permute-done.31.rest_1_), channel_id=1, source_target_pairs={{0,2},{2,0},{4,6},{6,4},{1,3},{3,1},{5,7},{7,5},{8,10},{10,8},{12,... | collective-permute-start | bytes 516104 | tf_op jit(solution)/shard_map/ppermute | solution.py:57
  88.8 12.0 %collective-permute-start.35 = (bf16[48,1792]{1,0:T(8,128)(2,1)}, bf16[48,1792]{1,0:T(8,128)(2,1)}, u32[]{:S(2)}, u32[]{:S(2)}) collective-permute-start(bf16[48,1792]{1,0:T(8,128)(2,1)} %collective-permute-done.31.rest_1_), channel_id=1, source_target_pairs={{0,4},{2,6},{4,0},{6,2},{1,5},{3,7},{5,1},{7,3},{8,12},{10,14},{12... | collective-permute-start | bytes 516104 | tf_op jit(solution)/shard_map/ppermute | solution.py:57
  90.4 11.9 %collective-permute-start.37 = (bf16[48,1792]{1,0:T(8,128)(2,1)S(1)}, bf16[48,1792]{1,0:T(8,128)(2,1)}, u32[]{:S(2)}, u32[]{:S(2)}) collective-permute-start(bf16[48,1792]{1,0:T(8,128)(2,1)S(1)} %collective-permute-done.33.rest_3_), channel_id=1, source_target_pairs={{0,4},{2,6},{4,0},{6,2},{1,5},{3,7},{5,1},{7,3},{8,12},{10,14},{12... | collective-permute-start | bytes 516104 | tf_op jit(solution)/shard_map/ppermute | solution.py:57
  128.8 8.0 %collective-permute-start.48 = (bf16[512,768]{1,0:T(8,128)(2,1)}, bf16[512,768]{1,0:T(8,128)(2,1)S(1)}, u32[]{:S(2)}, u32[]{:S(2)}) collective-permute-start(bf16[512,768]{1,0:T(8,128)(2,1)} %get-tuple-element.91), channel_id=1, source_target_pairs={{0,2},{2,0},{4,6},{6,4},{1,3},{3,1},{5,7},{7,5},{8,10},{10,8},{12,... | collective-permute-start | bytes 2359304 | tf_op jit(solution)/shard_map/ppermute | solution.py:57
  128.9 13.2 %collective-permute-start.47 = (bf16[512,768]{1,0:T(8,128)(2,1)}, bf16[512,768]{1,0:T(8,128)(2,1)S(1)}, u32[]{:S(2)}, u32[]{:S(2)}) collective-permute-start(bf16[512,768]{1,0:T(8,128)(2,1)} %get-tuple-element.88), channel_id=1, source_target_pairs={{0,2},{2,0},{4,6},{6,4},{1,3},{3,1},{5,7},{7,5},{8,10},{10,8},{12,... | collective-permute-start | bytes 2359304 | tf_op jit(solution)/shard_map/ppermute | solution.py:57
  136.2 13.8 %collective-permute-start.68 = (bf16[192,2560]{1,0:T(8,128)(2,1)}, bf16[192,2560]{1,0:T(8,128)(2,1)S(1)}, u32[]{:S(2)}, u32[]{:S(2)}) collective-permute-start(bf16[192,2560]{1,0:T(8,128)(2,1)} %get-tuple-element.127), channel_id=1, source_target_pairs={{0,2},{2,0},{4,6},{6,4},{1,3},{3,1},{5,7},{7,5},{8,10},{10,8},{12,... | collective-permute-start | bytes 2949128 | tf_op jit(solution)/shard_map/ppermute | solution.py:57
  136.3 21.2 %collective-permute-start.67 = (bf16[192,2560]{1,0:T(8,128)(2,1)}, bf16[192,2560]{1,0:T(8,128)(2,1)S(1)}, u32[]{:S(2)}, u32[]{:S(2)}) collective-permute-start(bf16[192,2560]{1,0:T(8,128)(2,1)} %get-tuple-element.124), channel_id=1, source_target_pairs={{0,2},{2,0},{4,6},{6,4},{1,3},{3,1},{5,7},{7,5},{8,10},{10,8},{12,... | collective-permute-start | bytes 2949128 | tf_op jit(solution)/shard_map/ppermute | solution.py:57
  140.0 8.0 %collective-permute-start.53 = (bf16[128,768]{1,0:T(8,128)(2,1)}, bf16[128,768]{1,0:T(8,128)(2,1)S(1)}, u32[]{:S(2)}, u32[]{:S(2)}) collective-permute-start(bf16[128,768]{1,0:T(8,128)(2,1)} %get-tuple-element.98), channel_id=1, source_target_pairs={{0,4},{2,6},{4,0},{6,2},{1,5},{3,7},{5,1},{7,3},{8,12},{10,14},{12... | collective-permute-start | bytes 589832 | tf_op jit(solution)/shard_map/ppermute | solution.py:57
  141.0 26.1 %collective-permute-start.49 = (bf16[128,768]{1,0:T(8,128)(2,1)}, bf16[128,768]{1,0:T(8,128)(2,1)S(1)}, u32[]{:S(2)}, u32[]{:S(2)}) collective-permute-start(bf16[128,768]{1,0:T(8,128)(2,1)} %get-tuple-element.92), channel_id=1, source_target_pairs={{0,4},{2,6},{4,0},{6,2},{1,5},{3,7},{5,1},{7,3},{8,12},{10,14},{12... | collective-permute-start | bytes 589832 | tf_op jit(solution)/shard_map/ppermute | solution.py:57
  142.1 14.4 %collective-permute-start.50 = (bf16[128,768]{1,0:T(8,128)(2,1)}, bf16[128,768]{1,0:T(8,128)(2,1)S(1)}, u32[]{:S(2)}, u32[]{:S(2)}) collective-permute-start(bf16[128,768]{1,0:T(8,128)(2,1)} %get-tuple-element.94), channel_id=1, source_target_pairs={{0,4},{2,6},{4,0},{6,2},{1,5},{3,7},{5,1},{7,3},{8,12},{10,14},{12... | collective-permute-start | bytes 589832 | tf_op jit(solution)/shard_map/ppermute | solution.py:57
  148.0 12.9 %collective-permute-start.52 = (bf16[128,768]{1,0:T(8,128)(2,1)}, bf16[128,768]{1,0:T(8,128)(2,1)S(1)}, u32[]{:S(2)}, u32[]{:S(2)}) collective-permute-start(bf16[128,768]{1,0:T(8,128)(2,1)} %get-tuple-element.96), channel_id=1, source_target_pairs={{0,4},{2,6},{4,0},{6,2},{1,5},{3,7},{5,1},{7,3},{8,12},{10,14},{12... | collective-permute-start | bytes 589832 | tf_op jit(solution)/shard_map/ppermute | solution.py:57
  150.0 12.1 %collective-permute-start.54 = (bf16[128,768]{1,0:T(8,128)(2,1)S(1)}, bf16[128,768]{1,0:T(8,128)(2,1)S(1)}, u32[]{:S(2)}, u32[]{:S(2)}) collective-permute-start(bf16[128,768]{1,0:T(8,128)(2,1)S(1)} %add_convert_fusion.4), channel_id=1, source_target_pairs={{0,8},{8,0},{16,24},{24,16},{1,9},{9,1},{17,25},{25,17},{2,10},{10... | collective-permute-start | bytes 589832 | tf_op jit(solution)/shard_map/ppermute | solution.py:57
  156.5 9.5 %collective-permute-start.73 = (bf16[48,2560]{1,0:T(8,128)(2,1)}, bf16[48,2560]{1,0:T(8,128)(2,1)S(1)}, u32[]{:S(2)}, u32[]{:S(2)}) collective-permute-start(bf16[48,2560]{1,0:T(8,128)(2,1)} %get-tuple-element.134), channel_id=1, source_target_pairs={{0,4},{2,6},{4,0},{6,2},{1,5},{3,7},{5,1},{7,3},{8,12},{10,14},{12... | collective-permute-start | bytes 737288 | tf_op jit(solution)/shard_map/ppermute | solution.py:57
  157.5 11.6 %collective-permute-start.51 = (bf16[128,768]{1,0:T(8,128)(2,1)S(1)}, bf16[128,768]{1,0:T(8,128)(2,1)S(1)}, u32[]{:S(2)}, u32[]{:S(2)}) collective-permute-start(bf16[128,768]{1,0:T(8,128)(2,1)S(1)} %add_convert_fusion.5), channel_id=1, source_target_pairs={{0,8},{8,0},{16,24},{24,16},{1,9},{9,1},{17,25},{25,17},{2,10},{10... | collective-permute-start | bytes 589832 | tf_op jit(solution)/shard_map/ppermute | solution.py:57
  161.0 44.6 %collective-permute-start.69 = (bf16[48,2560]{1,0:T(8,128)(2,1)}, bf16[48,2560]{1,0:T(8,128)(2,1)S(1)}, u32[]{:S(2)}, u32[]{:S(2)}) collective-permute-start(bf16[48,2560]{1,0:T(8,128)(2,1)} %get-tuple-element.128), channel_id=1, source_target_pairs={{0,4},{2,6},{4,0},{6,2},{1,5},{3,7},{5,1},{7,3},{8,12},{10,14},{12... | collective-permute-start | bytes 737288 | tf_op jit(solution)/shard_map/ppermute | solution.py:57
  162.1 20.1 %collective-permute-start.70 = (bf16[48,2560]{1,0:T(8,128)(2,1)}, bf16[48,2560]{1,0:T(8,128)(2,1)S(1)}, u32[]{:S(2)}, u32[]{:S(2)}) collective-permute-start(bf16[48,2560]{1,0:T(8,128)(2,1)} %get-tuple-element.130), channel_id=1, source_target_pairs={{0,4},{2,6},{4,0},{6,2},{1,5},{3,7},{5,1},{7,3},{8,12},{10,14},{12... | collective-permute-start | bytes 737288 | tf_op jit(solution)/shard_map/ppermute | solution.py:57
  165.9 10.3 %collective-permute-start.55 = (bf16[128,768]{1,0:T(8,128)(2,1)S(1)}, bf16[128,768]{1,0:T(8,128)(2,1)S(1)}, u32[]{:S(2)}, u32[]{:S(2)}) collective-permute-start(bf16[128,768]{1,0:T(8,128)(2,1)S(1)} %add_convert_fusion.3), channel_id=1, source_target_pairs={{0,16},{8,24},{16,0},{24,8},{1,17},{9,25},{17,1},{25,9},{2,18},{10... | collective-permute-start | bytes 589832 | tf_op jit(solution)/shard_map/ppermute | solution.py:57
  168.1 18.4 %collective-permute-start.72 = (bf16[48,2560]{1,0:T(8,128)(2,1)S(1)}, bf16[48,2560]{1,0:T(8,128)(2,1)S(1)}, u32[]{:S(2)}, u32[]{:S(2)}) collective-permute-start(bf16[48,2560]{1,0:T(8,128)(2,1)S(1)} %copy-done.69), channel_id=1, source_target_pairs={{0,4},{2,6},{4,0},{6,2},{1,5},{3,7},{5,1},{7,3},{8,12},{10,14},{12... | collective-permute-start | bytes 737288 | tf_op jit(solution)/shard_map/ppermute | solution.py:57
  169.1 18.5 %collective-permute-start.74 = (bf16[48,2560]{1,0:T(8,128)(2,1)S(1)}, bf16[48,2560]{1,0:T(8,128)(2,1)S(1)}, u32[]{:S(2)}, u32[]{:S(2)}) collective-permute-start(bf16[48,2560]{1,0:T(8,128)(2,1)S(1)} %add_convert_fusion.1), channel_id=1, source_target_pairs={{0,8},{8,0},{16,24},{24,16},{1,9},{9,1},{17,25},{25,17},{2,10},{10... | collective-permute-start | bytes 737288 | tf_op jit(solution)/shard_map/ppermute | solution.py:57
  182.2 24.4 %collective-permute-start.71 = (bf16[48,2560]{1,0:T(8,128)(2,1)S(1)}, bf16[48,2560]{1,0:T(8,128)(2,1)S(1)}, u32[]{:S(2)}, u32[]{:S(2)}) collective-permute-start(bf16[48,2560]{1,0:T(8,128)(2,1)S(1)} %add_convert_fusion.2), channel_id=1, source_target_pairs={{0,8},{8,0},{16,24},{24,16},{1,9},{9,1},{17,25},{25,17},{2,10},{10... | collective-permute-start | bytes 737288 | tf_op jit(solution)/shard_map/ppermute | solution.py:57
  187.7 19.0 %collective-permute-start.75 = (bf16[48,2560]{1,0:T(8,128)(2,1)S(1)}, bf16[48,2560]{1,0:T(8,128)(2,1)S(1)}, u32[]{:S(2)}, u32[]{:S(2)}) collective-permute-start(bf16[48,2560]{1,0:T(8,128)(2,1)S(1)} %add_convert_fusion), channel_id=1, source_target_pairs={{0,16},{8,24},{16,0},{24,8},{1,17},{9,25},{17,1},{25,9},{2,18},{10... | collective-permute-start | bytes 737288 | tf_op jit(solution)/shard_map/ppermute | solution.py:57
  193.9 8.7 %collective-permute-start.65 = (bf16[48,768]{1,0:T(8,128)(2,1)S(1)}, bf16[48,768]{1,0:T(8,128)(2,1)S(1)}, u32[]{:S(2)}, u32[]{:S(2)}) collective-permute-start(bf16[48,768]{1,0:T(8,128)(2,1)S(1)} %add_convert_fusion.7), channel_id=1, source_target_pairs={{0,8},{8,0},{16,24},{24,16},{1,9},{9,1},{17,25},{25,17},{2,10},{10... | collective-permute-start | bytes 221192 | tf_op jit(solution)/shard_map/ppermute | solution.py:57
  196.5 19.7 %collective-permute-start.57 = (bf16[128,768]{1,0:T(8,128)(2,1)S(1)}, bf16[128,768]{1,0:T(8,128)(2,1)S(1)}, u32[]{:S(2)}, u32[]{:S(2)}) collective-permute-start(bf16[128,768]{1,0:T(8,128)(2,1)S(1)} %copy-done.50), channel_id=1, source_target_pairs={{0,1},{1,0},{2,3},{3,2},{4,5},{5,4},{6,7},{7,6},{8,9},{9,8},{10,11... | collective-permute-start | bytes 589832 | tf_op jit(solution)/shard_map/ppermute | solution.py:57
  202.5 13.7 %collective-permute-start.56 = (bf16[128,768]{1,0:T(8,128)(2,1)S(1)}, bf16[128,768]{1,0:T(8,128)(2,1)S(1)}, u32[]{:S(2)}, u32[]{:S(2)}) collective-permute-start(bf16[128,768]{1,0:T(8,128)(2,1)S(1)} %copy-done.51), channel_id=1, source_target_pairs={{0,1},{1,0},{2,3},{3,2},{4,5},{5,4},{6,7},{7,6},{8,9},{9,8},{10,11... | collective-permute-start | bytes 589832 | tf_op jit(solution)/shard_map/ppermute | solution.py:57
  (102 other events, 719.7 us)

commit v7 on v6

--- a/solution.py
+++ b/solution.py
@@ -36,6 +36,10 @@
 HBM = pl.BlockSpec(memory_space=pltpu.HBM)
 
 
+def near(x):
+    return pltpu.with_memory_space_constraint(x, pltpu.VMEM) if staged() else x
+
+
 def sds(shape, dtype):
     return jax.ShapeDtypeStruct(shape, dtype)
 
@@ -80,25 +84,20 @@
     return [got[j] for j in chunk_order()]
 
 
-def add_kernel(keep, recv, *rest):
+def add_kernel(keep, got, *rest):
     outs = rest[:4]
-    kept, got, done, sems = rest[4:]
+    kept, done, sems = rest[4:]
     rows = outs[0].shape[0]
     at = [pl.ds(i * rows, rows) for i in range(4)]
     loads = [
-        [
-            pltpu.make_async_copy(src.at[at[i], :], dst.at[at[i], :], sems.at[k, i])
-            for k, (src, dst) in enumerate(((keep, kept), (recv, got)))
-        ]
+        pltpu.make_async_copy(keep.at[at[i], :], kept.at[at[i], :], sems.at[0, i])
         for i in range(4)
     ]
-    stores = [pltpu.make_async_copy(done.at[at[i], :], outs[i], sems.at[2, i]) for i in range(4)]
-    for pair in loads:
-        for copy in pair:
-            copy.start()
+    stores = [pltpu.make_async_copy(done.at[at[i], :], outs[i], sems.at[1, i]) for i in range(4)]
+    for copy in loads:
+        copy.start()
     for i in range(4):
-        for copy in loads[i]:
-            copy.wait()
+        loads[i].wait()
         done[at[i], :] = (kept[at[i], :].astype(F32) + got[at[i], :].astype(F32)).astype(BF16)
         stores[i].start()
     for copy in stores:
@@ -110,11 +109,11 @@
     return pl.pallas_call(
         add_kernel,
         out_shape=[sds((rows, cols), BF16)] * 4,
-        in_specs=[HBM, HBM],
+        in_specs=[HBM, VM],
         out_specs=[HBM] * 4,
-        scratch_shapes=[pltpu.VMEM(keep.shape, BF16)] * 3 + [pltpu.SemaphoreType.DMA((3, 4))],
+        scratch_shapes=[pltpu.VMEM(keep.shape, BF16)] * 2 + [pltpu.SemaphoreType.DMA((2, 4))],
         name="pair_add",
-    )(keep, recv)
+    )(keep, near(recv))
 
 
 def native_sum(part):
@@ -594,7 +593,7 @@
         [sds((d, toks), BF16), sds((toks, width), BF16), sds((toks, 2 * width), BF16), sds((8, d), F32)],
         [SM, VM, VM, VM] + [ANY] * nw,
         [pltpu.VMEM((d, wq_cols), BF16), wsem],
-        [order, inputs, cos, sin] + first_chunks,
+        [order, inputs, cos, sin] + [near(x) for x in first_chunks],
     )
     keys = gather(kv)
     rest_chunks = gather(w_rest)
@@ -616,7 +615,7 @@
             ksem,
             wsem,
         ],
-        [order, q] + keys + first_chunks,
+        [order, q] + [near(x) for x in keys] + first_chunks,
     )
     out_other = head_swap(out_part)
 
@@ -632,7 +631,7 @@
         ],
         [SM] + [VM] * 5 + [ANY] * nw,
         [pltpu.VMEM((d, rest_cols), BF16), wsem],
-        [order, inputs, out_part, out_other, cotangent, g] + rest_chunks,
+        [order, inputs, out_part, near(out_other), cotangent, g] + [near(x) for x in rest_chunks],
     )
     db_other = head_swap(db_part)
     ffn_other = head_swap(ffn_part)
@@ -668,7 +667,7 @@
             ksem,
             wsem,
         ],
-        [order, q, attn, lse, hidden, cotangent, g, db_part, db_other, cos, sin]
+        [order, q, attn, lse, hidden, cotangent, g, db_part, near(db_other), cos, sin]
         + keys
         + first_chunks,
     )
@@ -693,7 +692,7 @@
         [sds((d // parts, 2 * width), BF16)] * parts + [sds((toks, d), BF16)],
         [SM] + [VM] * 4 + [VM] * nt + [ANY] * nw,
         [pltpu.VMEM((d, 3 * width), BF16), wsem],
-        [order, a_t, dqp, cos, sin] + kv_terms + first_chunks,
+        [order, a_t, dqp, cos, sin] + [near(x) for x in kv_terms] + first_chunks,
     )
     da_other = head_swap(da_part)
     input_grad, outputs = call(
@@ -701,7 +700,7 @@
         [sds((toks, d), F32)] * 2,
         [VM] * 8,
         [],
-        [inputs, da_part, da_other, dhid, g, hidden, ffn_part, ffn_other],
+        [inputs, da_part, near(da_other), dhid, g, hidden, ffn_part, near(ffn_other)],
     )
     if staged():
         first_terms = scatter_sum(w_groups, pair_swap(w_groups))
@@ -713,7 +712,7 @@
         [sds(full, F32), sds(gains.shape, F32)],
         [VM] * (1 + 2 * nt),
         [],
-        [weights] + first_terms + rest_terms,
+        [weights] + [near(x) for x in first_terms + rest_terms],
     )
     gain_other = head_swap(gain_part)
     step_rows = rows // 2 if rows % 16 == 0 else rows
@@ -731,7 +730,7 @@
         [sds(gains.shape, F32)] * 4,
         [VM] * 5,
         [],
-        [gain_part, gain_other, gains, gain_moment, gain_second],
+        [near(gain_part), near(gain_other), gains, gain_moment, gain_second],
     )
     return (
         outputs,

time: 226 us -> 229 us (1.013)
  Pallas kernels: 61.8 us -> 66.5 us
  waiting for transfers between devices: 87.3 us -> 84.3 us
    pallas_call x8, Pallas kernels: 38.9 us -> 44 us  [call(): pl.pallas_call(kernel, out_shape=out_shape, in_specs=specs, out_specs=jax...]
    ppermute x77, waiting for transfers between devices: 87.3 us -> 84.3 us  [swap(): return lax.ppermute(x, axis, [(i, i ^ bits) for i in range(size)])]
    unnamed x146 -> x114, local copies, waits for them, and re-layouts: 9.89 us -> 9 us
  transfers between devices with their start and end apart: 77 -> 77, of which waited for: 24 -> 25; matrix products, arithmetic and copies ran while one was open for 2% -> 2% of each run, Pallas kernels for 20% -> 22%
where the time goes in v7:
time: 229 us; the launch traced here: 228 us
  waiting for transfers between devices  84.3 us (37%)
  Pallas kernels  66.5 us (29%)
  starting transfers between devices  59.1 us (26%)
  local copies, waits for them, and re-layouts  9.14 us (4%)
  other arithmetic  7.07 us (3%)
    ppermute x77, waiting for transfers between devices, swap(): return lax.ppermute(x, axis, [(i, i ^ bits) for i in range(size)])  84.3 us
    ppermute x77, starting transfers between devices, swap(): return lax.ppermute(x, axis, [(i, i ^ bits) for i in range(size)])  59.1 us
    pallas_call x8, Pallas kernels, call(): pl.pallas_call(kernel, out_shape=out_shape, in_specs=specs, out_specs=jax...  44 us
    pallas_call x6, Pallas kernels, pair_add(): pl.pallas_call(add_kernel, out_shape=[sds((rows, cols), BF16)] * 4, in_sp...  12.9 us
    unnamed x114, local copies, waits for them, and re-layouts  9 us
  transfers between devices with their start and end apart: 77, of which 25 were waited for; matrix products, arithmetic and copies ran while one was open for 2% of the time, Pallas kernels for 22%

profile of v7, /device:TPU:0, one launch (start us, length us, event | category | flops | bytes accessed | tf_op | source)
XLA Modules:
  0.0 227.7 jit_solution(17247216381809266340)
XLA Ops:
  2.6 3.0 %collective-permute-start.3 = (bf16[48,1664]{1,0:T(8,128)(2,1)S(1)}, bf16[48,1664]{1,0:T(8,128)(2,1)S(1)}, u32[]{:S(2)}, u32[]{:S(2)}) collective-permute-start(bf16[48,1664]{1,0:T(8,128)(2,1)S(1)} %fusion.1.rest_0_.rest_16_.rest_4_), channel_id=1, source_target_pairs={{0,4},{2,6},{4,0},{6,2},{1,5},{3,7},{5,1},{7,3},{8,12},{10,14},{12... | collective-permute-start | bytes 479240 | tf_op jit(solution)/shard_map/ppermute | solution.py:61
  5.6 2.6 %collective-permute-start.1 = (bf16[48,1664]{1,0:T(8,128)(2,1)S(1)}, bf16[48,1664]{1,0:T(8,128)(2,1)S(1)}, u32[]{:S(2)}, u32[]{:S(2)}) collective-permute-start(bf16[48,1664]{1,0:T(8,128)(2,1)S(1)} %fusion.1.rest_0_.rest_16_.rest_4_), channel_id=1, source_target_pairs={{0,16},{8,24},{16,0},{24,8},{1,17},{9,25},{17,1},{25,9},{2,18},{10... | collective-permute-start | bytes 479240 | tf_op jit(solution)/shard_map/ppermute | solution.py:61
  8.2 1.6 collective-permute-start
  10.0 5.6 %collective-permute-done.1.rest_2_.rest_18_.rest_6_ = bf16[48,1664]{1,0:T(8,128)(2,1)S(1)} collective-permute-done((bf16[48,1664]{1,0:T(8,128)(2,1)S(1)}, bf16[48,1664]{1,0:T(8,128)(2,1)S(1)}, u32[]{:S(2)}, u32[]{:S(2)}) %collective-permute-start.1) | collective-permute-done | bytes 159776 | tf_op jit(solution)/shard_map/ppermute | solution.py:61
  18.5 2.4 %collective-permute-done.2.rest_3_.rest_19_.rest_7_ = bf16[48,1664]{1,0:T(8,128)(2,1)S(1)} collective-permute-done((bf16[48,1664]{1,0:T(8,128)(2,1)S(1)}, bf16[48,1664]{1,0:T(8,128)(2,1)S(1)}, u32[]{:S(2)}, u32[]{:S(2)}) %collective-permute-start.2) | collective-permute-done | bytes 159776 | tf_op jit(solution)/shard_map/ppermute | solution.py:61
  21.5 1.6 collective-permute-start.34
  23.8 2.9 %collective-permute-done.4.rest_5_.rest_21_.rest_9_ = bf16[48,1664]{1,0:T(8,128)(2,1)S(1)} collective-permute-done((bf16[48,1664]{1,0:T(8,128)(2,1)S(1)}, bf16[48,1664]{1,0:T(8,128)(2,1)S(1)}, u32[]{:S(2)}, u32[]{:S(2)}) %collective-permute-start.4) | collective-permute-done | bytes 159776 | tf_op jit(solution)/shard_map/ppermute | solution.py:61
  26.7 3.4 %collective-permute-done.6.rest_7_.rest_23_.rest_11_ = bf16[48,1664]{1,0:T(8,128)(2,1)S(1)} collective-permute-done((bf16[48,1664]{1,0:T(8,128)(2,1)S(1)}, bf16[48,1664]{1,0:T(8,128)(2,1)S(1)}, u32[]{:S(2)}, u32[]{:S(2)}) %collective-permute-start.6) | collective-permute-done | bytes 159776 | tf_op jit(solution)/shard_map/ppermute | solution.py:61
  31.9 6.5 %shard_map.159 = (bf16[768,128]{1,0:T(8,128)(2,1)}, bf16[128,384]{1,0:T(8,128)(2,1)}, bf16[128,768]{1,0:T(8,128)(2,1)}, f32[8,768]{1,0:T(8,128)}) custom-call(s32[1]{0:T(128)} %bitcast.order_ref, f32[128,768]{1,0:T(8,128)} %x_ref.5, f32[128,128]{1,0:T(8,128)} %get-tuple-element.145.cos_ref, f32[128,128]{1,0:T(8,128)} %get-tuple-element.144.sin_ref, ...), custom_call_target="tpu_custom_call" | custom-call | tf_op jit(solution)/shard_map/pallas_call | solution.py:488
  39.2 3.4 %collective-permute-start.16 = (bf16[128,768]{1,0:T(8,128)(2,1)}, bf16[128,768]{1,0:T(8,128)(2,1)S(1)}, u32[]{:S(2)}, u32[]{:S(2)}) collective-permute-start(bf16[128,768]{1,0:T(8,128)(2,1)} %get-tuple-element.79.rest_0_), channel_id=1, source_target_pairs={{0,16},{8,24},{16,0},{24,8},{1,17},{9,25},{17,1},{25,9},{2,18},{10... | collective-permute-start | bytes 589832 | tf_op jit(solution)/shard_map/ppermute | solution.py:61
  45.4 14.2 %collective-permute-done.32.rest_2_ = bf16[48,1792]{1,0:T(8,128)(2,1)S(1)} collective-permute-done((bf16[48,1792]{1,0:T(8,128)(2,1)S(1)}, bf16[48,1792]{1,0:T(8,128)(2,1)S(1)}, u32[]{:S(2)}, u32[]{:S(2)}) %collective-permute-start.32) | collective-permute-done | bytes 172064 | tf_op jit(solution)/shard_map/ppermute | solution.py:61
  59.6 2.0 collective-permute-start.17
  62.4 12.7 %collective-permute-done.33.rest_3_ = bf16[48,1792]{1,0:T(8,128)(2,1)} collective-permute-done((bf16[48,1792]{1,0:T(8,128)(2,1)S(1)}, bf16[48,1792]{1,0:T(8,128)(2,1)}, u32[]{:S(2)}, u32[]{:S(2)}) %collective-permute-start.33) | collective-permute-done | bytes 172064 | tf_op jit(solution)/shard_map/ppermute | solution.py:61
  75.6 1.6 collective-permute-start.19
  77.7 5.1 %collective-permute-done.20.rest_6_ = bf16[128,768]{1,0:T(8,128)(2,1)S(1)} collective-permute-done((bf16[128,768]{1,0:T(8,128)(2,1)S(1)}, bf16[128,768]{1,0:T(8,128)(2,1)S(1)}, u32[]{:S(2)}, u32[]{:S(2)}) %collective-permute-start.20) | collective-permute-done | bytes 196640 | tf_op jit(solution)/shard_map/ppermute | solution.py:61
  83.4 3.7 %collective-permute-done.19.rest_5_ = bf16[128,768]{1,0:T(8,128)(2,1)S(1)} collective-permute-done((bf16[128,768]{1,0:T(8,128)(2,1)S(1)}, bf16[128,768]{1,0:T(8,128)(2,1)S(1)}, u32[]{:S(2)}, u32[]{:S(2)}) %collective-permute-start.19) | collective-permute-done | bytes 196640 | tf_op jit(solution)/shard_map/ppermute | solution.py:61
  87.1 2.8 %collective-permute-done.21.rest_7_ = bf16[128,768]{1,0:T(8,128)(2,1)S(1)} collective-permute-done((bf16[128,768]{1,0:T(8,128)(2,1)S(1)}, bf16[128,768]{1,0:T(8,128)(2,1)S(1)}, u32[]{:S(2)}, u32[]{:S(2)}) %collective-permute-start.21) | collective-permute-done | bytes 196640 | tf_op jit(solution)/shard_map/ppermute | solution.py:61
  91.0 1.6 collective-permute-start.35
  94.0 10.3 %shard_map.160 = (bf16[128,384]{1,0:T(8,128)(2,1)}, f32[8,256]{1,0:T(8,128)}, bf16[128,768]{1,0:T(8,128)(2,1)}) custom-call(s32[1]{0:T(128)} %bitcast.order_ref, bf16[128,384]{1,0:T(8,128)(2,1)} %get-tuple-element.78.q_ref, bf16[128,768]{1,0:T(8,128)(2,1)S(1)} %copy-done.16, bf16[128,768]{1,0:T(8,128)(2,1)S(1)} %collective-permute-done.15.rest_1_, ...), custom_call_target="tpu_custom_call" | custom-call | tf_op jit(solution)/shard_map/pallas_call | solution.py:488
  104.5 1.6 collective-permute-start.30
  108.5 3.0 %collective-permute-done.30.pb_ref = bf16[128,768]{1,0:T(8,128)(2,1)S(1)} collective-permute-done((bf16[128,768]{1,0:T(8,128)(2,1)}, bf16[128,768]{1,0:T(8,128)(2,1)S(1)}, u32[]{:S(2)}, u32[]{:S(2)}) %collective-permute-start.30) | collective-permute-done | bytes 196640 | tf_op jit(solution)/shard_map/ppermute | solution.py:61
  115.2 6.3 %shard_map.161 = (f32[128,768]{1,0:T(8,128)}, bf16[128,768]{1,0:T(8,128)(2,1)}, bf16[128,768]{1,0:T(8,128)(2,1)}, bf16[128,768]{1,0:T(8,128)(2,1)}, bf16[128,1152]{1,0:T(8,128)(2,1)}, /*index=5*/bf16[128,576]{1,0:T(8,128)(2,1)}) custom-call(s32[1]{0:T(128)} %bitcast.order_ref, f32[128,768]{1,0:T(8,128)} %x_ref.5, bf16[128,768]{1,0:T(8,128)(2,1)} %get-tuple-element.82.pa_ref, ...), custom_call_target="tpu_custom_call" | custom-call | tf_op jit(solution)/shard_map/pallas_call | solution.py:488
  121.5 1.6 collective-permute-start.46
  123.0 4.5 %collective-permute-done.46.db_ref = bf16[128,768]{1,0:T(8,128)(2,1)S(1)} collective-permute-done((bf16[128,768]{1,0:T(8,128)(2,1)}, bf16[128,768]{1,0:T(8,128)(2,1)S(1)}, u32[]{:S(2)}, u32[]{:S(2)}) %collective-permute-start.46) | collective-permute-done | bytes 196640 | tf_op jit(solution)/shard_map/ppermute | solution.py:61
  127.6 9.7 %shard_map.162 = (bf16[512,768]{1,0:T(8,128)(2,1)}, bf16[512,768]{1,0:T(8,128)(2,1)}, bf16[512,768]{1,0:T(8,128)(2,1)}, bf16[512,768]{1,0:T(8,128)(2,1)}, f32[128,768]{1,0:T(8,128)}, /*index=5*/bf16[128,384]{1,0:T(8,128)(2,1)}) custom-call(s32[1]{0:T(128)} %bitcast.order_ref, bf16[128,384]{1,0:T(8,128)(2,1)} %get-tuple-element.78.q_ref, ...), custom_call_target="tpu_custom_call" | custom-call | tf_op jit(solution)/shard_map/pallas_call | solution.py:488
  137.8 4.0 %ffngrad.1 = (bf16[192,2560]{1,0:T(8,128)(2,1)}, bf16[192,2560]{1,0:T(8,128)(2,1)}, bf16[192,2560]{1,0:T(8,128)(2,1)}, bf16[192,2560]{1,0:T(8,128)(2,1)}) custom-call(s32[1]{0:T(128)} %bitcast.order_ref, bf16[128,768]{1,0:T(8,128)(2,1)} %get-tuple-element.116.b_ref, bf16[128,1152]{1,0:T(8,128)(2,1)} %get-tuple-element.117.dz_ref, f32[128,768]{1,0:T(8,128)} %cot_ref.5, ...), custom_call_target="tpu_custom_call" | custom-call | tf_op jit(solution)/shard_map/ffngrad/pallas_call | solution.py:641
  141.8 2.7 %oqgrad.1 = (bf16[192,2560]{1,0:T(8,128)(2,1)}, bf16[192,2560]{1,0:T(8,128)(2,1)}, bf16[192,2560]{1,0:T(8,128)(2,1)}, bf16[192,2560]{1,0:T(8,128)(2,1)}) custom-call(s32[1]{0:T(128)} %bitcast.order_ref, bf16[768,128]{1,0:T(8,128)(2,1)} %get-tuple-element.77.at_ref, ...), custom_call_target="tpu_custom_call", output_to_operand_aliasing={{0}: (5, {}), {1}: (6, {}), {2}: (7, {}), {3}: (8, {})} | custom-call | tf_op jit(solution)/shard_map/oqgrad/pallas_call | solution.py:674
  145.1 2.0 pair_add.7
  147.2 1.6 collective-permute-start.53
  150.7 3.1 %pair_add.6 = (bf16[128,768]{1,0:T(8,128)(2,1)}, bf16[128,768]{1,0:T(8,128)(2,1)}, bf16[128,768]{1,0:T(8,128)(2,1)}, bf16[128,768]{1,0:T(8,128)(2,1)}) custom-call(bf16[512,768]{1,0:T(8,128)(2,1)} %get-tuple-element.87.keep, bf16[512,768]{1,0:T(8,128)(2,1)} %collective-permute-done.47.got), custom_call_target="tpu_custom_call" | custom-call | tf_op jit(solution)/shard_map/pair_add/pallas_call | solution.py:109
  158.3 2.2 pair_add.11
  160.5 3.1 %collective-permute-done.50 = bf16[128,768]{1,0:T(8,128)(2,1)S(1)} collective-permute-done((bf16[128,768]{1,0:T(8,128)(2,1)}, bf16[128,768]{1,0:T(8,128)(2,1)S(1)}, u32[]{:S(2)}, u32[]{:S(2)}) %collective-permute-start.50) | collective-permute-done | bytes 196640 | tf_op jit(solution)/shard_map/ppermute | solution.py:61
  165.8 2.2 pair_add.10
  170.2 2.9 %collective-permute-done.73 = bf16[48,2560]{1,0:T(8,128)(2,1)S(1)} collective-permute-done((bf16[48,2560]{1,0:T(8,128)(2,1)}, bf16[48,2560]{1,0:T(8,128)(2,1)S(1)}, u32[]{:S(2)}, u32[]{:S(2)}) %collective-permute-start.73) | collective-permute-done | bytes 245792 | tf_op jit(solution)/shard_map/ppermute | solution.py:61
  175.2 1.5 collective-permute-start.72
  178.2 5.2 %collective-permute-done.55.rest_3_ = bf16[128,768]{1,0:T(8,128)(2,1)S(1)} collective-permute-done((bf16[128,768]{1,0:T(8,128)(2,1)S(1)}, bf16[128,768]{1,0:T(8,128)(2,1)S(1)}, u32[]{:S(2)}, u32[]{:S(2)}) %collective-permute-start.55) | collective-permute-done | bytes 196640 | tf_op jit(solution)/shard_map/ppermute | solution.py:61
  183.5 5.0 %shard_map.163 = (bf16[192,768]{1,0:T(8,128)(2,1)}, bf16[192,768]{1,0:T(8,128)(2,1)}, bf16[192,768]{1,0:T(8,128)(2,1)}, bf16[192,768]{1,0:T(8,128)(2,1)}, bf16[128,768]{1,0:T(8,128)(2,1)}) custom-call(s32[1]{0:T(128)} %bitcast.order_ref, bf16[768,128]{1,0:T(8,128)(2,1)} %get-tuple-element.77.at_ref, bf16[128,384]{1,0:T(8,128)(2,1)} %get-tuple-element.86.dqp_ref, ...), custom_call_target="tpu_custom_call" | custom-call | tf_op jit(solution)/shard_map/pallas_call | solution.py:488
  188.7 1.6 collective-permute-done.59.got
  190.5 1.7 pair_add.9
  195.6 1.7 pair_add.8
  197.4 1.6 collective-permute-start.63
  202.4 1.6 collective-permute-start.57
  204.0 5.4 %collective-permute-done.65 = bf16[48,768]{1,0:T(8,128)(2,1)S(1)} collective-permute-done((bf16[48,768]{1,0:T(8,128)(2,1)S(1)}, bf16[48,768]{1,0:T(8,128)(2,1)S(1)}, u32[]{:S(2)}, u32[]{:S(2)}) %collective-permute-start.65) | collective-permute-done | bytes 73760 | tf_op jit(solution)/shard_map/ppermute | solution.py:61
  209.4 1.5 collective-permute-start.56
  212.4 2.7 %collective-permute-start.66 = (bf16[48,768]{1,0:T(8,128)(2,1)S(1)}, bf16[48,768]{1,0:T(8,128)(2,1)S(1)}, u32[]{:S(2)}, u32[]{:S(2)}) collective-permute-start(bf16[48,768]{1,0:T(8,128)(2,1)S(1)} %add_convert_fusion.6), channel_id=1, source_target_pairs={{0,16},{8,24},{16,0},{24,8},{1,17},{9,25},{17,1},{25,9},{2,18},{10... | collective-permute-start | bytes 221192 | tf_op jit(solution)/shard_map/ppermute | solution.py:61
  217.7 2.2 shard_map.165
  220.9 2.6 %shard_map.164 = (f32[128,768]{1,0:T(8,128)}, f32[128,768]{1,0:T(8,128)}) custom-call(f32[128,768]{1,0:T(8,128)} %x_ref.5, bf16[128,768]{1,0:T(8,128)(2,1)} %get-tuple-element.99.da_ref, bf16[128,768]{1,0:T(8,128)(2,1)S(1)} %collective-permute-done.56.db_ref, f32[128,768]{1,0:T(8,128)} %get-tuple-element.100.dhid_ref, f32[8,768]{1,0:T(8,128)} %get-tuple-element.83.g_ref, ...), custom_call_target="tpu_custom_call" | custom-call | tf_op jit(solution)/shard_map/pallas_call | solution.py:488
  223.5 2.8 %adam.1 = (f32[48,3264]{1,0:T(8,128)}, f32[48,3264]{1,0:T(8,128)}, f32[48,3264]{1,0:T(8,128)}) custom-call(f32[48,3264]{1,0:T(8,128)} %w_ref.5, f32[48,3264]{1,0:T(8,128)} %get-tuple-element.69.g_ref, f32[48,3264]{1,0:T(8,128)} %m_ref.3, f32[48,3264]{1,0:T(8,128)} %v_ref.3), custom_call_target="tpu_custom_call" | custom-call | tf_op jit(solution)/shard_map/adam/pallas_call | solution.py:720
  (257 shorter events, 51.4 us)
Async XLA Ops:
  5.6 10.0 %collective-permute-start.1 = (bf16[48,1664]{1,0:T(8,128)(2,1)S(1)}, bf16[48,1664]{1,0:T(8,128)(2,1)S(1)}, u32[]{:S(2)}, u32[]{:S(2)}) collective-permute-start(bf16[48,1664]{1,0:T(8,128)(2,1)S(1)} %fusion.1.rest_0_.rest_16_.rest_4_), channel_id=1, source_target_pairs={{0,16},{8,24},{16,0},{24,8},{1,17},{9,25},{17,1},{25,9},{2,18},{10... | collective-permute-start | bytes 479240 | tf_op jit(solution)/shard_map/ppermute | solution.py:61
  8.2 8.0 %collective-permute-start.7 = (bf16[48,1664]{1,0:T(8,128)(2,1)S(1)}, bf16[48,1664]{1,0:T(8,128)(2,1)S(1)}, u32[]{:S(2)}, u32[]{:S(2)}) collective-permute-start(bf16[48,1664]{1,0:T(8,128)(2,1)S(1)} %fusion.1.rest_0_.rest_16_.rest_4_), channel_id=1, source_target_pairs={{0,2},{2,0},{4,6},{6,4},{1,3},{3,1},{5,7},{7,5},{8,10},{10,8},{12,... | collective-permute-start | bytes 479240 | tf_op jit(solution)/shard_map/ppermute | solution.py:61
  8.2 8.8 %collective-permute-start = (bf16[48,1664]{1,0:T(8,128)(2,1)S(1)}, bf16[48,1664]{1,0:T(8,128)(2,1)S(1)}, u32[]{:S(2)}, u32[]{:S(2)}) collective-permute-start(bf16[48,1664]{1,0:T(8,128)(2,1)S(1)} %fusion.1.rest_0_.rest_16_.rest_4_), channel_id=1, source_target_pairs={{0,8},{8,0},{16,24},{24,16},{1,9},{9,1},{17,25},{25,17},{2,10},{10... | collective-permute-start | bytes 479240 | tf_op jit(solution)/shard_map/ppermute | solution.py:61
  17.1 9.6 %collective-permute-start.4 = (bf16[48,1664]{1,0:T(8,128)(2,1)S(1)}, bf16[48,1664]{1,0:T(8,128)(2,1)S(1)}, u32[]{:S(2)}, u32[]{:S(2)}) collective-permute-start(bf16[48,1664]{1,0:T(8,128)(2,1)S(1)} %collective-permute-done.rest_1_.rest_17_.rest_5_), channel_id=1, source_target_pairs={{0,4},{2,6},{4,0},{6,2},{1,5},{3,7},{5,1},{7,3},{8,12},{10,14},{12... | collective-permute-start | bytes 479240 | tf_op jit(solution)/shard_map/ppermute | solution.py:61
  20.9 9.2 %collective-permute-start.6 = (bf16[48,1664]{1,0:T(8,128)(2,1)S(1)}, bf16[48,1664]{1,0:T(8,128)(2,1)S(1)}, u32[]{:S(2)}, u32[]{:S(2)}) collective-permute-start(bf16[48,1664]{1,0:T(8,128)(2,1)S(1)} %collective-permute-done.2.rest_3_.rest_19_.rest_7_), channel_id=1, source_target_pairs={{0,4},{2,6},{4,0},{6,2},{1,5},{3,7},{5,1},{7,3},{8,12},{10,14},{12... | collective-permute-start | bytes 479240 | tf_op jit(solution)/shard_map/ppermute | solution.py:61
  21.5 22.0 %collective-permute-start.34 = (bf16[48,1792]{1,0:T(8,128)(2,1)S(1)}, bf16[48,1792]{1,0:T(8,128)(2,1)S(1)}, u32[]{:S(2)}, u32[]{:S(2)}) collective-permute-start(bf16[48,1792]{1,0:T(8,128)(2,1)S(1)} %pad.9.rest_0_), channel_id=1, source_target_pairs={{0,4},{2,6},{4,0},{6,2},{1,5},{3,7},{5,1},{7,3},{8,12},{10,14},{12... | collective-permute-start | bytes 516104 | tf_op jit(solution)/shard_map/ppermute | solution.py:61
  23.3 8.5 %collective-permute-start.10 = (bf16[48,1664]{1,0:T(8,128)(2,1)S(1)}, bf16[48,1664]{1,0:T(8,128)(2,1)S(1)}, u32[]{:S(2)}, u32[]{:S(2)}) collective-permute-start(bf16[48,1664]{1,0:T(8,128)(2,1)S(1)} %collective-permute-done.2.rest_3_.rest_19_.rest_7_), channel_id=1, source_target_pairs={{0,2},{2,0},{4,6},{6,4},{1,3},{3,1},{5,7},{7,5},{8,10},{10,8},{12,... | collective-permute-start | bytes 479240 | tf_op jit(solution)/shard_map/ppermute | solution.py:61
  23.3 7.9 %collective-permute-start.13 = (bf16[48,1664]{1,0:T(8,128)(2,1)S(1)}, bf16[48,1664]{1,0:T(8,128)(2,1)S(1)}, u32[]{:S(2)}, u32[]{:S(2)}) collective-permute-start(bf16[48,1664]{1,0:T(8,128)(2,1)S(1)} %collective-permute-done.5.rest_6_.rest_22_.rest_10_), channel_id=1, source_target_pairs={{0,2},{2,0},{4,6},{6,4},{1,3},{3,1},{5,7},{7,5},{8,10},{10,8},{12,... | collective-permute-start | bytes 479240 | tf_op jit(solution)/shard_map/ppermute | solution.py:61
  31.3 12.9 %collective-permute-start.38 = (bf16[48,1792]{1,0:T(8,128)(2,1)S(1)}, bf16[48,1792]{1,0:T(8,128)(2,1)S(1)}, u32[]{:S(2)}, u32[]{:S(2)}) collective-permute-start(bf16[48,1792]{1,0:T(8,128)(2,1)S(1)} %pad.9.rest_0_), channel_id=1, source_target_pairs={{0,2},{2,0},{4,6},{6,4},{1,3},{3,1},{5,7},{7,5},{8,10},{10,8},{12,... | collective-permute-start | bytes 516104 | tf_op jit(solution)/shard_map/ppermute | solution.py:61
  39.2 20.4 %collective-permute-start.16 = (bf16[128,768]{1,0:T(8,128)(2,1)}, bf16[128,768]{1,0:T(8,128)(2,1)S(1)}, u32[]{:S(2)}, u32[]{:S(2)}) collective-permute-start(bf16[128,768]{1,0:T(8,128)(2,1)} %get-tuple-element.79.rest_0_), channel_id=1, source_target_pairs={{0,16},{8,24},{16,0},{24,8},{1,17},{9,25},{17,1},{25,9},{2,18},{10... | collective-permute-start | bytes 589832 | tf_op jit(solution)/shard_map/ppermute | solution.py:61
  42.6 16.9 %collective-permute-start.32 = (bf16[48,1792]{1,0:T(8,128)(2,1)S(1)}, bf16[48,1792]{1,0:T(8,128)(2,1)S(1)}, u32[]{:S(2)}, u32[]{:S(2)}) collective-permute-start(bf16[48,1792]{1,0:T(8,128)(2,1)S(1)} %pad.9.rest_0_), channel_id=1, source_target_pairs={{0,16},{8,24},{16,0},{24,8},{1,17},{9,25},{17,1},{25,9},{2,18},{10... | collective-permute-start | bytes 516104 | tf_op jit(solution)/shard_map/ppermute | solution.py:61
  42.7 16.9 %collective-permute-start.31 = (bf16[48,1792]{1,0:T(8,128)(2,1)S(1)}, bf16[48,1792]{1,0:T(8,128)(2,1)}, u32[]{:S(2)}, u32[]{:S(2)}) collective-permute-start(bf16[48,1792]{1,0:T(8,128)(2,1)S(1)} %pad.9.rest_0_), channel_id=1, source_target_pairs={{0,8},{8,0},{16,24},{24,16},{1,9},{9,1},{17,25},{25,17},{2,10},{10... | collective-permute-start | bytes 516104 | tf_op jit(solution)/shard_map/ppermute | solution.py:61
  43.5 18.1 %collective-permute-start.42 = (bf16[48,1792]{1,0:T(8,128)(2,1)S(1)}, bf16[48,1792]{1,0:T(8,128)(2,1)S(1)}, u32[]{:S(2)}, u32[]{:S(2)}) collective-permute-start(bf16[48,1792]{1,0:T(8,128)(2,1)S(1)} %collective-permute-done.34.rest_4_), channel_id=1, source_target_pairs={{0,2},{2,0},{4,6},{6,4},{1,3},{3,1},{5,7},{7,5},{8,10},{10,8},{12,... | collective-permute-start | bytes 516104 | tf_op jit(solution)/shard_map/ppermute | solution.py:61
  44.9 17.5 %collective-permute-start.18 = (bf16[128,768]{1,0:T(8,128)(2,1)}, bf16[128,768]{1,0:T(8,128)(2,1)S(1)}, u32[]{:S(2)}, u32[]{:S(2)}) collective-permute-start(bf16[128,768]{1,0:T(8,128)(2,1)} %get-tuple-element.79.rest_0_), channel_id=1, source_target_pairs={{0,4},{2,6},{4,0},{6,2},{1,5},{3,7},{5,1},{7,3},{8,12},{10,14},{12... | collective-permute-start | bytes 589832 | tf_op jit(solution)/shard_map/ppermute | solution.py:61
  59.5 16.1 %collective-permute-start.22 = (bf16[128,768]{1,0:T(8,128)(2,1)}, bf16[128,768]{1,0:T(8,128)(2,1)S(1)}, u32[]{:S(2)}, u32[]{:S(2)}) collective-permute-start(bf16[128,768]{1,0:T(8,128)(2,1)} %get-tuple-element.79.rest_0_), channel_id=1, source_target_pairs={{0,2},{2,0},{4,6},{6,4},{1,3},{3,1},{5,7},{7,5},{8,10},{10,8},{12,... | collective-permute-start | bytes 589832 | tf_op jit(solution)/shard_map/ppermute | solution.py:61
  59.5 16.1 %collective-permute-start.15 = (bf16[128,768]{1,0:T(8,128)(2,1)}, bf16[128,768]{1,0:T(8,128)(2,1)S(1)}, u32[]{:S(2)}, u32[]{:S(2)}) collective-permute-start(bf16[128,768]{1,0:T(8,128)(2,1)} %get-tuple-element.79.rest_0_), channel_id=1, source_target_pairs={{0,8},{8,0},{16,24},{24,16},{1,9},{9,1},{17,25},{25,17},{2,10},{10... | collective-permute-start | bytes 589832 | tf_op jit(solution)/shard_map/ppermute | solution.py:61
  59.6 17.6 %collective-permute-start.17 = (bf16[128,768]{1,0:T(8,128)(2,1)S(1)}, bf16[128,768]{1,0:T(8,128)(2,1)S(1)}, u32[]{:S(2)}, u32[]{:S(2)}) collective-permute-start(bf16[128,768]{1,0:T(8,128)(2,1)S(1)} %collective-permute-done.16.rest_2_), channel_id=1, source_target_pairs={{0,8},{8,0},{16,24},{24,16},{1,9},{9,1},{17,25},{25,17},{2,10},{10... | collective-permute-start | bytes 589832 | tf_op jit(solution)/shard_map/ppermute | solution.py:61
  62.3 12.8 %collective-permute-start.33 = (bf16[48,1792]{1,0:T(8,128)(2,1)S(1)}, bf16[48,1792]{1,0:T(8,128)(2,1)}, u32[]{:S(2)}, u32[]{:S(2)}) collective-permute-start(bf16[48,1792]{1,0:T(8,128)(2,1)S(1)} %collective-permute-done.32.rest_2_), channel_id=1, source_target_pairs={{0,8},{8,0},{16,24},{24,16},{1,9},{9,1},{17,25},{25,17},{2,10},{10... | collective-permute-start | bytes 516104 | tf_op jit(solution)/shard_map/ppermute | solution.py:61
  62.4 15.3 %collective-permute-start.26 = (bf16[128,768]{1,0:T(8,128)(2,1)S(1)}, bf16[128,768]{1,0:T(8,128)(2,1)S(1)}, u32[]{:S(2)}, u32[]{:S(2)}) collective-permute-start(bf16[128,768]{1,0:T(8,128)(2,1)S(1)} %collective-permute-done.18.rest_4_), channel_id=1, source_target_pairs={{0,2},{2,0},{4,6},{6,4},{1,3},{3,1},{5,7},{7,5},{8,10},{10,8},{12,... | collective-permute-start | bytes 589832 | tf_op jit(solution)/shard_map/ppermute | solution.py:61
  75.6 11.4 %collective-permute-start.19 = (bf16[128,768]{1,0:T(8,128)(2,1)S(1)}, bf16[128,768]{1,0:T(8,128)(2,1)S(1)}, u32[]{:S(2)}, u32[]{:S(2)}) collective-permute-start(bf16[128,768]{1,0:T(8,128)(2,1)S(1)} %collective-permute-done.15.rest_1_), channel_id=1, source_target_pairs={{0,4},{2,6},{4,0},{6,2},{1,5},{3,7},{5,1},{7,3},{8,12},{10,14},{12... | collective-permute-start | bytes 589832 | tf_op jit(solution)/shard_map/ppermute | solution.py:61
  77.2 12.7 %collective-permute-start.21 = (bf16[128,768]{1,0:T(8,128)(2,1)S(1)}, bf16[128,768]{1,0:T(8,128)(2,1)S(1)}, u32[]{:S(2)}, u32[]{:S(2)}) collective-permute-start(bf16[128,768]{1,0:T(8,128)(2,1)S(1)} %collective-permute-done.17.rest_3_), channel_id=1, source_target_pairs={{0,4},{2,6},{4,0},{6,2},{1,5},{3,7},{5,1},{7,3},{8,12},{10,14},{12... | collective-permute-start | bytes 589832 | tf_op jit(solution)/shard_map/ppermute | solution.py:61
  77.7 12.2 %collective-permute-start.23 = (bf16[128,768]{1,0:T(8,128)(2,1)S(1)}, bf16[128,768]{1,0:T(8,128)(2,1)S(1)}, u32[]{:S(2)}, u32[]{:S(2)}) collective-permute-start(bf16[128,768]{1,0:T(8,128)(2,1)S(1)} %collective-permute-done.15.rest_1_), channel_id=1, source_target_pairs={{0,2},{2,0},{4,6},{6,4},{1,3},{3,1},{5,7},{7,5},{8,10},{10,8},{12,... | collective-permute-start | bytes 589832 | tf_op jit(solution)/shard_map/ppermute | solution.py:61
  82.9 8.1 %collective-permute-start.25 = (bf16[128,768]{1,0:T(8,128)(2,1)S(1)}, bf16[128,768]{1,0:T(8,128)(2,1)S(1)}, u32[]{:S(2)}, u32[]{:S(2)}) collective-permute-start(bf16[128,768]{1,0:T(8,128)(2,1)S(1)} %collective-permute-done.17.rest_3_), channel_id=1, source_target_pairs={{0,2},{2,0},{4,6},{6,4},{1,3},{3,1},{5,7},{7,5},{8,10},{10,8},{12,... | collective-permute-start | bytes 589832 | tf_op jit(solution)/shard_map/ppermute | solution.py:61
  89.9 14.6 %collective-permute-start.40 = (bf16[48,1792]{1,0:T(8,128)(2,1)S(1)}, bf16[48,1792]{1,0:T(8,128)(2,1)}, u32[]{:S(2)}, u32[]{:S(2)}) collective-permute-start(bf16[48,1792]{1,0:T(8,128)(2,1)S(1)} %collective-permute-done.32.rest_2_), channel_id=1, source_target_pairs={{0,2},{2,0},{4,6},{6,4},{1,3},{3,1},{5,7},{7,5},{8,10},{10,8},{12,... | collective-permute-start | bytes 516104 | tf_op jit(solution)/shard_map/ppermute | solution.py:61
  90.4 15.7 %collective-permute-start.36 = (bf16[48,1792]{1,0:T(8,128)(2,1)S(1)}, bf16[48,1792]{1,0:T(8,128)(2,1)}, u32[]{:S(2)}, u32[]{:S(2)}) collective-permute-start(bf16[48,1792]{1,0:T(8,128)(2,1)S(1)} %collective-permute-done.32.rest_2_), channel_id=1, source_target_pairs={{0,4},{2,6},{4,0},{6,2},{1,5},{3,7},{5,1},{7,3},{8,12},{10,14},{12... | collective-permute-start | bytes 516104 | tf_op jit(solution)/shard_map/ppermute | solution.py:61
  90.9 15.2 %collective-permute-start.39 = (bf16[48,1792]{1,0:T(8,128)(2,1)}, bf16[48,1792]{1,0:T(8,128)(2,1)}, u32[]{:S(2)}, u32[]{:S(2)}) collective-permute-start(bf16[48,1792]{1,0:T(8,128)(2,1)} %collective-permute-done.31.rest_1_), channel_id=1, source_target_pairs={{0,2},{2,0},{4,6},{6,4},{1,3},{3,1},{5,7},{7,5},{8,10},{10,8},{12,... | collective-permute-start | bytes 516104 | tf_op jit(solution)/shard_map/ppermute | solution.py:61
  91.0 15.7 %collective-permute-start.35 = (bf16[48,1792]{1,0:T(8,128)(2,1)}, bf16[48,1792]{1,0:T(8,128)(2,1)}, u32[]{:S(2)}, u32[]{:S(2)}) collective-permute-start(bf16[48,1792]{1,0:T(8,128)(2,1)} %collective-permute-done.31.rest_1_), channel_id=1, source_target_pairs={{0,4},{2,6},{4,0},{6,2},{1,5},{3,7},{5,1},{7,3},{8,12},{10,14},{12... | collective-permute-start | bytes 516104 | tf_op jit(solution)/shard_map/ppermute | solution.py:61
  92.5 14.2 %collective-permute-start.37 = (bf16[48,1792]{1,0:T(8,128)(2,1)}, bf16[48,1792]{1,0:T(8,128)(2,1)}, u32[]{:S(2)}, u32[]{:S(2)}) collective-permute-start(bf16[48,1792]{1,0:T(8,128)(2,1)} %collective-permute-done.33.rest_3_), channel_id=1, source_target_pairs={{0,4},{2,6},{4,0},{6,2},{1,5},{3,7},{5,1},{7,3},{8,12},{10,14},{12... | collective-permute-start | bytes 516104 | tf_op jit(solution)/shard_map/ppermute | solution.py:61
  137.3 11.9 %collective-permute-start.47 = (bf16[512,768]{1,0:T(8,128)(2,1)}, bf16[512,768]{1,0:T(8,128)(2,1)}, u32[]{:S(2)}, u32[]{:S(2)}) collective-permute-start(bf16[512,768]{1,0:T(8,128)(2,1)} %get-tuple-element.88), channel_id=1, source_target_pairs={{0,2},{2,0},{4,6},{6,4},{1,3},{3,1},{5,7},{7,5},{8,10},{10,8},{12,... | collective-permute-start | bytes 2359304 | tf_op jit(solution)/shard_map/ppermute | solution.py:61
  144.6 13.1 %collective-permute-start.68 = (bf16[192,2560]{1,0:T(8,128)(2,1)}, bf16[192,2560]{1,0:T(8,128)(2,1)S(1)}, u32[]{:S(2)}, u32[]{:S(2)}) collective-permute-start(bf16[192,2560]{1,0:T(8,128)(2,1)} %get-tuple-element.127), channel_id=1, source_target_pairs={{0,2},{2,0},{4,6},{6,4},{1,3},{3,1},{5,7},{7,5},{8,10},{10,8},{12,... | collective-permute-start | bytes 2949128 | tf_op jit(solution)/shard_map/ppermute | solution.py:61
  144.7 20.5 %collective-permute-start.67 = (bf16[192,2560]{1,0:T(8,128)(2,1)}, bf16[192,2560]{1,0:T(8,128)(2,1)S(1)}, u32[]{:S(2)}, u32[]{:S(2)}) collective-permute-start(bf16[192,2560]{1,0:T(8,128)(2,1)} %get-tuple-element.124), channel_id=1, source_target_pairs={{0,2},{2,0},{4,6},{6,4},{1,3},{3,1},{5,7},{7,5},{8,10},{10,8},{12,... | collective-permute-start | bytes 2949128 | tf_op jit(solution)/shard_map/ppermute | solution.py:61
  147.2 8.0 %collective-permute-start.53 = (bf16[128,768]{1,0:T(8,128)(2,1)}, bf16[128,768]{1,0:T(8,128)(2,1)S(1)}, u32[]{:S(2)}, u32[]{:S(2)}) collective-permute-start(bf16[128,768]{1,0:T(8,128)(2,1)} %get-tuple-element.98), channel_id=1, source_target_pairs={{0,4},{2,6},{4,0},{6,2},{1,5},{3,7},{5,1},{7,3},{8,12},{10,14},{12... | collective-permute-start | bytes 589832 | tf_op jit(solution)/shard_map/ppermute | solution.py:61
  148.7 25.7 %collective-permute-start.49 = (bf16[128,768]{1,0:T(8,128)(2,1)}, bf16[128,768]{1,0:T(8,128)(2,1)S(1)}, u32[]{:S(2)}, u32[]{:S(2)}) collective-permute-start(bf16[128,768]{1,0:T(8,128)(2,1)} %get-tuple-element.92), channel_id=1, source_target_pairs={{0,4},{2,6},{4,0},{6,2},{1,5},{3,7},{5,1},{7,3},{8,12},{10,14},{12... | collective-permute-start | bytes 589832 | tf_op jit(solution)/shard_map/ppermute | solution.py:61
  149.2 14.4 %collective-permute-start.50 = (bf16[128,768]{1,0:T(8,128)(2,1)}, bf16[128,768]{1,0:T(8,128)(2,1)S(1)}, u32[]{:S(2)}, u32[]{:S(2)}) collective-permute-start(bf16[128,768]{1,0:T(8,128)(2,1)} %get-tuple-element.94), channel_id=1, source_target_pairs={{0,4},{2,6},{4,0},{6,2},{1,5},{3,7},{5,1},{7,3},{8,12},{10,14},{12... | collective-permute-start | bytes 589832 | tf_op jit(solution)/shard_map/ppermute | solution.py:61
  155.2 12.8 %collective-permute-start.52 = (bf16[128,768]{1,0:T(8,128)(2,1)}, bf16[128,768]{1,0:T(8,128)(2,1)S(1)}, u32[]{:S(2)}, u32[]{:S(2)}) collective-permute-start(bf16[128,768]{1,0:T(8,128)(2,1)} %get-tuple-element.96), channel_id=1, source_target_pairs={{0,4},{2,6},{4,0},{6,2},{1,5},{3,7},{5,1},{7,3},{8,12},{10,14},{12... | collective-permute-start | bytes 589832 | tf_op jit(solution)/shard_map/ppermute | solution.py:61
  157.7 11.7 %collective-permute-start.54 = (bf16[128,768]{1,0:T(8,128)(2,1)S(1)}, bf16[128,768]{1,0:T(8,128)(2,1)S(1)}, u32[]{:S(2)}, u32[]{:S(2)}) collective-permute-start(bf16[128,768]{1,0:T(8,128)(2,1)S(1)} %add_convert_fusion.4), channel_id=1, source_target_pairs={{0,8},{8,0},{16,24},{24,16},{1,9},{9,1},{17,25},{25,17},{2,10},{10... | collective-permute-start | bytes 589832 | tf_op jit(solution)/shard_map/ppermute | solution.py:61
  163.6 9.5 %collective-permute-start.73 = (bf16[48,2560]{1,0:T(8,128)(2,1)}, bf16[48,2560]{1,0:T(8,128)(2,1)S(1)}, u32[]{:S(2)}, u32[]{:S(2)}) collective-permute-start(bf16[48,2560]{1,0:T(8,128)(2,1)} %get-tuple-element.134), channel_id=1, source_target_pairs={{0,4},{2,6},{4,0},{6,2},{1,5},{3,7},{5,1},{7,3},{8,12},{10,14},{12... | collective-permute-start | bytes 737288 | tf_op jit(solution)/shard_map/ppermute | solution.py:61
  165.2 11.6 %collective-permute-start.51 = (bf16[128,768]{1,0:T(8,128)(2,1)S(1)}, bf16[128,768]{1,0:T(8,128)(2,1)S(1)}, u32[]{:S(2)}, u32[]{:S(2)}) collective-permute-start(bf16[128,768]{1,0:T(8,128)(2,1)S(1)} %add_convert_fusion.5), channel_id=1, source_target_pairs={{0,8},{8,0},{16,24},{24,16},{1,9},{9,1},{17,25},{25,17},{2,10},{10... | collective-permute-start | bytes 589832 | tf_op jit(solution)/shard_map/ppermute | solution.py:61
  168.0 43.9 %collective-permute-start.69 = (bf16[48,2560]{1,0:T(8,128)(2,1)S(1)}, bf16[48,2560]{1,0:T(8,128)(2,1)S(1)}, u32[]{:S(2)}, u32[]{:S(2)}) collective-permute-start(bf16[48,2560]{1,0:T(8,128)(2,1)S(1)} %copy-done.52), channel_id=1, source_target_pairs={{0,4},{2,6},{4,0},{6,2},{1,5},{3,7},{5,1},{7,3},{8,12},{10,14},{12... | collective-permute-start | bytes 737288 | tf_op jit(solution)/shard_map/ppermute | solution.py:61
  169.3 19.2 %collective-permute-start.70 = (bf16[48,2560]{1,0:T(8,128)(2,1)}, bf16[48,2560]{1,0:T(8,128)(2,1)S(1)}, u32[]{:S(2)}, u32[]{:S(2)}) collective-permute-start(bf16[48,2560]{1,0:T(8,128)(2,1)} %get-tuple-element.130), channel_id=1, source_target_pairs={{0,4},{2,6},{4,0},{6,2},{1,5},{3,7},{5,1},{7,3},{8,12},{10,14},{12... | collective-permute-start | bytes 737288 | tf_op jit(solution)/shard_map/ppermute | solution.py:61
  173.1 10.3 %collective-permute-start.55 = (bf16[128,768]{1,0:T(8,128)(2,1)S(1)}, bf16[128,768]{1,0:T(8,128)(2,1)S(1)}, u32[]{:S(2)}, u32[]{:S(2)}) collective-permute-start(bf16[128,768]{1,0:T(8,128)(2,1)S(1)} %add_convert_fusion.3), channel_id=1, source_target_pairs={{0,16},{8,24},{16,0},{24,8},{1,17},{9,25},{17,1},{25,9},{2,18},{10... | collective-permute-start | bytes 589832 | tf_op jit(solution)/shard_map/ppermute | solution.py:61
  175.2 17.0 %collective-permute-start.72 = (bf16[48,2560]{1,0:T(8,128)(2,1)S(1)}, bf16[48,2560]{1,0:T(8,128)(2,1)S(1)}, u32[]{:S(2)}, u32[]{:S(2)}) collective-permute-start(bf16[48,2560]{1,0:T(8,128)(2,1)S(1)} %copy-done.53), channel_id=1, source_target_pairs={{0,4},{2,6},{4,0},{6,2},{1,5},{3,7},{5,1},{7,3},{8,12},{10,14},{12... | collective-permute-start | bytes 737288 | tf_op jit(solution)/shard_map/ppermute | solution.py:61
  176.8 16.9 %collective-permute-start.74 = (bf16[48,2560]{1,0:T(8,128)(2,1)S(1)}, bf16[48,2560]{1,0:T(8,128)(2,1)S(1)}, u32[]{:S(2)}, u32[]{:S(2)}) collective-permute-start(bf16[48,2560]{1,0:T(8,128)(2,1)S(1)} %add_convert_fusion.1), channel_id=1, source_target_pairs={{0,8},{8,0},{16,24},{24,16},{1,9},{9,1},{17,25},{25,17},{2,10},{10... | collective-permute-start | bytes 737288 | tf_op jit(solution)/shard_map/ppermute | solution.py:61
  188.7 23.8 %collective-permute-start.71 = (bf16[48,2560]{1,0:T(8,128)(2,1)S(1)}, bf16[48,2560]{1,0:T(8,128)(2,1)S(1)}, u32[]{:S(2)}, u32[]{:S(2)}) collective-permute-start(bf16[48,2560]{1,0:T(8,128)(2,1)S(1)} %add_convert_fusion.2), channel_id=1, source_target_pairs={{0,8},{8,0},{16,24},{24,16},{1,9},{9,1},{17,25},{25,17},{2,10},{10... | collective-permute-start | bytes 737288 | tf_op jit(solution)/shard_map/ppermute | solution.py:61
  193.8 18.6 %collective-permute-start.75 = (bf16[48,2560]{1,0:T(8,128)(2,1)S(1)}, bf16[48,2560]{1,0:T(8,128)(2,1)S(1)}, u32[]{:S(2)}, u32[]{:S(2)}) collective-permute-start(bf16[48,2560]{1,0:T(8,128)(2,1)S(1)} %add_convert_fusion), channel_id=1, source_target_pairs={{0,16},{8,24},{16,0},{24,8},{1,17},{9,25},{17,1},{25,9},{2,18},{10... | collective-permute-start | bytes 737288 | tf_op jit(solution)/shard_map/ppermute | solution.py:61
  199.9 9.5 %collective-permute-start.65 = (bf16[48,768]{1,0:T(8,128)(2,1)S(1)}, bf16[48,768]{1,0:T(8,128)(2,1)S(1)}, u32[]{:S(2)}, u32[]{:S(2)}) collective-permute-start(bf16[48,768]{1,0:T(8,128)(2,1)S(1)} %add_convert_fusion.7), channel_id=1, source_target_pairs={{0,8},{8,0},{16,24},{24,16},{1,9},{9,1},{17,25},{25,17},{2,10},{10... | collective-permute-start | bytes 221192 | tf_op jit(solution)/shard_map/ppermute | solution.py:61
  202.4 18.5 %collective-permute-start.57 = (bf16[128,768]{1,0:T(8,128)(2,1)S(1)}, bf16[128,768]{1,0:T(8,128)(2,1)S(1)}, u32[]{:S(2)}, u32[]{:S(2)}) collective-permute-start(bf16[128,768]{1,0:T(8,128)(2,1)S(1)} %copy-done.49), channel_id=1, source_target_pairs={{0,1},{1,0},{2,3},{3,2},{4,5},{5,4},{6,7},{7,6},{8,9},{9,8},{10,11... | collective-permute-start | bytes 589832 | tf_op jit(solution)/shard_map/ppermute | solution.py:61
  209.4 11.5 %collective-permute-start.56 = (bf16[128,768]{1,0:T(8,128)(2,1)S(1)}, bf16[128,768]{1,0:T(8,128)(2,1)S(1)}, u32[]{:S(2)}, u32[]{:S(2)}) collective-permute-start(bf16[128,768]{1,0:T(8,128)(2,1)S(1)} %copy-done.50), channel_id=1, source_target_pairs={{0,1},{1,0},{2,3},{3,2},{4,5},{5,4},{6,7},{7,6},{8,9},{9,8},{10,11... | collective-permute-start | bytes 589832 | tf_op jit(solution)/shard_map/ppermute | solution.py:61
  (86 other events, 838.4 us)

commit v8 on v7

--- a/solution.py
+++ b/solution.py
@@ -593,7 +593,7 @@
         [sds((d, toks), BF16), sds((toks, width), BF16), sds((toks, 2 * width), BF16), sds((8, d), F32)],
         [SM, VM, VM, VM] + [ANY] * nw,
         [pltpu.VMEM((d, wq_cols), BF16), wsem],
-        [order, inputs, cos, sin] + [near(x) for x in first_chunks],
+        [order, inputs, cos, sin] + first_chunks,
     )
     keys = gather(kv)
     rest_chunks = gather(w_rest)
@@ -615,7 +615,7 @@
             ksem,
             wsem,
         ],
-        [order, q] + [near(x) for x in keys] + first_chunks,
+        [order, q] + keys + first_chunks,
     )
     out_other = head_swap(out_part)
 
@@ -631,7 +631,7 @@
         ],
         [SM] + [VM] * 5 + [ANY] * nw,
         [pltpu.VMEM((d, rest_cols), BF16), wsem],
-        [order, inputs, out_part, near(out_other), cotangent, g] + [near(x) for x in rest_chunks],
+        [order, inputs, out_part, near(out_other), cotangent, g] + rest_chunks,
     )
     db_other = head_swap(db_part)
     ffn_other = head_swap(ffn_part)
@@ -730,7 +730,7 @@
         [sds(gains.shape, F32)] * 4,
         [VM] * 5,
         [],
-        [near(gain_part), near(gain_other), gains, gain_moment, gain_second],
+        [gain_part, near(gain_other), gains, gain_moment, gain_second],
     )
     return (
         outputs,

time: 229 us -> 220 us (0.961)
  Pallas kernels: 66.5 us -> 60.5 us
  local copies, waits for them, and re-layouts: 9.14 us -> 3.33 us
  waiting for transfers between devices: 84.3 us -> 89.5 us
    pallas_call x8, Pallas kernels: 44 us -> 38 us  [call(): pl.pallas_call(kernel, out_shape=out_shape, in_specs=specs, out_specs=jax...]
    unnamed x114, local copies, waits for them, and re-layouts: 9 us -> 3.18 us
    ppermute x77, waiting for transfers between devices: 84.3 us -> 89.5 us  [swap(): return lax.ppermute(x, axis, [(i, i ^ bits) for i in range(size)])]
  transfers between devices with their start and end apart: 77 -> 77, of which waited for: 25 -> 27; matrix products, arithmetic and copies ran while one was open for 2% -> 2% of each run, Pallas kernels for 22% -> 20%
where the time goes in v8:
time: 220 us; the launch traced here: 219 us
  waiting for transfers between devices  89.5 us (41%)
  Pallas kernels  60.5 us (28%)
  starting transfers between devices  56.9 us (26%)
  other arithmetic  7.06 us (3%)
  local copies, waits for them, and re-layouts  3.33 us (2%)
    ppermute x77, waiting for transfers between devices, swap(): return lax.ppermute(x, axis, [(i, i ^ bits) for i in range(size)])  89.5 us
    ppermute x77, starting transfers between devices, swap(): return lax.ppermute(x, axis, [(i, i ^ bits) for i in range(size)])  56.9 us
    pallas_call x8, Pallas kernels, call(): pl.pallas_call(kernel, out_shape=out_shape, in_specs=specs, out_specs=jax...  38 us
    pallas_call x6, Pallas kernels, pair_add(): pl.pallas_call(add_kernel, out_shape=[sds((rows, cols), BF16)] * 4, in_sp...  12.9 us
  transfers between devices with their start and end apart: 77, of which 27 were waited for; matrix products, arithmetic and copies ran while one was open for 2% of the time, Pallas kernels for 20%

profile of v8, /device:TPU:0, one launch (start us, length us, event | category | flops | bytes accessed | tf_op | source)
XLA Modules:
  0.0 218.8 jit_solution(2981122088487362753)
XLA Ops:
  2.6 3.0 %collective-permute-start.3 = (bf16[48,1664]{1,0:T(8,128)(2,1)S(1)}, bf16[48,1664]{1,0:T(8,128)(2,1)S(1)}, u32[]{:S(2)}, u32[]{:S(2)}) collective-permute-start(bf16[48,1664]{1,0:T(8,128)(2,1)S(1)} %fusion.1.rest_0_.rest_16_.rest_4_), channel_id=1, source_target_pairs={{0,4},{2,6},{4,0},{6,2},{1,5},{3,7},{5,1},{7,3},{8,12},{10,14},{12... | collective-permute-start | bytes 479240 | tf_op jit(solution)/shard_map/ppermute | solution.py:61
  5.6 2.6 %collective-permute-start.1 = (bf16[48,1664]{1,0:T(8,128)(2,1)S(1)}, bf16[48,1664]{1,0:T(8,128)(2,1)S(1)}, u32[]{:S(2)}, u32[]{:S(2)}) collective-permute-start(bf16[48,1664]{1,0:T(8,128)(2,1)S(1)} %fusion.1.rest_0_.rest_16_.rest_4_), channel_id=1, source_target_pairs={{0,16},{8,24},{16,0},{24,8},{1,17},{9,25},{17,1},{25,9},{2,18},{10... | collective-permute-start | bytes 479240 | tf_op jit(solution)/shard_map/ppermute | solution.py:61
  8.2 1.6 collective-permute-start
  10.0 5.6 %collective-permute-done.1.rest_2_.rest_18_.rest_6_ = bf16[48,1664]{1,0:T(8,128)(2,1)S(1)} collective-permute-done((bf16[48,1664]{1,0:T(8,128)(2,1)S(1)}, bf16[48,1664]{1,0:T(8,128)(2,1)S(1)}, u32[]{:S(2)}, u32[]{:S(2)}) %collective-permute-start.1) | collective-permute-done | bytes 159776 | tf_op jit(solution)/shard_map/ppermute | solution.py:61
  17.1 1.4 collective-permute-start.4
  18.5 2.4 %collective-permute-done.2.rest_3_.rest_19_.rest_7_ = bf16[48,1664]{1,0:T(8,128)(2,1)S(1)} collective-permute-done((bf16[48,1664]{1,0:T(8,128)(2,1)S(1)}, bf16[48,1664]{1,0:T(8,128)(2,1)S(1)}, u32[]{:S(2)}, u32[]{:S(2)}) %collective-permute-start.2) | collective-permute-done | bytes 159776 | tf_op jit(solution)/shard_map/ppermute | solution.py:61
  21.5 1.6 collective-permute-start.34
  23.8 2.9 %collective-permute-done.4.rest_5_.rest_21_.rest_9_ = bf16[48,1664]{1,0:T(8,128)(2,1)S(1)} collective-permute-done((bf16[48,1664]{1,0:T(8,128)(2,1)S(1)}, bf16[48,1664]{1,0:T(8,128)(2,1)S(1)}, u32[]{:S(2)}, u32[]{:S(2)}) %collective-permute-start.4) | collective-permute-done | bytes 159776 | tf_op jit(solution)/shard_map/ppermute | solution.py:61
  26.7 3.4 %collective-permute-done.6.rest_7_.rest_23_.rest_11_ = bf16[48,1664]{1,0:T(8,128)(2,1)S(1)} collective-permute-done((bf16[48,1664]{1,0:T(8,128)(2,1)S(1)}, bf16[48,1664]{1,0:T(8,128)(2,1)S(1)}, u32[]{:S(2)}, u32[]{:S(2)}) %collective-permute-start.6) | collective-permute-done | bytes 159776 | tf_op jit(solution)/shard_map/ppermute | solution.py:61
  32.7 4.3 %shard_map.159 = (bf16[768,128]{1,0:T(8,128)(2,1)}, bf16[128,384]{1,0:T(8,128)(2,1)}, bf16[128,768]{1,0:T(8,128)(2,1)}, f32[8,768]{1,0:T(8,128)}) custom-call(s32[1]{0:T(128)} %bitcast.order_ref, f32[128,768]{1,0:T(8,128)} %x_ref.5, f32[128,128]{1,0:T(8,128)} %get-tuple-element.145.cos_ref, f32[128,128]{1,0:T(8,128)} %get-tuple-element.144.sin_ref, ...), custom_call_target="tpu_custom_call" | custom-call | tf_op jit(solution)/shard_map/pallas_call | solution.py:488
  37.0 3.5 %collective-permute-start.16 = (bf16[128,768]{1,0:T(8,128)(2,1)}, bf16[128,768]{1,0:T(8,128)(2,1)S(1)}, u32[]{:S(2)}, u32[]{:S(2)}) collective-permute-start(bf16[128,768]{1,0:T(8,128)(2,1)} %get-tuple-element.79.rest_0_), channel_id=1, source_target_pairs={{0,16},{8,24},{16,0},{24,8},{1,17},{9,25},{17,1},{25,9},{2,18},{10... | collective-permute-start | bytes 589832 | tf_op jit(solution)/shard_map/ppermute | solution.py:61
  41.9 15.5 %collective-permute-done.32.rest_2_ = bf16[48,1792]{1,0:T(8,128)(2,1)} collective-permute-done((bf16[48,1792]{1,0:T(8,128)(2,1)S(1)}, bf16[48,1792]{1,0:T(8,128)(2,1)}, u32[]{:S(2)}, u32[]{:S(2)}) %collective-permute-start.32) | collective-permute-done | bytes 172064 | tf_op jit(solution)/shard_map/ppermute | solution.py:61
  57.5 2.0 collective-permute-start.17
  59.6 13.3 %collective-permute-done.33.rest_3_ = bf16[48,1792]{1,0:T(8,128)(2,1)S(1)} collective-permute-done((bf16[48,1792]{1,0:T(8,128)(2,1)}, bf16[48,1792]{1,0:T(8,128)(2,1)S(1)}, u32[]{:S(2)}, u32[]{:S(2)}) %collective-permute-start.33) | collective-permute-done | bytes 172064 | tf_op jit(solution)/shard_map/ppermute | solution.py:61
  73.4 1.6 collective-permute-start.19
  75.6 5.0 %collective-permute-done.20.rest_6_ = bf16[128,768]{1,0:T(8,128)(2,1)S(1)} collective-permute-done((bf16[128,768]{1,0:T(8,128)(2,1)S(1)}, bf16[128,768]{1,0:T(8,128)(2,1)S(1)}, u32[]{:S(2)}, u32[]{:S(2)}) %collective-permute-start.20) | collective-permute-done | bytes 196640 | tf_op jit(solution)/shard_map/ppermute | solution.py:61
  81.2 3.7 %collective-permute-done.19.rest_5_ = bf16[128,768]{1,0:T(8,128)(2,1)S(1)} collective-permute-done((bf16[128,768]{1,0:T(8,128)(2,1)S(1)}, bf16[128,768]{1,0:T(8,128)(2,1)S(1)}, u32[]{:S(2)}, u32[]{:S(2)}) %collective-permute-start.19) | collective-permute-done | bytes 196640 | tf_op jit(solution)/shard_map/ppermute | solution.py:61
  84.9 2.9 %collective-permute-done.21.rest_7_ = bf16[128,768]{1,0:T(8,128)(2,1)S(1)} collective-permute-done((bf16[128,768]{1,0:T(8,128)(2,1)S(1)}, bf16[128,768]{1,0:T(8,128)(2,1)S(1)}, u32[]{:S(2)}, u32[]{:S(2)}) %collective-permute-start.21) | collective-permute-done | bytes 196640 | tf_op jit(solution)/shard_map/ppermute | solution.py:61
  88.8 1.6 collective-permute-start.35
  91.1 7.5 %shard_map.160 = (bf16[128,384]{1,0:T(8,128)(2,1)}, f32[8,256]{1,0:T(8,128)}, bf16[128,768]{1,0:T(8,128)(2,1)}) custom-call(s32[1]{0:T(128)} %bitcast.order_ref, bf16[128,384]{1,0:T(8,128)(2,1)} %get-tuple-element.78.q_ref, bf16[128,768]{1,0:T(8,128)(2,1)} %get-tuple-element.79.rest_0_, bf16[128,768]{1,0:T(8,128)(2,1)} %copy-done.22, ...), custom_call_target="tpu_custom_call" | custom-call | tf_op jit(solution)/shard_map/pallas_call | solution.py:488
  99.3 1.6 collective-permute-start.30
  104.0 2.5 %collective-permute-done.30.pb_ref = bf16[128,768]{1,0:T(8,128)(2,1)S(1)} collective-permute-done((bf16[128,768]{1,0:T(8,128)(2,1)}, bf16[128,768]{1,0:T(8,128)(2,1)S(1)}, u32[]{:S(2)}, u32[]{:S(2)}) %collective-permute-start.30) | collective-permute-done | bytes 196640 | tf_op jit(solution)/shard_map/ppermute | solution.py:61
  106.5 5.4 %shard_map.161 = (f32[128,768]{1,0:T(8,128)}, bf16[128,768]{1,0:T(8,128)(2,1)}, bf16[128,768]{1,0:T(8,128)(2,1)}, bf16[128,768]{1,0:T(8,128)(2,1)}, bf16[128,1152]{1,0:T(8,128)(2,1)}, /*index=5*/bf16[128,576]{1,0:T(8,128)(2,1)}) custom-call(s32[1]{0:T(128)} %bitcast.order_ref, f32[128,768]{1,0:T(8,128)} %x_ref.5, bf16[128,768]{1,0:T(8,128)(2,1)} %get-tuple-element.82.pa_ref, ...), custom_call_target="tpu_custom_call" | custom-call | tf_op jit(solution)/shard_map/pallas_call | solution.py:488
  111.9 1.6 collective-permute-start.46
  113.4 4.8 %collective-permute-done.46.db_ref = bf16[128,768]{1,0:T(8,128)(2,1)S(1)} collective-permute-done((bf16[128,768]{1,0:T(8,128)(2,1)}, bf16[128,768]{1,0:T(8,128)(2,1)S(1)}, u32[]{:S(2)}, u32[]{:S(2)}) %collective-permute-start.46) | collective-permute-done | bytes 196640 | tf_op jit(solution)/shard_map/ppermute | solution.py:61
  118.2 9.9 %shard_map.162 = (bf16[512,768]{1,0:T(8,128)(2,1)}, bf16[512,768]{1,0:T(8,128)(2,1)}, bf16[512,768]{1,0:T(8,128)(2,1)}, bf16[512,768]{1,0:T(8,128)(2,1)}, f32[128,768]{1,0:T(8,128)}, /*index=5*/bf16[128,384]{1,0:T(8,128)(2,1)}) custom-call(s32[1]{0:T(128)} %bitcast.order_ref, bf16[128,384]{1,0:T(8,128)(2,1)} %get-tuple-element.78.q_ref, ...), custom_call_target="tpu_custom_call" | custom-call | tf_op jit(solution)/shard_map/pallas_call | solution.py:488
  128.7 4.1 %ffngrad.1 = (bf16[192,2560]{1,0:T(8,128)(2,1)}, bf16[192,2560]{1,0:T(8,128)(2,1)}, bf16[192,2560]{1,0:T(8,128)(2,1)}, bf16[192,2560]{1,0:T(8,128)(2,1)}) custom-call(s32[1]{0:T(128)} %bitcast.order_ref, bf16[128,768]{1,0:T(8,128)(2,1)} %get-tuple-element.116.b_ref, bf16[128,1152]{1,0:T(8,128)(2,1)} %get-tuple-element.117.dz_ref, f32[128,768]{1,0:T(8,128)} %cot_ref.5, ...), custom_call_target="tpu_custom_call" | custom-call | tf_op jit(solution)/shard_map/ffngrad/pallas_call | solution.py:641
  132.7 2.7 %oqgrad.1 = (bf16[192,2560]{1,0:T(8,128)(2,1)}, bf16[192,2560]{1,0:T(8,128)(2,1)}, bf16[192,2560]{1,0:T(8,128)(2,1)}, bf16[192,2560]{1,0:T(8,128)(2,1)}) custom-call(s32[1]{0:T(128)} %bitcast.order_ref, bf16[768,128]{1,0:T(8,128)(2,1)} %get-tuple-element.77.at_ref, ...), custom_call_target="tpu_custom_call", output_to_operand_aliasing={{0}: (5, {}), {1}: (6, {}), {2}: (7, {}), {3}: (8, {})} | custom-call | tf_op jit(solution)/shard_map/oqgrad/pallas_call | solution.py:674
  136.0 2.0 pair_add.7
  141.1 3.1 %pair_add.6 = (bf16[128,768]{1,0:T(8,128)(2,1)}, bf16[128,768]{1,0:T(8,128)(2,1)}, bf16[128,768]{1,0:T(8,128)(2,1)}, bf16[128,768]{1,0:T(8,128)(2,1)}) custom-call(bf16[512,768]{1,0:T(8,128)(2,1)} %get-tuple-element.87.keep, bf16[512,768]{1,0:T(8,128)(2,1)} %collective-permute-done.47.got), custom_call_target="tpu_custom_call" | custom-call | tf_op jit(solution)/shard_map/pair_add/pallas_call | solution.py:109
  144.3 1.8 collective-permute-done.53
  148.7 2.2 pair_add.11
  150.9 3.7 %collective-permute-done.50 = bf16[128,768]{1,0:T(8,128)(2,1)S(1)} collective-permute-done((bf16[128,768]{1,0:T(8,128)(2,1)}, bf16[128,768]{1,0:T(8,128)(2,1)S(1)}, u32[]{:S(2)}, u32[]{:S(2)}) %collective-permute-start.50) | collective-permute-done | bytes 196640 | tf_op jit(solution)/shard_map/ppermute | solution.py:61
  156.2 2.2 pair_add.10
  160.8 3.2 %collective-permute-done.73 = bf16[48,2560]{1,0:T(8,128)(2,1)S(1)} collective-permute-done((bf16[48,2560]{1,0:T(8,128)(2,1)}, bf16[48,2560]{1,0:T(8,128)(2,1)S(1)}, u32[]{:S(2)}, u32[]{:S(2)}) %collective-permute-start.73) | collective-permute-done | bytes 245792 | tf_op jit(solution)/shard_map/ppermute | solution.py:61
  168.6 5.7 %collective-permute-done.55.rest_3_ = bf16[128,768]{1,0:T(8,128)(2,1)S(1)} collective-permute-done((bf16[128,768]{1,0:T(8,128)(2,1)S(1)}, bf16[128,768]{1,0:T(8,128)(2,1)S(1)}, u32[]{:S(2)}, u32[]{:S(2)}) %collective-permute-start.55) | collective-permute-done | bytes 196640 | tf_op jit(solution)/shard_map/ppermute | solution.py:61
  174.3 4.8 %shard_map.163 = (bf16[192,768]{1,0:T(8,128)(2,1)}, bf16[192,768]{1,0:T(8,128)(2,1)}, bf16[192,768]{1,0:T(8,128)(2,1)}, bf16[192,768]{1,0:T(8,128)(2,1)}, bf16[128,768]{1,0:T(8,128)(2,1)}) custom-call(s32[1]{0:T(128)} %bitcast.order_ref, bf16[768,128]{1,0:T(8,128)(2,1)} %get-tuple-element.77.at_ref, bf16[128,384]{1,0:T(8,128)(2,1)} %get-tuple-element.86.dqp_ref, ...), custom_call_target="tpu_custom_call" | custom-call | tf_op jit(solution)/shard_map/pallas_call | solution.py:488
  179.3 1.6 collective-permute-done.59.got
  181.1 1.7 pair_add.9
  186.2 1.7 pair_add.8
  190.0 1.6 collective-permute-start.65
  192.6 1.6 collective-permute-start.57
  194.2 5.5 %collective-permute-done.65 = bf16[48,768]{1,0:T(8,128)(2,1)S(1)} collective-permute-done((bf16[48,768]{1,0:T(8,128)(2,1)S(1)}, bf16[48,768]{1,0:T(8,128)(2,1)S(1)}, u32[]{:S(2)}, u32[]{:S(2)}) %collective-permute-start.65) | collective-permute-done | bytes 73760 | tf_op jit(solution)/shard_map/ppermute | solution.py:61
  199.7 1.5 collective-permute-start.56
  203.2 2.6 %collective-permute-start.66 = (bf16[48,768]{1,0:T(8,128)(2,1)S(1)}, bf16[48,768]{1,0:T(8,128)(2,1)S(1)}, u32[]{:S(2)}, u32[]{:S(2)}) collective-permute-start(bf16[48,768]{1,0:T(8,128)(2,1)S(1)} %add_convert_fusion.6), channel_id=1, source_target_pairs={{0,16},{8,24},{16,0},{24,8},{1,17},{9,25},{17,1},{25,9},{2,18},{10... | collective-permute-start | bytes 221192 | tf_op jit(solution)/shard_map/ppermute | solution.py:61
  208.5 2.2 shard_map.165
  212.0 2.6 %shard_map.164 = (f32[128,768]{1,0:T(8,128)}, f32[128,768]{1,0:T(8,128)}) custom-call(f32[128,768]{1,0:T(8,128)} %x_ref.5, bf16[128,768]{1,0:T(8,128)(2,1)} %get-tuple-element.99.da_ref, bf16[128,768]{1,0:T(8,128)(2,1)S(1)} %collective-permute-done.56.db_ref, f32[128,768]{1,0:T(8,128)} %get-tuple-element.100.dhid_ref, f32[8,768]{1,0:T(8,128)} %get-tuple-element.83.g_ref, ...), custom_call_target="tpu_custom_call" | custom-call | tf_op jit(solution)/shard_map/pallas_call | solution.py:488
  214.6 2.8 %adam.1 = (f32[48,3264]{1,0:T(8,128)}, f32[48,3264]{1,0:T(8,128)}, f32[48,3264]{1,0:T(8,128)}) custom-call(f32[48,3264]{1,0:T(8,128)} %w_ref.5, f32[48,3264]{1,0:T(8,128)} %get-tuple-element.69.g_ref, f32[48,3264]{1,0:T(8,128)} %m_ref.3, f32[48,3264]{1,0:T(8,128)} %v_ref.3), custom_call_target="tpu_custom_call" | custom-call | tf_op jit(solution)/shard_map/adam/pallas_call | solution.py:720
  (257 shorter events, 45.3 us)
Async XLA Ops:
  5.6 10.0 %collective-permute-start.1 = (bf16[48,1664]{1,0:T(8,128)(2,1)S(1)}, bf16[48,1664]{1,0:T(8,128)(2,1)S(1)}, u32[]{:S(2)}, u32[]{:S(2)}) collective-permute-start(bf16[48,1664]{1,0:T(8,128)(2,1)S(1)} %fusion.1.rest_0_.rest_16_.rest_4_), channel_id=1, source_target_pairs={{0,16},{8,24},{16,0},{24,8},{1,17},{9,25},{17,1},{25,9},{2,18},{10... | collective-permute-start | bytes 479240 | tf_op jit(solution)/shard_map/ppermute | solution.py:61
  8.2 8.0 %collective-permute-start.7 = (bf16[48,1664]{1,0:T(8,128)(2,1)S(1)}, bf16[48,1664]{1,0:T(8,128)(2,1)S(1)}, u32[]{:S(2)}, u32[]{:S(2)}) collective-permute-start(bf16[48,1664]{1,0:T(8,128)(2,1)S(1)} %fusion.1.rest_0_.rest_16_.rest_4_), channel_id=1, source_target_pairs={{0,2},{2,0},{4,6},{6,4},{1,3},{3,1},{5,7},{7,5},{8,10},{10,8},{12,... | collective-permute-start | bytes 479240 | tf_op jit(solution)/shard_map/ppermute | solution.py:61
  8.2 8.8 %collective-permute-start = (bf16[48,1664]{1,0:T(8,128)(2,1)S(1)}, bf16[48,1664]{1,0:T(8,128)(2,1)S(1)}, u32[]{:S(2)}, u32[]{:S(2)}) collective-permute-start(bf16[48,1664]{1,0:T(8,128)(2,1)S(1)} %fusion.1.rest_0_.rest_16_.rest_4_), channel_id=1, source_target_pairs={{0,8},{8,0},{16,24},{24,16},{1,9},{9,1},{17,25},{25,17},{2,10},{10... | collective-permute-start | bytes 479240 | tf_op jit(solution)/shard_map/ppermute | solution.py:61
  17.1 9.6 %collective-permute-start.4 = (bf16[48,1664]{1,0:T(8,128)(2,1)S(1)}, bf16[48,1664]{1,0:T(8,128)(2,1)S(1)}, u32[]{:S(2)}, u32[]{:S(2)}) collective-permute-start(bf16[48,1664]{1,0:T(8,128)(2,1)S(1)} %collective-permute-done.rest_1_.rest_17_.rest_5_), channel_id=1, source_target_pairs={{0,4},{2,6},{4,0},{6,2},{1,5},{3,7},{5,1},{7,3},{8,12},{10,14},{12... | collective-permute-start | bytes 479240 | tf_op jit(solution)/shard_map/ppermute | solution.py:61
  20.9 9.2 %collective-permute-start.6 = (bf16[48,1664]{1,0:T(8,128)(2,1)S(1)}, bf16[48,1664]{1,0:T(8,128)(2,1)S(1)}, u32[]{:S(2)}, u32[]{:S(2)}) collective-permute-start(bf16[48,1664]{1,0:T(8,128)(2,1)S(1)} %collective-permute-done.2.rest_3_.rest_19_.rest_7_), channel_id=1, source_target_pairs={{0,4},{2,6},{4,0},{6,2},{1,5},{3,7},{5,1},{7,3},{8,12},{10,14},{12... | collective-permute-start | bytes 479240 | tf_op jit(solution)/shard_map/ppermute | solution.py:61
  21.5 19.8 %collective-permute-start.34 = (bf16[48,1792]{1,0:T(8,128)(2,1)S(1)}, bf16[48,1792]{1,0:T(8,128)(2,1)S(1)}, u32[]{:S(2)}, u32[]{:S(2)}) collective-permute-start(bf16[48,1792]{1,0:T(8,128)(2,1)S(1)} %pad.9.rest_0_), channel_id=1, source_target_pairs={{0,4},{2,6},{4,0},{6,2},{1,5},{3,7},{5,1},{7,3},{8,12},{10,14},{12... | collective-permute-start | bytes 516104 | tf_op jit(solution)/shard_map/ppermute | solution.py:61
  23.3 8.6 %collective-permute-start.10 = (bf16[48,1664]{1,0:T(8,128)(2,1)S(1)}, bf16[48,1664]{1,0:T(8,128)(2,1)S(1)}, u32[]{:S(2)}, u32[]{:S(2)}) collective-permute-start(bf16[48,1664]{1,0:T(8,128)(2,1)S(1)} %collective-permute-done.2.rest_3_.rest_19_.rest_7_), channel_id=1, source_target_pairs={{0,2},{2,0},{4,6},{6,4},{1,3},{3,1},{5,7},{7,5},{8,10},{10,8},{12,... | collective-permute-start | bytes 479240 | tf_op jit(solution)/shard_map/ppermute | solution.py:61
  23.3 7.9 %collective-permute-start.13 = (bf16[48,1664]{1,0:T(8,128)(2,1)S(1)}, bf16[48,1664]{1,0:T(8,128)(2,1)S(1)}, u32[]{:S(2)}, u32[]{:S(2)}) collective-permute-start(bf16[48,1664]{1,0:T(8,128)(2,1)S(1)} %collective-permute-done.5.rest_6_.rest_22_.rest_10_), channel_id=1, source_target_pairs={{0,2},{2,0},{4,6},{6,4},{1,3},{3,1},{5,7},{7,5},{8,10},{10,8},{12,... | collective-permute-start | bytes 479240 | tf_op jit(solution)/shard_map/ppermute | solution.py:61
  31.3 10.1 %collective-permute-start.38 = (bf16[48,1792]{1,0:T(8,128)(2,1)S(1)}, bf16[48,1792]{1,0:T(8,128)(2,1)S(1)}, u32[]{:S(2)}, u32[]{:S(2)}) collective-permute-start(bf16[48,1792]{1,0:T(8,128)(2,1)S(1)} %pad.9.rest_0_), channel_id=1, source_target_pairs={{0,2},{2,0},{4,6},{6,4},{1,3},{3,1},{5,7},{7,5},{8,10},{10,8},{12,... | collective-permute-start | bytes 516104 | tf_op jit(solution)/shard_map/ppermute | solution.py:61
  37.0 20.5 %collective-permute-start.16 = (bf16[128,768]{1,0:T(8,128)(2,1)}, bf16[128,768]{1,0:T(8,128)(2,1)S(1)}, u32[]{:S(2)}, u32[]{:S(2)}) collective-permute-start(bf16[128,768]{1,0:T(8,128)(2,1)} %get-tuple-element.79.rest_0_), channel_id=1, source_target_pairs={{0,16},{8,24},{16,0},{24,8},{1,17},{9,25},{17,1},{25,9},{2,18},{10... | collective-permute-start | bytes 589832 | tf_op jit(solution)/shard_map/ppermute | solution.py:61
  40.5 17.0 %collective-permute-start.32 = (bf16[48,1792]{1,0:T(8,128)(2,1)S(1)}, bf16[48,1792]{1,0:T(8,128)(2,1)}, u32[]{:S(2)}, u32[]{:S(2)}) collective-permute-start(bf16[48,1792]{1,0:T(8,128)(2,1)S(1)} %pad.9.rest_0_), channel_id=1, source_target_pairs={{0,16},{8,24},{16,0},{24,8},{1,17},{9,25},{17,1},{25,9},{2,18},{10... | collective-permute-start | bytes 516104 | tf_op jit(solution)/shard_map/ppermute | solution.py:61
  40.5 16.9 %collective-permute-start.31 = (bf16[48,1792]{1,0:T(8,128)(2,1)S(1)}, bf16[48,1792]{1,0:T(8,128)(2,1)}, u32[]{:S(2)}, u32[]{:S(2)}) collective-permute-start(bf16[48,1792]{1,0:T(8,128)(2,1)S(1)} %pad.9.rest_0_), channel_id=1, source_target_pairs={{0,8},{8,0},{16,24},{24,16},{1,9},{9,1},{17,25},{25,17},{2,10},{10... | collective-permute-start | bytes 516104 | tf_op jit(solution)/shard_map/ppermute | solution.py:61
  41.4 18.1 %collective-permute-start.42 = (bf16[48,1792]{1,0:T(8,128)(2,1)S(1)}, bf16[48,1792]{1,0:T(8,128)(2,1)S(1)}, u32[]{:S(2)}, u32[]{:S(2)}) collective-permute-start(bf16[48,1792]{1,0:T(8,128)(2,1)S(1)} %collective-permute-done.34.rest_4_), channel_id=1, source_target_pairs={{0,2},{2,0},{4,6},{6,4},{1,3},{3,1},{5,7},{7,5},{8,10},{10,8},{12,... | collective-permute-start | bytes 516104 | tf_op jit(solution)/shard_map/ppermute | solution.py:61
  41.4 18.2 %collective-permute-start.18 = (bf16[128,768]{1,0:T(8,128)(2,1)}, bf16[128,768]{1,0:T(8,128)(2,1)S(1)}, u32[]{:S(2)}, u32[]{:S(2)}) collective-permute-start(bf16[128,768]{1,0:T(8,128)(2,1)} %get-tuple-element.79.rest_0_), channel_id=1, source_target_pairs={{0,4},{2,6},{4,0},{6,2},{1,5},{3,7},{5,1},{7,3},{8,12},{10,14},{12... | collective-permute-start | bytes 589832 | tf_op jit(solution)/shard_map/ppermute | solution.py:61
  57.5 16.0 %collective-permute-start.22 = (bf16[128,768]{1,0:T(8,128)(2,1)}, bf16[128,768]{1,0:T(8,128)(2,1)S(1)}, u32[]{:S(2)}, u32[]{:S(2)}) collective-permute-start(bf16[128,768]{1,0:T(8,128)(2,1)} %get-tuple-element.79.rest_0_), channel_id=1, source_target_pairs={{0,2},{2,0},{4,6},{6,4},{1,3},{3,1},{5,7},{7,5},{8,10},{10,8},{12,... | collective-permute-start | bytes 589832 | tf_op jit(solution)/shard_map/ppermute | solution.py:61
  57.5 16.0 %collective-permute-start.15 = (bf16[128,768]{1,0:T(8,128)(2,1)}, bf16[128,768]{1,0:T(8,128)(2,1)S(1)}, u32[]{:S(2)}, u32[]{:S(2)}) collective-permute-start(bf16[128,768]{1,0:T(8,128)(2,1)} %get-tuple-element.79.rest_0_), channel_id=1, source_target_pairs={{0,8},{8,0},{16,24},{24,16},{1,9},{9,1},{17,25},{25,17},{2,10},{10... | collective-permute-start | bytes 589832 | tf_op jit(solution)/shard_map/ppermute | solution.py:61
  57.5 17.5 %collective-permute-start.17 = (bf16[128,768]{1,0:T(8,128)(2,1)S(1)}, bf16[128,768]{1,0:T(8,128)(2,1)S(1)}, u32[]{:S(2)}, u32[]{:S(2)}) collective-permute-start(bf16[128,768]{1,0:T(8,128)(2,1)S(1)} %collective-permute-done.16.rest_2_), channel_id=1, source_target_pairs={{0,8},{8,0},{16,24},{24,16},{1,9},{9,1},{17,25},{25,17},{2,10},{10... | collective-permute-start | bytes 589832 | tf_op jit(solution)/shard_map/ppermute | solution.py:61
  59.5 13.4 %collective-permute-start.33 = (bf16[48,1792]{1,0:T(8,128)(2,1)}, bf16[48,1792]{1,0:T(8,128)(2,1)S(1)}, u32[]{:S(2)}, u32[]{:S(2)}) collective-permute-start(bf16[48,1792]{1,0:T(8,128)(2,1)} %collective-permute-done.32.rest_2_), channel_id=1, source_target_pairs={{0,8},{8,0},{16,24},{24,16},{1,9},{9,1},{17,25},{25,17},{2,10},{10... | collective-permute-start | bytes 516104 | tf_op jit(solution)/shard_map/ppermute | solution.py:61
  59.6 16.0 %collective-permute-start.26 = (bf16[128,768]{1,0:T(8,128)(2,1)S(1)}, bf16[128,768]{1,0:T(8,128)(2,1)S(1)}, u32[]{:S(2)}, u32[]{:S(2)}) collective-permute-start(bf16[128,768]{1,0:T(8,128)(2,1)S(1)} %collective-permute-done.18.rest_4_), channel_id=1, source_target_pairs={{0,2},{2,0},{4,6},{6,4},{1,3},{3,1},{5,7},{7,5},{8,10},{10,8},{12,... | collective-permute-start | bytes 589832 | tf_op jit(solution)/shard_map/ppermute | solution.py:61
  73.4 11.4 %collective-permute-start.19 = (bf16[128,768]{1,0:T(8,128)(2,1)S(1)}, bf16[128,768]{1,0:T(8,128)(2,1)S(1)}, u32[]{:S(2)}, u32[]{:S(2)}) collective-permute-start(bf16[128,768]{1,0:T(8,128)(2,1)S(1)} %collective-permute-done.15.rest_1_), channel_id=1, source_target_pairs={{0,4},{2,6},{4,0},{6,2},{1,5},{3,7},{5,1},{7,3},{8,12},{10,14},{12... | collective-permute-start | bytes 589832 | tf_op jit(solution)/shard_map/ppermute | solution.py:61
  75.0 12.8 %collective-permute-start.21 = (bf16[128,768]{1,0:T(8,128)(2,1)S(1)}, bf16[128,768]{1,0:T(8,128)(2,1)S(1)}, u32[]{:S(2)}, u32[]{:S(2)}) collective-permute-start(bf16[128,768]{1,0:T(8,128)(2,1)S(1)} %collective-permute-done.17.rest_3_), channel_id=1, source_target_pairs={{0,4},{2,6},{4,0},{6,2},{1,5},{3,7},{5,1},{7,3},{8,12},{10,14},{12... | collective-permute-start | bytes 589832 | tf_op jit(solution)/shard_map/ppermute | solution.py:61
  75.6 12.2 %collective-permute-start.23 = (bf16[128,768]{1,0:T(8,128)(2,1)S(1)}, bf16[128,768]{1,0:T(8,128)(2,1)S(1)}, u32[]{:S(2)}, u32[]{:S(2)}) collective-permute-start(bf16[128,768]{1,0:T(8,128)(2,1)S(1)} %collective-permute-done.15.rest_1_), channel_id=1, source_target_pairs={{0,2},{2,0},{4,6},{6,4},{1,3},{3,1},{5,7},{7,5},{8,10},{10,8},{12,... | collective-permute-start | bytes 589832 | tf_op jit(solution)/shard_map/ppermute | solution.py:61
  80.7 8.1 %collective-permute-start.25 = (bf16[128,768]{1,0:T(8,128)(2,1)S(1)}, bf16[128,768]{1,0:T(8,128)(2,1)S(1)}, u32[]{:S(2)}, u32[]{:S(2)}) collective-permute-start(bf16[128,768]{1,0:T(8,128)(2,1)S(1)} %collective-permute-done.17.rest_3_), channel_id=1, source_target_pairs={{0,2},{2,0},{4,6},{6,4},{1,3},{3,1},{5,7},{7,5},{8,10},{10,8},{12,... | collective-permute-start | bytes 589832 | tf_op jit(solution)/shard_map/ppermute | solution.py:61
  87.8 10.8 %collective-permute-start.40 = (bf16[48,1792]{1,0:T(8,128)(2,1)}, bf16[48,1792]{1,0:T(8,128)(2,1)S(1)}, u32[]{:S(2)}, u32[]{:S(2)}) collective-permute-start(bf16[48,1792]{1,0:T(8,128)(2,1)} %collective-permute-done.32.rest_2_), channel_id=1, source_target_pairs={{0,2},{2,0},{4,6},{6,4},{1,3},{3,1},{5,7},{7,5},{8,10},{10,8},{12,... | collective-permute-start | bytes 516104 | tf_op jit(solution)/shard_map/ppermute | solution.py:61
  88.3 12.6 %collective-permute-start.36 = (bf16[48,1792]{1,0:T(8,128)(2,1)}, bf16[48,1792]{1,0:T(8,128)(2,1)}, u32[]{:S(2)}, u32[]{:S(2)}) collective-permute-start(bf16[48,1792]{1,0:T(8,128)(2,1)} %collective-permute-done.32.rest_2_), channel_id=1, source_target_pairs={{0,4},{2,6},{4,0},{6,2},{1,5},{3,7},{5,1},{7,3},{8,12},{10,14},{12... | collective-permute-start | bytes 516104 | tf_op jit(solution)/shard_map/ppermute | solution.py:61
  88.8 12.1 %collective-permute-start.39 = (bf16[48,1792]{1,0:T(8,128)(2,1)}, bf16[48,1792]{1,0:T(8,128)(2,1)}, u32[]{:S(2)}, u32[]{:S(2)}) collective-permute-start(bf16[48,1792]{1,0:T(8,128)(2,1)} %collective-permute-done.31.rest_1_), channel_id=1, source_target_pairs={{0,2},{2,0},{4,6},{6,4},{1,3},{3,1},{5,7},{7,5},{8,10},{10,8},{12,... | collective-permute-start | bytes 516104 | tf_op jit(solution)/shard_map/ppermute | solution.py:61
  88.8 12.6 %collective-permute-start.35 = (bf16[48,1792]{1,0:T(8,128)(2,1)}, bf16[48,1792]{1,0:T(8,128)(2,1)}, u32[]{:S(2)}, u32[]{:S(2)}) collective-permute-start(bf16[48,1792]{1,0:T(8,128)(2,1)} %collective-permute-done.31.rest_1_), channel_id=1, source_target_pairs={{0,4},{2,6},{4,0},{6,2},{1,5},{3,7},{5,1},{7,3},{8,12},{10,14},{12... | collective-permute-start | bytes 516104 | tf_op jit(solution)/shard_map/ppermute | solution.py:61
  90.4 11.9 %collective-permute-start.37 = (bf16[48,1792]{1,0:T(8,128)(2,1)S(1)}, bf16[48,1792]{1,0:T(8,128)(2,1)}, u32[]{:S(2)}, u32[]{:S(2)}) collective-permute-start(bf16[48,1792]{1,0:T(8,128)(2,1)S(1)} %collective-permute-done.33.rest_3_), channel_id=1, source_target_pairs={{0,4},{2,6},{4,0},{6,2},{1,5},{3,7},{5,1},{7,3},{8,12},{10,14},{12... | collective-permute-start | bytes 516104 | tf_op jit(solution)/shard_map/ppermute | solution.py:61
  128.2 12.0 %collective-permute-start.47 = (bf16[512,768]{1,0:T(8,128)(2,1)}, bf16[512,768]{1,0:T(8,128)(2,1)}, u32[]{:S(2)}, u32[]{:S(2)}) collective-permute-start(bf16[512,768]{1,0:T(8,128)(2,1)} %get-tuple-element.88), channel_id=1, source_target_pairs={{0,2},{2,0},{4,6},{6,4},{1,3},{3,1},{5,7},{7,5},{8,10},{10,8},{12,... | collective-permute-start | bytes 2359304 | tf_op jit(solution)/shard_map/ppermute | solution.py:61
  135.5 12.6 %collective-permute-start.68 = (bf16[192,2560]{1,0:T(8,128)(2,1)}, bf16[192,2560]{1,0:T(8,128)(2,1)S(1)}, u32[]{:S(2)}, u32[]{:S(2)}) collective-permute-start(bf16[192,2560]{1,0:T(8,128)(2,1)} %get-tuple-element.127), channel_id=1, source_target_pairs={{0,2},{2,0},{4,6},{6,4},{1,3},{3,1},{5,7},{7,5},{8,10},{10,8},{12,... | collective-permute-start | bytes 2949128 | tf_op jit(solution)/shard_map/ppermute | solution.py:61
  135.6 20.0 %collective-permute-start.67 = (bf16[192,2560]{1,0:T(8,128)(2,1)}, bf16[192,2560]{1,0:T(8,128)(2,1)S(1)}, u32[]{:S(2)}, u32[]{:S(2)}) collective-permute-start(bf16[192,2560]{1,0:T(8,128)(2,1)} %get-tuple-element.124), channel_id=1, source_target_pairs={{0,2},{2,0},{4,6},{6,4},{1,3},{3,1},{5,7},{7,5},{8,10},{10,8},{12,... | collective-permute-start | bytes 2949128 | tf_op jit(solution)/shard_map/ppermute | solution.py:61
  138.0 8.0 %collective-permute-start.53 = (bf16[128,768]{1,0:T(8,128)(2,1)}, bf16[128,768]{1,0:T(8,128)(2,1)S(1)}, u32[]{:S(2)}, u32[]{:S(2)}) collective-permute-start(bf16[128,768]{1,0:T(8,128)(2,1)} %get-tuple-element.98), channel_id=1, source_target_pairs={{0,4},{2,6},{4,0},{6,2},{1,5},{3,7},{5,1},{7,3},{8,12},{10,14},{12... | collective-permute-start | bytes 589832 | tf_op jit(solution)/shard_map/ppermute | solution.py:61
  139.1 26.1 %collective-permute-start.49 = (bf16[128,768]{1,0:T(8,128)(2,1)}, bf16[128,768]{1,0:T(8,128)(2,1)S(1)}, u32[]{:S(2)}, u32[]{:S(2)}) collective-permute-start(bf16[128,768]{1,0:T(8,128)(2,1)} %get-tuple-element.92), channel_id=1, source_target_pairs={{0,4},{2,6},{4,0},{6,2},{1,5},{3,7},{5,1},{7,3},{8,12},{10,14},{12... | collective-permute-start | bytes 589832 | tf_op jit(solution)/shard_map/ppermute | solution.py:61
  140.1 14.4 %collective-permute-start.50 = (bf16[128,768]{1,0:T(8,128)(2,1)}, bf16[128,768]{1,0:T(8,128)(2,1)S(1)}, u32[]{:S(2)}, u32[]{:S(2)}) collective-permute-start(bf16[128,768]{1,0:T(8,128)(2,1)} %get-tuple-element.94), channel_id=1, source_target_pairs={{0,4},{2,6},{4,0},{6,2},{1,5},{3,7},{5,1},{7,3},{8,12},{10,14},{12... | collective-permute-start | bytes 589832 | tf_op jit(solution)/shard_map/ppermute | solution.py:61
  146.1 12.6 %collective-permute-start.52 = (bf16[128,768]{1,0:T(8,128)(2,1)}, bf16[128,768]{1,0:T(8,128)(2,1)S(1)}, u32[]{:S(2)}, u32[]{:S(2)}) collective-permute-start(bf16[128,768]{1,0:T(8,128)(2,1)} %get-tuple-element.96), channel_id=1, source_target_pairs={{0,4},{2,6},{4,0},{6,2},{1,5},{3,7},{5,1},{7,3},{8,12},{10,14},{12... | collective-permute-start | bytes 589832 | tf_op jit(solution)/shard_map/ppermute | solution.py:61
  148.1 11.7 %collective-permute-start.54 = (bf16[128,768]{1,0:T(8,128)(2,1)S(1)}, bf16[128,768]{1,0:T(8,128)(2,1)S(1)}, u32[]{:S(2)}, u32[]{:S(2)}) collective-permute-start(bf16[128,768]{1,0:T(8,128)(2,1)S(1)} %add_convert_fusion.4), channel_id=1, source_target_pairs={{0,8},{8,0},{16,24},{24,16},{1,9},{9,1},{17,25},{25,17},{2,10},{10... | collective-permute-start | bytes 589832 | tf_op jit(solution)/shard_map/ppermute | solution.py:61
  154.5 9.5 %collective-permute-start.73 = (bf16[48,2560]{1,0:T(8,128)(2,1)}, bf16[48,2560]{1,0:T(8,128)(2,1)S(1)}, u32[]{:S(2)}, u32[]{:S(2)}) collective-permute-start(bf16[48,2560]{1,0:T(8,128)(2,1)} %get-tuple-element.134), channel_id=1, source_target_pairs={{0,4},{2,6},{4,0},{6,2},{1,5},{3,7},{5,1},{7,3},{8,12},{10,14},{12... | collective-permute-start | bytes 737288 | tf_op jit(solution)/shard_map/ppermute | solution.py:61
  155.6 11.6 %collective-permute-start.51 = (bf16[128,768]{1,0:T(8,128)(2,1)S(1)}, bf16[128,768]{1,0:T(8,128)(2,1)S(1)}, u32[]{:S(2)}, u32[]{:S(2)}) collective-permute-start(bf16[128,768]{1,0:T(8,128)(2,1)S(1)} %add_convert_fusion.5), channel_id=1, source_target_pairs={{0,8},{8,0},{16,24},{24,16},{1,9},{9,1},{17,25},{25,17},{2,10},{10... | collective-permute-start | bytes 589832 | tf_op jit(solution)/shard_map/ppermute | solution.py:61
  158.7 43.4 %collective-permute-start.69 = (bf16[48,2560]{1,0:T(8,128)(2,1)}, bf16[48,2560]{1,0:T(8,128)(2,1)S(1)}, u32[]{:S(2)}, u32[]{:S(2)}) collective-permute-start(bf16[48,2560]{1,0:T(8,128)(2,1)} %get-tuple-element.128), channel_id=1, source_target_pairs={{0,4},{2,6},{4,0},{6,2},{1,5},{3,7},{5,1},{7,3},{8,12},{10,14},{12... | collective-permute-start | bytes 737288 | tf_op jit(solution)/shard_map/ppermute | solution.py:61
  159.7 19.4 %collective-permute-start.70 = (bf16[48,2560]{1,0:T(8,128)(2,1)}, bf16[48,2560]{1,0:T(8,128)(2,1)S(1)}, u32[]{:S(2)}, u32[]{:S(2)}) collective-permute-start(bf16[48,2560]{1,0:T(8,128)(2,1)} %get-tuple-element.130), channel_id=1, source_target_pairs={{0,4},{2,6},{4,0},{6,2},{1,5},{3,7},{5,1},{7,3},{8,12},{10,14},{12... | collective-permute-start | bytes 737288 | tf_op jit(solution)/shard_map/ppermute | solution.py:61
  164.0 10.3 %collective-permute-start.55 = (bf16[128,768]{1,0:T(8,128)(2,1)S(1)}, bf16[128,768]{1,0:T(8,128)(2,1)S(1)}, u32[]{:S(2)}, u32[]{:S(2)}) collective-permute-start(bf16[128,768]{1,0:T(8,128)(2,1)S(1)} %add_convert_fusion.3), channel_id=1, source_target_pairs={{0,16},{8,24},{16,0},{24,8},{1,17},{9,25},{17,1},{25,9},{2,18},{10... | collective-permute-start | bytes 589832 | tf_op jit(solution)/shard_map/ppermute | solution.py:61
  166.1 16.7 %collective-permute-start.72 = (bf16[48,2560]{1,0:T(8,128)(2,1)S(1)}, bf16[48,2560]{1,0:T(8,128)(2,1)S(1)}, u32[]{:S(2)}, u32[]{:S(2)}) collective-permute-start(bf16[48,2560]{1,0:T(8,128)(2,1)S(1)} %copy-done.53), channel_id=1, source_target_pairs={{0,4},{2,6},{4,0},{6,2},{1,5},{3,7},{5,1},{7,3},{8,12},{10,14},{12... | collective-permute-start | bytes 737288 | tf_op jit(solution)/shard_map/ppermute | solution.py:61
  167.1 16.7 %collective-permute-start.74 = (bf16[48,2560]{1,0:T(8,128)(2,1)S(1)}, bf16[48,2560]{1,0:T(8,128)(2,1)S(1)}, u32[]{:S(2)}, u32[]{:S(2)}) collective-permute-start(bf16[48,2560]{1,0:T(8,128)(2,1)S(1)} %add_convert_fusion.1), channel_id=1, source_target_pairs={{0,8},{8,0},{16,24},{24,16},{1,9},{9,1},{17,25},{25,17},{2,10},{10... | collective-permute-start | bytes 737288 | tf_op jit(solution)/shard_map/ppermute | solution.py:61
  179.3 23.9 %collective-permute-start.71 = (bf16[48,2560]{1,0:T(8,128)(2,1)S(1)}, bf16[48,2560]{1,0:T(8,128)(2,1)S(1)}, u32[]{:S(2)}, u32[]{:S(2)}) collective-permute-start(bf16[48,2560]{1,0:T(8,128)(2,1)S(1)} %add_convert_fusion.2), channel_id=1, source_target_pairs={{0,8},{8,0},{16,24},{24,16},{1,9},{9,1},{17,25},{25,17},{2,10},{10... | collective-permute-start | bytes 737288 | tf_op jit(solution)/shard_map/ppermute | solution.py:61
  184.0 19.2 %collective-permute-start.75 = (bf16[48,2560]{1,0:T(8,128)(2,1)S(1)}, bf16[48,2560]{1,0:T(8,128)(2,1)S(1)}, u32[]{:S(2)}, u32[]{:S(2)}) collective-permute-start(bf16[48,2560]{1,0:T(8,128)(2,1)S(1)} %add_convert_fusion), channel_id=1, source_target_pairs={{0,16},{8,24},{16,0},{24,8},{1,17},{9,25},{17,1},{25,9},{2,18},{10... | collective-permute-start | bytes 737288 | tf_op jit(solution)/shard_map/ppermute | solution.py:61
  190.0 9.7 %collective-permute-start.65 = (bf16[48,768]{1,0:T(8,128)(2,1)S(1)}, bf16[48,768]{1,0:T(8,128)(2,1)S(1)}, u32[]{:S(2)}, u32[]{:S(2)}) collective-permute-start(bf16[48,768]{1,0:T(8,128)(2,1)S(1)} %add_convert_fusion.7), channel_id=1, source_target_pairs={{0,8},{8,0},{16,24},{24,16},{1,9},{9,1},{17,25},{25,17},{2,10},{10... | collective-permute-start | bytes 221192 | tf_op jit(solution)/shard_map/ppermute | solution.py:61
  192.6 19.4 %collective-permute-start.57 = (bf16[128,768]{1,0:T(8,128)(2,1)S(1)}, bf16[128,768]{1,0:T(8,128)(2,1)S(1)}, u32[]{:S(2)}, u32[]{:S(2)}) collective-permute-start(bf16[128,768]{1,0:T(8,128)(2,1)S(1)} %copy-done.40), channel_id=1, source_target_pairs={{0,1},{1,0},{2,3},{3,2},{4,5},{5,4},{6,7},{7,6},{8,9},{9,8},{10,11... | collective-permute-start | bytes 589832 | tf_op jit(solution)/shard_map/ppermute | solution.py:61
  199.7 12.3 %collective-permute-start.56 = (bf16[128,768]{1,0:T(8,128)(2,1)S(1)}, bf16[128,768]{1,0:T(8,128)(2,1)S(1)}, u32[]{:S(2)}, u32[]{:S(2)}) collective-permute-start(bf16[128,768]{1,0:T(8,128)(2,1)S(1)} %copy-done.41), channel_id=1, source_target_pairs={{0,1},{1,0},{2,3},{3,2},{4,5},{5,4},{6,7},{7,6},{8,9},{9,8},{10,11... | collective-permute-start | bytes 589832 | tf_op jit(solution)/shard_map/ppermute | solution.py:61
  (86 other events, 714.9 us)

commit v9 on v8

--- a/solution.py
+++ b/solution.py
@@ -38,6 +38,10 @@
 
 def near(x):
     return pltpu.with_memory_space_constraint(x, pltpu.VMEM) if staged() else x
+
+
+def near_out(shape, dtype):
+    return pltpu.VMEM(shape, dtype) if staged() else jax.ShapeDtypeStruct(shape, dtype)
 
 
 def sds(shape, dtype):
@@ -604,7 +608,7 @@
 
     attn, lse, out_part = call(
         partial(attend_kernel, nk, nw, blocks),
-        [sds((toks, width), BF16), sds((8, 2 * toks), F32), sds((toks, d), BF16)],
+        [sds((toks, width), BF16), sds((8, 2 * toks), F32), near_out((toks, d), BF16)],
         [SM, VM] + [ANY] * (nk + nw),
         [
             pltpu.VMEM((block_rows, 2 * width), BF16),
@@ -624,14 +628,14 @@
         [
             sds((toks, d), F32),
             sds((toks, d), BF16),
-            sds((toks, d), BF16),
+            near_out((toks, d), BF16),
             sds((toks, d), BF16),
             sds((toks, 2 * units), BF16),
             sds((toks, units), BF16),
         ],
         [SM] + [VM] * 5 + [ANY] * nw,
         [pltpu.VMEM((d, rest_cols), BF16), wsem],
-        [order, inputs, out_part, near(out_other), cotangent, g] + rest_chunks,
+        [order, inputs, near(out_part), near(out_other), cotangent, g] + rest_chunks,
     )
     db_other = head_swap(db_part)
     ffn_other = head_swap(ffn_part)
@@ -667,7 +671,7 @@
             ksem,
             wsem,
         ],
-        [order, q, attn, lse, hidden, cotangent, g, db_part, near(db_other), cos, sin]
+        [order, q, attn, lse, hidden, cotangent, g, near(db_part), near(db_other), cos, sin]
         + keys
         + first_chunks,
     )
@@ -709,7 +713,7 @@
     full = weights.shape
     weight_grad, gain_part = call(
         partial(gsum_kernel, nt, width, units),
-        [sds(full, F32), sds(gains.shape, F32)],
+        [sds(full, F32), near_out(gains.shape, F32)],
         [VM] * (1 + 2 * nt),
         [],
         [weights] + [near(x) for x in first_terms + rest_terms],
@@ -730,7 +734,7 @@
         [sds(gains.shape, F32)] * 4,
         [VM] * 5,
         [],
-        [gain_part, near(gain_other), gains, gain_moment, gain_second],
+        [near(gain_part), near(gain_other), gains, gain_moment, gain_second],
     )
     return (
         outputs,

time: 220 us -> 217 us (0.986)
  transfers between devices with their start and end apart: 77 -> 77, of which waited for: 27 -> 25; matrix products, arithmetic and copies ran while one was open for 2% -> 2% of each run, Pallas kernels for 20% -> 20%
where the time goes in v9:
time: 217 us
  waiting for transfers between devices  88.1 us (41%)
  Pallas kernels  60.1 us (28%)
  starting transfers between devices  57.2 us (26%)
  other arithmetic  7.06 us (3%)
  local copies, waits for them, and re-layouts  2.5 us (1%)
    ppermute x77, waiting for transfers between devices, swap(): return lax.ppermute(x, axis, [(i, i ^ bits) for i in range(size)])  88.1 us
    ppermute x77, starting transfers between devices, swap(): return lax.ppermute(x, axis, [(i, i ^ bits) for i in range(size)])  57.2 us
    pallas_call x8, Pallas kernels, call(): pl.pallas_call(kernel, out_shape=out_shape, in_specs=specs, out_specs=jax...  37.5 us
    pallas_call x6, Pallas kernels, pair_add(): pl.pallas_call(add_kernel, out_shape=[sds((rows, cols), BF16)] * 4, in_sp...  12.9 us
  transfers between devices with their start and end apart: 77, of which 25 were waited for; matrix products, arithmetic and copies ran while one was open for 2% of the time, Pallas kernels for 20%

profile of v9, /device:TPU:0, one launch (start us, length us, event | category | flops | bytes accessed | tf_op | source)
XLA Modules:
  0.0 216.5 jit_solution(13902552823195694085)
XLA Ops:
  2.6 3.0 %collective-permute-start.3 = (bf16[48,1664]{1,0:T(8,128)(2,1)S(1)}, bf16[48,1664]{1,0:T(8,128)(2,1)S(1)}, u32[]{:S(2)}, u32[]{:S(2)}) collective-permute-start(bf16[48,1664]{1,0:T(8,128)(2,1)S(1)} %fusion.1.rest_0_.rest_16_.rest_4_), channel_id=1, source_target_pairs={{0,4},{2,6},{4,0},{6,2},{1,5},{3,7},{5,1},{7,3},{8,12},{10,14},{12... | collective-permute-start | bytes 479240 | tf_op jit(solution)/shard_map/ppermute | solution.py:65
  5.6 2.6 %collective-permute-start.1 = (bf16[48,1664]{1,0:T(8,128)(2,1)S(1)}, bf16[48,1664]{1,0:T(8,128)(2,1)S(1)}, u32[]{:S(2)}, u32[]{:S(2)}) collective-permute-start(bf16[48,1664]{1,0:T(8,128)(2,1)S(1)} %fusion.1.rest_0_.rest_16_.rest_4_), channel_id=1, source_target_pairs={{0,16},{8,24},{16,0},{24,8},{1,17},{9,25},{17,1},{25,9},{2,18},{10... | collective-permute-start | bytes 479240 | tf_op jit(solution)/shard_map/ppermute | solution.py:65
  8.2 1.6 collective-permute-start
  10.0 5.6 %collective-permute-done.1.rest_2_.rest_18_.rest_6_ = bf16[48,1664]{1,0:T(8,128)(2,1)S(1)} collective-permute-done((bf16[48,1664]{1,0:T(8,128)(2,1)S(1)}, bf16[48,1664]{1,0:T(8,128)(2,1)S(1)}, u32[]{:S(2)}, u32[]{:S(2)}) %collective-permute-start.1) | collective-permute-done | bytes 159776 | tf_op jit(solution)/shard_map/ppermute | solution.py:65
  18.5 2.4 %collective-permute-done.2.rest_3_.rest_19_.rest_7_ = bf16[48,1664]{1,0:T(8,128)(2,1)S(1)} collective-permute-done((bf16[48,1664]{1,0:T(8,128)(2,1)S(1)}, bf16[48,1664]{1,0:T(8,128)(2,1)S(1)}, u32[]{:S(2)}, u32[]{:S(2)}) %collective-permute-start.2) | collective-permute-done | bytes 159776 | tf_op jit(solution)/shard_map/ppermute | solution.py:65
  21.5 1.6 collective-permute-start.34
  23.8 2.9 %collective-permute-done.4.rest_5_.rest_21_.rest_9_ = bf16[48,1664]{1,0:T(8,128)(2,1)S(1)} collective-permute-done((bf16[48,1664]{1,0:T(8,128)(2,1)S(1)}, bf16[48,1664]{1,0:T(8,128)(2,1)S(1)}, u32[]{:S(2)}, u32[]{:S(2)}) %collective-permute-start.4) | collective-permute-done | bytes 159776 | tf_op jit(solution)/shard_map/ppermute | solution.py:65
  26.7 3.4 %collective-permute-done.6.rest_7_.rest_23_.rest_11_ = bf16[48,1664]{1,0:T(8,128)(2,1)S(1)} collective-permute-done((bf16[48,1664]{1,0:T(8,128)(2,1)S(1)}, bf16[48,1664]{1,0:T(8,128)(2,1)S(1)}, u32[]{:S(2)}, u32[]{:S(2)}) %collective-permute-start.6) | collective-permute-done | bytes 159776 | tf_op jit(solution)/shard_map/ppermute | solution.py:65
  32.7 4.3 %shard_map.159 = (bf16[768,128]{1,0:T(8,128)(2,1)}, bf16[128,384]{1,0:T(8,128)(2,1)}, bf16[128,768]{1,0:T(8,128)(2,1)}, f32[8,768]{1,0:T(8,128)}) custom-call(s32[1]{0:T(128)} %bitcast.order_ref, f32[128,768]{1,0:T(8,128)} %x_ref.5, f32[128,128]{1,0:T(8,128)} %get-tuple-element.145.cos_ref, f32[128,128]{1,0:T(8,128)} %get-tuple-element.144.sin_ref, ...), custom_call_target="tpu_custom_call" | custom-call | tf_op jit(solution)/shard_map/pallas_call | solution.py:492
  36.9 3.5 %collective-permute-start.16 = (bf16[128,768]{1,0:T(8,128)(2,1)}, bf16[128,768]{1,0:T(8,128)(2,1)S(1)}, u32[]{:S(2)}, u32[]{:S(2)}) collective-permute-start(bf16[128,768]{1,0:T(8,128)(2,1)} %get-tuple-element.79.rest_0_), channel_id=1, source_target_pairs={{0,16},{8,24},{16,0},{24,8},{1,17},{9,25},{17,1},{25,9},{2,18},{10... | collective-permute-start | bytes 589832 | tf_op jit(solution)/shard_map/ppermute | solution.py:65
  41.9 15.4 %collective-permute-done.32.rest_2_ = bf16[48,1792]{1,0:T(8,128)(2,1)S(1)} collective-permute-done((bf16[48,1792]{1,0:T(8,128)(2,1)S(1)}, bf16[48,1792]{1,0:T(8,128)(2,1)S(1)}, u32[]{:S(2)}, u32[]{:S(2)}) %collective-permute-start.32) | collective-permute-done | bytes 172064 | tf_op jit(solution)/shard_map/ppermute | solution.py:65
  57.4 2.0 collective-permute-start.17
  60.1 12.8 %collective-permute-done.33.rest_3_ = bf16[48,1792]{1,0:T(8,128)(2,1)} collective-permute-done((bf16[48,1792]{1,0:T(8,128)(2,1)S(1)}, bf16[48,1792]{1,0:T(8,128)(2,1)}, u32[]{:S(2)}, u32[]{:S(2)}) %collective-permute-start.33) | collective-permute-done | bytes 172064 | tf_op jit(solution)/shard_map/ppermute | solution.py:65
  73.4 1.6 collective-permute-start.19
  75.6 5.0 %collective-permute-done.20.rest_6_ = bf16[128,768]{1,0:T(8,128)(2,1)S(1)} collective-permute-done((bf16[128,768]{1,0:T(8,128)(2,1)S(1)}, bf16[128,768]{1,0:T(8,128)(2,1)S(1)}, u32[]{:S(2)}, u32[]{:S(2)}) %collective-permute-start.20) | collective-permute-done | bytes 196640 | tf_op jit(solution)/shard_map/ppermute | solution.py:65
  81.1 3.7 %collective-permute-done.19.rest_5_ = bf16[128,768]{1,0:T(8,128)(2,1)S(1)} collective-permute-done((bf16[128,768]{1,0:T(8,128)(2,1)S(1)}, bf16[128,768]{1,0:T(8,128)(2,1)S(1)}, u32[]{:S(2)}, u32[]{:S(2)}) %collective-permute-start.19) | collective-permute-done | bytes 196640 | tf_op jit(solution)/shard_map/ppermute | solution.py:65
  84.8 2.8 %collective-permute-done.21.rest_7_ = bf16[128,768]{1,0:T(8,128)(2,1)S(1)} collective-permute-done((bf16[128,768]{1,0:T(8,128)(2,1)S(1)}, bf16[128,768]{1,0:T(8,128)(2,1)S(1)}, u32[]{:S(2)}, u32[]{:S(2)}) %collective-permute-start.21) | collective-permute-done | bytes 196640 | tf_op jit(solution)/shard_map/ppermute | solution.py:65
  88.8 1.6 collective-permute-start.35
  91.0 7.2 %shard_map.160 = (bf16[128,384]{1,0:T(8,128)(2,1)}, f32[8,256]{1,0:T(8,128)}, bf16[128,768]{1,0:T(8,128)(2,1)S(1)}) custom-call(s32[1]{0:T(128)} %bitcast.order_ref, bf16[128,384]{1,0:T(8,128)(2,1)} %get-tuple-element.78.q_ref, bf16[128,768]{1,0:T(8,128)(2,1)} %get-tuple-element.79.rest_0_, bf16[128,768]{1,0:T(8,128)(2,1)} %copy-done.22, ...), custom_call_target="tpu_custom_call" | custom-call | tf_op jit(solution)/shard_map/pallas_call | solution.py:492
  98.2 1.6 collective-permute-start.30
  100.4 1.7 collective-permute-done.37.rest_7_
  102.1 1.6 collective-permute-done.45.rest_15_
  105.2 5.3 %shard_map.161 = (f32[128,768]{1,0:T(8,128)}, bf16[128,768]{1,0:T(8,128)(2,1)}, bf16[128,768]{1,0:T(8,128)(2,1)S(1)}, bf16[128,768]{1,0:T(8,128)(2,1)}, bf16[128...) custom-call(s32[1]{0:T(128)} %bitcast.order_ref, f32[128,768]{1,0:T(8,128)} %x_ref.5, ...), custom_call_target="tpu_custom_call" | custom-call | tf_op jit(solution)/shard_map/pallas_call | solution.py:492
  110.5 1.6 collective-permute-start.46
  112.1 4.5 %collective-permute-done.46.db_ref = bf16[128,768]{1,0:T(8,128)(2,1)S(1)} collective-permute-done((bf16[128,768]{1,0:T(8,128)(2,1)S(1)}, bf16[128,768]{1,0:T(8,128)(2,1)S(1)}, u32[]{:S(2)}, u32[]{:S(2)}) %collective-permute-start.46) | collective-permute-done | bytes 196640 | tf_op jit(solution)/shard_map/ppermute | solution.py:65
  116.7 9.8 %shard_map.162 = (bf16[512,768]{1,0:T(8,128)(2,1)}, bf16[512,768]{1,0:T(8,128)(2,1)}, bf16[512,768]{1,0:T(8,128)(2,1)}, bf16[512,768]{1,0:T(8,128)(2,1)}, f32[128,768]{1,0:T(8,128)}, /*index=5*/bf16[128,384]{1,0:T(8,128)(2,1)}) custom-call(s32[1]{0:T(128)} %bitcast.order_ref, bf16[128,384]{1,0:T(8,128)(2,1)} %get-tuple-element.78.q_ref, ...), custom_call_target="tpu_custom_call" | custom-call | tf_op jit(solution)/shard_map/pallas_call | solution.py:492
  127.0 4.0 %ffngrad.1 = (bf16[192,2560]{1,0:T(8,128)(2,1)}, bf16[192,2560]{1,0:T(8,128)(2,1)}, bf16[192,2560]{1,0:T(8,128)(2,1)}, bf16[192,2560]{1,0:T(8,128)(2,1)}) custom-call(s32[1]{0:T(128)} %bitcast.order_ref, bf16[128,768]{1,0:T(8,128)(2,1)} %get-tuple-element.116.b_ref, bf16[128,1152]{1,0:T(8,128)(2,1)} %get-tuple-element.117.dz_ref, f32[128,768]{1,0:T(8,128)} %cot_ref.5, ...), custom_call_target="tpu_custom_call" | custom-call | tf_op jit(solution)/shard_map/ffngrad/pallas_call | solution.py:645
  131.0 2.8 %oqgrad.1 = (bf16[192,2560]{1,0:T(8,128)(2,1)}, bf16[192,2560]{1,0:T(8,128)(2,1)}, bf16[192,2560]{1,0:T(8,128)(2,1)}, bf16[192,2560]{1,0:T(8,128)(2,1)}) custom-call(s32[1]{0:T(128)} %bitcast.order_ref, bf16[768,128]{1,0:T(8,128)(2,1)} %get-tuple-element.77.at_ref, ...), custom_call_target="tpu_custom_call", output_to_operand_aliasing={{0}: (5, {}), {1}: (6, {}), {2}: (7, {}), {3}: (8, {})} | custom-call | tf_op jit(solution)/shard_map/oqgrad/pallas_call | solution.py:678
  134.4 2.0 pair_add.7
  139.5 3.1 %pair_add.6 = (bf16[128,768]{1,0:T(8,128)(2,1)}, bf16[128,768]{1,0:T(8,128)(2,1)}, bf16[128,768]{1,0:T(8,128)(2,1)}, bf16[128,768]{1,0:T(8,128)(2,1)}) custom-call(bf16[512,768]{1,0:T(8,128)(2,1)} %get-tuple-element.87.keep, bf16[512,768]{1,0:T(8,128)(2,1)} %collective-permute-done.47.got), custom_call_target="tpu_custom_call" | custom-call | tf_op jit(solution)/shard_map/pair_add/pallas_call | solution.py:113
  142.7 1.8 collective-permute-done.53
  147.1 2.2 pair_add.11
  149.3 3.6 %collective-permute-done.50 = bf16[128,768]{1,0:T(8,128)(2,1)S(1)} collective-permute-done((bf16[128,768]{1,0:T(8,128)(2,1)}, bf16[128,768]{1,0:T(8,128)(2,1)S(1)}, u32[]{:S(2)}, u32[]{:S(2)}) %collective-permute-start.50) | collective-permute-done | bytes 196640 | tf_op jit(solution)/shard_map/ppermute | solution.py:65
  154.6 2.2 pair_add.10
  159.2 3.2 %collective-permute-done.73 = bf16[48,2560]{1,0:T(8,128)(2,1)S(1)} collective-permute-done((bf16[48,2560]{1,0:T(8,128)(2,1)}, bf16[48,2560]{1,0:T(8,128)(2,1)S(1)}, u32[]{:S(2)}, u32[]{:S(2)}) %collective-permute-start.73) | collective-permute-done | bytes 245792 | tf_op jit(solution)/shard_map/ppermute | solution.py:65
  167.0 5.6 %collective-permute-done.55.rest_3_ = bf16[128,768]{1,0:T(8,128)(2,1)S(1)} collective-permute-done((bf16[128,768]{1,0:T(8,128)(2,1)S(1)}, bf16[128,768]{1,0:T(8,128)(2,1)S(1)}, u32[]{:S(2)}, u32[]{:S(2)}) %collective-permute-start.55) | collective-permute-done | bytes 196640 | tf_op jit(solution)/shard_map/ppermute | solution.py:65
  172.7 4.8 %shard_map.163 = (bf16[192,768]{1,0:T(8,128)(2,1)}, bf16[192,768]{1,0:T(8,128)(2,1)}, bf16[192,768]{1,0:T(8,128)(2,1)}, bf16[192,768]{1,0:T(8,128)(2,1)}, bf16[128,768]{1,0:T(8,128)(2,1)}) custom-call(s32[1]{0:T(128)} %bitcast.order_ref, bf16[768,128]{1,0:T(8,128)(2,1)} %get-tuple-element.77.at_ref, bf16[128,384]{1,0:T(8,128)(2,1)} %get-tuple-element.86.dqp_ref, ...), custom_call_target="tpu_custom_call" | custom-call | tf_op jit(solution)/shard_map/pallas_call | solution.py:492
  177.8 1.6 collective-permute-done.59.got
  179.5 1.8 pair_add.9
  184.6 1.7 pair_add.8
  188.4 1.6 collective-permute-start.65
  191.0 1.6 collective-permute-start.57
  192.6 5.5 %collective-permute-done.65 = bf16[48,768]{1,0:T(8,128)(2,1)S(1)} collective-permute-done((bf16[48,768]{1,0:T(8,128)(2,1)S(1)}, bf16[48,768]{1,0:T(8,128)(2,1)S(1)}, u32[]{:S(2)}, u32[]{:S(2)}) %collective-permute-start.65) | collective-permute-done | bytes 73760 | tf_op jit(solution)/shard_map/ppermute | solution.py:65
  198.1 1.5 collective-permute-start.56
  201.7 2.6 %collective-permute-start.66 = (bf16[48,768]{1,0:T(8,128)(2,1)S(1)}, bf16[48,768]{1,0:T(8,128)(2,1)S(1)}, u32[]{:S(2)}, u32[]{:S(2)}) collective-permute-start(bf16[48,768]{1,0:T(8,128)(2,1)S(1)} %add_convert_fusion.6), channel_id=1, source_target_pairs={{0,16},{8,24},{16,0},{24,8},{1,17},{9,25},{17,1},{25,9},{2,18},{10... | collective-permute-start | bytes 221192 | tf_op jit(solution)/shard_map/ppermute | solution.py:65
  207.0 2.2 %shard_map.165 = (f32[48,3264]{1,0:T(8,128)}, f32[2,48]{1,0:T(2,128)S(1)}) custom-call(f32[48,3264]{1,0:T(8,128)} %w_ref.5, bf16[48,768]{1,0:T(8,128)(2,1)S(1)} %copy-done.2, bf16[48,768]{1,0:T(8,128)(2,1)S(1)} %collective-permute-done.60.rest_1_, bf16[48,768]{1,0:T(8,128)(2,1)S(1)} %collective-permute-done.62.rest_2_, ...), custom_call_target="tpu_custom_call" | custom-call | tf_op jit(solution)/shard_map/pallas_call | solution.py:492
  209.7 2.6 %shard_map.164 = (f32[128,768]{1,0:T(8,128)}, f32[128,768]{1,0:T(8,128)}) custom-call(f32[128,768]{1,0:T(8,128)} %x_ref.5, bf16[128,768]{1,0:T(8,128)(2,1)} %get-tuple-element.99.da_ref, bf16[128,768]{1,0:T(8,128)(2,1)S(1)} %collective-permute-done.56.db_ref, f32[128,768]{1,0:T(8,128)} %get-tuple-element.100.dhid_ref, f32[8,768]{1,0:T(8,128)} %get-tuple-element.83.g_ref, ...), custom_call_target="tpu_custom_call" | custom-call | tf_op jit(solution)/shard_map/pallas_call | solution.py:492
  212.3 2.8 %adam.1 = (f32[48,3264]{1,0:T(8,128)}, f32[48,3264]{1,0:T(8,128)}, f32[48,3264]{1,0:T(8,128)}) custom-call(f32[48,3264]{1,0:T(8,128)} %w_ref.5, f32[48,3264]{1,0:T(8,128)} %get-tuple-element.69.g_ref, f32[48,3264]{1,0:T(8,128)} %m_ref.3, f32[48,3264]{1,0:T(8,128)} %v_ref.3), custom_call_target="tpu_custom_call" | custom-call | tf_op jit(solution)/shard_map/adam/pallas_call | solution.py:724
  (253 shorter events, 45.3 us)
Async XLA Ops:
  5.6 10.0 %collective-permute-start.1 = (bf16[48,1664]{1,0:T(8,128)(2,1)S(1)}, bf16[48,1664]{1,0:T(8,128)(2,1)S(1)}, u32[]{:S(2)}, u32[]{:S(2)}) collective-permute-start(bf16[48,1664]{1,0:T(8,128)(2,1)S(1)} %fusion.1.rest_0_.rest_16_.rest_4_), channel_id=1, source_target_pairs={{0,16},{8,24},{16,0},{24,8},{1,17},{9,25},{17,1},{25,9},{2,18},{10... | collective-permute-start | bytes 479240 | tf_op jit(solution)/shard_map/ppermute | solution.py:65
  8.2 8.0 %collective-permute-start.7 = (bf16[48,1664]{1,0:T(8,128)(2,1)S(1)}, bf16[48,1664]{1,0:T(8,128)(2,1)S(1)}, u32[]{:S(2)}, u32[]{:S(2)}) collective-permute-start(bf16[48,1664]{1,0:T(8,128)(2,1)S(1)} %fusion.1.rest_0_.rest_16_.rest_4_), channel_id=1, source_target_pairs={{0,2},{2,0},{4,6},{6,4},{1,3},{3,1},{5,7},{7,5},{8,10},{10,8},{12,... | collective-permute-start | bytes 479240 | tf_op jit(solution)/shard_map/ppermute | solution.py:65
  8.2 8.8 %collective-permute-start = (bf16[48,1664]{1,0:T(8,128)(2,1)S(1)}, bf16[48,1664]{1,0:T(8,128)(2,1)S(1)}, u32[]{:S(2)}, u32[]{:S(2)}) collective-permute-start(bf16[48,1664]{1,0:T(8,128)(2,1)S(1)} %fusion.1.rest_0_.rest_16_.rest_4_), channel_id=1, source_target_pairs={{0,8},{8,0},{16,24},{24,16},{1,9},{9,1},{17,25},{25,17},{2,10},{10... | collective-permute-start | bytes 479240 | tf_op jit(solution)/shard_map/ppermute | solution.py:65
  17.1 9.6 %collective-permute-start.4 = (bf16[48,1664]{1,0:T(8,128)(2,1)S(1)}, bf16[48,1664]{1,0:T(8,128)(2,1)S(1)}, u32[]{:S(2)}, u32[]{:S(2)}) collective-permute-start(bf16[48,1664]{1,0:T(8,128)(2,1)S(1)} %collective-permute-done.rest_1_.rest_17_.rest_5_), channel_id=1, source_target_pairs={{0,4},{2,6},{4,0},{6,2},{1,5},{3,7},{5,1},{7,3},{8,12},{10,14},{12... | collective-permute-start | bytes 479240 | tf_op jit(solution)/shard_map/ppermute | solution.py:65
  20.9 9.2 %collective-permute-start.6 = (bf16[48,1664]{1,0:T(8,128)(2,1)S(1)}, bf16[48,1664]{1,0:T(8,128)(2,1)S(1)}, u32[]{:S(2)}, u32[]{:S(2)}) collective-permute-start(bf16[48,1664]{1,0:T(8,128)(2,1)S(1)} %collective-permute-done.2.rest_3_.rest_19_.rest_7_), channel_id=1, source_target_pairs={{0,4},{2,6},{4,0},{6,2},{1,5},{3,7},{5,1},{7,3},{8,12},{10,14},{12... | collective-permute-start | bytes 479240 | tf_op jit(solution)/shard_map/ppermute | solution.py:65
  21.5 19.8 %collective-permute-start.34 = (bf16[48,1792]{1,0:T(8,128)(2,1)S(1)}, bf16[48,1792]{1,0:T(8,128)(2,1)S(1)}, u32[]{:S(2)}, u32[]{:S(2)}) collective-permute-start(bf16[48,1792]{1,0:T(8,128)(2,1)S(1)} %pad.9.rest_0_), channel_id=1, source_target_pairs={{0,4},{2,6},{4,0},{6,2},{1,5},{3,7},{5,1},{7,3},{8,12},{10,14},{12... | collective-permute-start | bytes 516104 | tf_op jit(solution)/shard_map/ppermute | solution.py:65
  23.3 8.6 %collective-permute-start.10 = (bf16[48,1664]{1,0:T(8,128)(2,1)S(1)}, bf16[48,1664]{1,0:T(8,128)(2,1)S(1)}, u32[]{:S(2)}, u32[]{:S(2)}) collective-permute-start(bf16[48,1664]{1,0:T(8,128)(2,1)S(1)} %collective-permute-done.2.rest_3_.rest_19_.rest_7_), channel_id=1, source_target_pairs={{0,2},{2,0},{4,6},{6,4},{1,3},{3,1},{5,7},{7,5},{8,10},{10,8},{12,... | collective-permute-start | bytes 479240 | tf_op jit(solution)/shard_map/ppermute | solution.py:65
  31.3 10.1 %collective-permute-start.38 = (bf16[48,1792]{1,0:T(8,128)(2,1)S(1)}, bf16[48,1792]{1,0:T(8,128)(2,1)S(1)}, u32[]{:S(2)}, u32[]{:S(2)}) collective-permute-start(bf16[48,1792]{1,0:T(8,128)(2,1)S(1)} %pad.9.rest_0_), channel_id=1, source_target_pairs={{0,2},{2,0},{4,6},{6,4},{1,3},{3,1},{5,7},{7,5},{8,10},{10,8},{12,... | collective-permute-start | bytes 516104 | tf_op jit(solution)/shard_map/ppermute | solution.py:65
  36.9 20.5 %collective-permute-start.16 = (bf16[128,768]{1,0:T(8,128)(2,1)}, bf16[128,768]{1,0:T(8,128)(2,1)S(1)}, u32[]{:S(2)}, u32[]{:S(2)}) collective-permute-start(bf16[128,768]{1,0:T(8,128)(2,1)} %get-tuple-element.79.rest_0_), channel_id=1, source_target_pairs={{0,16},{8,24},{16,0},{24,8},{1,17},{9,25},{17,1},{25,9},{2,18},{10... | collective-permute-start | bytes 589832 | tf_op jit(solution)/shard_map/ppermute | solution.py:65
  40.4 16.9 %collective-permute-start.32 = (bf16[48,1792]{1,0:T(8,128)(2,1)S(1)}, bf16[48,1792]{1,0:T(8,128)(2,1)S(1)}, u32[]{:S(2)}, u32[]{:S(2)}) collective-permute-start(bf16[48,1792]{1,0:T(8,128)(2,1)S(1)} %pad.9.rest_0_), channel_id=1, source_target_pairs={{0,16},{8,24},{16,0},{24,8},{1,17},{9,25},{17,1},{25,9},{2,18},{10... | collective-permute-start | bytes 516104 | tf_op jit(solution)/shard_map/ppermute | solution.py:65
  40.5 16.8 %collective-permute-start.31 = (bf16[48,1792]{1,0:T(8,128)(2,1)S(1)}, bf16[48,1792]{1,0:T(8,128)(2,1)}, u32[]{:S(2)}, u32[]{:S(2)}) collective-permute-start(bf16[48,1792]{1,0:T(8,128)(2,1)S(1)} %pad.9.rest_0_), channel_id=1, source_target_pairs={{0,8},{8,0},{16,24},{24,16},{1,9},{9,1},{17,25},{25,17},{2,10},{10... | collective-permute-start | bytes 516104 | tf_op jit(solution)/shard_map/ppermute | solution.py:65
  41.3 18.1 %collective-permute-start.42 = (bf16[48,1792]{1,0:T(8,128)(2,1)S(1)}, bf16[48,1792]{1,0:T(8,128)(2,1)S(1)}, u32[]{:S(2)}, u32[]{:S(2)}) collective-permute-start(bf16[48,1792]{1,0:T(8,128)(2,1)S(1)} %collective-permute-done.34.rest_4_), channel_id=1, source_target_pairs={{0,2},{2,0},{4,6},{6,4},{1,3},{3,1},{5,7},{7,5},{8,10},{10,8},{12,... | collective-permute-start | bytes 516104 | tf_op jit(solution)/shard_map/ppermute | solution.py:65
  41.4 18.7 %collective-permute-start.18 = (bf16[128,768]{1,0:T(8,128)(2,1)}, bf16[128,768]{1,0:T(8,128)(2,1)S(1)}, u32[]{:S(2)}, u32[]{:S(2)}) collective-permute-start(bf16[128,768]{1,0:T(8,128)(2,1)} %get-tuple-element.79.rest_0_), channel_id=1, source_target_pairs={{0,4},{2,6},{4,0},{6,2},{1,5},{3,7},{5,1},{7,3},{8,12},{10,14},{12... | collective-permute-start | bytes 589832 | tf_op jit(solution)/shard_map/ppermute | solution.py:65
  57.3 16.1 %collective-permute-start.22 = (bf16[128,768]{1,0:T(8,128)(2,1)}, bf16[128,768]{1,0:T(8,128)(2,1)S(1)}, u32[]{:S(2)}, u32[]{:S(2)}) collective-permute-start(bf16[128,768]{1,0:T(8,128)(2,1)} %get-tuple-element.79.rest_0_), channel_id=1, source_target_pairs={{0,2},{2,0},{4,6},{6,4},{1,3},{3,1},{5,7},{7,5},{8,10},{10,8},{12,... | collective-permute-start | bytes 589832 | tf_op jit(solution)/shard_map/ppermute | solution.py:65
  57.3 16.1 %collective-permute-start.15 = (bf16[128,768]{1,0:T(8,128)(2,1)}, bf16[128,768]{1,0:T(8,128)(2,1)S(1)}, u32[]{:S(2)}, u32[]{:S(2)}) collective-permute-start(bf16[128,768]{1,0:T(8,128)(2,1)} %get-tuple-element.79.rest_0_), channel_id=1, source_target_pairs={{0,8},{8,0},{16,24},{24,16},{1,9},{9,1},{17,25},{25,17},{2,10},{10... | collective-permute-start | bytes 589832 | tf_op jit(solution)/shard_map/ppermute | solution.py:65
  57.4 17.6 %collective-permute-start.17 = (bf16[128,768]{1,0:T(8,128)(2,1)S(1)}, bf16[128,768]{1,0:T(8,128)(2,1)S(1)}, u32[]{:S(2)}, u32[]{:S(2)}) collective-permute-start(bf16[128,768]{1,0:T(8,128)(2,1)S(1)} %collective-permute-done.16.rest_2_), channel_id=1, source_target_pairs={{0,8},{8,0},{16,24},{24,16},{1,9},{9,1},{17,25},{25,17},{2,10},{10... | collective-permute-start | bytes 589832 | tf_op jit(solution)/shard_map/ppermute | solution.py:65
  59.4 13.4 %collective-permute-start.33 = (bf16[48,1792]{1,0:T(8,128)(2,1)S(1)}, bf16[48,1792]{1,0:T(8,128)(2,1)}, u32[]{:S(2)}, u32[]{:S(2)}) collective-permute-start(bf16[48,1792]{1,0:T(8,128)(2,1)S(1)} %collective-permute-done.32.rest_2_), channel_id=1, source_target_pairs={{0,8},{8,0},{16,24},{24,16},{1,9},{9,1},{17,25},{25,17},{2,10},{10... | collective-permute-start | bytes 516104 | tf_op jit(solution)/shard_map/ppermute | solution.py:65
  60.1 15.5 %collective-permute-start.26 = (bf16[128,768]{1,0:T(8,128)(2,1)S(1)}, bf16[128,768]{1,0:T(8,128)(2,1)S(1)}, u32[]{:S(2)}, u32[]{:S(2)}) collective-permute-start(bf16[128,768]{1,0:T(8,128)(2,1)S(1)} %collective-permute-done.18.rest_4_), channel_id=1, source_target_pairs={{0,2},{2,0},{4,6},{6,4},{1,3},{3,1},{5,7},{7,5},{8,10},{10,8},{12,... | collective-permute-start | bytes 589832 | tf_op jit(solution)/shard_map/ppermute | solution.py:65
  73.4 11.4 %collective-permute-start.19 = (bf16[128,768]{1,0:T(8,128)(2,1)S(1)}, bf16[128,768]{1,0:T(8,128)(2,1)S(1)}, u32[]{:S(2)}, u32[]{:S(2)}) collective-permute-start(bf16[128,768]{1,0:T(8,128)(2,1)S(1)} %collective-permute-done.15.rest_1_), channel_id=1, source_target_pairs={{0,4},{2,6},{4,0},{6,2},{1,5},{3,7},{5,1},{7,3},{8,12},{10,14},{12... | collective-permute-start | bytes 589832 | tf_op jit(solution)/shard_map/ppermute | solution.py:65
  75.0 12.7 %collective-permute-start.21 = (bf16[128,768]{1,0:T(8,128)(2,1)S(1)}, bf16[128,768]{1,0:T(8,128)(2,1)S(1)}, u32[]{:S(2)}, u32[]{:S(2)}) collective-permute-start(bf16[128,768]{1,0:T(8,128)(2,1)S(1)} %collective-permute-done.17.rest_3_), channel_id=1, source_target_pairs={{0,4},{2,6},{4,0},{6,2},{1,5},{3,7},{5,1},{7,3},{8,12},{10,14},{12... | collective-permute-start | bytes 589832 | tf_op jit(solution)/shard_map/ppermute | solution.py:65
  75.6 12.1 %collective-permute-start.23 = (bf16[128,768]{1,0:T(8,128)(2,1)S(1)}, bf16[128,768]{1,0:T(8,128)(2,1)S(1)}, u32[]{:S(2)}, u32[]{:S(2)}) collective-permute-start(bf16[128,768]{1,0:T(8,128)(2,1)S(1)} %collective-permute-done.15.rest_1_), channel_id=1, source_target_pairs={{0,2},{2,0},{4,6},{6,4},{1,3},{3,1},{5,7},{7,5},{8,10},{10,8},{12,... | collective-permute-start | bytes 589832 | tf_op jit(solution)/shard_map/ppermute | solution.py:65
  80.6 8.1 %collective-permute-start.25 = (bf16[128,768]{1,0:T(8,128)(2,1)S(1)}, bf16[128,768]{1,0:T(8,128)(2,1)S(1)}, u32[]{:S(2)}, u32[]{:S(2)}) collective-permute-start(bf16[128,768]{1,0:T(8,128)(2,1)S(1)} %collective-permute-done.17.rest_3_), channel_id=1, source_target_pairs={{0,2},{2,0},{4,6},{6,4},{1,3},{3,1},{5,7},{7,5},{8,10},{10,8},{12,... | collective-permute-start | bytes 589832 | tf_op jit(solution)/shard_map/ppermute | solution.py:65
  87.7 10.5 %collective-permute-start.40 = (bf16[48,1792]{1,0:T(8,128)(2,1)S(1)}, bf16[48,1792]{1,0:T(8,128)(2,1)}, u32[]{:S(2)}, u32[]{:S(2)}) collective-permute-start(bf16[48,1792]{1,0:T(8,128)(2,1)S(1)} %collective-permute-done.32.rest_2_), channel_id=1, source_target_pairs={{0,2},{2,0},{4,6},{6,4},{1,3},{3,1},{5,7},{7,5},{8,10},{10,8},{12,... | collective-permute-start | bytes 516104 | tf_op jit(solution)/shard_map/ppermute | solution.py:65
  88.2 11.6 %collective-permute-start.36 = (bf16[48,1792]{1,0:T(8,128)(2,1)S(1)}, bf16[48,1792]{1,0:T(8,128)(2,1)}, u32[]{:S(2)}, u32[]{:S(2)}) collective-permute-start(bf16[48,1792]{1,0:T(8,128)(2,1)S(1)} %collective-permute-done.32.rest_2_), channel_id=1, source_target_pairs={{0,4},{2,6},{4,0},{6,2},{1,5},{3,7},{5,1},{7,3},{8,12},{10,14},{12... | collective-permute-start | bytes 516104 | tf_op jit(solution)/shard_map/ppermute | solution.py:65
  88.7 11.1 %collective-permute-start.39 = (bf16[48,1792]{1,0:T(8,128)(2,1)}, bf16[48,1792]{1,0:T(8,128)(2,1)}, u32[]{:S(2)}, u32[]{:S(2)}) collective-permute-start(bf16[48,1792]{1,0:T(8,128)(2,1)} %collective-permute-done.31.rest_1_), channel_id=1, source_target_pairs={{0,2},{2,0},{4,6},{6,4},{1,3},{3,1},{5,7},{7,5},{8,10},{10,8},{12,... | collective-permute-start | bytes 516104 | tf_op jit(solution)/shard_map/ppermute | solution.py:65
  88.8 11.6 %collective-permute-start.35 = (bf16[48,1792]{1,0:T(8,128)(2,1)}, bf16[48,1792]{1,0:T(8,128)(2,1)}, u32[]{:S(2)}, u32[]{:S(2)}) collective-permute-start(bf16[48,1792]{1,0:T(8,128)(2,1)} %collective-permute-done.31.rest_1_), channel_id=1, source_target_pairs={{0,4},{2,6},{4,0},{6,2},{1,5},{3,7},{5,1},{7,3},{8,12},{10,14},{12... | collective-permute-start | bytes 516104 | tf_op jit(solution)/shard_map/ppermute | solution.py:65
  90.3 11.7 %collective-permute-start.37 = (bf16[48,1792]{1,0:T(8,128)(2,1)}, bf16[48,1792]{1,0:T(8,128)(2,1)}, u32[]{:S(2)}, u32[]{:S(2)}) collective-permute-start(bf16[48,1792]{1,0:T(8,128)(2,1)} %collective-permute-done.33.rest_3_), channel_id=1, source_target_pairs={{0,4},{2,6},{4,0},{6,2},{1,5},{3,7},{5,1},{7,3},{8,12},{10,14},{12... | collective-permute-start | bytes 516104 | tf_op jit(solution)/shard_map/ppermute | solution.py:65
  126.4 8.0 %collective-permute-start.48 = (bf16[512,768]{1,0:T(8,128)(2,1)}, bf16[512,768]{1,0:T(8,128)(2,1)S(1)}, u32[]{:S(2)}, u32[]{:S(2)}) collective-permute-start(bf16[512,768]{1,0:T(8,128)(2,1)} %get-tuple-element.91), channel_id=1, source_target_pairs={{0,2},{2,0},{4,6},{6,4},{1,3},{3,1},{5,7},{7,5},{8,10},{10,8},{12,... | collective-permute-start | bytes 2359304 | tf_op jit(solution)/shard_map/ppermute | solution.py:65
  126.5 12.0 %collective-permute-start.47 = (bf16[512,768]{1,0:T(8,128)(2,1)}, bf16[512,768]{1,0:T(8,128)(2,1)}, u32[]{:S(2)}, u32[]{:S(2)}) collective-permute-start(bf16[512,768]{1,0:T(8,128)(2,1)} %get-tuple-element.88), channel_id=1, source_target_pairs={{0,2},{2,0},{4,6},{6,4},{1,3},{3,1},{5,7},{7,5},{8,10},{10,8},{12,... | collective-permute-start | bytes 2359304 | tf_op jit(solution)/shard_map/ppermute | solution.py:65
  133.8 12.6 %collective-permute-start.68 = (bf16[192,2560]{1,0:T(8,128)(2,1)}, bf16[192,2560]{1,0:T(8,128)(2,1)S(1)}, u32[]{:S(2)}, u32[]{:S(2)}) collective-permute-start(bf16[192,2560]{1,0:T(8,128)(2,1)} %get-tuple-element.127), channel_id=1, source_target_pairs={{0,2},{2,0},{4,6},{6,4},{1,3},{3,1},{5,7},{7,5},{8,10},{10,8},{12,... | collective-permute-start | bytes 2949128 | tf_op jit(solution)/shard_map/ppermute | solution.py:65
  134.0 20.0 %collective-permute-start.67 = (bf16[192,2560]{1,0:T(8,128)(2,1)}, bf16[192,2560]{1,0:T(8,128)(2,1)S(1)}, u32[]{:S(2)}, u32[]{:S(2)}) collective-permute-start(bf16[192,2560]{1,0:T(8,128)(2,1)} %get-tuple-element.124), channel_id=1, source_target_pairs={{0,2},{2,0},{4,6},{6,4},{1,3},{3,1},{5,7},{7,5},{8,10},{10,8},{12,... | collective-permute-start | bytes 2949128 | tf_op jit(solution)/shard_map/ppermute | solution.py:65
  136.4 8.0 %collective-permute-start.53 = (bf16[128,768]{1,0:T(8,128)(2,1)}, bf16[128,768]{1,0:T(8,128)(2,1)S(1)}, u32[]{:S(2)}, u32[]{:S(2)}) collective-permute-start(bf16[128,768]{1,0:T(8,128)(2,1)} %get-tuple-element.98), channel_id=1, source_target_pairs={{0,4},{2,6},{4,0},{6,2},{1,5},{3,7},{5,1},{7,3},{8,12},{10,14},{12... | collective-permute-start | bytes 589832 | tf_op jit(solution)/shard_map/ppermute | solution.py:65
  137.5 26.1 %collective-permute-start.49 = (bf16[128,768]{1,0:T(8,128)(2,1)}, bf16[128,768]{1,0:T(8,128)(2,1)S(1)}, u32[]{:S(2)}, u32[]{:S(2)}) collective-permute-start(bf16[128,768]{1,0:T(8,128)(2,1)} %get-tuple-element.92), channel_id=1, source_target_pairs={{0,4},{2,6},{4,0},{6,2},{1,5},{3,7},{5,1},{7,3},{8,12},{10,14},{12... | collective-permute-start | bytes 589832 | tf_op jit(solution)/shard_map/ppermute | solution.py:65
  138.5 14.4 %collective-permute-start.50 = (bf16[128,768]{1,0:T(8,128)(2,1)}, bf16[128,768]{1,0:T(8,128)(2,1)S(1)}, u32[]{:S(2)}, u32[]{:S(2)}) collective-permute-start(bf16[128,768]{1,0:T(8,128)(2,1)} %get-tuple-element.94), channel_id=1, source_target_pairs={{0,4},{2,6},{4,0},{6,2},{1,5},{3,7},{5,1},{7,3},{8,12},{10,14},{12... | collective-permute-start | bytes 589832 | tf_op jit(solution)/shard_map/ppermute | solution.py:65
  144.5 12.6 %collective-permute-start.52 = (bf16[128,768]{1,0:T(8,128)(2,1)}, bf16[128,768]{1,0:T(8,128)(2,1)S(1)}, u32[]{:S(2)}, u32[]{:S(2)}) collective-permute-start(bf16[128,768]{1,0:T(8,128)(2,1)} %get-tuple-element.96), channel_id=1, source_target_pairs={{0,4},{2,6},{4,0},{6,2},{1,5},{3,7},{5,1},{7,3},{8,12},{10,14},{12... | collective-permute-start | bytes 589832 | tf_op jit(solution)/shard_map/ppermute | solution.py:65
  146.5 11.7 %collective-permute-start.54 = (bf16[128,768]{1,0:T(8,128)(2,1)S(1)}, bf16[128,768]{1,0:T(8,128)(2,1)S(1)}, u32[]{:S(2)}, u32[]{:S(2)}) collective-permute-start(bf16[128,768]{1,0:T(8,128)(2,1)S(1)} %add_convert_fusion.4), channel_id=1, source_target_pairs={{0,8},{8,0},{16,24},{24,16},{1,9},{9,1},{17,25},{25,17},{2,10},{10... | collective-permute-start | bytes 589832 | tf_op jit(solution)/shard_map/ppermute | solution.py:65
  152.9 9.5 %collective-permute-start.73 = (bf16[48,2560]{1,0:T(8,128)(2,1)}, bf16[48,2560]{1,0:T(8,128)(2,1)S(1)}, u32[]{:S(2)}, u32[]{:S(2)}) collective-permute-start(bf16[48,2560]{1,0:T(8,128)(2,1)} %get-tuple-element.134), channel_id=1, source_target_pairs={{0,4},{2,6},{4,0},{6,2},{1,5},{3,7},{5,1},{7,3},{8,12},{10,14},{12... | collective-permute-start | bytes 737288 | tf_op jit(solution)/shard_map/ppermute | solution.py:65
  154.0 11.6 %collective-permute-start.51 = (bf16[128,768]{1,0:T(8,128)(2,1)S(1)}, bf16[128,768]{1,0:T(8,128)(2,1)S(1)}, u32[]{:S(2)}, u32[]{:S(2)}) collective-permute-start(bf16[128,768]{1,0:T(8,128)(2,1)S(1)} %add_convert_fusion.5), channel_id=1, source_target_pairs={{0,8},{8,0},{16,24},{24,16},{1,9},{9,1},{17,25},{25,17},{2,10},{10... | collective-permute-start | bytes 589832 | tf_op jit(solution)/shard_map/ppermute | solution.py:65
  157.1 43.5 %collective-permute-start.69 = (bf16[48,2560]{1,0:T(8,128)(2,1)}, bf16[48,2560]{1,0:T(8,128)(2,1)S(1)}, u32[]{:S(2)}, u32[]{:S(2)}) collective-permute-start(bf16[48,2560]{1,0:T(8,128)(2,1)} %get-tuple-element.128), channel_id=1, source_target_pairs={{0,4},{2,6},{4,0},{6,2},{1,5},{3,7},{5,1},{7,3},{8,12},{10,14},{12... | collective-permute-start | bytes 737288 | tf_op jit(solution)/shard_map/ppermute | solution.py:65
  158.1 19.4 %collective-permute-start.70 = (bf16[48,2560]{1,0:T(8,128)(2,1)}, bf16[48,2560]{1,0:T(8,128)(2,1)S(1)}, u32[]{:S(2)}, u32[]{:S(2)}) collective-permute-start(bf16[48,2560]{1,0:T(8,128)(2,1)} %get-tuple-element.130), channel_id=1, source_target_pairs={{0,4},{2,6},{4,0},{6,2},{1,5},{3,7},{5,1},{7,3},{8,12},{10,14},{12... | collective-permute-start | bytes 737288 | tf_op jit(solution)/shard_map/ppermute | solution.py:65
  162.4 10.3 %collective-permute-start.55 = (bf16[128,768]{1,0:T(8,128)(2,1)S(1)}, bf16[128,768]{1,0:T(8,128)(2,1)S(1)}, u32[]{:S(2)}, u32[]{:S(2)}) collective-permute-start(bf16[128,768]{1,0:T(8,128)(2,1)S(1)} %add_convert_fusion.3), channel_id=1, source_target_pairs={{0,16},{8,24},{16,0},{24,8},{1,17},{9,25},{17,1},{25,9},{2,18},{10... | collective-permute-start | bytes 589832 | tf_op jit(solution)/shard_map/ppermute | solution.py:65
  164.5 16.7 %collective-permute-start.72 = (bf16[48,2560]{1,0:T(8,128)(2,1)S(1)}, bf16[48,2560]{1,0:T(8,128)(2,1)S(1)}, u32[]{:S(2)}, u32[]{:S(2)}) collective-permute-start(bf16[48,2560]{1,0:T(8,128)(2,1)S(1)} %copy-done.51), channel_id=1, source_target_pairs={{0,4},{2,6},{4,0},{6,2},{1,5},{3,7},{5,1},{7,3},{8,12},{10,14},{12... | collective-permute-start | bytes 737288 | tf_op jit(solution)/shard_map/ppermute | solution.py:65
  165.6 16.8 %collective-permute-start.74 = (bf16[48,2560]{1,0:T(8,128)(2,1)S(1)}, bf16[48,2560]{1,0:T(8,128)(2,1)S(1)}, u32[]{:S(2)}, u32[]{:S(2)}) collective-permute-start(bf16[48,2560]{1,0:T(8,128)(2,1)S(1)} %add_convert_fusion.1), channel_id=1, source_target_pairs={{0,8},{8,0},{16,24},{24,16},{1,9},{9,1},{17,25},{25,17},{2,10},{10... | collective-permute-start | bytes 737288 | tf_op jit(solution)/shard_map/ppermute | solution.py:65
  177.7 24.0 %collective-permute-start.71 = (bf16[48,2560]{1,0:T(8,128)(2,1)S(1)}, bf16[48,2560]{1,0:T(8,128)(2,1)S(1)}, u32[]{:S(2)}, u32[]{:S(2)}) collective-permute-start(bf16[48,2560]{1,0:T(8,128)(2,1)S(1)} %add_convert_fusion.2), channel_id=1, source_target_pairs={{0,8},{8,0},{16,24},{24,16},{1,9},{9,1},{17,25},{25,17},{2,10},{10... | collective-permute-start | bytes 737288 | tf_op jit(solution)/shard_map/ppermute | solution.py:65
  182.4 19.3 %collective-permute-start.75 = (bf16[48,2560]{1,0:T(8,128)(2,1)S(1)}, bf16[48,2560]{1,0:T(8,128)(2,1)S(1)}, u32[]{:S(2)}, u32[]{:S(2)}) collective-permute-start(bf16[48,2560]{1,0:T(8,128)(2,1)S(1)} %add_convert_fusion), channel_id=1, source_target_pairs={{0,16},{8,24},{16,0},{24,8},{1,17},{9,25},{17,1},{25,9},{2,18},{10... | collective-permute-start | bytes 737288 | tf_op jit(solution)/shard_map/ppermute | solution.py:65
  188.4 9.7 %collective-permute-start.65 = (bf16[48,768]{1,0:T(8,128)(2,1)S(1)}, bf16[48,768]{1,0:T(8,128)(2,1)S(1)}, u32[]{:S(2)}, u32[]{:S(2)}) collective-permute-start(bf16[48,768]{1,0:T(8,128)(2,1)S(1)} %add_convert_fusion.7), channel_id=1, source_target_pairs={{0,8},{8,0},{16,24},{24,16},{1,9},{9,1},{17,25},{25,17},{2,10},{10... | collective-permute-start | bytes 221192 | tf_op jit(solution)/shard_map/ppermute | solution.py:65
  191.0 18.7 %collective-permute-start.57 = (bf16[128,768]{1,0:T(8,128)(2,1)S(1)}, bf16[128,768]{1,0:T(8,128)(2,1)S(1)}, u32[]{:S(2)}, u32[]{:S(2)}) collective-permute-start(bf16[128,768]{1,0:T(8,128)(2,1)S(1)} %copy-done.40), channel_id=1, source_target_pairs={{0,1},{1,0},{2,3},{3,2},{4,5},{5,4},{6,7},{7,6},{8,9},{9,8},{10,11... | collective-permute-start | bytes 589832 | tf_op jit(solution)/shard_map/ppermute | solution.py:65
  198.1 11.6 %collective-permute-start.56 = (bf16[128,768]{1,0:T(8,128)(2,1)S(1)}, bf16[128,768]{1,0:T(8,128)(2,1)S(1)}, u32[]{:S(2)}, u32[]{:S(2)}) collective-permute-start(bf16[128,768]{1,0:T(8,128)(2,1)S(1)} %copy-done.41), channel_id=1, source_target_pairs={{0,1},{1,0},{2,3},{3,2},{4,5},{5,4},{6,7},{7,6},{8,9},{9,8},{10,11... | collective-permute-start | bytes 589832 | tf_op jit(solution)/shard_map/ppermute | solution.py:65
  (84 other events, 699.9 us)

commit v10 on v9

--- a/solution.py
+++ b/solution.py
@@ -88,7 +88,14 @@
     return [got[j] for j in chunk_order()]
 
 
-def add_kernel(keep, got, *rest):
+def add_kernel(keep, recv, *outs):
+    for i, out in enumerate(outs):
+        rows = out.shape[0]
+        at = pl.ds(i * rows, rows)
+        out[...] = (keep[at, :].astype(F32) + recv[at, :].astype(F32)).astype(BF16)
+
+
+def add_far_kernel(keep, got, *rest):
     outs = rest[:4]
     kept, done, sems = rest[4:]
     rows = outs[0].shape[0]
@@ -108,16 +115,18 @@
         copy.wait()
 
 
-def pair_add(keep, recv):
+def pair_add(keep, recv, name):
     rows, cols = keep.shape[0] // 4, keep.shape[1]
+    close = name[0] == "d"
+    scratch = [pltpu.VMEM(keep.shape, BF16)] * 2 + [pltpu.SemaphoreType.DMA((2, 4))]
     return pl.pallas_call(
-        add_kernel,
-        out_shape=[sds((rows, cols), BF16)] * 4,
-        in_specs=[HBM, VM],
-        out_specs=[HBM] * 4,
-        scratch_shapes=[pltpu.VMEM(keep.shape, BF16)] * 2 + [pltpu.SemaphoreType.DMA((2, 4))],
+        add_kernel if close else add_far_kernel,
+        out_shape=[(near_out if close else sds)((rows, cols), BF16)] * 4,
+        in_specs=[VM if close else HBM, VM],
+        out_specs=[VM if close else HBM] * 4,
+        scratch_shapes=[] if close else scratch,
         name="pair_add",
-    )(keep, near(recv))
+    )(near(keep) if close else keep, near(recv))
 
 
 def native_sum(part):
@@ -128,10 +137,10 @@
     return [swap(groups[2 + x], "shard", 1) for x in (1, 0)][::-1]
 
 
-def scatter_sum(groups, recv):
-    s = pair_add(groups[1], recv[1])
+def scatter_sum(groups, recv, tag):
+    s = pair_add(groups[1], recv[1], f"{tag}add1")
     got = {z: swap(s[z], "shard", 2) for z in (3, 2, 1, 0)}
-    keep = pair_add(groups[0], recv[0])
+    keep = pair_add(groups[0], recv[0], f"{tag}add0")
 
     def block(z, *more):
         return total([keep[z], got[z], *more]).astype(BF16)
@@ -685,15 +694,15 @@
         name="oqgrad",
     )(order, a_t, dqp, dhid, attn, *rest_grads)
     if staged():
-        kv_terms = scatter_sum(kv_groups, pair_swap(kv_groups))
-        rest_terms = scatter_sum(rest_grads, pair_swap(rest_grads))
+        kv_terms = scatter_sum(kv_groups, pair_swap(kv_groups), "b")
+        rest_terms = scatter_sum(rest_grads, pair_swap(rest_grads), "f")
     else:
         kv_terms = native_sum(*kv_groups)
         rest_terms = native_sum(*rest_grads)
     nt = len(kv_terms)
     *w_groups, da_part = call(
         partial(qkv_grad_kernel, nw, nt, parts),
-        [sds((d // parts, 2 * width), BF16)] * parts + [sds((toks, d), BF16)],
+        [near_out((d // parts, 2 * width), BF16)] * parts + [near_out((toks, d), BF16)],
         [SM] + [VM] * 4 + [VM] * nt + [ANY] * nw,
         [pltpu.VMEM((d, 3 * width), BF16), wsem],
         [order, a_t, dqp, cos, sin] + [near(x) for x in kv_terms] + first_chunks,
@@ -704,10 +713,10 @@
         [sds((toks, d), F32)] * 2,
         [VM] * 8,
         [],
-        [inputs, da_part, near(da_other), dhid, g, hidden, ffn_part, near(ffn_other)],
+        [inputs, near(da_part), near(da_other), dhid, g, hidden, ffn_part, near(ffn_other)],
     )
     if staged():
-        first_terms = scatter_sum(w_groups, pair_swap(w_groups))
+        first_terms = scatter_sum(w_groups, pair_swap(w_groups), "d")
     else:
         first_terms = native_sum(*w_groups)
     full = weights.shape

time: 217 us -> 214 us (0.986)
  Pallas kernels: 60.1 us -> 55.9 us
  waiting for transfers between devices: 88.1 us -> 92 us
    ppermute x77, waiting for transfers between devices: 88.1 us -> 92 us  [swap(): return lax.ppermute(x, axis, [(i, i ^ bits) for i in range(size)])]
    pallas_call x6, Pallas kernels: 12.9 us -> 9.62 us  [pair_add(): pl.pallas_call(add_kernel if close else add_far_kernel, out_shape=[(near_...]
  transfers between devices with their start and end apart: 77 -> 77, of which waited for: 25 -> 27; matrix products, arithmetic and copies ran while one was open for 2% -> 2% of each run, Pallas kernels for 20% -> 19%
where the time goes in v10:
time: 214 us
  waiting for transfers between devices  92 us (43%)
  starting transfers between devices  56.1 us (26%)
  Pallas kernels  55.9 us (26%)
  other arithmetic  6.31 us (3%)
    ppermute x77, waiting for transfers between devices, swap(): return lax.ppermute(x, axis, [(i, i ^ bits) for i in range(size)])  92 us
    ppermute x77, starting transfers between devices, swap(): return lax.ppermute(x, axis, [(i, i ^ bits) for i in range(size)])  56.1 us
    pallas_call x8, Pallas kernels, call(): pl.pallas_call(kernel, out_shape=out_shape, in_specs=specs, out_specs=jax...  36.7 us
    pallas_call x6, Pallas kernels, pair_add(): pl.pallas_call(add_kernel if close else add_far_kernel, out_shape=[(near_...  9.62 us
  transfers between devices with their start and end apart: 77, of which 27 were waited for; matrix products, arithmetic and copies ran while one was open for 2% of the time, Pallas kernels for 19%

profile of v10, /device:TPU:0, one launch (start us, length us, event | category | flops | bytes accessed | tf_op | source)
XLA Modules:
  0.0 213.5 jit_solution(15906734345430242243)
XLA Ops:
  2.6 3.0 %collective-permute-start.3 = (bf16[48,1664]{1,0:T(8,128)(2,1)S(1)}, bf16[48,1664]{1,0:T(8,128)(2,1)S(1)}, u32[]{:S(2)}, u32[]{:S(2)}) collective-permute-start(bf16[48,1664]{1,0:T(8,128)(2,1)S(1)} %fusion.1.rest_0_.rest_16_.rest_4_), channel_id=1, source_target_pairs={{0,4},{2,6},{4,0},{6,2},{1,5},{3,7},{5,1},{7,3},{8,12},{10,14},{12... | collective-permute-start | bytes 479240 | tf_op jit(solution)/shard_map/ppermute | solution.py:65
  5.6 2.6 %collective-permute-start.1 = (bf16[48,1664]{1,0:T(8,128)(2,1)S(1)}, bf16[48,1664]{1,0:T(8,128)(2,1)S(1)}, u32[]{:S(2)}, u32[]{:S(2)}) collective-permute-start(bf16[48,1664]{1,0:T(8,128)(2,1)S(1)} %fusion.1.rest_0_.rest_16_.rest_4_), channel_id=1, source_target_pairs={{0,16},{8,24},{16,0},{24,8},{1,17},{9,25},{17,1},{25,9},{2,18},{10... | collective-permute-start | bytes 479240 | tf_op jit(solution)/shard_map/ppermute | solution.py:65
  8.2 1.6 collective-permute-start
  10.0 5.6 %collective-permute-done.1.rest_2_.rest_18_.rest_6_ = bf16[48,1664]{1,0:T(8,128)(2,1)S(1)} collective-permute-done((bf16[48,1664]{1,0:T(8,128)(2,1)S(1)}, bf16[48,1664]{1,0:T(8,128)(2,1)S(1)}, u32[]{:S(2)}, u32[]{:S(2)}) %collective-permute-start.1) | collective-permute-done | bytes 159776 | tf_op jit(solution)/shard_map/ppermute | solution.py:65
  18.5 2.4 %collective-permute-done.2.rest_3_.rest_19_.rest_7_ = bf16[48,1664]{1,0:T(8,128)(2,1)S(1)} collective-permute-done((bf16[48,1664]{1,0:T(8,128)(2,1)S(1)}, bf16[48,1664]{1,0:T(8,128)(2,1)S(1)}, u32[]{:S(2)}, u32[]{:S(2)}) %collective-permute-start.2) | collective-permute-done | bytes 159776 | tf_op jit(solution)/shard_map/ppermute | solution.py:65
  21.5 1.6 collective-permute-start.34
  23.8 2.9 %collective-permute-done.4.rest_5_.rest_21_.rest_9_ = bf16[48,1664]{1,0:T(8,128)(2,1)S(1)} collective-permute-done((bf16[48,1664]{1,0:T(8,128)(2,1)S(1)}, bf16[48,1664]{1,0:T(8,128)(2,1)S(1)}, u32[]{:S(2)}, u32[]{:S(2)}) %collective-permute-start.4) | collective-permute-done | bytes 159776 | tf_op jit(solution)/shard_map/ppermute | solution.py:65
  26.7 3.4 %collective-permute-done.6.rest_7_.rest_23_.rest_11_ = bf16[48,1664]{1,0:T(8,128)(2,1)S(1)} collective-permute-done((bf16[48,1664]{1,0:T(8,128)(2,1)S(1)}, bf16[48,1664]{1,0:T(8,128)(2,1)S(1)}, u32[]{:S(2)}, u32[]{:S(2)}) %collective-permute-start.6) | collective-permute-done | bytes 159776 | tf_op jit(solution)/shard_map/ppermute | solution.py:65
  32.7 4.3 %shard_map.159 = (bf16[768,128]{1,0:T(8,128)(2,1)}, bf16[128,384]{1,0:T(8,128)(2,1)}, bf16[128,768]{1,0:T(8,128)(2,1)}, f32[8,768]{1,0:T(8,128)}) custom-call(s32[1]{0:T(128)} %bitcast.order_ref, f32[128,768]{1,0:T(8,128)} %x_ref.5, f32[128,128]{1,0:T(8,128)} %get-tuple-element.145.cos_ref, f32[128,128]{1,0:T(8,128)} %get-tuple-element.144.sin_ref, ...), custom_call_target="tpu_custom_call" | custom-call | tf_op jit(solution)/shard_map/pallas_call | solution.py:501
  36.9 3.5 %collective-permute-start.16 = (bf16[128,768]{1,0:T(8,128)(2,1)}, bf16[128,768]{1,0:T(8,128)(2,1)S(1)}, u32[]{:S(2)}, u32[]{:S(2)}) collective-permute-start(bf16[128,768]{1,0:T(8,128)(2,1)} %get-tuple-element.79.rest_0_), channel_id=1, source_target_pairs={{0,16},{8,24},{16,0},{24,8},{1,17},{9,25},{17,1},{25,9},{2,18},{10... | collective-permute-start | bytes 589832 | tf_op jit(solution)/shard_map/ppermute | solution.py:65
  41.9 15.5 %collective-permute-done.32.rest_2_ = bf16[48,1792]{1,0:T(8,128)(2,1)} collective-permute-done((bf16[48,1792]{1,0:T(8,128)(2,1)S(1)}, bf16[48,1792]{1,0:T(8,128)(2,1)}, u32[]{:S(2)}, u32[]{:S(2)}) %collective-permute-start.32) | collective-permute-done | bytes 172064 | tf_op jit(solution)/shard_map/ppermute | solution.py:65
  57.5 2.0 collective-permute-start.17
  60.2 12.8 %collective-permute-done.33.rest_3_ = bf16[48,1792]{1,0:T(8,128)(2,1)} collective-permute-done((bf16[48,1792]{1,0:T(8,128)(2,1)}, bf16[48,1792]{1,0:T(8,128)(2,1)}, u32[]{:S(2)}, u32[]{:S(2)}) %collective-permute-start.33) | collective-permute-done | bytes 172064 | tf_op jit(solution)/shard_map/ppermute | solution.py:65
  73.5 1.6 collective-permute-start.19
  75.6 5.1 %collective-permute-done.20.rest_6_ = bf16[128,768]{1,0:T(8,128)(2,1)S(1)} collective-permute-done((bf16[128,768]{1,0:T(8,128)(2,1)S(1)}, bf16[128,768]{1,0:T(8,128)(2,1)S(1)}, u32[]{:S(2)}, u32[]{:S(2)}) %collective-permute-start.20) | collective-permute-done | bytes 196640 | tf_op jit(solution)/shard_map/ppermute | solution.py:65
  81.3 3.7 %collective-permute-done.19.rest_5_ = bf16[128,768]{1,0:T(8,128)(2,1)S(1)} collective-permute-done((bf16[128,768]{1,0:T(8,128)(2,1)S(1)}, bf16[128,768]{1,0:T(8,128)(2,1)S(1)}, u32[]{:S(2)}, u32[]{:S(2)}) %collective-permute-start.19) | collective-permute-done | bytes 196640 | tf_op jit(solution)/shard_map/ppermute | solution.py:65
  85.0 2.9 %collective-permute-done.21.rest_7_ = bf16[128,768]{1,0:T(8,128)(2,1)S(1)} collective-permute-done((bf16[128,768]{1,0:T(8,128)(2,1)S(1)}, bf16[128,768]{1,0:T(8,128)(2,1)S(1)}, u32[]{:S(2)}, u32[]{:S(2)}) %collective-permute-start.21) | collective-permute-done | bytes 196640 | tf_op jit(solution)/shard_map/ppermute | solution.py:65
  88.9 1.6 collective-permute-start.35
  91.2 7.1 %shard_map.160 = (bf16[128,384]{1,0:T(8,128)(2,1)}, f32[8,256]{1,0:T(8,128)}, bf16[128,768]{1,0:T(8,128)(2,1)S(1)}) custom-call(s32[1]{0:T(128)} %bitcast.order_ref, bf16[128,384]{1,0:T(8,128)(2,1)} %get-tuple-element.78.q_ref, bf16[128,768]{1,0:T(8,128)(2,1)} %get-tuple-element.79.rest_0_, bf16[128,768]{1,0:T(8,128)(2,1)} %copy-done.21, ...), custom_call_target="tpu_custom_call" | custom-call | tf_op jit(solution)/shard_map/pallas_call | solution.py:501
  98.4 1.6 collective-permute-start.30
  100.6 1.9 collective-permute-done.37.rest_7_
  102.5 1.6 collective-permute-done.45.rest_15_
  105.4 5.3 %shard_map.161 = (f32[128,768]{1,0:T(8,128)}, bf16[128,768]{1,0:T(8,128)(2,1)}, bf16[128,768]{1,0:T(8,128)(2,1)S(1)}, bf16[128,768]{1,0:T(8,128)(2,1)}, bf16[128...) custom-call(s32[1]{0:T(128)} %bitcast.order_ref, f32[128,768]{1,0:T(8,128)} %x_ref.5, ...), custom_call_target="tpu_custom_call" | custom-call | tf_op jit(solution)/shard_map/pallas_call | solution.py:501
  110.7 1.6 collective-permute-start.46
  112.3 4.7 %collective-permute-done.46.db_ref = bf16[128,768]{1,0:T(8,128)(2,1)S(1)} collective-permute-done((bf16[128,768]{1,0:T(8,128)(2,1)S(1)}, bf16[128,768]{1,0:T(8,128)(2,1)S(1)}, u32[]{:S(2)}, u32[]{:S(2)}) %collective-permute-start.46) | collective-permute-done | bytes 196640 | tf_op jit(solution)/shard_map/ppermute | solution.py:65
  117.0 9.8 %shard_map.162 = (bf16[512,768]{1,0:T(8,128)(2,1)}, bf16[512,768]{1,0:T(8,128)(2,1)}, bf16[512,768]{1,0:T(8,128)(2,1)}, bf16[512,768]{1,0:T(8,128)(2,1)}, f32[128,768]{1,0:T(8,128)}, /*index=5*/bf16[128,384]{1,0:T(8,128)(2,1)}) custom-call(s32[1]{0:T(128)} %bitcast.order_ref, bf16[128,384]{1,0:T(8,128)(2,1)} %get-tuple-element.78.q_ref, ...), custom_call_target="tpu_custom_call" | custom-call | tf_op jit(solution)/shard_map/pallas_call | solution.py:501
  127.4 4.0 %ffngrad.1 = (bf16[192,2560]{1,0:T(8,128)(2,1)}, bf16[192,2560]{1,0:T(8,128)(2,1)}, bf16[192,2560]{1,0:T(8,128)(2,1)}, bf16[192,2560]{1,0:T(8,128)(2,1)}) custom-call(s32[1]{0:T(128)} %bitcast.order_ref, bf16[128,768]{1,0:T(8,128)(2,1)} %get-tuple-element.116.b_ref, bf16[128,1152]{1,0:T(8,128)(2,1)} %get-tuple-element.117.dz_ref, f32[128,768]{1,0:T(8,128)} %cot_ref.5, ...), custom_call_target="tpu_custom_call" | custom-call | tf_op jit(solution)/shard_map/ffngrad/pallas_call | solution.py:654
  131.5 2.7 %oqgrad.1 = (bf16[192,2560]{1,0:T(8,128)(2,1)}, bf16[192,2560]{1,0:T(8,128)(2,1)}, bf16[192,2560]{1,0:T(8,128)(2,1)}, bf16[192,2560]{1,0:T(8,128)(2,1)}) custom-call(s32[1]{0:T(128)} %bitcast.order_ref, bf16[768,128]{1,0:T(8,128)(2,1)} %get-tuple-element.77.at_ref, ...), custom_call_target="tpu_custom_call", output_to_operand_aliasing={{0}: (5, {}), {1}: (6, {}), {2}: (7, {}), {3}: (8, {})} | custom-call | tf_op jit(solution)/shard_map/oqgrad/pallas_call | solution.py:687
  134.8 2.0 pair_add.7
  139.7 3.1 %pair_add.6 = (bf16[128,768]{1,0:T(8,128)(2,1)}, bf16[128,768]{1,0:T(8,128)(2,1)}, bf16[128,768]{1,0:T(8,128)(2,1)}, bf16[128,768]{1,0:T(8,128)(2,1)}) custom-call(bf16[512,768]{1,0:T(8,128)(2,1)} %get-tuple-element.87.keep, bf16[512,768]{1,0:T(8,128)(2,1)} %collective-permute-done.47.got), custom_call_target="tpu_custom_call" | custom-call | tf_op jit(solution)/shard_map/pair_add/pallas_call | solution.py:122
  142.9 2.0 collective-permute-done.53
  147.2 2.2 %pair_add.11 = (bf16[48,2560]{1,0:T(8,128)(2,1)}, bf16[48,2560]{1,0:T(8,128)(2,1)}, bf16[48,2560]{1,0:T(8,128)(2,1)}, bf16[48,2560]{1,0:T(8,128)(2,1)}) custom-call(bf16[192,2560]{1,0:T(8,128)(2,1)} %get-tuple-element.126.keep, bf16[192,2560]{1,0:T(8,128)(2,1)S(1)} %collective-permute-done.68.got), custom_call_target="tpu_custom_call" | custom-call | tf_op jit(solution)/shard_map/pair_add/pallas_call | solution.py:122
  149.4 3.8 %collective-permute-done.50 = bf16[128,768]{1,0:T(8,128)(2,1)S(1)} collective-permute-done((bf16[128,768]{1,0:T(8,128)(2,1)}, bf16[128,768]{1,0:T(8,128)(2,1)S(1)}, u32[]{:S(2)}, u32[]{:S(2)}) %collective-permute-start.50) | collective-permute-done | bytes 196640 | tf_op jit(solution)/shard_map/ppermute | solution.py:65
  154.8 2.2 %pair_add.10 = (bf16[48,2560]{1,0:T(8,128)(2,1)}, bf16[48,2560]{1,0:T(8,128)(2,1)}, bf16[48,2560]{1,0:T(8,128)(2,1)}, bf16[48,2560]{1,0:T(8,128)(2,1)}) custom-call(bf16[192,2560]{1,0:T(8,128)(2,1)} %get-tuple-element.123.keep, bf16[192,2560]{1,0:T(8,128)(2,1)S(1)} %collective-permute-done.67.got), custom_call_target="tpu_custom_call" | custom-call | tf_op jit(solution)/shard_map/pair_add/pallas_call | solution.py:122
  159.6 3.2 %collective-permute-done.73 = bf16[48,2560]{1,0:T(8,128)(2,1)S(1)} collective-permute-done((bf16[48,2560]{1,0:T(8,128)(2,1)}, bf16[48,2560]{1,0:T(8,128)(2,1)S(1)}, u32[]{:S(2)}, u32[]{:S(2)}) %collective-permute-start.73) | collective-permute-done | bytes 245792 | tf_op jit(solution)/shard_map/ppermute | solution.py:65
  164.9 1.5 collective-permute-start.74
  166.4 6.6 %collective-permute-done.55.rest_3_ = bf16[128,768]{1,0:T(8,128)(2,1)S(1)} collective-permute-done((bf16[128,768]{1,0:T(8,128)(2,1)S(1)}, bf16[128,768]{1,0:T(8,128)(2,1)S(1)}, u32[]{:S(2)}, u32[]{:S(2)}) %collective-permute-start.55) | collective-permute-done | bytes 196640 | tf_op jit(solution)/shard_map/ppermute | solution.py:65
  173.0 4.2 %shard_map.163 = (bf16[192,768]{1,0:T(8,128)(2,1)S(1)}, bf16[192,768]{1,0:T(8,128)(2,1)S(1)}, bf16[192,768]{1,0:T(8,128)(2,1)S(1)}, bf16[192,768]{1,0:T(8,128)(2,1)S(1)}, bf16[128,768]{1,0:T(8,128)(2,1)S(1)}) custom-call(s32[1]{0:T(128)} %bitcast.order_ref, bf16[768,128]{1,0:T(8,128)(2,1)} %get-tuple-element.77.at_ref, ...), custom_call_target="tpu_custom_call" | custom-call | tf_op jit(solution)/shard_map/pallas_call | solution.py:501
  181.1 2.3 %collective-permute-start.75 = (bf16[48,2560]{1,0:T(8,128)(2,1)S(1)}, bf16[48,2560]{1,0:T(8,128)(2,1)S(1)}, u32[]{:S(2)}, u32[]{:S(2)}) collective-permute-start(bf16[48,2560]{1,0:T(8,128)(2,1)S(1)} %add_convert_fusion), channel_id=1, source_target_pairs={{0,16},{8,24},{16,0},{24,8},{1,17},{9,25},{17,1},{25,9},{2,18},{10... | collective-permute-start | bytes 737288 | tf_op jit(solution)/shard_map/ppermute | solution.py:65
  185.6 2.8 %collective-permute-done.61 = bf16[48,768]{1,0:T(8,128)(2,1)S(1)} collective-permute-done((bf16[48,768]{1,0:T(8,128)(2,1)S(1)}, bf16[48,768]{1,0:T(8,128)(2,1)S(1)}, u32[]{:S(2)}, u32[]{:S(2)}) %collective-permute-start.61) | collective-permute-done | bytes 73760 | tf_op jit(solution)/shard_map/ppermute | solution.py:65
  189.2 1.5 collective-permute-start.57
  190.8 5.2 %collective-permute-done.65 = bf16[48,768]{1,0:T(8,128)(2,1)S(1)} collective-permute-done((bf16[48,768]{1,0:T(8,128)(2,1)S(1)}, bf16[48,768]{1,0:T(8,128)(2,1)S(1)}, u32[]{:S(2)}, u32[]{:S(2)}) %collective-permute-start.65) | collective-permute-done | bytes 73760 | tf_op jit(solution)/shard_map/ppermute | solution.py:65
  196.0 1.8 collective-permute-start.56
  197.8 1.4 collective-permute-start.60
  199.2 2.5 %collective-permute-start.66 = (bf16[48,768]{1,0:T(8,128)(2,1)S(1)}, bf16[48,768]{1,0:T(8,128)(2,1)S(1)}, u32[]{:S(2)}, u32[]{:S(2)}) collective-permute-start(bf16[48,768]{1,0:T(8,128)(2,1)S(1)} %add_convert_fusion.6), channel_id=1, source_target_pairs={{0,16},{8,24},{16,0},{24,8},{1,17},{9,25},{17,1},{25,9},{2,18},{10... | collective-permute-start | bytes 221192 | tf_op jit(solution)/shard_map/ppermute | solution.py:65
  204.6 2.2 %shard_map.165 = (f32[48,3264]{1,0:T(8,128)}, f32[2,48]{1,0:T(2,128)S(1)}) custom-call(f32[48,3264]{1,0:T(8,128)} %w_ref.5, bf16[48,768]{1,0:T(8,128)(2,1)S(1)} %get-tuple-element.106.rest_0_, bf16[48,768]{1,0:T(8,128)(2,1)S(1)} %collective-permute-done.60.rest_1_, bf16[48,768]{1,0:T(8,128)(2,1)S(1)} %collective-permute-done.62.rest_2_, ...), custom_call_target="tpu_custom_call" | custom-call | tf_op jit(solution)/shard_map/pallas_call | solution.py:501
  206.8 2.5 %shard_map.164 = (f32[128,768]{1,0:T(8,128)}, f32[128,768]{1,0:T(8,128)}) custom-call(f32[128,768]{1,0:T(8,128)} %x_ref.5, bf16[128,768]{1,0:T(8,128)(2,1)S(1)} %get-tuple-element.99.da_ref, bf16[128,768]{1,0:T(8,128)(2,1)S(1)} %collective-permute-done.56.db_ref, f32[128,768]{1,0:T(8,128)} %get-tuple-element.100.dhid_ref, f32[8,768]{1,0:T(8,128)} %get-tuple-element.83.g_ref, ...), custom_call_target="tpu_custom_call" | custom-call | tf_op jit(solution)/shard_map/pallas_call | solution.py:501
  209.4 2.8 %adam.1 = (f32[48,3264]{1,0:T(8,128)}, f32[48,3264]{1,0:T(8,128)}, f32[48,3264]{1,0:T(8,128)}) custom-call(f32[48,3264]{1,0:T(8,128)} %w_ref.5, f32[48,3264]{1,0:T(8,128)} %get-tuple-element.69.g_ref, f32[48,3264]{1,0:T(8,128)} %m_ref.3, f32[48,3264]{1,0:T(8,128)} %v_ref.3), custom_call_target="tpu_custom_call" | custom-call | tf_op jit(solution)/shard_map/adam/pallas_call | solution.py:733
  (237 shorter events, 39.8 us)
Async XLA Ops:
  5.6 10.0 %collective-permute-start.1 = (bf16[48,1664]{1,0:T(8,128)(2,1)S(1)}, bf16[48,1664]{1,0:T(8,128)(2,1)S(1)}, u32[]{:S(2)}, u32[]{:S(2)}) collective-permute-start(bf16[48,1664]{1,0:T(8,128)(2,1)S(1)} %fusion.1.rest_0_.rest_16_.rest_4_), channel_id=1, source_target_pairs={{0,16},{8,24},{16,0},{24,8},{1,17},{9,25},{17,1},{25,9},{2,18},{10... | collective-permute-start | bytes 479240 | tf_op jit(solution)/shard_map/ppermute | solution.py:65
  8.2 8.0 %collective-permute-start.7 = (bf16[48,1664]{1,0:T(8,128)(2,1)S(1)}, bf16[48,1664]{1,0:T(8,128)(2,1)S(1)}, u32[]{:S(2)}, u32[]{:S(2)}) collective-permute-start(bf16[48,1664]{1,0:T(8,128)(2,1)S(1)} %fusion.1.rest_0_.rest_16_.rest_4_), channel_id=1, source_target_pairs={{0,2},{2,0},{4,6},{6,4},{1,3},{3,1},{5,7},{7,5},{8,10},{10,8},{12,... | collective-permute-start | bytes 479240 | tf_op jit(solution)/shard_map/ppermute | solution.py:65
  8.2 8.8 %collective-permute-start = (bf16[48,1664]{1,0:T(8,128)(2,1)S(1)}, bf16[48,1664]{1,0:T(8,128)(2,1)S(1)}, u32[]{:S(2)}, u32[]{:S(2)}) collective-permute-start(bf16[48,1664]{1,0:T(8,128)(2,1)S(1)} %fusion.1.rest_0_.rest_16_.rest_4_), channel_id=1, source_target_pairs={{0,8},{8,0},{16,24},{24,16},{1,9},{9,1},{17,25},{25,17},{2,10},{10... | collective-permute-start | bytes 479240 | tf_op jit(solution)/shard_map/ppermute | solution.py:65
  17.1 9.6 %collective-permute-start.4 = (bf16[48,1664]{1,0:T(8,128)(2,1)S(1)}, bf16[48,1664]{1,0:T(8,128)(2,1)S(1)}, u32[]{:S(2)}, u32[]{:S(2)}) collective-permute-start(bf16[48,1664]{1,0:T(8,128)(2,1)S(1)} %collective-permute-done.rest_1_.rest_17_.rest_5_), channel_id=1, source_target_pairs={{0,4},{2,6},{4,0},{6,2},{1,5},{3,7},{5,1},{7,3},{8,12},{10,14},{12... | collective-permute-start | bytes 479240 | tf_op jit(solution)/shard_map/ppermute | solution.py:65
  20.9 9.2 %collective-permute-start.6 = (bf16[48,1664]{1,0:T(8,128)(2,1)S(1)}, bf16[48,1664]{1,0:T(8,128)(2,1)S(1)}, u32[]{:S(2)}, u32[]{:S(2)}) collective-permute-start(bf16[48,1664]{1,0:T(8,128)(2,1)S(1)} %collective-permute-done.2.rest_3_.rest_19_.rest_7_), channel_id=1, source_target_pairs={{0,4},{2,6},{4,0},{6,2},{1,5},{3,7},{5,1},{7,3},{8,12},{10,14},{12... | collective-permute-start | bytes 479240 | tf_op jit(solution)/shard_map/ppermute | solution.py:65
  21.5 19.8 %collective-permute-start.34 = (bf16[48,1792]{1,0:T(8,128)(2,1)S(1)}, bf16[48,1792]{1,0:T(8,128)(2,1)S(1)}, u32[]{:S(2)}, u32[]{:S(2)}) collective-permute-start(bf16[48,1792]{1,0:T(8,128)(2,1)S(1)} %pad.9.rest_0_), channel_id=1, source_target_pairs={{0,4},{2,6},{4,0},{6,2},{1,5},{3,7},{5,1},{7,3},{8,12},{10,14},{12... | collective-permute-start | bytes 516104 | tf_op jit(solution)/shard_map/ppermute | solution.py:65
  23.3 8.6 %collective-permute-start.10 = (bf16[48,1664]{1,0:T(8,128)(2,1)S(1)}, bf16[48,1664]{1,0:T(8,128)(2,1)S(1)}, u32[]{:S(2)}, u32[]{:S(2)}) collective-permute-start(bf16[48,1664]{1,0:T(8,128)(2,1)S(1)} %collective-permute-done.2.rest_3_.rest_19_.rest_7_), channel_id=1, source_target_pairs={{0,2},{2,0},{4,6},{6,4},{1,3},{3,1},{5,7},{7,5},{8,10},{10,8},{12,... | collective-permute-start | bytes 479240 | tf_op jit(solution)/shard_map/ppermute | solution.py:65
  23.3 7.9 %collective-permute-start.13 = (bf16[48,1664]{1,0:T(8,128)(2,1)S(1)}, bf16[48,1664]{1,0:T(8,128)(2,1)S(1)}, u32[]{:S(2)}, u32[]{:S(2)}) collective-permute-start(bf16[48,1664]{1,0:T(8,128)(2,1)S(1)} %collective-permute-done.5.rest_6_.rest_22_.rest_10_), channel_id=1, source_target_pairs={{0,2},{2,0},{4,6},{6,4},{1,3},{3,1},{5,7},{7,5},{8,10},{10,8},{12,... | collective-permute-start | bytes 479240 | tf_op jit(solution)/shard_map/ppermute | solution.py:65
  31.3 10.1 %collective-permute-start.38 = (bf16[48,1792]{1,0:T(8,128)(2,1)S(1)}, bf16[48,1792]{1,0:T(8,128)(2,1)S(1)}, u32[]{:S(2)}, u32[]{:S(2)}) collective-permute-start(bf16[48,1792]{1,0:T(8,128)(2,1)S(1)} %pad.9.rest_0_), channel_id=1, source_target_pairs={{0,2},{2,0},{4,6},{6,4},{1,3},{3,1},{5,7},{7,5},{8,10},{10,8},{12,... | collective-permute-start | bytes 516104 | tf_op jit(solution)/shard_map/ppermute | solution.py:65
  36.9 20.5 %collective-permute-start.16 = (bf16[128,768]{1,0:T(8,128)(2,1)}, bf16[128,768]{1,0:T(8,128)(2,1)S(1)}, u32[]{:S(2)}, u32[]{:S(2)}) collective-permute-start(bf16[128,768]{1,0:T(8,128)(2,1)} %get-tuple-element.79.rest_0_), channel_id=1, source_target_pairs={{0,16},{8,24},{16,0},{24,8},{1,17},{9,25},{17,1},{25,9},{2,18},{10... | collective-permute-start | bytes 589832 | tf_op jit(solution)/shard_map/ppermute | solution.py:65
  40.4 17.0 %collective-permute-start.32 = (bf16[48,1792]{1,0:T(8,128)(2,1)S(1)}, bf16[48,1792]{1,0:T(8,128)(2,1)}, u32[]{:S(2)}, u32[]{:S(2)}) collective-permute-start(bf16[48,1792]{1,0:T(8,128)(2,1)S(1)} %pad.9.rest_0_), channel_id=1, source_target_pairs={{0,16},{8,24},{16,0},{24,8},{1,17},{9,25},{17,1},{25,9},{2,18},{10... | collective-permute-start | bytes 516104 | tf_op jit(solution)/shard_map/ppermute | solution.py:65
  40.5 16.9 %collective-permute-start.31 = (bf16[48,1792]{1,0:T(8,128)(2,1)S(1)}, bf16[48,1792]{1,0:T(8,128)(2,1)}, u32[]{:S(2)}, u32[]{:S(2)}) collective-permute-start(bf16[48,1792]{1,0:T(8,128)(2,1)S(1)} %pad.9.rest_0_), channel_id=1, source_target_pairs={{0,8},{8,0},{16,24},{24,16},{1,9},{9,1},{17,25},{25,17},{2,10},{10... | collective-permute-start | bytes 516104 | tf_op jit(solution)/shard_map/ppermute | solution.py:65
  41.3 18.1 %collective-permute-start.42 = (bf16[48,1792]{1,0:T(8,128)(2,1)S(1)}, bf16[48,1792]{1,0:T(8,128)(2,1)S(1)}, u32[]{:S(2)}, u32[]{:S(2)}) collective-permute-start(bf16[48,1792]{1,0:T(8,128)(2,1)S(1)} %collective-permute-done.34.rest_4_), channel_id=1, source_target_pairs={{0,2},{2,0},{4,6},{6,4},{1,3},{3,1},{5,7},{7,5},{8,10},{10,8},{12,... | collective-permute-start | bytes 516104 | tf_op jit(solution)/shard_map/ppermute | solution.py:65
  41.4 18.8 %collective-permute-start.18 = (bf16[128,768]{1,0:T(8,128)(2,1)}, bf16[128,768]{1,0:T(8,128)(2,1)S(1)}, u32[]{:S(2)}, u32[]{:S(2)}) collective-permute-start(bf16[128,768]{1,0:T(8,128)(2,1)} %get-tuple-element.79.rest_0_), channel_id=1, source_target_pairs={{0,4},{2,6},{4,0},{6,2},{1,5},{3,7},{5,1},{7,3},{8,12},{10,14},{12... | collective-permute-start | bytes 589832 | tf_op jit(solution)/shard_map/ppermute | solution.py:65
  57.4 16.1 %collective-permute-start.22 = (bf16[128,768]{1,0:T(8,128)(2,1)}, bf16[128,768]{1,0:T(8,128)(2,1)S(1)}, u32[]{:S(2)}, u32[]{:S(2)}) collective-permute-start(bf16[128,768]{1,0:T(8,128)(2,1)} %get-tuple-element.79.rest_0_), channel_id=1, source_target_pairs={{0,2},{2,0},{4,6},{6,4},{1,3},{3,1},{5,7},{7,5},{8,10},{10,8},{12,... | collective-permute-start | bytes 589832 | tf_op jit(solution)/shard_map/ppermute | solution.py:65
  57.4 16.1 %collective-permute-start.15 = (bf16[128,768]{1,0:T(8,128)(2,1)}, bf16[128,768]{1,0:T(8,128)(2,1)S(1)}, u32[]{:S(2)}, u32[]{:S(2)}) collective-permute-start(bf16[128,768]{1,0:T(8,128)(2,1)} %get-tuple-element.79.rest_0_), channel_id=1, source_target_pairs={{0,8},{8,0},{16,24},{24,16},{1,9},{9,1},{17,25},{25,17},{2,10},{10... | collective-permute-start | bytes 589832 | tf_op jit(solution)/shard_map/ppermute | solution.py:65
  57.5 17.6 %collective-permute-start.17 = (bf16[128,768]{1,0:T(8,128)(2,1)S(1)}, bf16[128,768]{1,0:T(8,128)(2,1)S(1)}, u32[]{:S(2)}, u32[]{:S(2)}) collective-permute-start(bf16[128,768]{1,0:T(8,128)(2,1)S(1)} %collective-permute-done.16.rest_2_), channel_id=1, source_target_pairs={{0,8},{8,0},{16,24},{24,16},{1,9},{9,1},{17,25},{25,17},{2,10},{10... | collective-permute-start | bytes 589832 | tf_op jit(solution)/shard_map/ppermute | solution.py:65
  59.5 13.5 %collective-permute-start.33 = (bf16[48,1792]{1,0:T(8,128)(2,1)}, bf16[48,1792]{1,0:T(8,128)(2,1)}, u32[]{:S(2)}, u32[]{:S(2)}) collective-permute-start(bf16[48,1792]{1,0:T(8,128)(2,1)} %collective-permute-done.32.rest_2_), channel_id=1, source_target_pairs={{0,8},{8,0},{16,24},{24,16},{1,9},{9,1},{17,25},{25,17},{2,10},{10... | collective-permute-start | bytes 516104 | tf_op jit(solution)/shard_map/ppermute | solution.py:65
  60.1 15.5 %collective-permute-start.26 = (bf16[128,768]{1,0:T(8,128)(2,1)S(1)}, bf16[128,768]{1,0:T(8,128)(2,1)S(1)}, u32[]{:S(2)}, u32[]{:S(2)}) collective-permute-start(bf16[128,768]{1,0:T(8,128)(2,1)S(1)} %collective-permute-done.18.rest_4_), channel_id=1, source_target_pairs={{0,2},{2,0},{4,6},{6,4},{1,3},{3,1},{5,7},{7,5},{8,10},{10,8},{12,... | collective-permute-start | bytes 589832 | tf_op jit(solution)/shard_map/ppermute | solution.py:65
  73.5 11.4 %collective-permute-start.19 = (bf16[128,768]{1,0:T(8,128)(2,1)S(1)}, bf16[128,768]{1,0:T(8,128)(2,1)S(1)}, u32[]{:S(2)}, u32[]{:S(2)}) collective-permute-start(bf16[128,768]{1,0:T(8,128)(2,1)S(1)} %collective-permute-done.15.rest_1_), channel_id=1, source_target_pairs={{0,4},{2,6},{4,0},{6,2},{1,5},{3,7},{5,1},{7,3},{8,12},{10,14},{12... | collective-permute-start | bytes 589832 | tf_op jit(solution)/shard_map/ppermute | solution.py:65
  75.1 12.8 %collective-permute-start.21 = (bf16[128,768]{1,0:T(8,128)(2,1)S(1)}, bf16[128,768]{1,0:T(8,128)(2,1)S(1)}, u32[]{:S(2)}, u32[]{:S(2)}) collective-permute-start(bf16[128,768]{1,0:T(8,128)(2,1)S(1)} %collective-permute-done.17.rest_3_), channel_id=1, source_target_pairs={{0,4},{2,6},{4,0},{6,2},{1,5},{3,7},{5,1},{7,3},{8,12},{10,14},{12... | collective-permute-start | bytes 589832 | tf_op jit(solution)/shard_map/ppermute | solution.py:65
  75.6 12.2 %collective-permute-start.23 = (bf16[128,768]{1,0:T(8,128)(2,1)S(1)}, bf16[128,768]{1,0:T(8,128)(2,1)S(1)}, u32[]{:S(2)}, u32[]{:S(2)}) collective-permute-start(bf16[128,768]{1,0:T(8,128)(2,1)S(1)} %collective-permute-done.15.rest_1_), channel_id=1, source_target_pairs={{0,2},{2,0},{4,6},{6,4},{1,3},{3,1},{5,7},{7,5},{8,10},{10,8},{12,... | collective-permute-start | bytes 589832 | tf_op jit(solution)/shard_map/ppermute | solution.py:65
  80.8 8.1 %collective-permute-start.25 = (bf16[128,768]{1,0:T(8,128)(2,1)S(1)}, bf16[128,768]{1,0:T(8,128)(2,1)S(1)}, u32[]{:S(2)}, u32[]{:S(2)}) collective-permute-start(bf16[128,768]{1,0:T(8,128)(2,1)S(1)} %collective-permute-done.17.rest_3_), channel_id=1, source_target_pairs={{0,2},{2,0},{4,6},{6,4},{1,3},{3,1},{5,7},{7,5},{8,10},{10,8},{12,... | collective-permute-start | bytes 589832 | tf_op jit(solution)/shard_map/ppermute | solution.py:65
  87.9 10.5 %collective-permute-start.40 = (bf16[48,1792]{1,0:T(8,128)(2,1)}, bf16[48,1792]{1,0:T(8,128)(2,1)}, u32[]{:S(2)}, u32[]{:S(2)}) collective-permute-start(bf16[48,1792]{1,0:T(8,128)(2,1)} %collective-permute-done.32.rest_2_), channel_id=1, source_target_pairs={{0,2},{2,0},{4,6},{6,4},{1,3},{3,1},{5,7},{7,5},{8,10},{10,8},{12,... | collective-permute-start | bytes 516104 | tf_op jit(solution)/shard_map/ppermute | solution.py:65
  88.4 11.6 %collective-permute-start.36 = (bf16[48,1792]{1,0:T(8,128)(2,1)}, bf16[48,1792]{1,0:T(8,128)(2,1)}, u32[]{:S(2)}, u32[]{:S(2)}) collective-permute-start(bf16[48,1792]{1,0:T(8,128)(2,1)} %collective-permute-done.32.rest_2_), channel_id=1, source_target_pairs={{0,4},{2,6},{4,0},{6,2},{1,5},{3,7},{5,1},{7,3},{8,12},{10,14},{12... | collective-permute-start | bytes 516104 | tf_op jit(solution)/shard_map/ppermute | solution.py:65
  88.9 11.1 %collective-permute-start.39 = (bf16[48,1792]{1,0:T(8,128)(2,1)}, bf16[48,1792]{1,0:T(8,128)(2,1)}, u32[]{:S(2)}, u32[]{:S(2)}) collective-permute-start(bf16[48,1792]{1,0:T(8,128)(2,1)} %collective-permute-done.31.rest_1_), channel_id=1, source_target_pairs={{0,2},{2,0},{4,6},{6,4},{1,3},{3,1},{5,7},{7,5},{8,10},{10,8},{12,... | collective-permute-start | bytes 516104 | tf_op jit(solution)/shard_map/ppermute | solution.py:65
  88.9 11.6 %collective-permute-start.35 = (bf16[48,1792]{1,0:T(8,128)(2,1)}, bf16[48,1792]{1,0:T(8,128)(2,1)}, u32[]{:S(2)}, u32[]{:S(2)}) collective-permute-start(bf16[48,1792]{1,0:T(8,128)(2,1)} %collective-permute-done.31.rest_1_), channel_id=1, source_target_pairs={{0,4},{2,6},{4,0},{6,2},{1,5},{3,7},{5,1},{7,3},{8,12},{10,14},{12... | collective-permute-start | bytes 516104 | tf_op jit(solution)/shard_map/ppermute | solution.py:65
  90.5 11.9 %collective-permute-start.37 = (bf16[48,1792]{1,0:T(8,128)(2,1)}, bf16[48,1792]{1,0:T(8,128)(2,1)}, u32[]{:S(2)}, u32[]{:S(2)}) collective-permute-start(bf16[48,1792]{1,0:T(8,128)(2,1)} %collective-permute-done.33.rest_3_), channel_id=1, source_target_pairs={{0,4},{2,6},{4,0},{6,2},{1,5},{3,7},{5,1},{7,3},{8,12},{10,14},{12... | collective-permute-start | bytes 516104 | tf_op jit(solution)/shard_map/ppermute | solution.py:65
  126.8 7.9 %collective-permute-start.48 = (bf16[512,768]{1,0:T(8,128)(2,1)}, bf16[512,768]{1,0:T(8,128)(2,1)S(1)}, u32[]{:S(2)}, u32[]{:S(2)}) collective-permute-start(bf16[512,768]{1,0:T(8,128)(2,1)} %get-tuple-element.91), channel_id=1, source_target_pairs={{0,2},{2,0},{4,6},{6,4},{1,3},{3,1},{5,7},{7,5},{8,10},{10,8},{12,... | collective-permute-start | bytes 2359304 | tf_op jit(solution)/shard_map/ppermute | solution.py:65
  126.9 12.0 %collective-permute-start.47 = (bf16[512,768]{1,0:T(8,128)(2,1)}, bf16[512,768]{1,0:T(8,128)(2,1)}, u32[]{:S(2)}, u32[]{:S(2)}) collective-permute-start(bf16[512,768]{1,0:T(8,128)(2,1)} %get-tuple-element.88), channel_id=1, source_target_pairs={{0,2},{2,0},{4,6},{6,4},{1,3},{3,1},{5,7},{7,5},{8,10},{10,8},{12,... | collective-permute-start | bytes 2359304 | tf_op jit(solution)/shard_map/ppermute | solution.py:65
  134.2 12.5 %collective-permute-start.68 = (bf16[192,2560]{1,0:T(8,128)(2,1)}, bf16[192,2560]{1,0:T(8,128)(2,1)S(1)}, u32[]{:S(2)}, u32[]{:S(2)}) collective-permute-start(bf16[192,2560]{1,0:T(8,128)(2,1)} %get-tuple-element.127), channel_id=1, source_target_pairs={{0,2},{2,0},{4,6},{6,4},{1,3},{3,1},{5,7},{7,5},{8,10},{10,8},{12,... | collective-permute-start | bytes 2949128 | tf_op jit(solution)/shard_map/ppermute | solution.py:65
  134.3 19.8 %collective-permute-start.67 = (bf16[192,2560]{1,0:T(8,128)(2,1)}, bf16[192,2560]{1,0:T(8,128)(2,1)S(1)}, u32[]{:S(2)}, u32[]{:S(2)}) collective-permute-start(bf16[192,2560]{1,0:T(8,128)(2,1)} %get-tuple-element.124), channel_id=1, source_target_pairs={{0,2},{2,0},{4,6},{6,4},{1,3},{3,1},{5,7},{7,5},{8,10},{10,8},{12,... | collective-permute-start | bytes 2949128 | tf_op jit(solution)/shard_map/ppermute | solution.py:65
  136.8 8.1 %collective-permute-start.53 = (bf16[128,768]{1,0:T(8,128)(2,1)}, bf16[128,768]{1,0:T(8,128)(2,1)S(1)}, u32[]{:S(2)}, u32[]{:S(2)}) collective-permute-start(bf16[128,768]{1,0:T(8,128)(2,1)} %get-tuple-element.98), channel_id=1, source_target_pairs={{0,4},{2,6},{4,0},{6,2},{1,5},{3,7},{5,1},{7,3},{8,12},{10,14},{12... | collective-permute-start | bytes 589832 | tf_op jit(solution)/shard_map/ppermute | solution.py:65
  137.7 26.3 %collective-permute-start.49 = (bf16[128,768]{1,0:T(8,128)(2,1)}, bf16[128,768]{1,0:T(8,128)(2,1)S(1)}, u32[]{:S(2)}, u32[]{:S(2)}) collective-permute-start(bf16[128,768]{1,0:T(8,128)(2,1)} %get-tuple-element.92), channel_id=1, source_target_pairs={{0,4},{2,6},{4,0},{6,2},{1,5},{3,7},{5,1},{7,3},{8,12},{10,14},{12... | collective-permute-start | bytes 589832 | tf_op jit(solution)/shard_map/ppermute | solution.py:65
  138.9 14.4 %collective-permute-start.50 = (bf16[128,768]{1,0:T(8,128)(2,1)}, bf16[128,768]{1,0:T(8,128)(2,1)S(1)}, u32[]{:S(2)}, u32[]{:S(2)}) collective-permute-start(bf16[128,768]{1,0:T(8,128)(2,1)} %get-tuple-element.94), channel_id=1, source_target_pairs={{0,4},{2,6},{4,0},{6,2},{1,5},{3,7},{5,1},{7,3},{8,12},{10,14},{12... | collective-permute-start | bytes 589832 | tf_op jit(solution)/shard_map/ppermute | solution.py:65
  144.8 12.6 %collective-permute-start.52 = (bf16[128,768]{1,0:T(8,128)(2,1)}, bf16[128,768]{1,0:T(8,128)(2,1)S(1)}, u32[]{:S(2)}, u32[]{:S(2)}) collective-permute-start(bf16[128,768]{1,0:T(8,128)(2,1)} %get-tuple-element.96), channel_id=1, source_target_pairs={{0,4},{2,6},{4,0},{6,2},{1,5},{3,7},{5,1},{7,3},{8,12},{10,14},{12... | collective-permute-start | bytes 589832 | tf_op jit(solution)/shard_map/ppermute | solution.py:65
  146.7 11.7 %collective-permute-start.54 = (bf16[128,768]{1,0:T(8,128)(2,1)S(1)}, bf16[128,768]{1,0:T(8,128)(2,1)S(1)}, u32[]{:S(2)}, u32[]{:S(2)}) collective-permute-start(bf16[128,768]{1,0:T(8,128)(2,1)S(1)} %add_convert_fusion.4), channel_id=1, source_target_pairs={{0,8},{8,0},{16,24},{24,16},{1,9},{9,1},{17,25},{25,17},{2,10},{10... | collective-permute-start | bytes 589832 | tf_op jit(solution)/shard_map/ppermute | solution.py:65
  153.3 9.5 %collective-permute-start.73 = (bf16[48,2560]{1,0:T(8,128)(2,1)}, bf16[48,2560]{1,0:T(8,128)(2,1)S(1)}, u32[]{:S(2)}, u32[]{:S(2)}) collective-permute-start(bf16[48,2560]{1,0:T(8,128)(2,1)} %get-tuple-element.134), channel_id=1, source_target_pairs={{0,4},{2,6},{4,0},{6,2},{1,5},{3,7},{5,1},{7,3},{8,12},{10,14},{12... | collective-permute-start | bytes 737288 | tf_op jit(solution)/shard_map/ppermute | solution.py:65
  154.2 10.7 %collective-permute-start.51 = (bf16[128,768]{1,0:T(8,128)(2,1)S(1)}, bf16[128,768]{1,0:T(8,128)(2,1)S(1)}, u32[]{:S(2)}, u32[]{:S(2)}) collective-permute-start(bf16[128,768]{1,0:T(8,128)(2,1)S(1)} %add_convert_fusion.5), channel_id=1, source_target_pairs={{0,8},{8,0},{16,24},{24,16},{1,9},{9,1},{17,25},{25,17},{2,10},{10... | collective-permute-start | bytes 589832 | tf_op jit(solution)/shard_map/ppermute | solution.py:65
  157.5 40.3 %collective-permute-start.69 = (bf16[48,2560]{1,0:T(8,128)(2,1)}, bf16[48,2560]{1,0:T(8,128)(2,1)S(1)}, u32[]{:S(2)}, u32[]{:S(2)}) collective-permute-start(bf16[48,2560]{1,0:T(8,128)(2,1)} %get-tuple-element.128), channel_id=1, source_target_pairs={{0,4},{2,6},{4,0},{6,2},{1,5},{3,7},{5,1},{7,3},{8,12},{10,14},{12... | collective-permute-start | bytes 737288 | tf_op jit(solution)/shard_map/ppermute | solution.py:65
  158.3 19.0 %collective-permute-start.70 = (bf16[48,2560]{1,0:T(8,128)(2,1)}, bf16[48,2560]{1,0:T(8,128)(2,1)}, u32[]{:S(2)}, u32[]{:S(2)}) collective-permute-start(bf16[48,2560]{1,0:T(8,128)(2,1)} %get-tuple-element.130), channel_id=1, source_target_pairs={{0,4},{2,6},{4,0},{6,2},{1,5},{3,7},{5,1},{7,3},{8,12},{10,14},{12... | collective-permute-start | bytes 737288 | tf_op jit(solution)/shard_map/ppermute | solution.py:65
  162.7 10.3 %collective-permute-start.55 = (bf16[128,768]{1,0:T(8,128)(2,1)S(1)}, bf16[128,768]{1,0:T(8,128)(2,1)S(1)}, u32[]{:S(2)}, u32[]{:S(2)}) collective-permute-start(bf16[128,768]{1,0:T(8,128)(2,1)S(1)} %add_convert_fusion.3), channel_id=1, source_target_pairs={{0,16},{8,24},{16,0},{24,8},{1,17},{9,25},{17,1},{25,9},{2,18},{10... | collective-permute-start | bytes 589832 | tf_op jit(solution)/shard_map/ppermute | solution.py:65
  164.0 15.1 %collective-permute-start.72 = (bf16[48,2560]{1,0:T(8,128)(2,1)}, bf16[48,2560]{1,0:T(8,128)(2,1)}, u32[]{:S(2)}, u32[]{:S(2)}) collective-permute-start(bf16[48,2560]{1,0:T(8,128)(2,1)} %get-tuple-element.132), channel_id=1, source_target_pairs={{0,4},{2,6},{4,0},{6,2},{1,5},{3,7},{5,1},{7,3},{8,12},{10,14},{12... | collective-permute-start | bytes 737288 | tf_op jit(solution)/shard_map/ppermute | solution.py:65
  164.9 15.0 %collective-permute-start.74 = (bf16[48,2560]{1,0:T(8,128)(2,1)S(1)}, bf16[48,2560]{1,0:T(8,128)(2,1)}, u32[]{:S(2)}, u32[]{:S(2)}) collective-permute-start(bf16[48,2560]{1,0:T(8,128)(2,1)S(1)} %add_convert_fusion.1), channel_id=1, source_target_pairs={{0,8},{8,0},{16,24},{24,16},{1,9},{9,1},{17,25},{25,17},{2,10},{10... | collective-permute-start | bytes 737288 | tf_op jit(solution)/shard_map/ppermute | solution.py:65
  178.3 20.9 %collective-permute-start.71 = (bf16[48,2560]{1,0:T(8,128)(2,1)S(1)}, bf16[48,2560]{1,0:T(8,128)(2,1)S(1)}, u32[]{:S(2)}, u32[]{:S(2)}) collective-permute-start(bf16[48,2560]{1,0:T(8,128)(2,1)S(1)} %add_convert_fusion.2), channel_id=1, source_target_pairs={{0,8},{8,0},{16,24},{24,16},{1,9},{9,1},{17,25},{25,17},{2,10},{10... | collective-permute-start | bytes 737288 | tf_op jit(solution)/shard_map/ppermute | solution.py:65
  181.1 18.1 %collective-permute-start.75 = (bf16[48,2560]{1,0:T(8,128)(2,1)S(1)}, bf16[48,2560]{1,0:T(8,128)(2,1)S(1)}, u32[]{:S(2)}, u32[]{:S(2)}) collective-permute-start(bf16[48,2560]{1,0:T(8,128)(2,1)S(1)} %add_convert_fusion), channel_id=1, source_target_pairs={{0,16},{8,24},{16,0},{24,8},{1,17},{9,25},{17,1},{25,9},{2,18},{10... | collective-permute-start | bytes 737288 | tf_op jit(solution)/shard_map/ppermute | solution.py:65
  189.2 17.6 %collective-permute-start.57 = (bf16[128,768]{1,0:T(8,128)(2,1)S(1)}, bf16[128,768]{1,0:T(8,128)(2,1)S(1)}, u32[]{:S(2)}, u32[]{:S(2)}) collective-permute-start(bf16[128,768]{1,0:T(8,128)(2,1)S(1)} %copy-done.39), channel_id=1, source_target_pairs={{0,1},{1,0},{2,3},{3,2},{4,5},{5,4},{6,7},{7,6},{8,9},{9,8},{10,11... | collective-permute-start | bytes 589832 | tf_op jit(solution)/shard_map/ppermute | solution.py:65
  196.0 10.9 %collective-permute-start.56 = (bf16[128,768]{1,0:T(8,128)(2,1)S(1)}, bf16[128,768]{1,0:T(8,128)(2,1)S(1)}, u32[]{:S(2)}, u32[]{:S(2)}) collective-permute-start(bf16[128,768]{1,0:T(8,128)(2,1)S(1)} %get-tuple-element.99.da_ref), channel_id=1, source_target_pairs={{0,1},{1,0},{2,3},{3,2},{4,5},{5,4},{6,7},{7,6},{8,9},{9,8},{10,11... | collective-permute-start | bytes 589832 | tf_op jit(solution)/shard_map/ppermute | solution.py:65
  (76 other events, 646.8 us)
